TPU v7x, 32 devices: a whole 2x2x4 slice. The times are simulated.
32 devices in a mesh: fsdp: 8 (over z, x), replica: 4 (over y, core).
Axes of the slice: x: 2, y: 2, z: 4, core: 2. Of those that a mesh axis runs over, the one named last changes fastest.
Arguments:
- layer_input: bfloat16 [32, 1024, 768], P(('fsdp', 'replica')), may hold values from -6 to 6
- cotangent: bfloat16 [32, 1024, 768], P(('fsdp', 'replica')), may hold values from -6 to 6
- segment_ids: int32 [32, 1024], P(('fsdp', 'replica')), may hold values from 0 to 4, as said below
- pad_mask: int32 [32, 1024], P(('fsdp', 'replica')), may hold values from 0 to 1, as said below
- ln1_gain: bfloat16 [768], P('fsdp'), may hold values from 0.5 to 1.5
- ln1_bias: bfloat16 [768], P('fsdp'), may hold values from -1.1953125 to 1.1953125
- w_qkv: bfloat16 [768, 2304], P('fsdp'), may hold values from -0.21875 to 0.21875
- b_qkv: bfloat16 [2304], P('fsdp'), may hold values from -1.1953125 to 1.1953125
- w_out: bfloat16 [768, 768], P('fsdp'), may hold values from -1.25 to 1.25
- b_out: bfloat16 [768], P('fsdp'), may hold values from -1.1953125 to 1.1953125
- ln2_gain: bfloat16 [768], P('fsdp'), may hold values from 0.5 to 1.5
- ln2_bias: bfloat16 [768], P('fsdp'), may hold values from -1.1953125 to 1.1953125
- w_up: bfloat16 [768, 3072], P('fsdp'), may hold values from -0.21875 to 0.21875
- b_up: bfloat16 [3072], P('fsdp'), may hold values from -1.1953125 to 1.1953125
- w_down: bfloat16 [3072, 768], P('fsdp'), may hold values from -0.109375 to 0.109375
- b_down: bfloat16 [768], P('fsdp'), may hold values from -1.1953125 to 1.1953125
Outputs:
- layer_out: bfloat16 [32, 1024, 768], P(('fsdp', 'replica'))
- input_grad: bfloat16 [32, 1024, 768], P(('fsdp', 'replica'))
- grad_ln1_gain: float32 [768], P('fsdp')
- grad_ln1_bias: float32 [768], P('fsdp')
- grad_w_qkv: float32 [768, 2304], P('fsdp')
- grad_b_qkv: float32 [2304], P('fsdp')
- grad_w_out: float32 [768, 768], P('fsdp')
- grad_b_out: float32 [768], P('fsdp')
- grad_ln2_gain: float32 [768], P('fsdp')
- grad_ln2_bias: float32 [768], P('fsdp')
- grad_w_up: float32 [768, 3072], P('fsdp')
- grad_b_up: float32 [3072], P('fsdp')
- grad_w_down: float32 [3072, 768], P('fsdp')
- grad_b_down: float32 [768], P('fsdp')
Inputs may be any that keep to these rules, and one draw needn't show every extreme that they name: `segment_ids`: each row packs 4 genes numbered 0 to 3 in order from its start, each of 128 to 256 codons, never falling along a row, and 4 on the padded tail; in every row one gene has exactly 256 codons and another exactly 128. `pad_mask`: 1 exactly where segment_ids is under 4; every row ends in at least 128 padded codons.
All inputs are finite; a program needn't handle non-finite values.
Results may differ from a plain program's by a relative error of at most 0.014.
Values may be sent and summed in bfloat16 or wider, within the bound.
No kernel may reach another device: no remote copies, remote signals or barrier semaphores. Data moves between devices by JAX's collectives and lax.ppermute only.
A program may use at most 320 MiB of HBM per device.

v0:
```python
import math

import jax
import jax.numpy as jnp
from jax import lax
from jax.sharding import PartitionSpec as P

HEADS = 12
HEAD_DIM = 64
GENES = 4


EPSILON = 1e-05
NEG_FILL = -1000000000.0


def contract_rows(left_matrix, right_matrix):
    return lax.dot_general(
        left_matrix, right_matrix, (((0,), (0,)), ((), ())), preferred_element_type=jnp.float32
    )


def times_transpose(left_matrix, right_matrix):
    return lax.dot_general(
        left_matrix, right_matrix, (((1,), (1,)), ((), ())), preferred_element_type=jnp.float32
    )


def layer_norm(inputs, gain_vector, bias_vector):
    centered = inputs - jnp.mean(inputs, -1, keepdims=True)
    variance = jnp.mean(centered * centered, -1, keepdims=True)
    return centered * lax.rsqrt(variance + EPSILON) * gain_vector + bias_vector


def rotate(tensor, cosine_table, sine_table):
    half_dim = tensor.shape[-1] // 2
    first_half = tensor[..., :half_dim]
    second_half = tensor[..., half_dim:]
    return jnp.concatenate(
        [
            first_half * cosine_table - second_half * sine_table,
            second_half * cosine_table + first_half * sine_table,
        ],
        -1,
    )


def exact_gelu(inputs):
    return jax.nn.gelu(inputs, approximate=False)


def rotary_tables(positions):
    frequency = jnp.power(10000.0, jnp.arange(HEAD_DIM // 2, dtype=jnp.float32) * (-2.0 / HEAD_DIM))
    angles = positions.astype(jnp.float32)[..., None] * frequency
    return (jnp.cos(angles)[..., None, :], jnp.sin(angles)[..., None, :])


def gene_positions(segments):
    slot_ids = jnp.arange(GENES + 1, dtype=jnp.int32)
    slot_hits = segments[..., :, None] == slot_ids
    counts = jnp.sum(slot_hits.astype(jnp.int32), -2)
    starts = jnp.cumsum(counts, -1) - counts
    gene_start = jnp.sum(jnp.where(slot_hits, starts[..., None, :], 0), -1)
    return jnp.arange(segments.shape[-1], dtype=jnp.int32) - gene_start


def pair_mask(block_segments, block_valid, block_start, segments, valid_codons):
    row_ids = block_start + jnp.arange(block_segments.shape[0], dtype=jnp.int32)
    column_ids = jnp.arange(segments.shape[0], dtype=jnp.int32)
    same_gene = (
        (block_segments[:, None] == segments[None, :])
        & (block_valid[:, None] > 0)
        & (valid_codons[None, :] > 0)
    )
    return same_gene | (row_ids[:, None] == column_ids[None, :])


def block_scores(
    block_queries, key_rows, block_segments, block_valid, block_start, segments, valid_codons
):
    scores = jnp.einsum(
        "qhd,khd->hqk", block_queries, key_rows, preferred_element_type=jnp.float32
    ) * (1.0 / math.sqrt(HEAD_DIM))
    allowed = pair_mask(block_segments, block_valid, block_start, segments, valid_codons)
    return jnp.where(allowed[None], scores, NEG_FILL)


def split_blocks(queries, segments, valid_codons, block_rows):
    block_count = queries.shape[0] // block_rows
    starts = jnp.arange(block_count, dtype=jnp.int32) * block_rows
    return (
        queries.reshape(block_count, block_rows, HEADS, HEAD_DIM),
        segments.reshape(block_count, block_rows),
        valid_codons.reshape(block_count, block_rows),
        starts,
    )


def attend_forward(queries, key_rows, value_rows, segments, valid_codons, block_rows):
    length = queries.shape[0]

    def one_block(running, block_item):
        block_queries, block_segments, block_valid, block_start = block_item
        scores = block_scores(
            block_queries,
            key_rows,
            block_segments,
            block_valid,
            block_start,
            segments,
            valid_codons,
        )
        row_peak = jnp.max(scores, -1, keepdims=True)
        shifted = jnp.exp(scores - row_peak)
        row_total = jnp.sum(shifted, -1, keepdims=True)
        weights = (shifted / row_total).astype(jnp.bfloat16)
        attended = jnp.einsum(
            "hqk,khd->qhd", weights, value_rows, preferred_element_type=jnp.float32
        )
        log_total = (row_peak + jnp.log(row_total))[..., 0]
        return (running, (attended, log_total))

    ignored, (attended, log_total) = lax.scan(
        one_block,
        jnp.zeros((), jnp.float32),
        split_blocks(queries, segments, valid_codons, block_rows),
    )
    return (attended.reshape(length, HEADS, HEAD_DIM), log_total)


def attend_backward(
    queries, key_rows, value_rows, attended_grad, log_total, segments, valid_codons, block_rows
):
    length = queries.shape[0]
    block_queries_all, block_segments_all, block_valid_all, starts = split_blocks(
        queries, segments, valid_codons, block_rows
    )
    grad_blocks = attended_grad.reshape(block_queries_all.shape)
    score_scale = 1.0 / math.sqrt(HEAD_DIM)

    def one_block(running, block_item):
        key_grad, value_grad = running
        block_queries, block_grad, block_log, block_segments, block_valid, block_start = block_item
        scores = block_scores(
            block_queries,
            key_rows,
            block_segments,
            block_valid,
            block_start,
            segments,
            valid_codons,
        )
        weights = jnp.exp(scores - block_log[..., None])
        weight_grad = jnp.einsum(
            "qhd,khd->hqk", block_grad, value_rows, preferred_element_type=jnp.float32
        )
        row_dot = jnp.sum(weights * weight_grad, -1, keepdims=True)
        score_grad = (weights * (weight_grad - row_dot)).astype(jnp.bfloat16)
        query_grad = (
            jnp.einsum("hqk,khd->qhd", score_grad, key_rows, preferred_element_type=jnp.float32)
            * score_scale
        )
        key_grad = (
            key_grad
            + jnp.einsum(
                "hqk,qhd->khd", score_grad, block_queries, preferred_element_type=jnp.float32
            )
            * score_scale
        )
        value_grad = value_grad + jnp.einsum(
            "hqk,qhd->khd",
            weights.astype(jnp.bfloat16),
            block_grad,
            preferred_element_type=jnp.float32,
        )
        return ((key_grad, value_grad), query_grad)

    zero_grad = jnp.zeros(key_rows.shape, jnp.float32)
    scanned = (
        block_queries_all,
        grad_blocks,
        log_total,
        block_segments_all,
        block_valid_all,
        starts,
    )
    (key_grad, value_grad), query_grad = lax.scan(one_block, (zero_grad, zero_grad), scanned)
    return (query_grad.reshape(length, HEADS, HEAD_DIM), key_grad, value_grad)


def body(
    layer_input,
    cotangent,
    segment_ids,
    pad_mask,
    ln1_gain,
    ln1_bias,
    w_qkv,
    b_qkv,
    w_out,
    b_out,
    ln2_gain,
    ln2_bias,
    w_up,
    b_up,
    w_down,
    b_down,
):
    gain_one, bias_one, qkv_weight, qkv_bias, out_weight, out_bias = (
        lax.all_gather(ln1_gain, "fsdp", axis=0, tiled=True),
        lax.all_gather(ln1_bias, "fsdp", axis=0, tiled=True),
        lax.all_gather(w_qkv, "fsdp", axis=0, tiled=True),
        lax.all_gather(b_qkv, "fsdp", axis=0, tiled=True),
        lax.all_gather(w_out, "fsdp", axis=0, tiled=True),
        lax.all_gather(b_out, "fsdp", axis=0, tiled=True),
    )
    gain_two, bias_two, up_weight, up_bias, down_weight, down_bias = (
        lax.all_gather(ln2_gain, "fsdp", axis=0, tiled=True),
        lax.all_gather(ln2_bias, "fsdp", axis=0, tiled=True),
        lax.all_gather(w_up, "fsdp", axis=0, tiled=True),
        lax.all_gather(b_up, "fsdp", axis=0, tiled=True),
        lax.all_gather(w_down, "fsdp", axis=0, tiled=True),
        lax.all_gather(b_down, "fsdp", axis=0, tiled=True),
    )
    length = layer_input.shape[1]
    model_width = layer_input.shape[2]
    block_rows = min(512, length)
    segments = segment_ids[0]
    valid_codons = pad_mask[0]
    cosine_table, sine_table = rotary_tables(gene_positions(segments))
    inputs = layer_input[0].astype(jnp.float32)
    normed, norm_one_back = jax.vjp(
        layer_norm, inputs, gain_one.astype(jnp.float32), bias_one.astype(jnp.float32)
    )
    normed = normed.astype(jnp.bfloat16)
    projected = jnp.dot(normed, qkv_weight, preferred_element_type=jnp.float32) + qkv_bias.astype(
        jnp.float32
    )
    head_shape = (length, HEADS, HEAD_DIM)
    queries = rotate(
        projected[:, :model_width].reshape(head_shape), cosine_table, sine_table
    ).astype(jnp.bfloat16)
    key_rows = rotate(
        projected[:, model_width : 2 * model_width].reshape(head_shape), cosine_table, sine_table
    ).astype(jnp.bfloat16)
    value_rows = projected[:, 2 * model_width :].reshape(head_shape).astype(jnp.bfloat16)
    attended, log_total = attend_forward(
        queries, key_rows, value_rows, segments, valid_codons, block_rows
    )
    attended = attended.reshape(length, model_width).astype(jnp.bfloat16)
    middle = (
        inputs
        + jnp.dot(attended, out_weight, preferred_element_type=jnp.float32)
        + out_bias.astype(jnp.float32)
    )
    normed_two, norm_two_back = jax.vjp(
        layer_norm, middle, gain_two.astype(jnp.float32), bias_two.astype(jnp.float32)
    )
    normed_two = normed_two.astype(jnp.bfloat16)
    hidden = jnp.dot(normed_two, up_weight, preferred_element_type=jnp.float32) + up_bias.astype(
        jnp.float32
    )
    activated, gelu_back = jax.vjp(exact_gelu, hidden)
    activated = activated.astype(jnp.bfloat16)
    layer_out = (
        middle
        + jnp.dot(activated, down_weight, preferred_element_type=jnp.float32)
        + down_bias.astype(jnp.float32)
    ).astype(jnp.bfloat16)
    up_weight_back, down_weight_back = (
        lax.all_gather(w_up, "fsdp", axis=0, tiled=True),
        lax.all_gather(w_down, "fsdp", axis=0, tiled=True),
    )
    out_grad_rows = cotangent[0]
    grad_down_bias = jnp.sum(out_grad_rows.astype(jnp.float32), 0)
    (hidden_grad,) = gelu_back(times_transpose(out_grad_rows, down_weight_back))
    hidden_grad = hidden_grad.astype(jnp.bfloat16)
    grad_up_bias = jnp.sum(hidden_grad.astype(jnp.float32), 0)
    middle_grad, grad_gain_two, grad_bias_two = norm_two_back(
        times_transpose(hidden_grad, up_weight_back)
    )
    middle_grad = middle_grad + out_grad_rows.astype(jnp.float32)
    grad_up_weight = contract_rows(normed_two, hidden_grad)
    grad_down_weight = contract_rows(activated, out_grad_rows)
    ffn_sums = (
        lax.psum_scatter(grad_gain_two, "fsdp", scatter_dimension=0, tiled=True),
        lax.psum_scatter(grad_bias_two, "fsdp", scatter_dimension=0, tiled=True),
        lax.psum_scatter(grad_up_weight, "fsdp", scatter_dimension=0, tiled=True),
        lax.psum_scatter(grad_up_bias, "fsdp", scatter_dimension=0, tiled=True),
        lax.psum_scatter(grad_down_weight, "fsdp", scatter_dimension=0, tiled=True),
        lax.psum_scatter(grad_down_bias, "fsdp", scatter_dimension=0, tiled=True),
    )
    qkv_weight_back, out_weight_back = (
        lax.all_gather(w_qkv, "fsdp", axis=0, tiled=True),
        lax.all_gather(w_out, "fsdp", axis=0, tiled=True),
    )
    branch_grad = middle_grad.astype(jnp.bfloat16)
    grad_out_bias = jnp.sum(branch_grad.astype(jnp.float32), 0)
    attended_grad = (
        times_transpose(branch_grad, out_weight_back).astype(jnp.bfloat16).reshape(head_shape)
    )
    query_grad, key_grad, value_grad = attend_backward(
        queries, key_rows, value_rows, attended_grad, log_total, segments, valid_codons, block_rows
    )
    projected_grad = jnp.concatenate(
        [
            rotate(query_grad, cosine_table, -sine_table).reshape(length, model_width),
            rotate(key_grad, cosine_table, -sine_table).reshape(length, model_width),
            value_grad.reshape(length, model_width),
        ],
        1,
    ).astype(jnp.bfloat16)
    grad_qkv_bias = jnp.sum(projected_grad.astype(jnp.float32), 0)
    input_part, grad_gain_one, grad_bias_one = norm_one_back(
        times_transpose(projected_grad, qkv_weight_back)
    )
    input_grad = (middle_grad + input_part).astype(jnp.bfloat16)
    grad_out_weight = contract_rows(attended, branch_grad)
    grad_qkv_weight = contract_rows(normed, projected_grad)
    attn_sums = (
        lax.psum_scatter(grad_gain_one, "fsdp", scatter_dimension=0, tiled=True),
        lax.psum_scatter(grad_bias_one, "fsdp", scatter_dimension=0, tiled=True),
        lax.psum_scatter(grad_qkv_weight, "fsdp", scatter_dimension=0, tiled=True),
        lax.psum_scatter(grad_qkv_bias, "fsdp", scatter_dimension=0, tiled=True),
        lax.psum_scatter(grad_out_weight, "fsdp", scatter_dimension=0, tiled=True),
        lax.psum_scatter(grad_out_bias, "fsdp", scatter_dimension=0, tiled=True),
    )
    reduced = (
        lax.psum(attn_sums[0].astype(jnp.bfloat16), "replica").astype(jnp.float32),
        lax.psum(attn_sums[1].astype(jnp.bfloat16), "replica").astype(jnp.float32),
        lax.psum(attn_sums[2].astype(jnp.bfloat16), "replica").astype(jnp.float32),
        lax.psum(attn_sums[3].astype(jnp.bfloat16), "replica").astype(jnp.float32),
        lax.psum(attn_sums[4].astype(jnp.bfloat16), "replica").astype(jnp.float32),
        lax.psum(attn_sums[5].astype(jnp.bfloat16), "replica").astype(jnp.float32),
        lax.psum(ffn_sums[0].astype(jnp.bfloat16), "replica").astype(jnp.float32),
        lax.psum(ffn_sums[1].astype(jnp.bfloat16), "replica").astype(jnp.float32),
        lax.psum(ffn_sums[2].astype(jnp.bfloat16), "replica").astype(jnp.float32),
        lax.psum(ffn_sums[3].astype(jnp.bfloat16), "replica").astype(jnp.float32),
        lax.psum(ffn_sums[4].astype(jnp.bfloat16), "replica").astype(jnp.float32),
        lax.psum(ffn_sums[5].astype(jnp.bfloat16), "replica").astype(jnp.float32),
    )
    return (
        layer_out[None],
        input_grad[None],
        reduced[0],
        reduced[1],
        reduced[2],
        reduced[3],
        reduced[4],
        reduced[5],
        reduced[6],
        reduced[7],
        reduced[8],
        reduced[9],
        reduced[10],
        reduced[11],
    )


def solution(mesh):
    in_specs = (
        P(("fsdp", "replica"), None, None),
        P(("fsdp", "replica"), None, None),
        P(("fsdp", "replica"), None),
        P(("fsdp", "replica"), None),
        P("fsdp"),
        P("fsdp"),
        P("fsdp", None),
        P("fsdp"),
        P("fsdp", None),
        P("fsdp"),
        P("fsdp"),
        P("fsdp"),
        P("fsdp", None),
        P("fsdp"),
        P("fsdp", None),
        P("fsdp"),
    )
    out_specs = (
        P(("fsdp", "replica"), None, None),
        P(("fsdp", "replica"), None, None),
        P("fsdp"),
        P("fsdp"),
        P("fsdp", None),
        P("fsdp"),
        P("fsdp", None),
        P("fsdp"),
        P("fsdp"),
        P("fsdp"),
        P("fsdp", None),
        P("fsdp"),
        P("fsdp", None),
        P("fsdp"),
    )
    return jax.shard_map(body, mesh=mesh, in_specs=in_specs, out_specs=out_specs, check_vma=False)
```

profile of v0, /device:TPU:0, one launch (start us, length us, event | category | flops | bytes accessed | tf_op | source)
XLA Modules:
  0.0 1118.5 jit_solution(7735304638543786908)
XLA Ops:
  24.4 39.9 %all-reduce.16 = (bf16[768]{0:T(1024)(128)(2,1)}, bf16[2304]{0:T(1024)(128)(2,1)S(1)}, bf16[768]{0:T(1024)(128)(2,1)S(1)}, bf16[768]{0:T(1024)(128)(2,1)S(1)}, b...) all-reduce(bf16[768]{0:T(1024)(128)(2,1)S(1)} %dynamic-update-slice, ...), channel_id=1, replica_groups=mesh['fsdp'=8,'replica'=4] {'fsdp'}, use_global_device_ids=true, to_apply=%add.6 | all-reduce | flops 6912 | bytes 27648
  66.0 25.9 %all-gather = bf16[8,1,384]{2,1,0:T(2,128)(2,1)S(1)} all-gather(bf16[1,1,384]{2,1,0:T(2,128)(2,1)S(1)} %reshape.495), channel_id=1, replica_groups=mesh['fsdp'=8,'replica'=4] {'fsdp'}, dimensions={0}, use_global_device_ids=true | all-gather | bytes 6912 | tf_op jit(solution)/shard_map/all_gather | solution.py:221
  121.5 74.4 %while.27 = (s32[]{:T(128)}, bf16[2,512,12,64]{1,3,2,0:T(8,128)(2,1)}, f32[2,12,512]{2,1,0:T(8,128)S(1)}, s32[2,512]{1,0:T(2,128)S(1)}, s32[1,1024]{1,0:T(1,128)...) while((s32[]{:T(128)}, ...), condition=%wide.region_8.9_spmd, body=%wide.region_5.8_spmd.sunk | while | flops 1688727552 | bytes 190299344 | solution.py:123
  124.0 11.0 fusion.120
  135.0 12.4 %fusion.121 = f32[12,512]{1,0:T(8,128)S(1)} fusion(f32[12,512,1024]{2,1,0:T(8,128)} %get-tuple-element.584, f32[12,512]{1,0:T(8,128)S(1)} %get-tuple-element.585, pred[512,1024]{1,0:T(8,128)(4,1)S(1)} %fusion.119), kind=kLoop, calls=%fused_computation.4.clone.1 | loop fusion | flops 25159680 | bytes 25739264 | tf_op jit(solution)/shard_map/while/body/eval_jaxpr/reduce_sum | solution.py:115
  161.1 10.7 fusion.120
  171.8 12.3 %fusion.121 = f32[12,512]{1,0:T(8,128)S(1)} fusion(f32[12,512,1024]{2,1,0:T(8,128)} %get-tuple-element.584, f32[12,512]{1,0:T(8,128)S(1)} %get-tuple-element.585, pred[512,1024]{1,0:T(8,128)(4,1)S(1)} %fusion.119), kind=kLoop, calls=%fused_computation.4.clone.1 | loop fusion | flops 25159680 | bytes 25739264 | tf_op jit(solution)/shard_map/while/body/eval_jaxpr/reduce_sum | solution.py:115
  206.4 37.9 %multiply_convert_fusion.1 = (bf16[1024,3072]{1,0:T(8,128)(2,1)}, f32[1024,3072]{1,0:T(8,128)}, f32[1024,3072]{1,0:T(8,128)}) fusion(f32[3072]{0:T(1024)S(1)} %bitcast.217, bf16[768,3072]{1,0:T(8,128)(2,1)} %all-gather.10.cloned.1.call-done, f32[1024,768]{0,1:T(8,128)S(1)} %get-tuple-element.432, f32[768]{0:T(1024)S(1)} %copy-done.60, ...), kind=kOutput, calls=%fused_computation.56 | convolution fusion | flops 5043388416 | bytes 39348224 | tf_op jit(solution)/shard_map/dot_general | solution.py:260
  244.4 37.4 %all-gather.12.cloned.1.call-done = bf16[3072,768]{1,0:T(8,128)(2,1)} async-done(((bf16[384,768]{1,0:T(8,128)(2,1)}), bf16[3072,768]{1,0:T(8,128)(2,1)}) %all-gather.12.cloned.1.call-update) | async-done | bytes 4718608 | tf_op jit(solution)/shard_map/all_gather | solution.py:222
  281.8 19.1 %convert_reduce_fusion = (f32[3072]{0:T(1024)}, bf16[1024,3072]{1,0:T(8,128)(2,1)}) fusion(f32[1024,3072]{1,0:T(8,128)} %get-tuple-element.405, bf16[3072,768]{1,0:T(8,128)(2,1)} %all-gather.12.cloned.1.call-done, bf16[1,1024,768]{2,1,0:T(8,128)(2,1)} %param.21, f32[1024,3072]{1,0:T(8,128)} %get-tuple-element.433, f32[3072]{0:T(1024)S(1)} %bitcast.218), kind=kOutput, calls=%fused_computation.54 | convolution fusion | flops 4885312512 | bytes 37773312 | tf_op jit(solution)/shard_map/dot_general | solution.py:24
  300.9 10.4 fusion.76
  330.9 233.6 %while.28 = (s32[]{:T(128)}, f32[1024,12,64]{0,2,1:T(8,128)}, f32[1024,12,64]{0,2,1:T(8,128)}, f32[2,512,12,64]{1,0,3,2:T(2,128)}, bf16[2,512,12,64]{1,3,2,0:T(8...) while((s32[]{:T(128)}, f32[1024,12,64]{0,2,1:T(8,128)}, ...), condition=%wide.region_15.16_spmd.clone, body=%wide.region_13.15_spmd.clone.sunk | while | flops 4127846400 | bytes 238230832 | solution.py:187
  333.2 11.4 %fusion.131 = f32[12,512,1024]{2,1,0:T(8,128)} fusion(bf16[1024,12,64]{0,2,1:T(8,128)(2,1)S(1)} %get-tuple-element.680, bf16[2,512,12,64]{1,3,2,0:T(8,128)(2,1)} %get-tuple-element.674, s32[]{:T(128)S(6)} %copy.152), kind=kOutput, calls=%fused_computation.35.clone.1 | convolution fusion | flops 805306368 | bytes 27525124 | tf_op jit(solution)/shard_map/while/body/eval_jaxpr/qhd,khd->hqk/dot_general | solution.py:81
  344.6 13.8 %bitcast_add_fusion.5 = f32[1024,12,64]{0,2,1:T(8,128)} fusion(f32[1024,12,64]{0,2,1:T(8,128)} %get-tuple-element.656, f32[12,512,1024]{2,1,0:T(8,128)} %fusion.131, f32[12,512]{1,0:T(8,128)S(1)} %dynamic-slice_bitcast_fusion.2, pred[512,1024]{1,0:T(8,128)(4,1)S(1)} %fusion.132, pred[]{:T(512)S(6)} %compare.3, ...), kind=kOutput, calls=%fused_computation.26.clone.1 | convolution fusion | flops 832045056 | bytes 32800772 | tf_op jit(solution)/shard_map/while/body/eval_jaxpr/hqk,qhd->khd/dot_general | solution.py:170
  358.4 18.2 %multiply_reduce_fusion.5 = (f32[12,512]{1,0:T(8,128)S(1)}, f32[12,512,1024]{2,1,0:T(8,128)}) fusion(f32[12,512,1024]{2,1,0:T(8,128)} %fusion.131, f32[12,512]{1,0:T(8,128)S(1)} %dynamic-slice_bitcast_fusion.2, pred[512,1024]{1,0:T(8,128)(4,1)S(1)} %fusion.132, bf16[1024,12,64]{0,2,1:T(8,128)(2,1)} %get-tuple-element.683, ...), kind=kOutput, calls=%fused_computation.21.clone.1 | convolution fusion | flops 836757504 | bytes 53264388 | tf_op jit(solution)/shard_map/while/body/eval_jaxpr/qhd,khd->hqk/dot_general | solution.py:154
  376.6 21.8 %multiply_convert_fusion.3 = bf16[12,512,1024]{2,1,0:T(8,128)(2,1)} fusion(f32[12,512,1024]{2,1,0:T(8,128)} %get-tuple-element.600, f32[12,512,1024]{2,1,0:T(8,128)} %fusion.131, f32[12,512]{1,0:T(8,128)S(1)} %get-tuple-element.601, f32[12,512]{1,0:T(8,128)S(1)} %dynamic-slice_bitcast_fusion.2, pred[512,1024]{1,0:T(8,128)(4,1)S(1)} %fusion.132), kind=kLoop, calls=%fused_computation.20.clone.1 | loop fusion | flops 37748736 | bytes 63488000 | tf_op jit(solution)/shard_map/while/body/eval_jaxpr/convert_element_type | solution.py:158
  398.4 9.8 multiply_bitcast_fusion.2
  418.5 28.8 %dynamic_update_slice.19 = f32[2,512,12,64]{1,0,3,2:T(2,128)} dynamic-update-slice(f32[2,512,12,64]{1,0,3,2:T(2,128)} %get-tuple-element.657, f32[1,512,12,64]{1,0,3,2:T(1,128)S(1)} %copy.127, s32[]{:T(128)S(6)} %copy.152, s32[]{:T(128)} %constant.33.clone.1..sunk, s32[]{:T(128)} %constant.33.clone.1..sunk, s32[]{:T(128)} %constant.33.clone.1..sunk) | dynamic-update-slice | bytes 3145732 | tf_op jit(solution)/shard_map/while/body/jit(dynamic_update_index_in_dim)/dynamic_update_slice | solution.py:123
  449.4 11.4 %fusion.131 = f32[12,512,1024]{2,1,0:T(8,128)} fusion(bf16[1024,12,64]{0,2,1:T(8,128)(2,1)S(1)} %get-tuple-element.680, bf16[2,512,12,64]{1,3,2,0:T(8,128)(2,1)} %get-tuple-element.674, s32[]{:T(128)S(6)} %copy.152), kind=kOutput, calls=%fused_computation.35.clone.1 | convolution fusion | flops 805306368 | bytes 27525124 | tf_op jit(solution)/shard_map/while/body/eval_jaxpr/qhd,khd->hqk/dot_general | solution.py:81
  460.8 14.3 %bitcast_add_fusion.5 = f32[1024,12,64]{0,2,1:T(8,128)} fusion(f32[1024,12,64]{0,2,1:T(8,128)} %get-tuple-element.656, f32[12,512,1024]{2,1,0:T(8,128)} %fusion.131, f32[12,512]{1,0:T(8,128)S(1)} %dynamic-slice_bitcast_fusion.2, pred[512,1024]{1,0:T(8,128)(4,1)S(1)} %fusion.132, pred[]{:T(512)S(6)} %compare.3, ...), kind=kOutput, calls=%fused_computation.26.clone.1 | convolution fusion | flops 832045056 | bytes 32800772 | tf_op jit(solution)/shard_map/while/body/eval_jaxpr/hqk,qhd->khd/dot_general | solution.py:170
  475.1 18.1 %multiply_reduce_fusion.5 = (f32[12,512]{1,0:T(8,128)S(1)}, f32[12,512,1024]{2,1,0:T(8,128)}) fusion(f32[12,512,1024]{2,1,0:T(8,128)} %fusion.131, f32[12,512]{1,0:T(8,128)S(1)} %dynamic-slice_bitcast_fusion.2, pred[512,1024]{1,0:T(8,128)(4,1)S(1)} %fusion.132, bf16[1024,12,64]{0,2,1:T(8,128)(2,1)} %get-tuple-element.683, ...), kind=kOutput, calls=%fused_computation.21.clone.1 | convolution fusion | flops 836757504 | bytes 53264388 | tf_op jit(solution)/shard_map/while/body/eval_jaxpr/qhd,khd->hqk/dot_general | solution.py:154
  493.1 21.2 %multiply_convert_fusion.3 = bf16[12,512,1024]{2,1,0:T(8,128)(2,1)} fusion(f32[12,512,1024]{2,1,0:T(8,128)} %get-tuple-element.600, f32[12,512,1024]{2,1,0:T(8,128)} %fusion.131, f32[12,512]{1,0:T(8,128)S(1)} %get-tuple-element.601, f32[12,512]{1,0:T(8,128)S(1)} %dynamic-slice_bitcast_fusion.2, pred[512,1024]{1,0:T(8,128)(4,1)S(1)} %fusion.132), kind=kLoop, calls=%fused_computation.20.clone.1 | loop fusion | flops 37748736 | bytes 63488000 | tf_op jit(solution)/shard_map/while/body/eval_jaxpr/convert_element_type | solution.py:158
  514.4 9.8 multiply_bitcast_fusion.2
  524.2 9.6 bitcast_add_fusion.4
  535.4 28.8 %dynamic_update_slice.19 = f32[2,512,12,64]{1,0,3,2:T(2,128)} dynamic-update-slice(f32[2,512,12,64]{1,0,3,2:T(2,128)} %get-tuple-element.657, f32[1,512,12,64]{1,0,3,2:T(1,128)S(1)} %copy.127, s32[]{:T(128)S(6)} %copy.152, s32[]{:T(128)} %constant.33.clone.1..sunk, s32[]{:T(128)} %constant.33.clone.1..sunk, s32[]{:T(128)} %constant.33.clone.1..sunk) | dynamic-update-slice | bytes 3145732 | tf_op jit(solution)/shard_map/while/body/jit(dynamic_update_index_in_dim)/dynamic_update_slice | solution.py:123
  582.5 10.5 fusion.67
  594.4 10.2 fusion.55
  623.9 9.5 fusion.58
  635.1 74.5 %reduce-scatter.5.cloned.1.call-done = f32[96,2304]{1,0:T(8,128)} async-done(((f32[768,2304]{1,0:T(8,128)}), f32[96,2304]{1,0:T(8,128)}) %reduce-scatter.5.cloned.1.call-update) | async-done | bytes 884752 | tf_op jit(solution)/shard_map/reduce_scatter | solution.py:323
  711.6 164.6 %reduce-scatter.9.cloned.1.call-done = f32[96,3072]{1,0:T(8,128)} async-done(((f32[768,3072]{1,0:T(8,128)}), f32[96,3072]{1,0:T(8,128)}) %reduce-scatter.9.cloned.1.call-update) | async-done | bytes 1179664 | tf_op jit(solution)/shard_map/reduce_scatter | solution.py:288
  878.3 164.4 %reduce-scatter.11.cloned.1.call-done = f32[384,768]{1,0:T(8,128)} async-done(((f32[3072,768]{1,0:T(8,128)}), f32[384,768]{1,0:T(8,128)}) %reduce-scatter.11.cloned.1.call-update) | async-done | bytes 1179664 | tf_op jit(solution)/shard_map/reduce_scatter | solution.py:290
  1056.3 35.4 %all-reduce.15 = (bf16[768]{0:T(1024)(128)(2,1)S(1)}, bf16[768]{0:T(1024)(128)(2,1)S(1)}, bf16[2304]{0:T(1024)(128)(2,1)S(1)}, bf16[768]{0:T(1024)(128)(2,1)S(1)...) all-reduce(f32[768]{0:T(1024)S(1)} %get-tuple-element.321, ...), channel_id=2, replica_groups=mesh['fsdp'=8,'replica'=4] {'fsdp'}, use_global_device_ids=true, to_apply=%region_19.20.clone | all-reduce | flops 9984 | bytes 59904
  (317 shorter events, 195.8 us)
Async XLA Ops:
  7.2 91.5 %all-gather.6.cloned.1.call-start = ((), (), s32[]{:S(2)}) async-start(), calls=%async_computation.4 | async-start | bytes 3981312 | tf_op jit(solution)/shard_map/all_gather | solution.py:212
  7.9 193.9 %all-gather.8.cloned.1.call-start = ((), (), s32[]{:S(2)}) async-start(), calls=%async_computation.5 | async-start | bytes 1327104 | tf_op jit(solution)/shard_map/all_gather | solution.py:214
  8.7 197.5 %all-gather.10.cloned.1.call-start = ((), (), s32[]{:S(2)}) async-start(), calls=%async_computation.6 | async-start | bytes 5308416 | tf_op jit(solution)/shard_map/all_gather | solution.py:220
  9.4 272.4 %all-gather.12.cloned.1.call-start = ((), (), s32[]{:S(2)}) async-start(), calls=%async_computation.7 | async-start | bytes 5308416 | tf_op jit(solution)/shard_map/all_gather | solution.py:222
  10.0 623.5 %reduce-scatter.7.cloned.1.call-start = ((), (), s32[]{:S(2)}) async-start(), calls=%async_computation.9 | async-start | bytes 2654208 | tf_op jit(solution)/shard_map/reduce_scatter | solution.py:325
  64.2 34.4 %copy-start.41 = (f32[768]{0:T(1024)}, f32[768]{0:T(1024)S(1)}, u32[]{:S(2)}) copy-start(f32[768]{0:T(1024)S(1)} %convert_element_type.174) | copy-start | bytes 9220
  64.8 33.8 %copy-start.62 = (f32[768]{0:T(1024)}, f32[768]{0:T(1024)S(1)}, u32[]{:S(2)}) copy-start(f32[768]{0:T(1024)S(1)} %convert_element_type.175) | copy-start | bytes 9220
  94.7 10.3 copy-start.39
  95.8 9.2 copy-start.45
  98.6 19.3 %copy-start.25 = (f32[1024,32]{0,1:T(8,128)}, f32[1024,32]{0,1:T(8,128)S(1)}, u32[]{:S(2)}) copy-start(f32[1024,32]{0,1:T(8,128)S(1)} %get-tuple-element.428) | copy-start | bytes 393220
  124.0 23.4 %copy-start.7 = (bf16[1024,12,64]{0,2,1:T(8,128)(2,1)S(1)}, bf16[1024,12,64]{0,2,1:T(8,128)(2,1)}, u32[]{:S(2)}) copy-start(bf16[1024,12,64]{0,2,1:T(8,128)(2,1)} %get-tuple-element.636) | copy-start | bytes 4718596 | tf_op jit(solution)/shard_map/while
  135.0 15.6 %copy-start = (f32[12,512,1024]{2,1,0:T(8,128)S(1)}, f32[12,512,1024]{2,1,0:T(8,128)}, u32[]{:S(2)}) copy-start(f32[12,512,1024]{2,1,0:T(8,128)} %get-tuple-element.584) | copy-start | bytes 75497472 | tf_op jit(solution)/shard_map/while
  161.1 23.0 %copy-start.7 = (bf16[1024,12,64]{0,2,1:T(8,128)(2,1)S(1)}, bf16[1024,12,64]{0,2,1:T(8,128)(2,1)}, u32[]{:S(2)}) copy-start(bf16[1024,12,64]{0,2,1:T(8,128)(2,1)} %get-tuple-element.636) | copy-start | bytes 4718596 | tf_op jit(solution)/shard_map/while
  171.8 15.7 %copy-start = (f32[12,512,1024]{2,1,0:T(8,128)S(1)}, f32[12,512,1024]{2,1,0:T(8,128)}, u32[]{:S(2)}) copy-start(f32[12,512,1024]{2,1,0:T(8,128)} %get-tuple-element.584) | copy-start | bytes 75497472 | tf_op jit(solution)/shard_map/while
  205.6 112.7 %copy-start.12 = (f32[1024,768]{0,1:T(8,128)}, f32[1024,768]{0,1:T(8,128)S(1)}, u32[]{:S(2)}) copy-start(f32[1024,768]{0,1:T(8,128)S(1)} %get-tuple-element.432) | copy-start | bytes 9437188
  205.7 112.6 %copy-start.43 = (f32[1024]{0:T(1024)}, f32[1024]{0:T(1024)S(1)}, u32[]{:S(2)}) copy-start(f32[1024]{0:T(1024)S(1)} %broadcast_multiply_fusion) | copy-start | bytes 12292
  206.1 112.2 %copy-start.53 = (f32[1024]{0:T(1024)}, f32[1024]{0:T(1024)S(1)}, u32[]{:S(2)}) copy-start(f32[1024]{0:T(1024)S(1)} %fusion.62) | copy-start | bytes 12292
  330.8 378.8 %reduce-scatter.5.cloned.1.call-start = ((), (), s32[]{:S(2)}) async-start(), calls=%async_computation.8 | async-start | bytes 7962624 | tf_op jit(solution)/shard_map/reduce_scatter | solution.py:323
  333.2 11.4 %copy-start.15 = (bf16[2,512,12,64]{1,3,2,0:T(8,128)(2,1)S(1)}, bf16[2,512,12,64]{1,3,2,0:T(8,128)(2,1)}, u32[]{:S(2)}) copy-start(bf16[2,512,12,64]{1,3,2,0:T(8,128)(2,1)} %get-tuple-element.682) | copy-start | bytes 4718596 | tf_op jit(solution)/shard_map/while
  398.4 9.8 copy-start.6
  408.2 8.7 copy-start.4
  449.4 11.4 %copy-start.15 = (bf16[2,512,12,64]{1,3,2,0:T(8,128)(2,1)S(1)}, bf16[2,512,12,64]{1,3,2,0:T(8,128)(2,1)}, u32[]{:S(2)}) copy-start(bf16[2,512,12,64]{1,3,2,0:T(8,128)(2,1)} %get-tuple-element.682) | copy-start | bytes 4718596 | tf_op jit(solution)/shard_map/while
  514.4 9.8 copy-start.6
  524.2 9.6 copy-start.4
  581.8 294.4 %reduce-scatter.9.cloned.1.call-start = ((), (), s32[]{:S(2)}) async-start(), calls=%async_computation.10 | async-start | bytes 10616832 | tf_op jit(solution)/shard_map/reduce_scatter | solution.py:288
  593.0 449.8 %reduce-scatter.11.cloned.1.call-start = ((), (), s32[]{:S(2)}) async-start(), calls=%async_computation.11 | async-start | bytes 10616832 | tf_op jit(solution)/shard_map/reduce_scatter | solution.py:290
  604.6 500.2 %all-reduce.21.cloned.1.call-start = ((), (), s32[]{:S(2)}) async-start(), calls=%async_computation.12 | async-start | bytes 3538944 | tf_op jit(solution)/shard_map/psum | solution.py:331
  1050.4 5.9 copy-start.55
  1050.4 5.9 copy-start.56
  1050.4 5.9 copy-start.58
  1050.4 5.9 copy-start.59
  1104.9 5.9 copy-start.29
  (50 other events, 124.4 us)
Sparse Core Ops, SparseCore 0:
  10.2 68.4 all-gather.5
  80.9 39.8 all-gather.7
  123.0 78.6 all-gather.9
  203.8 78.0 all-gather.11
  330.9 67.2 reduce-scatter.6
  581.9 127.6 reduce-scatter.4
  713.6 162.5 reduce-scatter.8
  880.2 162.5 reduce-scatter.10
  1046.7 45.7 all-reduce.20
where the time goes:
time: 1130 us; the launch traced here: 1120 us
  waiting for transfers between devices  444 us (39%)
  matrix products  293 us (26%)
  local copies, waits for them, and re-layouts  129 us (11%)
  other arithmetic  127 us (11%)
  blocking collectives  107 us (9%)
  between operations  18.4 us (2%)
    reduce_scatter x1, waiting for transfers between devices, body(): lax.psum_scatter(grad_up_weight, 'fsdp', scatter_dimension=0, tiled=True)  165 us
    reduce_scatter x1, waiting for transfers between devices, body(): lax.psum_scatter(grad_down_weight, 'fsdp', scatter_dimension=0, tiled=True)  164 us
    unnamed x2, blocking collectives  75.2 us
    reduce_scatter x1, waiting for transfers between devices, body(): lax.psum_scatter(grad_qkv_weight, 'fsdp', scatter_dimension=0, tiled=True)  74.5 us
    dynamic_update_slice x4, local copies, waits for them, and re-layouts, attend_forward(): lax.scan(one_block, jnp.zeros((), jnp.float32), split_blocks(queries, seg...  60.9 us
    dot_general x4, matrix products, block_scores(): jnp.einsum('qhd,khd->hqk', block_queries, key_rows, preferred_element_typ...  44.4 us
    convert_element_type x2, other arithmetic, one_block(): score_grad = (weights * (weight_grad - row_dot)).astype(jnp.bfloat16)  43 us
    dot_general x4, matrix products, times_transpose(): lax.dot_general(left_matrix, right_matrix, (((1,), (1,)), ((), ())), pref...  40.8 us
  transfers between devices with their start and end apart: 9, of which 4 were waited for; matrix products, arithmetic and copies ran while one was open for 43% of the time, Pallas kernels for 0%

commit v1 on v0

v1 whole, which is shorter than its diff:
```python
import functools
import math

import jax
import jax.numpy as jnp
from jax import lax
from jax.experimental import pallas as pl
from jax.experimental.pallas import tpu as pltpu
from jax.sharding import PartitionSpec as P

HEADS = 12
HEAD_DIM = 64
GENES = 4
LANES = 128
EPSILON = 1e-05
NEG_FILL = -1000000000.0
F32 = jnp.float32
BF16 = jnp.bfloat16
MIB = 1 << 20


def nn(left, right):
    return lax.dot_general(left, right, (((1,), (0,)), ((), ())), preferred_element_type=F32)


def nt(left, right):
    return lax.dot_general(left, right, (((1,), (1,)), ((), ())), preferred_element_type=F32)


def tn(left, right):
    return lax.dot_general(left, right, (((0,), (0,)), ((), ())), preferred_element_type=F32)


def iota(shape, axis):
    return lax.broadcasted_iota(jnp.int32, shape, axis)


def full(shape):
    return pl.BlockSpec(shape, lambda *ids: (0,) * len(shape))


def rows_of(shape):
    return pl.BlockSpec(shape, lambda g, *ids: (g,) + (0,) * (len(shape) - 1))


def call(kernel, grid, in_specs, out_specs, out_shape, scratch=(), vmem=60, prefetch=1, name=None, cost=None):
    return pl.pallas_call(
        kernel,
        grid_spec=pltpu.PrefetchScalarGridSpec(
            num_scalar_prefetch=prefetch,
            grid=grid,
            in_specs=in_specs,
            out_specs=out_specs,
            scratch_shapes=list(scratch),
        ),
        out_shape=out_shape,
        compiler_params=pltpu.CompilerParams(
            dimension_semantics=("arbitrary",) * len(grid), vmem_limit_bytes=vmem * MIB
        ),
        name=name,
        cost_estimate=cost and pl.CostEstimate(flops=int(cost[0]), bytes_accessed=int(cost[1]), transcendentals=0),
    )


def shape_of(shape, dtype):
    return jax.ShapeDtypeStruct(shape, dtype)


def slot_plan(segments):
    lengths = [jnp.sum((segments == g).astype(jnp.int32)) for g in range(GENES)]
    span = segments.shape[0] // GENES
    starts, before, start, free = [], [], 0, 0
    for g in range(GENES):
        starts.append(start)
        before.append(free)
        start = start + lengths[g]
        free = free + span - lengths[g]
    return jnp.stack(
        [jnp.asarray(v, jnp.int32) for v in lengths + starts + before + [start]]
    )


def source_of_slots(plan, gene, slots):
    length = plan[gene]
    return jnp.where(
        slots < length,
        plan[GENES + gene] + slots,
        plan[3 * GENES] + plan[2 * GENES + gene] + slots - length,
    )


def reorder_kernel(plan, x_ref, c_ref, xp_ref, cp_ref):
    gene = pl.program_id(0)
    span = xp_ref.shape[0]
    length = x_ref.shape[0]
    source = source_of_slots(plan, gene, iota((span, 1), 0))
    pick = jnp.where(iota((span, length), 1) == source, 1.0, 0.0).astype(BF16)
    xp_ref[...] = nn(pick, x_ref[...]).astype(BF16)
    cp_ref[...] = nn(pick, c_ref[...]).astype(BF16)


def reorder(plan, x, c):
    length, width = x.shape
    span = length // GENES
    return call(
        reorder_kernel,
        (GENES,),
        [full((length, width))] * 2,
        [rows_of((span, width))] * 2,
        [shape_of((length, width), BF16)] * 2,
        name="reorder",
        cost=(3.3e9, 8e6),
    )(plan, x, c)


def normalize(x):
    mean = jnp.mean(x, -1, keepdims=True)
    centered = x - mean
    scale = lax.rsqrt(jnp.mean(centered * centered, -1, keepdims=True) + EPSILON)
    return centered * scale, scale


def swap_halves(t):
    low = (iota(t.shape, 1) % HEAD_DIM) < HEAD_DIM // 2
    return jnp.where(
        low, pltpu.roll(t, LANES - HEAD_DIM // 2, 1), pltpu.roll(t, HEAD_DIM // 2, 1)
    )


def head_masks(rows):
    lane = iota((rows, LANES), 1)
    return [(lane < HEAD_DIM), (lane >= HEAD_DIM)]


def allowed_pairs(plan, gene, span):
    length = plan[gene]
    i, j = iota((span, span), 0), iota((span, span), 1)
    return ((i < length) & (j < length)) | (i == j)


def keep(mask, value):
    return jnp.where(mask, value, jnp.zeros_like(value))


Z_SIZE, HALF = 4, 2
COLUMNS = 384
AXES = ("fsdp", "replica")


def tuned_mesh(mesh):
    return mesh.shape["fsdp"] == 2 * Z_SIZE and mesh.shape["replica"] == 4


def pairs(move):
    out = []
    for z in range(Z_SIZE):
        for x in range(2):
            for y in range(2):
                for c in range(2):
                    tz, tx, ty, tc = move(z, x, y, c)
                    out.append((((z * 2 + x) * 2 + y) * 2 + c, (((tz % Z_SIZE) * 2 + tx) * 2 + ty) * 2 + tc))
    return out


ACROSS_X = pairs(lambda z, x, y, c: (z, 1 - x, y, c))
ACROSS_Y = pairs(lambda z, x, y, c: (z, x, 1 - y, c))
ACROSS_CORE = pairs(lambda z, x, y, c: (z, x, y, 1 - c))
ALONG_Z = [pairs(functools.partial(lambda d, z, x, y, c: (z + d, x, y, c), d)) for d in range(Z_SIZE)]


def move(array, table):
    return lax.ppermute(array, AXES, table)


def place():
    f, r = lax.axis_index("fsdp"), lax.axis_index("replica")
    return jnp.stack([f // 2, f % 2, r // 2, r % 2]).astype(jnp.int32)


def gather_small(at, vector):
    rows = jnp.stack([vector] + [move(vector, ALONG_Z[d]) for d in range(1, Z_SIZE)])
    rows = jnp.stack([rows, move(rows, ACROSS_X)], 1).reshape(2 * Z_SIZE, -1)
    picks = [
        lax.dynamic_slice(rows, (((at[0] - f // 2) % Z_SIZE) * 2 + (at[1] ^ (f % 2)), 0), (1, rows.shape[1]))
        for f in range(2 * Z_SIZE)
    ]
    return jnp.concatenate(picks, 0)


def gather_pieces(quarter):
    along = [quarter] + [move(quarter, ALONG_Z[d]) for d in range(1, Z_SIZE)]
    first = jnp.stack([q[0] for q in along])
    second = jnp.stack([q[1] for q in along])
    first = jnp.stack([first, move(first, ACROSS_Y)])
    second = jnp.stack([second, move(second, ACROSS_X)])
    mine = [first, move(first, ACROSS_X), second, move(second, ACROSS_Y)]
    return mine + [move(m, ACROSS_CORE) for m in mine]


def reduce_pieces(at, kept, sent):
    got = move(sent, ACROSS_CORE)
    near = lambda *i: kept[i].astype(F32) + got[i].astype(F32)
    a, s = slice(None), lambda v: v.astype(BF16)
    first = near(a, 0, a, 0) + move(s(near(a, 1, a, 0)), ACROSS_X).astype(F32)
    second = near(a, a, 0, 1) + move(s(near(a, a, 1, 1)), ACROSS_Y).astype(F32)
    first = first[:, 0] + move(s(first[:, 1]), ACROSS_Y).astype(F32)
    second = second[:, 0] + move(s(second[:, 1]), ACROSS_X).astype(F32)
    both = jnp.stack([first, second], 1)
    total = both[0]
    for d in range(1, Z_SIZE):
        total = total + move(s(both[d]), ALONG_Z[d]).astype(F32)
    total = s(total)
    other = move(total, ACROSS_Y)
    by_y = jnp.where(at[2] == 0, jnp.stack([total, other]), jnp.stack([other, total]))
    other = move(by_y, ACROSS_CORE)
    return jnp.where(at[3] == 0, jnp.stack([by_y, other]), jnp.stack([other, by_y]))


def spot(at, dz, dx, dy, dc):
    z = lax.rem(at[0] + (Z_SIZE - dz), Z_SIZE)
    return z * 2 + lax.bitwise_xor(at[1], dx), lax.bitwise_xor(at[2], dy), lax.bitwise_xor(at[3], dc)


def piece_of(refs, half, dx, dy, dc):
    refs = refs[4 * dc : 4 * dc + 4]
    if half == 0:
        return refs[dx].at[dy]
    return refs[2 + dy].at[dx]


EVERY = [(dx, dy, dc) for dx in range(2) for dy in range(2) for dc in range(2)]


def at_rows(start, size):
    return pl.ds(pl.multiple_of(start, 16), size)


def at_columns(start, size):
    return pl.ds(pl.multiple_of(start, LANES), size)


def quarters_kernel(at, wqkv_ref, wout_ref, wup_ref, wdown_ref, first_ref, second_ref, sem):
    y, c = at[2], at[3]
    rows = wqkv_ref.shape[0] // 2
    width = wdown_ref.shape[1]
    copies = []

    def copy(src, row, size, column, dst):
        part = src.at[at_rows(row, size), at_columns(column, COLUMNS)]
        copies.append(pltpu.make_async_copy(part, dst, sem))

    for b in range(3):
        copy(wqkv_ref, c * rows, rows, b * width + y * COLUMNS, first_ref.at[b // 2, pl.ds((b % 2) * rows, rows)])
    copy(wout_ref, c * rows, rows, y * COLUMNS, first_ref.at[1, pl.ds(rows, rows)])
    for b in range(4):
        copy(wup_ref, c * rows, rows, b * width + y * COLUMNS, second_ref.at[0, pl.ds(b * rows, rows)])
    copy(wdown_ref, c * 4 * rows, 4 * rows, y * COLUMNS, second_ref.at[1])
    for one in copies:
        one.start()
    for one in copies:
        one.wait()


ANY = pl.BlockSpec(memory_space=pl.ANY)


def quarters(at, wqkv, wout, wup, wdown):
    rows = wqkv.shape[0] // 2
    return call(
        quarters_kernel,
        (1,),
        [ANY] * 4,
        [ANY] * 2,
        [shape_of((2, 2 * rows, COLUMNS), BF16), shape_of((2, 4 * rows, COLUMNS), BF16)],
        [pltpu.SemaphoreType.DMA],
        name="quarters",
    )(at, wqkv, wout, wup, wdown)


def run(copies):
    for one in copies:
        one.start()
    for one in copies:
        one.wait()


def attend_kernel(plan, at, *refs, pieces):
    (xp_ref, cos_ref, sin_ref, g1_ref, b1_ref, bqkv_ref, bout_ref), refs = refs[:7], refs[7:]
    source, refs = (refs[:8], refs[8:]) if pieces else (refs[:2], refs[2:])
    (qkv_ref, o_ref, lse_ref, x1_ref), refs = refs[:4], refs[4:]
    if pieces:
        whole, refs = refs[:2], refs[2:]
    wqkv_ref, wout_ref, mask_ref, sem = refs
    gene = pl.program_id(0)
    span, width = xp_ref.shape

    def wait_both():
        pltpu.make_async_copy(wqkv_ref, wqkv_ref, sem.at[0]).wait()
        pltpu.make_async_copy(wout_ref, wout_ref, sem.at[1]).wait()

    @pl.when(gene == 0)
    def _():
        if pieces:
            rows = width // (4 * Z_SIZE)

            def one(dz, carry):
                for dx, dy, dc in EVERY:
                    f, y, c = spot(at, dz, dx, dy, dc)
                    down = at_rows(f * 2 * rows + c * rows, rows)
                    for b in range(4):
                        src = piece_of(source, b // 2, dx, dy, dc).at[dz, pl.ds((b % 2) * rows, rows)]
                        across = at_columns((b % 3) * width + y * COLUMNS, COLUMNS)
                        if b < 3:
                            dst = wqkv_ref.at[down, across]
                        else:
                            dst = wout_ref.at[down, across]
                        pltpu.make_async_copy(src, dst, sem.at[b // 3]).start()
                return carry

            lax.fori_loop(0, Z_SIZE, one, 0)
        else:
            pltpu.make_async_copy(source[0], wqkv_ref, sem.at[0]).start()
            pltpu.make_async_copy(source[1], wout_ref, sem.at[1]).start()
        wait_both()
        if pieces:
            pltpu.make_async_copy(wqkv_ref, whole[0], sem.at[0]).start()
            pltpu.make_async_copy(wout_ref, whole[1], sem.at[1]).start()

    x = xp_ref[...].astype(F32)
    xhat, _ = normalize(x)
    a1 = (xhat * g1_ref[...] + b1_ref[...]).astype(BF16)
    cos, sin = cos_ref[...], sin_ref[...]
    for part in range(3):
        base = part * width
        t = nn(a1, wqkv_ref[:, base : base + width]) + bqkv_ref[:, base : base + width]
        for p in range(width // LANES):
            piece = t[:, p * LANES : (p + 1) * LANES]
            if part < 2:
                piece = piece * cos + swap_halves(piece) * sin
            qkv_ref[:, base + p * LANES : base + (p + 1) * LANES] = piece.astype(BF16)
    mask_ref[...] = jnp.where(allowed_pairs(plan, gene, span), 1.0, 0.0)
    masks = head_masks(span)
    for p in range(width // LANES):
        here = slice(p * LANES, (p + 1) * LANES)
        q = qkv_ref[:, p * LANES : (p + 1) * LANES]
        k = qkv_ref[:, width + p * LANES : width + (p + 1) * LANES] * BF16(1.0 / math.sqrt(HEAD_DIM))
        v = qkv_ref[:, 2 * width + p * LANES : 2 * width + (p + 1) * LANES]
        o = jnp.zeros((span, LANES), F32)
        for h in range(2):
            s = nt(keep(masks[h], k), q)
            s = jnp.where(mask_ref[...] > 0.5, s, NEG_FILL)
            peak = jnp.max(s, 0, keepdims=True)
            e = jnp.exp(s - peak)
            total = jnp.sum(e, 0, keepdims=True)
            weights = (e * (1.0 / total)).astype(BF16)
            o = o + tn(weights, keep(masks[h], v))
            lse_ref[pl.ds(2 * p + h, 1), :] = peak + jnp.log(total)
        o_ref[:, here] = o.astype(BF16)
    x1_ref[...] = x + nn(o_ref[...], wout_ref[...]) + bout_ref[...]
    if pieces:

        @pl.when(gene == pl.num_programs(0) - 1)
        def _():
            wait_both()


def attend(plan, at, xp, cos, sin, g1, b1, bqkv, bout, source):
    length, width = xp.shape
    span = length // GENES
    pieces = len(source) == 8
    weights = [shape_of((width, 3 * width), BF16), shape_of((width, width), BF16)]
    got = call(
        functools.partial(attend_kernel, pieces=pieces),
        (GENES,),
        [
            rows_of((span, width)),
            rows_of((span, LANES)),
            rows_of((span, LANES)),
            full((1, width)),
            full((1, width)),
            full((1, 3 * width)),
            full((1, width)),
        ]
        + [ANY] * len(source),
        [
            rows_of((span, 3 * width)),
            rows_of((span, width)),
            pl.BlockSpec((16, span), lambda g, *ids: (0, g)),
            rows_of((span, width)),
        ]
        + [ANY] * (2 if pieces else 0),
        [
            shape_of((length, 3 * width), BF16),
            shape_of((length, width), BF16),
            shape_of((16, length), F32),
            shape_of((length, width), F32),
        ]
        + (weights if pieces else []),
        [
            pltpu.VMEM((width, 3 * width), BF16),
            pltpu.VMEM((width, width), BF16),
            pltpu.VMEM((span, span), F32),
            pltpu.SemaphoreType.DMA((2,)),
        ],
        prefetch=2,
        name="attend",
        cost=(11e9, 20e6),
    )(plan, at, xp, cos, sin, g1, b1, bqkv, bout, *source)
    return got[:4], (got[4:] if pieces else source)


def feed_kernel(at, *refs, block, pieces, steps):
    (x1_ref, c_ref, g2_ref, b2_ref, bup_ref, bdown_ref), refs = refs[:6], refs[6:]
    source, refs = (refs[:8], refs[8:]) if pieces else (refs[:2], refs[2:])
    (out_ref, dx1_ref, da_ref, gbup_ref, sums_ref, first_ref, second_ref), refs = refs[:7], refs[7:]
    a2_ref, acc_ref, dh_ref, gr_ref, du_ref, wups, wdowns, gups, gdowns, load_sem, store_sem = refs
    step = pl.program_id(0)
    length, width = x1_ref.shape
    chunk = bup_ref.shape[1]
    blocks = length // block
    slot = lax.rem(step, 2)
    rows = width // (4 * Z_SIZE)

    def load(j, to):
        if pieces:

            def one(dz, carry):
                for dx, dy, dc in EVERY:
                    f, y, c = spot(at, dz, dx, dy, dc)
                    src = piece_of(source, 0, dx, dy, dc).at[dz, at_rows(j * rows, rows)]
                    dst = wups.at[to, at_rows(f * 2 * rows + c * rows, rows), at_columns(y * COLUMNS, COLUMNS)]
                    pltpu.make_async_copy(src, dst, load_sem.at[0, to]).start()
                return carry

            lax.fori_loop(0, Z_SIZE, one, 0)
            back = lax.rem(at[0] + (Z_SIZE - j), Z_SIZE)
            for dx, dy, dc in EVERY:
                f, y, c = spot(at, back, dx, dy, dc)
                x = lax.bitwise_xor(at[1], dx)
                src = piece_of(source, 1, dx, dy, dc).at[back]
                dst = wdowns.at[to, at_rows((x * 2 + c) * 4 * rows, 4 * rows), at_columns(y * COLUMNS, COLUMNS)]
                pltpu.make_async_copy(src, dst, load_sem.at[1, to]).start()
        else:
            part = source[0].at[:, at_columns(j * chunk, chunk)]
            pltpu.make_async_copy(part, wups.at[to], load_sem.at[0, to]).start()
            part = source[1].at[at_rows(j * chunk, chunk), :]
            pltpu.make_async_copy(part, wdowns.at[to], load_sem.at[1, to]).start()

    def store(j, to):
        if pieces:

            def one(dz, carry):
                for dx, dy, dc in EVERY:
                    f, y, c = spot(at, Z_SIZE - dz, dx, dy, dc)
                    src = gups.at[to, at_rows(f * 2 * rows + c * rows, rows), at_columns(y * COLUMNS, COLUMNS)]
                    dst = (first_ref, second_ref)[dc].at[dz, dx, dy, 0, at_rows(j * rows, rows)]
                    pltpu.make_async_copy(src, dst, store_sem.at[0, to]).start()
                return carry

            lax.fori_loop(0, Z_SIZE, one, 0)
            ahead = lax.rem(j + Z_SIZE - at[0], Z_SIZE)
            for dx, dy, dc in EVERY:
                f, y, c = spot(at, 0, dx, dy, dc)
                x = lax.bitwise_xor(at[1], dx)
                src = gdowns.at[to, at_rows((x * 2 + c) * 4 * rows, 4 * rows), at_columns(y * COLUMNS, COLUMNS)]
                dst = (first_ref, second_ref)[dc].at[ahead, dx, dy, 1]
                pltpu.make_async_copy(src, dst, store_sem.at[1, to]).start()
        else:
            part = first_ref.at[:, at_columns(j * chunk, chunk)]
            pltpu.make_async_copy(gups.at[to], part, store_sem.at[0, to]).start()
            part = second_ref.at[at_rows(j * chunk, chunk), :]
            pltpu.make_async_copy(gdowns.at[to], part, store_sem.at[1, to]).start()

    def wait_load(to):
        pltpu.make_async_copy(wups.at[to], wups.at[to], load_sem.at[0, to]).wait()
        pltpu.make_async_copy(wdowns.at[to], wdowns.at[to], load_sem.at[1, to]).wait()

    def wait_store(to):
        pltpu.make_async_copy(gups.at[to], gups.at[to], store_sem.at[0, to]).wait()
        pltpu.make_async_copy(gdowns.at[to], gdowns.at[to], store_sem.at[1, to]).wait()

    @pl.when(step == 0)
    def _():
        load(0, 0)

        def one(i, carry):
            here = pl.ds(i * block, block)
            xhat, _ = normalize(x1_ref[here, :])
            a2_ref[here, :] = (xhat * g2_ref[...] + b2_ref[...]).astype(BF16)
            return carry

        lax.fori_loop(0, blocks, one, 0)

    wait_load(slot)

    @pl.when(step < steps - 1)
    def _():
        load(step + 1, 1 - slot)

    wup_ref, wdown_ref = wups.at[slot], wdowns.at[slot]

    def one(i, bias_sum):
        here = pl.ds(i * block, block)
        u = nn(a2_ref[here, :], wup_ref[...]) + bup_ref[...]
        phi = 0.5 + 0.5 * lax.erf(u * math.sqrt(0.5))
        slope = phi + u * (jnp.exp(-0.5 * u * u) * (1.0 / math.sqrt(2.0 * math.pi)))
        gr = (u * phi).astype(BF16)
        gr_ref[here, :] = gr
        du = (nt(c_ref[here, :], wdown_ref[...]) * slope).astype(BF16)
        du_ref[here, :] = du
        out = nn(gr, wdown_ref[...])
        dh = nt(du, wup_ref[...])

        @pl.when(step == 0)
        def _():
            acc_ref[here, :] = out
            dh_ref[here, :] = dh

        @pl.when(step > 0)
        def _():
            acc_ref[here, :] += out
            dh_ref[here, :] += dh

        return bias_sum + jnp.sum(du.astype(F32), 0, keepdims=True)

    gbup_ref[...] = lax.fori_loop(0, blocks, one, jnp.zeros((1, chunk), F32))

    @pl.when(step >= 2)
    def _():
        wait_store(slot)

    gdowns[slot] = tn(gr_ref[...], c_ref[...]).astype(BF16)
    gups[slot] = tn(a2_ref[...], du_ref[...]).astype(BF16)
    store(step, slot)

    @pl.when(step == steps - 1)
    def _():
        def one(i, sums):
            here = pl.ds(i * block, block)
            x1 = x1_ref[here, :]
            xhat, scale = normalize(x1)
            out_ref[here, :] = (x1 + acc_ref[here, :] + bdown_ref[...]).astype(BF16)
            dh = dh_ref[here, :]
            c = c_ref[here, :].astype(F32)
            e = dh * g2_ref[...]
            dx1 = c + scale * (
                e - jnp.mean(e, -1, keepdims=True) - xhat * jnp.mean(e * xhat, -1, keepdims=True)
            )
            dx1_ref[here, :] = dx1
            da = dx1.astype(BF16)
            da_ref[here, :] = da
            new = (
                jnp.sum(dh * xhat, 0, keepdims=True),
                jnp.sum(dh, 0, keepdims=True),
                jnp.sum(c, 0, keepdims=True),
                jnp.sum(da.astype(F32), 0, keepdims=True),
            )
            return tuple(a + b for a, b in zip(sums, new))

        sums = lax.fori_loop(0, blocks, one, (jnp.zeros((1, width), F32),) * 4)
        for i in range(4):
            sums_ref[i : i + 1, :] = sums[i]
        wait_store(1 - slot)
        wait_store(slot)


def feed(at, x1, c, g2, b2, bup, bdown, source):
    length, width = x1.shape
    hidden = bup.shape[1]
    steps = 4
    chunk = hidden // steps
    pieces = len(source) == 8
    if pieces:
        rows = width // Z_SIZE
        stored = [shape_of((Z_SIZE, 2, 2, 2, rows, COLUMNS), BF16)] * 2
    else:
        stored = [shape_of((width, hidden), BF16), shape_of((hidden, width), BF16)]
    return call(
        functools.partial(feed_kernel, block=length // 4, pieces=pieces, steps=steps),
        (steps,),
        [
            full((length, width)),
            full((length, width)),
            full((1, width)),
            full((1, width)),
            pl.BlockSpec((1, chunk), lambda j, *ids: (0, j)),
            full((1, width)),
        ]
        + [ANY] * len(source),
        [
            full((length, width)),
            full((length, width)),
            full((length, width)),
            pl.BlockSpec((1, chunk), lambda j, *ids: (0, j)),
            full((8, width)),
            ANY,
            ANY,
        ],
        [
            shape_of((length, width), BF16),
            shape_of((length, width), F32),
            shape_of((length, width), BF16),
            shape_of((1, hidden), F32),
            shape_of((8, width), F32),
        ]
        + stored,
        [
            pltpu.VMEM((length, width), BF16),
            pltpu.VMEM((length, width), F32),
            pltpu.VMEM((length, width), F32),
            pltpu.VMEM((length, chunk), BF16),
            pltpu.VMEM((length, chunk), BF16),
            pltpu.VMEM((2, width, chunk), BF16),
            pltpu.VMEM((2, chunk, width), BF16),
            pltpu.VMEM((2, width, chunk), BF16),
            pltpu.VMEM((2, chunk, width), BF16),
            pltpu.SemaphoreType.DMA((2, 2)),
            pltpu.SemaphoreType.DMA((2, 2)),
        ],
        name="feed",
        cost=(29e9, 40e6),
    )(at, x1, c, g2, b2, bup, bdown, *source)


def attend_back_kernel(
    plan, qkv_ref, da_ref, lse_ref, cos_ref, sin_ref, xp_ref, dx1_ref, g1_ref, wout_ref, wqkv_ref,
    dqkv_ref, dxp_ref, sums_ref, dout_ref, mask_ref
):
    gene = pl.program_id(0)
    span, width = da_ref.shape
    score_scale = 1.0 / math.sqrt(HEAD_DIM)
    dout_ref[...] = nt(da_ref[...], wout_ref[...]).astype(BF16)
    mask_ref[...] = jnp.where(allowed_pairs(plan, gene, span), 1.0, 0.0)
    cos, sin = cos_ref[...], sin_ref[...]
    masks = head_masks(span)

    def back(t):
        return (t * cos - swap_halves(t) * sin).astype(BF16)

    for p in range(width // LANES):
        here = slice(p * LANES, (p + 1) * LANES)
        q = qkv_ref[:, p * LANES : (p + 1) * LANES]
        k = qkv_ref[:, width + p * LANES : width + (p + 1) * LANES] * BF16(score_scale)
        v = qkv_ref[:, 2 * width + p * LANES : 2 * width + (p + 1) * LANES]
        dout = dout_ref[:, here]
        dq = jnp.zeros((span, LANES), F32)
        dk = jnp.zeros((span, LANES), F32)
        dv = jnp.zeros((span, LANES), F32)
        for h in range(2):
            kh = keep(masks[h], k)
            s = nt(kh, q)
            s = jnp.where(mask_ref[...] > 0.5, s, NEG_FILL)
            weights = jnp.exp(s - lse_ref[pl.ds(2 * p + h, 1), :])
            dw = nt(keep(masks[h], v), dout)
            dot = jnp.sum(weights * dw, 0, keepdims=True)
            ds = (weights * (dw - dot)).astype(BF16)
            dv = dv + nn(weights.astype(BF16), keep(masks[h], dout))
            dk = dk + nn(ds, keep(masks[h], q))
            dq = dq + tn(ds, kh)
        dqkv_ref[:, p * LANES : (p + 1) * LANES] = back(dq)
        dqkv_ref[:, width + p * LANES : width + (p + 1) * LANES] = back(dk * score_scale)
        dqkv_ref[:, 2 * width + p * LANES : 2 * width + (p + 1) * LANES] = dv.astype(BF16)

    dh = nt(dqkv_ref[...], wqkv_ref[...])
    xhat, scale = normalize(xp_ref[...].astype(F32))
    e = dh * g1_ref[...]
    dx = dx1_ref[...] + scale * (
        e - jnp.mean(e, -1, keepdims=True) - xhat * jnp.mean(e * xhat, -1, keepdims=True)
    )
    dxp_ref[...] = dx.astype(BF16)
    gain = jnp.sum(dh * xhat, 0, keepdims=True)
    bias = jnp.sum(dh, 0, keepdims=True)

    @pl.when(gene == 0)
    def _():
        sums_ref[0:1, :] = gain
        sums_ref[1:2, :] = bias

    @pl.when(gene > 0)
    def _():
        sums_ref[0:1, :] += gain
        sums_ref[1:2, :] += bias


def attend_back(plan, qkv, da, lse, cos, sin, xp, dx1, g1, wout, wqkv):
    length, width = da.shape
    span = length // GENES
    return call(
        attend_back_kernel,
        (GENES,),
        [
            rows_of((span, 3 * width)),
            rows_of((span, width)),
            pl.BlockSpec((16, span), lambda g, *ids: (0, g)),
            rows_of((span, LANES)),
            rows_of((span, LANES)),
            rows_of((span, width)),
            rows_of((span, width)),
            full((1, width)),
            full((width, width)),
            full((width, 3 * width)),
        ],
        [rows_of((span, 3 * width)), rows_of((span, width)), full((8, width))],
        [
            shape_of((length, 3 * width), BF16),
            shape_of((length, width), BF16),
            shape_of((8, width), F32),
        ],
        [pltpu.VMEM((span, width), BF16), pltpu.VMEM((span, span), F32)],
        name="attend_back",
        cost=(16e9, 25e6),
    )(plan, qkv, da, lse, cos, sin, xp, dx1, g1, wout, wqkv)


def grads_kernel(at, *refs, pieces):
    (xp_ref, g1_ref, b1_ref, o_ref, da_ref, dqkv_ref, small_ref), refs = refs[:7], refs[7:]
    first_ref, second_ref, a1_ref, grad_ref, sem, small_sem = refs
    step = pl.program_id(0)
    width = xp_ref.shape[1]
    slot = lax.rem(step, 2)
    rows = width // (4 * Z_SIZE)

    def wait(to):
        pltpu.make_async_copy(grad_ref.at[to], grad_ref.at[to], sem.at[to]).wait()

    def store(half, base, to):
        def one(dz, carry):
            for dx, dy, dc in EVERY:
                f, y, c = spot(at, Z_SIZE - dz, dx, dy, dc)
                src = grad_ref.at[to, at_rows(f * 2 * rows + c * rows, rows), at_columns(y * COLUMNS, COLUMNS)]
                dst = (first_ref, second_ref)[dc].at[dz, dx, dy, half, pl.ds(base * rows, rows)]
                pltpu.make_async_copy(src, dst, sem.at[to]).start()
            return carry

        lax.fori_loop(0, Z_SIZE, one, 0)

    def smalls(act):
        def one(dz, carry):
            for dx, dy, dc in EVERY:
                f, y, c = spot(at, Z_SIZE - dz, dx, dy, dc)
                src = small_ref.at[f, y, c]
                dst = (first_ref, second_ref)[dc].at[dz, dx, dy, :, pl.ds(2 * rows, 8)]
                act(pltpu.make_async_copy(src, dst, small_sem))
            return carry

        lax.fori_loop(0, Z_SIZE, one, 0)

    @pl.when(step >= 2)
    def _():
        wait(slot)

    for j in range(4):

        @pl.when(step == j)
        def _(j=j):
            if j == 0:
                if pieces:
                    smalls(lambda copy: copy.start())
                xhat, _ = normalize(xp_ref[...].astype(F32))
                a1_ref[...] = (xhat * g1_ref[...] + b1_ref[...]).astype(BF16)
            if j < 3:
                grad_ref[j % 2] = tn(a1_ref[...], dqkv_ref[...]).astype(BF16)
            else:
                grad_ref[j % 2] = tn(o_ref[...], da_ref[...]).astype(BF16)
            if pieces:
                store(j // 2, j % 2, j % 2)
            elif j < 3:
                dst = first_ref.at[:, pl.ds(j * width, width)]
                pltpu.make_async_copy(grad_ref.at[j % 2], dst, sem.at[j % 2]).start()
            else:
                pltpu.make_async_copy(grad_ref.at[j % 2], second_ref, sem.at[j % 2]).start()
            if j == 3:
                wait(0)
                wait(1)
                if pieces:
                    smalls(lambda copy: copy.wait())


def grads(at, xp, g1, b1, o, da, dqkv, small, pieces):
    length, width = xp.shape
    if pieces:
        rows = width // (2 * Z_SIZE) + 8
        stored = [shape_of((Z_SIZE, 2, 2, 2, rows, COLUMNS), BF16)] * 2
    else:
        stored = [shape_of((width, 3 * width), BF16), shape_of((width, width), BF16)]
    return call(
        functools.partial(grads_kernel, pieces=pieces),
        (4,),
        [
            full((length, width)),
            full((1, width)),
            full((1, width)),
            full((length, width)),
            full((length, width)),
            pl.BlockSpec((length, width), lambda j, *ids: (0, jnp.minimum(j, 2))),
            ANY,
        ],
        [ANY, ANY],
        stored,
        [
            pltpu.VMEM((length, width), BF16),
            pltpu.VMEM((2, width, width), BF16),
            pltpu.SemaphoreType.DMA((2,)),
            pltpu.SemaphoreType.DMA,
        ],
        name="grads",
        cost=(5e9, 12e6),
    )(at, xp, g1, b1, o, da, dqkv, small)


def restore_kernel(src_ref, outp_ref, dxp_ref, out_ref, dx_ref):
    span, width = out_ref.shape
    codon = iota((span, outp_ref.shape[0]), 0) + pl.program_id(0) * span
    pick = jnp.where(codon == src_ref[0:1, :], 1.0, 0.0).astype(BF16)
    out_ref[...] = nn(pick, outp_ref[...]).astype(BF16)
    dx_ref[...] = nn(pick, dxp_ref[...]).astype(BF16)


def restore(src, outp, dxp):
    length, width = outp.shape
    span = length // GENES
    return call(
        restore_kernel,
        (GENES,),
        [full((1, length)), full((length, width)), full((length, width))],
        [rows_of((span, width))] * 2,
        [shape_of((length, width), BF16)] * 2,
        prefetch=0,
        name="restore",
        cost=(3.3e9, 8e6),
    )(src, outp, dxp)


def gather(shard):
    return lax.all_gather(shard, "fsdp", axis=0, tiled=True)


def reduce_rows(grad):
    part = lax.psum_scatter(grad, "fsdp", scatter_dimension=0, tiled=True)
    return lax.psum(part.astype(BF16), "replica").astype(F32)


def rotary_tables(positions):
    frequency = jnp.power(10000.0, jnp.arange(HEAD_DIM // 2, dtype=F32) * (-2.0 / HEAD_DIM))
    angles = positions.astype(F32)[:, None] * jnp.tile(frequency, LANES // (HEAD_DIM // 2))[None]
    sign = jnp.where(jnp.arange(LANES) % HEAD_DIM < HEAD_DIM // 2, -1.0, 1.0).astype(F32)
    return jnp.cos(angles), jnp.sin(angles) * sign


def split_rows(packed, sizes):
    out, start = [], 0
    for size in sizes:
        out.append(packed[:, start : start + size])
        start += size
    return out


def body(
    layer_input, cotangent, segment_ids, pad_mask, ln1_gain, ln1_bias, w_qkv, b_qkv, w_out, b_out,
    ln2_gain, ln2_bias, w_up, b_up, w_down, b_down, *, tuned,
):
    length, width = layer_input.shape[1:]
    span = length // GENES
    small = (ln1_gain, ln1_bias, b_qkv, b_out, ln2_gain, ln2_bias, b_up, b_down)
    sizes = [v.shape[0] for v in small]
    packed = jnp.concatenate(small)
    if tuned:
        at = place()
        first, second = quarters(at, w_qkv, w_out, w_up, w_down)
        packed = gather_small(at, packed)
        attention = gather_pieces(first)
        forward = gather_pieces(second)
    else:
        at = jnp.zeros((4,), jnp.int32)
        packed = gather(packed[None])
        attention = gather(w_qkv), gather(w_out)
        forward = gather(w_up), gather(w_down)
    g1, b1, bqkv, bout, g2, b2, bup, bdown = (
        v.reshape(1, -1).astype(F32) for v in split_rows(packed, sizes)
    )
    plan = slot_plan(segment_ids[0])
    slots = jnp.arange(length, dtype=jnp.int32)
    gene, slot = slots // span, slots % span
    src = source_of_slots(plan, gene, slot)
    start = jnp.where(slot < plan[gene], plan[GENES + gene], plan[3 * GENES])
    cos, sin = rotary_tables(src - start)
    xp, cp = reorder(plan, layer_input[0], cotangent[0])
    (qkv, o, lse, x1), (wqkv, wout) = attend(plan, at, xp, cos, sin, g1, b1, bqkv, bout, attention)
    outp, dx1, da, gbup, sums2, *pieces_f = feed(at, x1, cp, g2, b2, bup, bdown, forward)
    dqkv, dxp, sums1 = attend_back(plan, qkv, da, lse, cos, sin, xp, dx1, g1, wout, wqkv)
    gbqkv = jnp.sum(dqkv.astype(F32), 0)
    small = [sums1[0], sums1[1], gbqkv, sums2[3], sums2[0], sums2[1], gbup[0], sums2[2]]
    count = width // (sizes[0])
    small = jnp.concatenate([v.reshape(count, -1) for v in small], 1)
    if tuned:
        room = 8 * COLUMNS
        small = jnp.pad(small, ((0, 0), (0, room - small.shape[1]))).astype(BF16)
        small = small.reshape(count, 2, 2, 2, 1, COLUMNS)
        small = jnp.pad(small, ((0, 0),) * 4 + ((0, 7), (0, 0)))
    pieces_a = grads(at, xp, g1, b1, o, da, dqkv, small, tuned)
    layer_out, input_grad = restore(src[None], outp, dxp)
    if tuned:
        f = reduce_pieces(at, *pieces_f)
        a = reduce_pieces(at, *pieces_a)
        rows = width // (4 * Z_SIZE)
        up = f[:, :, 0].reshape(2, 2, 4, rows, COLUMNS).transpose(0, 3, 2, 1, 4).reshape(2 * rows, -1)
        down = f[:, :, 1].transpose(0, 2, 1, 3).reshape(8 * rows, width)
        blocks = a[:, :, :, : 2 * rows].reshape(2, 2, 4, rows, COLUMNS).transpose(0, 3, 2, 1, 4)
        blocks = blocks.reshape(2 * rows, 4 * width)
        qkv_grad, out_grad = blocks[:, : 3 * width], blocks[:, 3 * width :]
        small = a[:, :, :, 2 * rows].transpose(1, 0, 2, 3).reshape(1, -1)[:, : sum(sizes)].astype(F32)
        up, down, qkv_grad, out_grad = (v.astype(F32) for v in (up, down, qkv_grad, out_grad))
    else:
        qkv_grad, out_grad = map(reduce_rows, pieces_a)
        up, down = map(reduce_rows, pieces_f)
        small = reduce_rows(small)
    dg1, db1, dbqkv, dbout, dg2, db2, dbup, dbdown = (v.reshape(-1) for v in split_rows(small, sizes))
    return (
        layer_out[None], input_grad[None], dg1, db1, qkv_grad, dbqkv, out_grad, dbout, dg2, db2,
        up, dbup, down, dbdown,
    )


def solution(mesh):
    rows = ("fsdp", "replica")
    by_row = P(rows, None, None)
    vector, matrix = P("fsdp"), P("fsdp", None)
    params = (
        vector, vector, matrix, vector, matrix, vector, vector, vector, matrix, vector, matrix, vector,
    )
    in_specs = (by_row, by_row, P(rows, None), P(rows, None)) + params
    out_specs = (by_row, by_row) + params
    return jax.shard_map(
        functools.partial(body, tuned=tuned_mesh(mesh)),
        mesh=mesh, in_specs=in_specs, out_specs=out_specs, check_vma=False,
    )
```

time: 1130 us -> 427 us (0.38)
  matrix products: 293 us -> 0 us
  waiting for transfers between devices: 444 us -> 159 us
  Pallas kernels: 0 us -> 143 us
  blocking collectives: 107 us -> 0 us
  other arithmetic: 127 us -> 28.9 us
  local copies, waits for them, and re-layouts: 129 us -> 38.3 us
  starting transfers between devices: 0.53 us -> 46.7 us
    reduce_scatter x4 -> x0, waiting for transfers between devices: 404 us -> none  [the longest x1 165 us: body(): lax.psum_scatter(grad_up_weight, 'fsdp', scatter_dimension=0, tiled=True)]
    dot_general x26 -> x0, matrix products: 293 us -> none  [the longest x4 44.4 us: block_scores(): jnp.einsum('qhd,khd->hqk', block_queries, key_rows, preferred_element_typ...]
    ppermute x0 -> x46, waiting for transfers between devices: none -> 159 us  [move(): return lax.ppermute(array, AXES, table)]
    pallas_call x0 -> x7, Pallas kernels: none -> 143 us  [the longest x1 48.3 us: feed(): call(functools.partial(feed_kernel, block=length // 4, pieces=pieces, ste...]
    unnamed x2 -> x0, blocking collectives: 75.2 us -> none
    dynamic_update_slice x4 -> x0, local copies, waits for them, and re-layouts: 60.9 us -> none  [attend_forward(): lax.scan(one_block, jnp.zeros((), jnp.float32), split_blocks(queries, seg...]
    convert_element_type x27 -> x14, other arithmetic: 64.5 us -> 7.52 us  [the longest x6 3.91 us: reduce_pieces(): a, s = (slice(None), lambda v: v.astype(BF16))]
    ppermute x0 -> x46, starting transfers between devices: none -> 46.7 us  [move(): return lax.ppermute(array, AXES, table)]
  transfers between devices with their start and end apart: 9 -> 46, of which waited for: 4 -> 21; matrix products, arithmetic and copies ran while one was open for 43% -> 11% of each run, Pallas kernels for 0% -> 12%
where the time goes in v1:
time: 427 us; the launch traced here: 423 us
  waiting for transfers between devices  159 us (37%)
  Pallas kernels  143 us (33%)
  starting transfers between devices  46.7 us (11%)
  local copies, waits for them, and re-layouts  38.3 us (9%)
  other arithmetic  28.9 us (7%)
  between operations  7.15 us (2%)
    ppermute x46, waiting for transfers between devices, move(): return lax.ppermute(array, AXES, table)  159 us
    pallas_call x1, Pallas kernels, feed(): call(functools.partial(feed_kernel, block=length // 4, pieces=pieces, ste...  48.3 us
    ppermute x46, starting transfers between devices, move(): return lax.ppermute(array, AXES, table)  46.7 us
    pallas_call x1, Pallas kernels, attend_back(): call(attend_back_kernel, (GENES,), [rows_of((span, 3 * width)), rows_of((...  26.3 us
    pallas_call x1, Pallas kernels, attend(): call(functools.partial(attend_kernel, pieces=pieces), (GENES,), [rows_of(...  22.1 us
    pallas_call x1, Pallas kernels, grads(): call(functools.partial(grads_kernel, pieces=pieces), (4,), [full((length,...  16.8 us
    pallas_call x1, Pallas kernels, quarters(): call(quarters_kernel, (1,), [ANY] * 4, [ANY] * 2, [shape_of((2, 2 * rows,...  15.2 us
  transfers between devices with their start and end apart: 46, of which 21 were waited for; matrix products, arithmetic and copies ran while one was open for 11% of the time, Pallas kernels for 12%

profile of v1, /device:TPU:0, one launch (start us, length us, event | category | flops | bytes accessed | tf_op | source)
XLA Modules:
  0.0 423.1 jit_solution(14500428113732101054)
XLA Ops:
  0.7 5.5 %concatenate.38 = bf16[1248]{0:T(1024)(128)(2,1)S(1)} concatenate(bf16[96]{0:T(256)(128)(2,1)} %param.19, bf16[96]{0:T(256)(128)(2,1)} %param.20, bf16[288]{0:T(512)(128)(2,1)} %param.22, bf16[96]{0:T(256)(128)(2,1)} %param.24, bf16[96]{0:T(256)(128)(2,1)} %param.25, bf16[96]{0:T(256)(128)(2,1)} %param.26, bf16[384]{0:T(512)(128)(2,1)} %param.28, bf16[96]{0:T(256)(128)(2,1)} %param.30), dimensions={0} | concatenate | bytes 4992 | tf_op jit(solution)/shard_map/concatenate | solution.py:866
  6.1 5.0 %collective-permute-start.2 = (bf16[1248]{0:T(1024)(128)(2,1)S(1)}, bf16[1248]{0:T(1024)(128)(2,1)S(1)}, u32[]{:S(2)}, u32[]{:S(2)}) collective-permute-start(bf16[1248]{0:T(1024)(128)(2,1)S(1)} %concatenate.38), channel_id=1, source_target_pairs={{0,24},{1,25},{2,26},{3,27},{4,28},{5,29},{6,30},{7,31},{8,0},{9,1... | collective-permute-start | bytes 7496 | tf_op jit(solution)/shard_map/ppermute | solution.py:172
  12.9 15.2 %quarters.1 = (bf16[2,96,384]{2,1,0:T(8,128)(2,1)}, bf16[2,192,384]{2,1,0:T(8,128)(2,1)}) custom-call(s32[4]{0:T(128)} %pad_add_fusion.at, bf16[96,2304]{1,0:T(8,128)(2,1)} %wqkv_ref.1, bf16[96,768]{1,0:T(8,128)(2,1)} %wout_ref.1, bf16[96,3072]{1,0:T(8,128)(2,1)} %wup_ref.1, bf16[384,768]{1,0:T(8,128)(2,1)} %wdown_ref.1), custom_call_target="tpu_custom_call" | custom-call | tf_op jit(solution)/shard_map/quarters/pallas_call | solution.py:269
  28.0 2.9 collective-permute-start.6
  45.5 3.1 fusion.22
  48.6 3.9 stack.217.plan
  52.5 7.4 %reorder.1 = (bf16[1024,768]{1,0:T(8,128)(2,1)}, bf16[1024,768]{1,0:T(8,128)(2,1)}) custom-call(s32[13]{0:T(128)} %stack.217.plan, bf16[1024,768]{1,0:T(8,128)(2,1)} %bitcast.229, bf16[1024,768]{1,0:T(8,128)(2,1)} %bitcast.230), custom_call_target="tpu_custom_call" | custom-call | flops 3300000000 | bytes 8000000 | tf_op jit(solution)/shard_map/reorder/pallas_call | solution.py:105
  60.2 3.9 collective-permute-start.17
  65.0 3.7 collective-permute-done.4
  71.5 19.9 %collective-permute-done.16 = bf16[2,192,384]{2,1,0:T(8,128)(2,1)S(1)} collective-permute-done((bf16[2,192,384]{2,1,0:T(8,128)(2,1)S(1)}, bf16[2,192,384]{2,1,0:T(8,128)(2,1)S(1)}, u32[]{:S(2)}, u32[]{:S(2)}) %collective-permute-start.16) | collective-permute-done | bytes 294944 | tf_op jit(solution)/shard_map/ppermute | solution.py:172
  97.3 8.6 %collective-permute-done.18 = bf16[4,192,384]{2,1,0:T(8,128)(2,1)S(1)} collective-permute-done((bf16[4,192,384]{2,1,0:T(8,128)(2,1)S(1)}, bf16[4,192,384]{2,1,0:T(8,128)(2,1)S(1)}, u32[]{:S(2)}, u32[]{:S(2)}) %collective-permute-start.18) | collective-permute-done | bytes 589856 | tf_op jit(solution)/shard_map/ppermute | solution.py:172
  111.3 4.9 %collective-permute-done.9 = bf16[4,96,384]{2,1,0:T(8,128)(2,1)S(1)} collective-permute-done((bf16[4,96,384]{2,1,0:T(8,128)(2,1)S(1)}, bf16[4,96,384]{2,1,0:T(8,128)(2,1)S(1)}, u32[]{:S(2)}, u32[]{:S(2)}) %collective-permute-start.9) | collective-permute-done | bytes 294944 | tf_op jit(solution)/shard_map/ppermute | solution.py:172
  120.4 8.5 %collective-permute-done.8.refs_8_ = bf16[2,4,96,384]{3,2,1,0:T(8,128)(2,1)} collective-permute-done((bf16[2,4,96,384]{3,2,1,0:T(8,128)(2,1)S(1)}, bf16[2,4,96,384]{3,2,1,0:T(8,128)(2,1)}, u32[]{:S(2)}, u32[]{:S(2)}) %collective-permute-start.8) | collective-permute-done | bytes 589856 | tf_op jit(solution)/shard_map/ppermute | solution.py:172
  130.1 22.2 %collective-permute-done.10.refs_10_ = bf16[2,4,96,384]{3,2,1,0:T(8,128)(2,1)} collective-permute-done((bf16[2,4,96,384]{3,2,1,0:T(8,128)(2,1)S(1)}, bf16[2,4,96,384]{3,2,1,0:T(8,128)(2,1)}, u32[]{:S(2)}, u32[]{:S(2)}) %collective-permute-start.10) | collective-permute-done | bytes 589856 | tf_op jit(solution)/shard_map/ppermute | solution.py:172
  158.9 22.1 %attend.1 = (bf16[1024,2304]{1,0:T(8,128)(2,1)}, bf16[1024,768]{1,0:T(8,128)(2,1)}, f32[16,1024]{1,0:T(8,128)}, f32[1024,768]{1,0:T(8,128)}, bf16[768,2304]{1,0:T(8,128)(2,1)}, /*index=5*/bf16[768,768]{1,0:T(8,128)(2,1)}) custom-call(s32[13]{0:T(128)} %stack.217.plan, s32[4]{0:T(128)} %pad_add_fusion.at, bf16[1024,768]{1,0:T(8,128)(2,1)} %get-tuple-element.38.refs_0_.xp_ref, ...), custom_call_target="tpu_custom_call" | custom-call | flops 11000000512 | bytes 20000000 | tf_op jit(solution)/shard_map/attend/pallas_call | solution.py:372
  181.0 48.3 %feed.1 = (bf16[1024,768]{1,0:T(8,128)(2,1)}, f32[1024,768]{1,0:T(8,128)}, bf16[1024,768]{1,0:T(8,128)(2,1)}, f32[1,3072]{1,0:T(1,128)}, f32[8,768]{1,0:T(8,128)...) custom-call(s32[4]{0:T(128)} %pad_add_fusion.at, ...), custom_call_target="tpu_custom_call" | custom-call | flops 28999999488 | bytes 40000000 | tf_op jit(solution)/shard_map/feed/pallas_call | solution.py:578
  229.3 26.3 %attend_back.1 = (bf16[1024,2304]{1,0:T(8,128)(2,1)}, bf16[1024,768]{1,0:T(8,128)(2,1)}, f32[8,768]{1,0:T(8,128)}) custom-call(s32[13]{0:T(128)} %stack.217.plan, bf16[1024,2304]{1,0:T(8,128)(2,1)} %get-tuple-element.44.qkv_ref, bf16[1024,768]{1,0:T(8,128)(2,1)} %get-tuple-element.45.da_ref.refs_4_, f32[16,1024]{1,0:T(8,128)} %get-tuple-element.46.lse_ref, ...), custom_call_target="tpu_custom_call" | custom-call | flops 16000000000 | bytes 25000000 | tf_op jit(solution)/shard_map/attend_back/pallas_call | solution.py:688
  255.7 3.1 reduce.4
  260.5 16.8 %grads.1 = (bf16[4,2,2,2,104,384]{5,4,3,2,1,0:T(8,128)(2,1)}, bf16[4,2,2,2,104,384]{5,4,3,2,1,0:T(8,128)(2,1)}) custom-call(s32[4]{0:T(128)} %pad_add_fusion.at, bf16[1024,768]{1,0:T(8,128)(2,1)} %get-tuple-element.38.refs_0_.xp_ref, f32[1,768]{1,0:T(1,128)} %reshape.547.refs_3_.g1_ref.refs_1_, f32[1,768]{1,0:T(1,128)} %reshape.548.refs_4_.refs_2_, ...), custom_call_target="tpu_custom_call" | custom-call | flops 5000000000 | bytes 12000000 | tf_op jit(solution)/shard_map/grads/pallas_call | solution.py:786
  277.9 7.4 %collective-permute-done.26 = bf16[4,2,2,2,104,384]{5,4,3,2,1,0:T(8,128)(2,1)S(1)} collective-permute-done((bf16[4,2,2,2,104,384]{5,4,3,2,1,0:T(8,128)(2,1)}, bf16[4,2,2,2,104,384]{5,4,3,2,1,0:T(8,128)(2,1)S(1)}, u32[]{:S(2)}, u32[]{:S(2)}) %collective-permute-start.26) | collective-permute-done | bytes 2555936 | tf_op jit(solution)/shard_map/ppermute | solution.py:172
  290.0 13.3 %collective-permute-done.29 = bf16[4,2,104,384]{3,2,1,0:T(8,128)(2,1)S(1)} collective-permute-done((bf16[4,2,104,384]{3,2,1,0:T(8,128)(2,1)S(1)}, bf16[4,2,104,384]{3,2,1,0:T(8,128)(2,1)S(1)}, u32[]{:S(2)}, u32[]{:S(2)}) %collective-permute-start.29) | collective-permute-done | bytes 639008 | tf_op jit(solution)/shard_map/ppermute | solution.py:172
  306.7 5.9 %collective-permute-done.30 = bf16[4,104,384]{2,1,0:T(8,128)(2,1)S(1)} collective-permute-done((bf16[4,104,384]{2,1,0:T(8,128)(2,1)S(1)}, bf16[4,104,384]{2,1,0:T(8,128)(2,1)S(1)}, u32[]{:S(2)}, u32[]{:S(2)}) %collective-permute-start.30) | collective-permute-done | bytes 319520 | tf_op jit(solution)/shard_map/ppermute | solution.py:172
  315.7 3.8 collective-permute-start.33
  325.9 4.1 collective-permute-done.32
  331.3 19.6 %collective-permute-done.34 = bf16[2,104,384]{2,1,0:T(8,128)(2,1)S(1)} collective-permute-done((bf16[2,104,384]{2,1,0:T(8,128)(2,1)S(1)}, bf16[2,104,384]{2,1,0:T(8,128)(2,1)S(1)}, u32[]{:S(2)}, u32[]{:S(2)}) %collective-permute-start.34) | collective-permute-done | bytes 159776 | tf_op jit(solution)/shard_map/ppermute | solution.py:172
  358.2 6.6 %restore.1 = (bf16[1024,768]{1,0:T(8,128)(2,1)}, bf16[1024,768]{1,0:T(8,128)(2,1)}) custom-call(s32[1,1024]{1,0:T(1,128)} %compare_select_fusion.21.src_ref, bf16[1024,768]{1,0:T(8,128)(2,1)} %get-tuple-element.43.outp_ref, bf16[1024,768]{1,0:T(8,128)(2,1)} %get-tuple-element.50.dxp_ref), custom_call_target="tpu_custom_call" | custom-call | flops 3300000000 | bytes 8000000 | tf_op jit(solution)/shard_map/restore/pallas_call | solution.py:822
  370.5 2.9 collective-permute-done.38
  376.3 3.3 collective-permute-start.43
  382.3 5.5 %collective-permute-done.41 = bf16[2,192,384]{2,1,0:T(8,128)(2,1)S(1)} collective-permute-done((bf16[2,192,384]{2,1,0:T(8,128)(2,1)}, bf16[2,192,384]{2,1,0:T(8,128)(2,1)S(1)}, u32[]{:S(2)}, u32[]{:S(2)}) %collective-permute-start.41) | collective-permute-done | bytes 294944 | tf_op jit(solution)/shard_map/ppermute | solution.py:172
  387.8 4.0 collective-permute-done.43
  391.8 13.3 %collective-permute-done.42 = bf16[2,192,384]{2,1,0:T(8,128)(2,1)S(1)} collective-permute-done((bf16[2,192,384]{2,1,0:T(8,128)(2,1)}, bf16[2,192,384]{2,1,0:T(8,128)(2,1)S(1)}, u32[]{:S(2)}, u32[]{:S(2)}) %collective-permute-start.42) | collective-permute-done | bytes 294944 | tf_op jit(solution)/shard_map/ppermute | solution.py:172
  406.4 7.8 %collective-permute-done.44 = bf16[2,192,384]{2,1,0:T(8,128)(2,1)S(1)} collective-permute-done((bf16[2,192,384]{2,1,0:T(8,128)(2,1)S(1)}, bf16[2,192,384]{2,1,0:T(8,128)(2,1)S(1)}, u32[]{:S(2)}, u32[]{:S(2)}) %collective-permute-start.44) | collective-permute-done | bytes 294944 | tf_op jit(solution)/shard_map/ppermute | solution.py:172
  (239 shorter events, 87.1 us)
Async XLA Ops:
  6.1 54.0 %collective-permute-start.2 = (bf16[1248]{0:T(1024)(128)(2,1)S(1)}, bf16[1248]{0:T(1024)(128)(2,1)S(1)}, u32[]{:S(2)}, u32[]{:S(2)}) collective-permute-start(bf16[1248]{0:T(1024)(128)(2,1)S(1)} %concatenate.38), channel_id=1, source_target_pairs={{0,24},{1,25},{2,26},{3,27},{4,28},{5,29},{6,30},{7,31},{8,0},{9,1... | collective-permute-start | bytes 7496 | tf_op jit(solution)/shard_map/ppermute | solution.py:172
  11.2 49.0 %collective-permute-start.1 = (bf16[1248]{0:T(1024)(128)(2,1)S(1)}, bf16[1248]{0:T(1024)(128)(2,1)S(1)}, u32[]{:S(2)}, u32[]{:S(2)}) collective-permute-start(bf16[1248]{0:T(1024)(128)(2,1)S(1)} %concatenate.38), channel_id=1, source_target_pairs={{0,16},{1,17},{2,18},{3,19},{4,20},{5,21},{6,22},{7,23},{8,24},{9,... | collective-permute-start | bytes 7496 | tf_op jit(solution)/shard_map/ppermute | solution.py:172
  11.2 52.9 %collective-permute-start = (bf16[1248]{0:T(1024)(128)(2,1)S(1)}, bf16[1248]{0:T(1024)(128)(2,1)S(1)}, u32[]{:S(2)}, u32[]{:S(2)}) collective-permute-start(bf16[1248]{0:T(1024)(128)(2,1)S(1)} %concatenate.38), channel_id=1, source_target_pairs={{0,8},{1,9},{2,10},{3,11},{4,12},{5,13},{6,14},{7,15},{8,16},{9,17... | collective-permute-start | bytes 7496 | tf_op jit(solution)/shard_map/ppermute | solution.py:172
  28.0 36.1 %collective-permute-start.6 = (bf16[2,96,384]{2,1,0:T(8,128)(2,1)}, bf16[2,96,384]{2,1,0:T(8,128)(2,1)S(1)}, u32[]{:S(2)}, u32[]{:S(2)}) collective-permute-start(bf16[2,96,384]{2,1,0:T(8,128)(2,1)} %get-tuple-element.39), channel_id=1, source_target_pairs={{0,24},{1,25},{2,26},{3,27},{4,28},{5,29},{6,30},{7,31},{8,0},{9,1... | collective-permute-start | bytes 442376 | tf_op jit(solution)/shard_map/ppermute | solution.py:172
  30.9 34.1 %collective-permute-start.5 = (bf16[2,96,384]{2,1,0:T(8,128)(2,1)}, bf16[2,96,384]{2,1,0:T(8,128)(2,1)S(1)}, u32[]{:S(2)}, u32[]{:S(2)}) collective-permute-start(bf16[2,96,384]{2,1,0:T(8,128)(2,1)} %get-tuple-element.39), channel_id=1, source_target_pairs={{0,16},{1,17},{2,18},{3,19},{4,20},{5,21},{6,22},{7,23},{8,24},{9,... | collective-permute-start | bytes 442376 | tf_op jit(solution)/shard_map/ppermute | solution.py:172
  64.1 27.4 %collective-permute-start.16 = (bf16[2,192,384]{2,1,0:T(8,128)(2,1)S(1)}, bf16[2,192,384]{2,1,0:T(8,128)(2,1)S(1)}, u32[]{:S(2)}, u32[]{:S(2)}) collective-permute-start(bf16[2,192,384]{2,1,0:T(8,128)(2,1)S(1)} %copy-done.9), channel_id=1, source_target_pairs={{0,16},{1,17},{2,18},{3,19},{4,20},{5,21},{6,22},{7,23},{8,24},{9,... | collective-permute-start | bytes 884744 | tf_op jit(solution)/shard_map/ppermute | solution.py:172
  64.2 27.3 %collective-permute-start.15 = (bf16[2,192,384]{2,1,0:T(8,128)(2,1)S(1)}, bf16[2,192,384]{2,1,0:T(8,128)(2,1)S(1)}, u32[]{:S(2)}, u32[]{:S(2)}) collective-permute-start(bf16[2,192,384]{2,1,0:T(8,128)(2,1)S(1)} %copy-done.9), channel_id=1, source_target_pairs={{0,8},{1,9},{2,10},{3,11},{4,12},{5,13},{6,14},{7,15},{8,16},{9,17... | collective-permute-start | bytes 884744 | tf_op jit(solution)/shard_map/ppermute | solution.py:172
  68.8 28.3 %collective-permute-start.7 = (bf16[4,96,384]{2,1,0:T(8,128)(2,1)S(1)}, bf16[4,96,384]{2,1,0:T(8,128)(2,1)S(1)}, u32[]{:S(2)}, u32[]{:S(2)}) collective-permute-start(bf16[4,96,384]{2,1,0:T(8,128)(2,1)S(1)} %get-tuple-element.103), channel_id=1, source_target_pairs={{0,2},{1,3},{2,0},{3,1},{4,6},{5,7},{6,4},{7,5},{8,10},{9,11},{10,... | collective-permute-start | bytes 884744 | tf_op jit(solution)/shard_map/ppermute | solution.py:172
  93.3 16.3 %collective-permute-start.20 = (bf16[4,192,384]{2,1,0:T(8,128)(2,1)S(1)}, bf16[4,192,384]{2,1,0:T(8,128)(2,1)S(1)}, u32[]{:S(2)}, u32[]{:S(2)}) collective-permute-start(bf16[4,192,384]{2,1,0:T(8,128)(2,1)S(1)} %get-tuple-element.89), channel_id=1, source_target_pairs={{0,4},{1,5},{2,6},{3,7},{4,0},{5,1},{6,2},{7,3},{8,12},{9,13},{10,... | collective-permute-start | bytes 1769480 | tf_op jit(solution)/shard_map/ppermute | solution.py:172
  94.9 21.9 %collective-permute-start.3 = (bf16[4,1248]{1,0:T(4,128)(2,1)S(1)}, bf16[4,1248]{1,0:T(4,128)(2,1)S(1)}, u32[]{:S(2)}, u32[]{:S(2)}) collective-permute-start(bf16[4,1248]{1,0:T(4,128)(2,1)S(1)} %pad_maximum_fusion.11), channel_id=1, source_target_pairs={{0,4},{1,5},{2,6},{3,7},{4,0},{5,1},{6,2},{7,3},{8,12},{9,13},{10,... | collective-permute-start | bytes 29960 | tf_op jit(solution)/shard_map/ppermute | solution.py:172
  95.6 20.6 %collective-permute-start.9 = (bf16[4,96,384]{2,1,0:T(8,128)(2,1)S(1)}, bf16[4,96,384]{2,1,0:T(8,128)(2,1)S(1)}, u32[]{:S(2)}, u32[]{:S(2)}) collective-permute-start(bf16[4,96,384]{2,1,0:T(8,128)(2,1)S(1)} %get-tuple-element.101), channel_id=1, source_target_pairs={{0,4},{1,5},{2,6},{3,7},{4,0},{5,1},{6,2},{7,3},{8,12},{9,13},{10,... | collective-permute-start | bytes 884744 | tf_op jit(solution)/shard_map/ppermute | solution.py:172
  97.2 23.2 %collective-permute-start.11 = (bf16[2,4,96,384]{3,2,1,0:T(8,128)(2,1)S(1)}, bf16[2,4,96,384]{3,2,1,0:T(8,128)(2,1)}, u32[]{:S(2)}, u32[]{:S(2)}) collective-permute-start(bf16[2,4,96,384]{3,2,1,0:T(8,128)(2,1)S(1)} %pad_maximum_fusion.4.refs_7_), channel_id=1, source_target_pairs={{0,1},{1,0},{2,3},{3,2},{4,5},{5,4},{6,7},{7,6},{8,9},{9,8},{10,11... | collective-permute-start | bytes 1769480 | tf_op jit(solution)/shard_map/ppermute | solution.py:172
  106.0 23.0 %collective-permute-start.8 = (bf16[2,4,96,384]{3,2,1,0:T(8,128)(2,1)S(1)}, bf16[2,4,96,384]{3,2,1,0:T(8,128)(2,1)}, u32[]{:S(2)}, u32[]{:S(2)}) collective-permute-start(bf16[2,4,96,384]{3,2,1,0:T(8,128)(2,1)S(1)} %pad_maximum_fusion.4.refs_7_), channel_id=1, source_target_pairs={{0,4},{1,5},{2,6},{3,7},{4,0},{5,1},{6,2},{7,3},{8,12},{9,13},{10,... | collective-permute-start | bytes 1769480 | tf_op jit(solution)/shard_map/ppermute | solution.py:172
  109.7 44.7 %collective-permute-start.19 = (bf16[2,4,192,384]{3,2,1,0:T(8,128)(2,1)S(1)}, bf16[2,4,192,384]{3,2,1,0:T(8,128)(2,1)}, u32[]{:S(2)}, u32[]{:S(2)}) collective-permute-start(bf16[2,4,192,384]{3,2,1,0:T(8,128)(2,1)S(1)} %pad_maximum_fusion.2.refs_6_), channel_id=1, source_target_pairs={{0,4},{1,5},{2,6},{3,7},{4,0},{5,1},{6,2},{7,3},{8,12},{9,13},{10,... | collective-permute-start | bytes 3538952 | tf_op jit(solution)/shard_map/ppermute | solution.py:172
  116.2 38.6 %collective-permute-start.21 = (bf16[2,4,192,384]{3,2,1,0:T(8,128)(2,1)S(1)}, bf16[2,4,192,384]{3,2,1,0:T(8,128)(2,1)}, u32[]{:S(2)}, u32[]{:S(2)}) collective-permute-start(bf16[2,4,192,384]{3,2,1,0:T(8,128)(2,1)S(1)} %pad_maximum_fusion.3.refs_8_), channel_id=1, source_target_pairs={{0,2},{1,3},{2,0},{3,1},{4,6},{5,7},{6,4},{7,5},{8,10},{9,11},{10,... | collective-permute-start | bytes 3538952 | tf_op jit(solution)/shard_map/ppermute | solution.py:172
  116.8 35.5 %collective-permute-start.10 = (bf16[2,4,96,384]{3,2,1,0:T(8,128)(2,1)S(1)}, bf16[2,4,96,384]{3,2,1,0:T(8,128)(2,1)}, u32[]{:S(2)}, u32[]{:S(2)}) collective-permute-start(bf16[2,4,96,384]{3,2,1,0:T(8,128)(2,1)S(1)} %pad_maximum_fusion.5.refs_9_), channel_id=1, source_target_pairs={{0,2},{1,3},{2,0},{3,1},{4,6},{5,7},{6,4},{7,5},{8,10},{9,11},{10,... | collective-permute-start | bytes 1769480 | tf_op jit(solution)/shard_map/ppermute | solution.py:172
  120.4 33.3 %collective-permute-start.13 = (bf16[2,4,96,384]{3,2,1,0:T(8,128)(2,1)S(1)}, bf16[2,4,96,384]{3,2,1,0:T(8,128)(2,1)}, u32[]{:S(2)}, u32[]{:S(2)}) collective-permute-start(bf16[2,4,96,384]{3,2,1,0:T(8,128)(2,1)S(1)} %pad_maximum_fusion.5.refs_9_), channel_id=1, source_target_pairs={{0,1},{1,0},{2,3},{3,2},{4,5},{5,4},{6,7},{7,6},{8,9},{9,8},{10,11... | collective-permute-start | bytes 1769480 | tf_op jit(solution)/shard_map/ppermute | solution.py:172
  129.0 25.3 %collective-permute-start.12 = (bf16[2,4,96,384]{3,2,1,0:T(8,128)(2,1)}, bf16[2,4,96,384]{3,2,1,0:T(8,128)(2,1)}, u32[]{:S(2)}, u32[]{:S(2)}) collective-permute-start(bf16[2,4,96,384]{3,2,1,0:T(8,128)(2,1)} %collective-permute-done.8.refs_8_), channel_id=1, source_target_pairs={{0,1},{1,0},{2,3},{3,2},{4,5},{5,4},{6,7},{7,6},{8,9},{9,8},{10,11... | collective-permute-start | bytes 1769480 | tf_op jit(solution)/shard_map/ppermute | solution.py:172
  153.7 27.3 %collective-permute-start.22 = (bf16[2,4,192,384]{3,2,1,0:T(8,128)(2,1)S(1)}, bf16[2,4,192,384]{3,2,1,0:T(8,128)(2,1)}, u32[]{:S(2)}, u32[]{:S(2)}) collective-permute-start(bf16[2,4,192,384]{3,2,1,0:T(8,128)(2,1)S(1)} %pad_maximum_fusion.2.refs_6_), channel_id=1, source_target_pairs={{0,1},{1,0},{2,3},{3,2},{4,5},{5,4},{6,7},{7,6},{8,9},{9,8},{10,11... | collective-permute-start | bytes 3538952 | tf_op jit(solution)/shard_map/ppermute | solution.py:172
  154.2 26.8 %collective-permute-start.24 = (bf16[2,4,192,384]{3,2,1,0:T(8,128)(2,1)S(1)}, bf16[2,4,192,384]{3,2,1,0:T(8,128)(2,1)}, u32[]{:S(2)}, u32[]{:S(2)}) collective-permute-start(bf16[2,4,192,384]{3,2,1,0:T(8,128)(2,1)S(1)} %pad_maximum_fusion.3.refs_8_), channel_id=1, source_target_pairs={{0,1},{1,0},{2,3},{3,2},{4,5},{5,4},{6,7},{7,6},{8,9},{9,8},{10,11... | collective-permute-start | bytes 3538952 | tf_op jit(solution)/shard_map/ppermute | solution.py:172
  154.3 26.7 %collective-permute-start.23 = (bf16[2,4,192,384]{3,2,1,0:T(8,128)(2,1)}, bf16[2,4,192,384]{3,2,1,0:T(8,128)(2,1)}, u32[]{:S(2)}, u32[]{:S(2)}) collective-permute-start(bf16[2,4,192,384]{3,2,1,0:T(8,128)(2,1)} %collective-permute-done.19.refs_7_), channel_id=1, source_target_pairs={{0,1},{1,0},{2,3},{3,2},{4,5},{5,4},{6,7},{7,6},{8,9},{9,8},{10,11... | collective-permute-start | bytes 3538952 | tf_op jit(solution)/shard_map/ppermute | solution.py:172
  154.8 26.3 %collective-permute-start.25 = (bf16[2,4,192,384]{3,2,1,0:T(8,128)(2,1)}, bf16[2,4,192,384]{3,2,1,0:T(8,128)(2,1)}, u32[]{:S(2)}, u32[]{:S(2)}) collective-permute-start(bf16[2,4,192,384]{3,2,1,0:T(8,128)(2,1)} %collective-permute-done.21.refs_9_), channel_id=1, source_target_pairs={{0,1},{1,0},{2,3},{3,2},{4,5},{5,4},{6,7},{7,6},{8,9},{9,8},{10,11... | collective-permute-start | bytes 3538952 | tf_op jit(solution)/shard_map/ppermute | solution.py:172
  277.8 41.7 %collective-permute-start.36 = (bf16[4,2,2,2,192,384]{5,4,3,2,1,0:T(8,128)(2,1)}, bf16[4,2,2,2,192,384]{5,4,3,2,1,0:T(8,128)(2,1)}, u32[]{:S(2)}, u32[]{:S(2)}) collective-permute-start(bf16[4,2,2,2,192,384]{5,4,3,2,1,0:T(8,128)(2,1)} %get-tuple-element.61), channel_id=1, source_target_pairs={{0,1},{1,0},{2,3},{3,2},{4,5},{5,4},{6,7},{7,6},{8,9},{9,8},{10,11... | collective-permute-start | bytes 14155784 | tf_op jit(solution)/shard_map/ppermute | solution.py:172
  286.6 16.7 %collective-permute-start.29 = (bf16[4,2,104,384]{3,2,1,0:T(8,128)(2,1)S(1)}, bf16[4,2,104,384]{3,2,1,0:T(8,128)(2,1)S(1)}, u32[]{:S(2)}, u32[]{:S(2)}) collective-permute-start(bf16[4,2,104,384]{3,2,1,0:T(8,128)(2,1)S(1)} %fusion.9), channel_id=1, source_target_pairs={{0,2},{1,3},{2,0},{3,1},{4,6},{5,7},{6,4},{7,5},{8,10},{9,11},{10,... | collective-permute-start | bytes 1916936 | tf_op jit(solution)/shard_map/ppermute | solution.py:172
  288.5 16.7 %collective-permute-start.27 = (bf16[4,2,104,384]{3,2,0,1:T(8,128)(2,1)S(1)}, bf16[4,2,104,384]{3,2,0,1:T(8,128)(2,1)S(1)}, u32[]{:S(2)}, u32[]{:S(2)}) collective-permute-start(bf16[4,2,104,384]{3,2,0,1:T(8,128)(2,1)S(1)} %fusion.8), channel_id=1, source_target_pairs={{0,4},{1,5},{2,6},{3,7},{4,0},{5,1},{6,2},{7,3},{8,12},{9,13},{10,... | collective-permute-start | bytes 1916936 | tf_op jit(solution)/shard_map/ppermute | solution.py:172
  321.5 30.2 %collective-permute-start.39 = (bf16[4,2,192,384]{3,2,1,0:T(8,128)(2,1)S(1)}, bf16[4,2,192,384]{3,2,1,0:T(8,128)(2,1)S(1)}, u32[]{:S(2)}, u32[]{:S(2)}) collective-permute-start(bf16[4,2,192,384]{3,2,1,0:T(8,128)(2,1)S(1)} %fusion.3), channel_id=1, source_target_pairs={{0,2},{1,3},{2,0},{3,1},{4,6},{5,7},{6,4},{7,5},{8,10},{9,11},{10,... | collective-permute-start | bytes 3538952 | tf_op jit(solution)/shard_map/ppermute | solution.py:172
  324.3 30.7 %collective-permute-start.37 = (bf16[4,2,192,384]{3,2,0,1:T(8,128)(2,1)S(1)}, bf16[4,2,192,384]{3,2,0,1:T(8,128)(2,1)S(1)}, u32[]{:S(2)}, u32[]{:S(2)}) collective-permute-start(bf16[4,2,192,384]{3,2,0,1:T(8,128)(2,1)S(1)} %fusion.2), channel_id=1, source_target_pairs={{0,4},{1,5},{2,6},{3,7},{4,0},{5,1},{6,2},{7,3},{8,12},{9,13},{10,... | collective-permute-start | bytes 3538952 | tf_op jit(solution)/shard_map/ppermute | solution.py:172
  330.1 20.8 %collective-permute-start.34 = (bf16[2,104,384]{2,1,0:T(8,128)(2,1)S(1)}, bf16[2,104,384]{2,1,0:T(8,128)(2,1)S(1)}, u32[]{:S(2)}, u32[]{:S(2)}) collective-permute-start(bf16[2,104,384]{2,1,0:T(8,128)(2,1)S(1)} %fusion.30), channel_id=1, source_target_pairs={{0,2},{1,3},{2,0},{3,1},{4,6},{5,7},{6,4},{7,5},{8,10},{9,11},{10,... | collective-permute-start | bytes 479240 | tf_op jit(solution)/shard_map/ppermute | solution.py:172
  353.4 15.9 %collective-permute-start.40 = (bf16[4,192,384]{2,1,0:T(8,128)(2,1)S(1)}, bf16[4,192,384]{2,1,0:T(8,128)(2,1)}, u32[]{:S(2)}, u32[]{:S(2)}) collective-permute-start(bf16[4,192,384]{2,1,0:T(8,128)(2,1)S(1)} %fusion.15), channel_id=1, source_target_pairs={{0,4},{1,5},{2,6},{3,7},{4,0},{5,1},{6,2},{7,3},{8,12},{9,13},{10,... | collective-permute-start | bytes 1769480 | tf_op jit(solution)/shard_map/ppermute | solution.py:172
  357.7 15.8 %collective-permute-start.38 = (bf16[4,192,384]{2,1,0:T(8,128)(2,1)}, bf16[4,192,384]{2,1,0:T(8,128)(2,1)}, u32[]{:S(2)}, u32[]{:S(2)}) collective-permute-start(bf16[4,192,384]{2,1,0:T(8,128)(2,1)} %fusion.14), channel_id=1, source_target_pairs={{0,2},{1,3},{2,0},{3,1},{4,6},{5,7},{6,4},{7,5},{8,10},{9,11},{10,... | collective-permute-start | bytes 1769480 | tf_op jit(solution)/shard_map/ppermute | solution.py:172
  376.3 15.5 %collective-permute-start.43 = (bf16[2,192,384]{2,1,0:T(8,128)(2,1)}, bf16[2,192,384]{2,1,0:T(8,128)(2,1)S(1)}, u32[]{:S(2)}, u32[]{:S(2)}) collective-permute-start(bf16[2,192,384]{2,1,0:T(8,128)(2,1)} %get-tuple-element.83), channel_id=1, source_target_pairs={{0,24},{1,25},{2,26},{3,27},{4,28},{5,29},{6,30},{7,31},{8,0},{9,1... | collective-permute-start | bytes 884744 | tf_op jit(solution)/shard_map/ppermute | solution.py:172
  379.6 25.5 %collective-permute-start.42 = (bf16[2,192,384]{2,1,0:T(8,128)(2,1)}, bf16[2,192,384]{2,1,0:T(8,128)(2,1)S(1)}, u32[]{:S(2)}, u32[]{:S(2)}) collective-permute-start(bf16[2,192,384]{2,1,0:T(8,128)(2,1)} %get-tuple-element.84), channel_id=1, source_target_pairs={{0,16},{1,17},{2,18},{3,19},{4,20},{5,21},{6,22},{7,23},{8,24},{9,... | collective-permute-start | bytes 884744 | tf_op jit(solution)/shard_map/ppermute | solution.py:172
  (32 other events, 399.1 us)

commit v2 on v1

v2 whole, which is shorter than its diff:
```python
import functools
import math

import jax
import jax.numpy as jnp
import numpy as np
from jax import lax
from jax.experimental import pallas as pl
from jax.experimental.pallas import tpu as pltpu
from jax.sharding import PartitionSpec as P

HEADS = 12
HEAD_DIM = 64
GENES = 4
LANES = 128
EPSILON = 1e-05
NEG_FILL = -1000000000.0
F32 = jnp.float32
BF16 = jnp.bfloat16
MIB = 1 << 20


def nn(left, right):
    return lax.dot_general(left, right, (((1,), (0,)), ((), ())), preferred_element_type=F32)


def nt(left, right):
    return lax.dot_general(left, right, (((1,), (1,)), ((), ())), preferred_element_type=F32)


def tn(left, right):
    return lax.dot_general(left, right, (((0,), (0,)), ((), ())), preferred_element_type=F32)


def iota(shape, axis):
    return lax.broadcasted_iota(jnp.int32, shape, axis)


def full(shape):
    return pl.BlockSpec(shape, lambda *ids: (0,) * len(shape))


def rows_of(shape):
    return pl.BlockSpec(shape, lambda g, *ids: (g,) + (0,) * (len(shape) - 1))


def call(kernel, grid, in_specs, out_specs, out_shape, scratch=(), vmem=60, prefetch=1, name=None, cost=None, aliases=None):
    return pl.pallas_call(
        kernel,
        grid_spec=pltpu.PrefetchScalarGridSpec(
            num_scalar_prefetch=prefetch,
            grid=grid,
            in_specs=in_specs,
            out_specs=out_specs,
            scratch_shapes=list(scratch),
        ),
        out_shape=out_shape,
        input_output_aliases=aliases or {},
        compiler_params=pltpu.CompilerParams(
            dimension_semantics=("arbitrary",) * len(grid), vmem_limit_bytes=vmem * MIB
        ),
        name=name,
        cost_estimate=cost and pl.CostEstimate(flops=int(cost[0]), bytes_accessed=int(cost[1]), transcendentals=0),
    )


def shape_of(shape, dtype):
    return jax.ShapeDtypeStruct(shape, dtype)


def normalize(x):
    mean = jnp.mean(x, -1, keepdims=True)
    centered = x - mean
    scale = lax.rsqrt(jnp.mean(centered * centered, -1, keepdims=True) + EPSILON)
    return centered * scale, scale


def swap_halves(t):
    low = (iota(t.shape, 1) % HEAD_DIM) < HEAD_DIM // 2
    return jnp.where(
        low, pltpu.roll(t, LANES - HEAD_DIM // 2, 1), pltpu.roll(t, HEAD_DIM // 2, 1)
    )


def head_masks(rows):
    lane = iota((rows, LANES), 1)
    return [(lane < HEAD_DIM), (lane >= HEAD_DIM)]


def allowed_pairs(plan, gene, span):
    length = plan[gene]
    i, j = iota((span, span), 0), iota((span, span), 1)
    return ((i < length) & (j < length)) | (i == j)


def keep(mask, value):
    return jnp.where(mask, value, jnp.zeros_like(value))


Z_SIZE = 4
COLUMNS = 384
AXES = ("fsdp", "replica")
ANY = pl.BlockSpec(memory_space=pl.ANY)
PIECES = 32
EVERY = [(dx, dy, dc) for dx in range(2) for dy in range(2) for dc in range(2)]
SLOTS = (0, 128, 256, 640, 768, 896, 1024, 1408)
PACKED = 1536


def tuned_mesh(mesh):
    return mesh.shape["fsdp"] == 2 * Z_SIZE and mesh.shape["replica"] == 4


def pairs(step):
    out = []
    for z in range(Z_SIZE):
        for x in range(2):
            for y in range(2):
                for c in range(2):
                    tz, tx, ty, tc = step(z, x, y, c)
                    out.append((((z * 2 + x) * 2 + y) * 2 + c, (((tz % Z_SIZE) * 2 + tx) * 2 + ty) * 2 + tc))
    return out


ACROSS_X = pairs(lambda z, x, y, c: (z, 1 - x, y, c))
ACROSS_Y = pairs(lambda z, x, y, c: (z, x, 1 - y, c))
ACROSS_CORE = pairs(lambda z, x, y, c: (z, x, y, 1 - c))
ALONG_Z = [pairs(functools.partial(lambda d, z, x, y, c: (z + d, x, y, c), d)) for d in range(Z_SIZE)]
tie = lax.optimization_barrier


def move(array, table):
    return lax.ppermute(array, AXES, table)


def place():
    f, r = lax.axis_index("fsdp"), lax.axis_index("replica")
    return jnp.stack([f // 2, f % 2, r // 2, r % 2]).astype(jnp.int32)


def spot(at, dz, dx, dy, dc):
    z = lax.rem(at[0] + (Z_SIZE - dz), Z_SIZE)
    return z * 2 + lax.bitwise_xor(at[1], dx), lax.bitwise_xor(at[2], dy), lax.bitwise_xor(at[3], dc)


def piece_index(half, dz, dx, dy):
    own = 24 + dx * 4 + dy * 2 + half
    if isinstance(dz, int) and dz == 0:
        return own
    far = (12 + dy * 6 + dx * 3 if half else dx * 6 + dy * 3) + dz - 1
    return far if isinstance(dz, int) else jnp.where(dz == 0, own, far)


def at_rows(start, size):
    return pl.ds(pl.multiple_of(start, 16), size)


def at_columns(start, size):
    return pl.ds(pl.multiple_of(start, LANES), size)


def quarters_kernel(at, *refs):
    wqkv, wout, wup, wdown = refs[:4]
    vectors, (near1, near2, side, packed) = refs[4:12], refs[12:]
    width = wout.shape[1]
    rows = wout.shape[0] // 2
    packed[...] = jnp.zeros_like(packed)
    for ref, start in zip(vectors, SLOTS):
        packed[:, start : start + ref.shape[0]] = ref[...].reshape(1, -1)
    tail = jnp.zeros((8, COLUMNS), BF16)
    for i in range(4):
        part = jnp.broadcast_to(packed[:, i * COLUMNS : (i + 1) * COLUMNS], (8, COLUMNS))
        tail = jnp.where(iota((8, COLUMNS), 0) == i, part, tail)
    mine = at_rows(at[3] * rows, rows)
    for y in range(2):
        for b in range(4):
            ref, base = (wqkv, b * width) if b < 3 else (wout, 0)
            start = base + y * COLUMNS
            side[y, b // 2, (b % 2) * rows : (b % 2 + 1) * rows, :] = ref[mine, start : start + COLUMNS]
            start = b * width + y * COLUMNS
            side[y, 0, (2 + b) * rows : (3 + b) * rows, :] = wup[mine, start : start + COLUMNS]
        here = slice(y * COLUMNS, (y + 1) * COLUMNS)
        side[y, 1, 2 * rows : 6 * rows, :] = wdown[at_rows(at[3] * 4 * rows, 4 * rows), here]
        for h in range(2):
            side[y, h, 6 * rows : 6 * rows + 8, :] = tail
    near1[:, 0 : 2 * rows, :] = side[at[2], :, 0 : 2 * rows, :]
    near2[...] = side[at[2], :, 2 * rows : 6 * rows, :]
    for h in range(2):
        near1[h, 2 * rows : 2 * rows + 8, :] = tail


def quarters(at, wqkv, wout, wup, wdown, vectors):
    rows = wqkv.shape[0] // 2
    shapes = [
        (2, 2 * rows + 8, COLUMNS),
        (2, 4 * rows, COLUMNS),
        (2, 2, 6 * rows + 8, COLUMNS),
    ]
    matrices = (wqkv, wout, wup, wdown)
    return call(
        quarters_kernel,
        (1,),
        [full(v.shape) for v in matrices + tuple(vectors)],
        [full(s) for s in shapes],
        [shape_of(s, BF16) for s in shapes],
        [pltpu.VMEM((1, PACKED), BF16)],
        name="quarters",
        cost=(0, 6e6),
    )(at, *matrices, *vectors)


def rel_mask(at, shards, columns, size, x_bit):
    z = (at[0] + Z_SIZE - iota((shards, columns), 0)) % Z_SIZE
    shard = z * 2 + lax.bitwise_xor(at[1], x_bit)
    return (iota((shards, columns), 1) // size == shard) & (iota((shards, columns), 0) < Z_SIZE)


def spread(size, columns):
    lanes = -(-size // LANES) * LANES
    lane, column = iota((lanes, columns), 0), iota((lanes, columns), 1)
    return jnp.where(column % size == lane, 1.0, 0.0).astype(BF16)


def unpack_kernel(at, near_ref, far_ref, *refs):
    out, row_ref = refs[:8], refs[8]
    row_ref[...] = jnp.zeros_like(row_ref)
    for x_bit, rows in enumerate((near_ref, far_ref)):
        for d in range(Z_SIZE):
            for i in range(4):
                row_ref[x_bit, d : d + 1, i * COLUMNS : (i + 1) * COLUMNS] = rows[d, i : i + 1, :].astype(F32)
    for ref, start in zip(out, SLOTS):
        columns = ref.shape[1]
        size = columns // (2 * Z_SIZE)
        table = spread(size, columns)
        lanes = slice(start, start + table.shape[0])
        total = jnp.zeros((1, columns), F32)
        for x_bit in range(2):
            got = nn(row_ref[x_bit, :, lanes].astype(BF16), table)
            mask = rel_mask(at, 8, columns, size, x_bit)
            total = total + jnp.sum(jnp.where(mask, got, 0.0), 0, keepdims=True)
        ref[...] = total


def unpack(at, near, far, sizes):
    shapes = [(1, n * 2 * Z_SIZE) for n in sizes]
    return call(
        unpack_kernel,
        (1,),
        [full(near.shape)] * 2,
        [full(s) for s in shapes],
        [shape_of(s, F32) for s in shapes],
        [pltpu.VMEM((2, 8, PACKED), F32)],
        name="unpack",
        cost=(1e8, 1e5),
    )(at, near, far)


def plan_of(segments):
    lengths = [jnp.sum(jnp.where(segments == g, 1.0, 0.0)).astype(jnp.int32) for g in range(GENES)]
    span = segments.size // GENES
    starts, before, start, free = [], [], 0, 0
    for g in range(GENES):
        starts.append(start)
        before.append(free)
        start = start + lengths[g]
        free = free + span - lengths[g]
    return [jnp.asarray(v, jnp.int32) for v in lengths + starts + before + [start]]


def source_of_slots(plan, gene, slots):
    length = plan[gene]
    return jnp.where(
        slots < length,
        plan[GENES + gene] + slots,
        plan[3 * GENES] + plan[2 * GENES + gene] + slots - length,
    )


def prepare_kernel(seg_ref, x_ref, c_ref, freq_ref, plan_ref, xp_ref, cp_ref, cos_ref, sin_ref):
    gene = pl.program_id(0)
    span = xp_ref.shape[0]
    length = x_ref.shape[0]

    @pl.when(gene == 0)
    def _():
        for i, v in enumerate(plan_of(seg_ref[...])):
            plan_ref[i] = v

    slots = iota((span, 1), 0)
    source = source_of_slots(plan_ref, gene, slots)
    pick = jnp.where(iota((span, length), 1) == source, 1.0, 0.0).astype(BF16)
    xp_ref[...] = nn(pick, x_ref[...]).astype(BF16)
    cp_ref[...] = nn(pick, c_ref[...]).astype(BF16)
    start = jnp.where(slots < plan_ref[gene], plan_ref[GENES + gene], plan_ref[3 * GENES])
    angle = (source - start).astype(F32) * freq_ref[...]
    low = iota((span, LANES), 1) % HEAD_DIM < HEAD_DIM // 2
    cos_ref[...] = jnp.cos(angle)
    sine = jnp.sin(angle)
    sin_ref[...] = jnp.where(low, -sine, sine)


def prepare(segments, x, c):
    length, width = x.shape
    span = length // GENES
    frequency = np.power(10000.0, np.arange(HEAD_DIM // 2) * (-2.0 / HEAD_DIM))
    frequency = jnp.asarray(np.tile(frequency, LANES // (HEAD_DIM // 2))[None], F32)
    return call(
        prepare_kernel,
        (GENES,),
        [full((1, length)), full((length, width)), full((length, width)), full((1, LANES))],
        [
            pl.BlockSpec(memory_space=pltpu.SMEM),
            rows_of((span, width)),
            rows_of((span, width)),
            rows_of((span, LANES)),
            rows_of((span, LANES)),
        ],
        [
            shape_of((16,), jnp.int32),
            shape_of((length, width), BF16),
            shape_of((length, width), BF16),
            shape_of((length, LANES), F32),
            shape_of((length, LANES), F32),
        ],
        prefetch=0,
        name="prepare",
        cost=(3.3e9, 8e6),
    )(segments, x, c, frequency)


def far_piece(refs, half, dz, dx, dy, dc):
    refs = refs[4 * dc : 4 * dc + 4]
    ref, at = (refs[dx], (dy, dz - 1)) if half == 0 else (refs[2 + dy], (dx, dz - 1))
    return ref.at[(half,) + at] if len(ref.shape) == 5 else ref.at[at]


def load_matrices(at, source, wqkv_ref, wout_ref, sem):
    width = wout_ref.shape[0]
    rows = width // (4 * Z_SIZE)
    own = at_rows((at[0] * 2 + at[1]) * 2 * rows, 2 * rows)
    pltpu.make_async_copy(source[0], wqkv_ref.at[own], sem.at[0]).start()
    pltpu.make_async_copy(source[1], wout_ref.at[own], sem.at[1]).start()

    def put(piece, f, y, c):
        down = at_rows((f * 2 + c) * rows, rows)
        for b in range(4):
            src = piece(b // 2).at[pl.ds((b % 2) * rows, rows)]
            across = at_columns((b % 3) * width + y * COLUMNS, COLUMNS)
            dst = wqkv_ref if b < 3 else wout_ref
            pltpu.make_async_copy(src, dst.at[down, across], sem.at[b // 3]).start()

    for dc in range(2):
        f, _, c = spot(at, 0, 1, 0, dc)
        for y in range(2):
            put(lambda half: source[2 + dc].at[y, half, pl.ds(0, 2 * rows)], f, y, c)

    def one(dz, carry):
        for dx, dy, dc in EVERY:
            put(lambda half: far_piece(source[4:], half, dz, dx, dy, dc), *spot(at, dz, dx, dy, dc))
        return carry

    lax.fori_loop(1, Z_SIZE, one, 0)


def attend_kernel(plan, at, *refs, pieces):
    (xp_ref, cos_ref, sin_ref, g1_ref, b1_ref, bqkv_ref, bout_ref), refs = refs[:7], refs[7:]
    source, refs = (refs[:12], refs[12:]) if pieces else (refs[:2], refs[2:])
    (qkv_ref, o_ref, lse_ref, x1_ref), refs = refs[:4], refs[4:]
    if pieces:
        whole, refs = refs[:2], refs[2:]
    wqkv_ref, wout_ref, mask_ref, sem = refs
    gene = pl.program_id(0)
    span, width = xp_ref.shape

    def wait_both():
        pltpu.make_async_copy(wqkv_ref, wqkv_ref, sem.at[0]).wait()
        pltpu.make_async_copy(wout_ref, wout_ref, sem.at[1]).wait()

    @pl.when(gene == 0)
    def _():
        if pieces:
            load_matrices(at, source, wqkv_ref, wout_ref, sem)
        else:
            pltpu.make_async_copy(source[0], wqkv_ref, sem.at[0]).start()
            pltpu.make_async_copy(source[1], wout_ref, sem.at[1]).start()
        wait_both()
        if pieces:
            pltpu.make_async_copy(wqkv_ref, whole[0], sem.at[0]).start()
            pltpu.make_async_copy(wout_ref, whole[1], sem.at[1]).start()

    x = xp_ref[...].astype(F32)
    xhat, _ = normalize(x)
    a1 = (xhat * g1_ref[...] + b1_ref[...]).astype(BF16)
    cos, sin = cos_ref[...], sin_ref[...]
    for part in range(3):
        base = part * width
        t = nn(a1, wqkv_ref[:, base : base + width]) + bqkv_ref[:, base : base + width]
        for p in range(width // LANES):
            piece = t[:, p * LANES : (p + 1) * LANES]
            if part < 2:
                piece = piece * cos + swap_halves(piece) * sin
            qkv_ref[:, base + p * LANES : base + (p + 1) * LANES] = piece.astype(BF16)
    mask_ref[...] = jnp.where(allowed_pairs(plan, gene, span), 1.0, 0.0)
    masks = head_masks(span)
    for p in range(width // LANES):
        here = slice(p * LANES, (p + 1) * LANES)
        q = qkv_ref[:, p * LANES : (p + 1) * LANES]
        k = qkv_ref[:, width + p * LANES : width + (p + 1) * LANES] * BF16(1.0 / math.sqrt(HEAD_DIM))
        v = qkv_ref[:, 2 * width + p * LANES : 2 * width + (p + 1) * LANES]
        o = jnp.zeros((span, LANES), F32)
        for h in range(2):
            s = nt(keep(masks[h], k), q)
            s = jnp.where(mask_ref[...] > 0.5, s, NEG_FILL)
            peak = jnp.max(s, 0, keepdims=True)
            e = jnp.exp(s - peak)
            total = jnp.sum(e, 0, keepdims=True)
            weights = (e * (1.0 / total)).astype(BF16)
            o = o + tn(weights, keep(masks[h], v))
            lse_ref[pl.ds(2 * p + h, 1), :] = peak + jnp.log(total)
        o_ref[:, here] = o.astype(BF16)
    x1_ref[...] = x + nn(o_ref[...], wout_ref[...]) + bout_ref[...]
    if pieces:

        @pl.when(gene == pl.num_programs(0) - 1)
        def _():
            wait_both()


def attend(plan, at, xp, cos, sin, g1, b1, bqkv, bout, source):
    length, width = xp.shape
    span = length // GENES
    pieces = len(source) == 12
    weights = [shape_of((width, 3 * width), BF16), shape_of((width, width), BF16)]
    got = call(
        functools.partial(attend_kernel, pieces=pieces),
        (GENES,),
        [
            rows_of((span, width)),
            rows_of((span, LANES)),
            rows_of((span, LANES)),
            full((1, width)),
            full((1, width)),
            full((1, 3 * width)),
            full((1, width)),
        ]
        + [ANY] * len(source),
        [
            rows_of((span, 3 * width)),
            rows_of((span, width)),
            pl.BlockSpec((16, span), lambda g, *ids: (0, g)),
            rows_of((span, width)),
        ]
        + [ANY] * (2 if pieces else 0),
        [
            shape_of((length, 3 * width), BF16),
            shape_of((length, width), BF16),
            shape_of((16, length), F32),
            shape_of((length, width), F32),
        ]
        + (weights if pieces else []),
        [
            pltpu.VMEM((width, 3 * width), BF16),
            pltpu.VMEM((width, width), BF16),
            pltpu.VMEM((span, span), F32),
            pltpu.SemaphoreType.DMA((2,)),
        ],
        prefetch=2,
        name="attend",
        cost=(11e9, 20e6),
    )(plan, at, xp, cos, sin, g1, b1, bqkv, bout, *source)
    return got[:4], (got[4:] if pieces else source)


def feed_kernel(at, *refs, block, pieces, steps):
    (x1_ref, c_ref, g2_ref, b2_ref, bup_ref, bdown_ref), refs = refs[:6], refs[6:]
    source, refs = (refs[:12], refs[12:]) if pieces else (refs[:2], refs[2:])
    (out_ref, dx1_ref, da_ref, gbup_ref, sums_ref, first_ref, second_ref), refs = refs[:7], refs[7:]
    a2_ref, acc_ref, dh_ref, gr_ref, du_ref, wups, wdowns, gups, gdowns, load_sem, store_sem = refs
    step = pl.program_id(0)
    length, width = x1_ref.shape
    chunk = bup_ref.shape[1]
    blocks = length // block
    slot = lax.rem(step, 2)
    rows = width // (4 * Z_SIZE)

    def load(j, to):
        if pieces:
            own = at_rows((at[0] * 2 + at[1]) * 2 * rows, 2 * rows)
            src = source[0].at[:, at_columns(j * chunk, chunk)]
            pltpu.make_async_copy(src, wups.at[to, own], load_sem.at[0, to]).start()

            def put_up(piece, f, y, c):
                dst = wups.at[to, at_rows((f * 2 + c) * rows, rows), at_columns(y * COLUMNS, COLUMNS)]
                pltpu.make_async_copy(piece.at[at_rows(j * rows, rows)], dst, load_sem.at[0, to]).start()

            def put_down(piece, x, y, c):
                dst = wdowns.at[to, at_rows((x * 2 + c) * 4 * rows, 4 * rows), at_columns(y * COLUMNS, COLUMNS)]
                pltpu.make_async_copy(piece, dst, load_sem.at[1, to]).start()

            for dc in range(2):
                f, _, c = spot(at, 0, 1, 0, dc)
                for y in range(2):
                    put_up(source[2 + dc].at[y, 0, pl.ds(2 * rows, 4 * rows)], f, y, c)

            def one(dz, carry):
                for dx, dy, dc in EVERY:
                    put_up(far_piece(source[4:], 0, dz, dx, dy, dc), *spot(at, dz, dx, dy, dc))
                return carry

            lax.fori_loop(1, Z_SIZE, one, 0)

            @pl.when(j == at[0])
            def _():
                here = at_rows(at[1] * 8 * rows, 8 * rows)
                pltpu.make_async_copy(source[1], wdowns.at[to, here], load_sem.at[1, to]).start()
                for dc in range(2):
                    _, _, c = spot(at, 0, 1, 0, dc)
                    for y in range(2):
                        put_down(source[2 + dc].at[y, 1, pl.ds(2 * rows, 4 * rows)], 1 - at[1], y, c)

            @pl.when(j != at[0])
            def _():
                back = lax.rem(at[0] + (Z_SIZE - j), Z_SIZE)
                for dx, dy, dc in EVERY:
                    _, y, c = spot(at, back, dx, dy, dc)
                    put_down(far_piece(source[4:], 1, back, dx, dy, dc), lax.bitwise_xor(at[1], dx), y, c)

        else:
            part = source[0].at[:, at_columns(j * chunk, chunk)]
            pltpu.make_async_copy(part, wups.at[to], load_sem.at[0, to]).start()
            part = source[1].at[at_rows(j * chunk, chunk), :]
            pltpu.make_async_copy(part, wdowns.at[to], load_sem.at[1, to]).start()

    def store(j, to):
        if pieces:

            def one(dz, carry):
                for dx, dy, dc in EVERY:
                    f, y, c = spot(at, Z_SIZE - dz, dx, dy, dc)
                    src = gups.at[to, at_rows(f * 2 * rows + c * rows, rows), at_columns(y * COLUMNS, COLUMNS)]
                    dst = (first_ref, second_ref)[dc].at[piece_index(0, dz, dx, dy), at_rows(j * rows, rows)]
                    pltpu.make_async_copy(src, dst, store_sem.at[0, to]).start()
                return carry

            lax.fori_loop(0, Z_SIZE, one, 0)
            ahead = lax.rem(j + Z_SIZE - at[0], Z_SIZE)
            for dx, dy, dc in EVERY:
                f, y, c = spot(at, 0, dx, dy, dc)
                x = lax.bitwise_xor(at[1], dx)
                src = gdowns.at[to, at_rows((x * 2 + c) * 4 * rows, 4 * rows), at_columns(y * COLUMNS, COLUMNS)]
                dst = (first_ref, second_ref)[dc].at[piece_index(1, ahead, dx, dy)]
                pltpu.make_async_copy(src, dst, store_sem.at[1, to]).start()
        else:
            part = first_ref.at[:, at_columns(j * chunk, chunk)]
            pltpu.make_async_copy(gups.at[to], part, store_sem.at[0, to]).start()
            part = second_ref.at[at_rows(j * chunk, chunk), :]
            pltpu.make_async_copy(gdowns.at[to], part, store_sem.at[1, to]).start()

    def wait_load(to):
        pltpu.make_async_copy(wups.at[to], wups.at[to], load_sem.at[0, to]).wait()
        pltpu.make_async_copy(wdowns.at[to], wdowns.at[to], load_sem.at[1, to]).wait()

    def wait_store(to):
        pltpu.make_async_copy(gups.at[to], gups.at[to], store_sem.at[0, to]).wait()
        pltpu.make_async_copy(gdowns.at[to], gdowns.at[to], store_sem.at[1, to]).wait()

    @pl.when(step == 0)
    def _():
        load(0, 0)

        def one(i, carry):
            here = pl.ds(i * block, block)
            xhat, _ = normalize(x1_ref[here, :])
            a2_ref[here, :] = (xhat * g2_ref[...] + b2_ref[...]).astype(BF16)
            return carry

        lax.fori_loop(0, blocks, one, 0)

    wait_load(slot)

    @pl.when(step < steps - 1)
    def _():
        load(step + 1, 1 - slot)

    wup_ref, wdown_ref = wups.at[slot], wdowns.at[slot]

    def one(i, bias_sum):
        here = pl.ds(i * block, block)
        u = nn(a2_ref[here, :], wup_ref[...]) + bup_ref[...]
        phi = 0.5 + 0.5 * lax.erf(u * math.sqrt(0.5))
        slope = phi + u * (jnp.exp(-0.5 * u * u) * (1.0 / math.sqrt(2.0 * math.pi)))
        gr = (u * phi).astype(BF16)
        gr_ref[here, :] = gr
        du = (nt(c_ref[here, :], wdown_ref[...]) * slope).astype(BF16)
        du_ref[here, :] = du
        out = nn(gr, wdown_ref[...])
        dh = nt(du, wup_ref[...])

        @pl.when(step == 0)
        def _():
            acc_ref[here, :] = out
            dh_ref[here, :] = dh

        @pl.when(step > 0)
        def _():
            acc_ref[here, :] += out
            dh_ref[here, :] += dh

        return bias_sum + jnp.sum(du.astype(F32), 0, keepdims=True)

    gbup_ref[...] = lax.fori_loop(0, blocks, one, jnp.zeros((1, chunk), F32))

    @pl.when(step >= 2)
    def _():
        wait_store(slot)

    gdowns[slot] = tn(gr_ref[...], c_ref[...]).astype(BF16)
    gups[slot] = tn(a2_ref[...], du_ref[...]).astype(BF16)
    store(step, slot)

    @pl.when(step == steps - 1)
    def _():
        def one(i, sums):
            here = pl.ds(i * block, block)
            x1 = x1_ref[here, :]
            xhat, scale = normalize(x1)
            out_ref[here, :] = (x1 + acc_ref[here, :] + bdown_ref[...]).astype(BF16)
            dh = dh_ref[here, :]
            c = c_ref[here, :].astype(F32)
            e = dh * g2_ref[...]
            dx1 = c + scale * (
                e - jnp.mean(e, -1, keepdims=True) - xhat * jnp.mean(e * xhat, -1, keepdims=True)
            )
            dx1_ref[here, :] = dx1
            da = dx1.astype(BF16)
            da_ref[here, :] = da
            new = (
                jnp.sum(dh * xhat, 0, keepdims=True),
                jnp.sum(dh, 0, keepdims=True),
                jnp.sum(c, 0, keepdims=True),
                jnp.sum(da.astype(F32), 0, keepdims=True),
            )
            return tuple(a + b for a, b in zip(sums, new))

        sums = lax.fori_loop(0, blocks, one, (jnp.zeros((1, width), F32),) * 4)
        for i in range(4):
            sums_ref[i : i + 1, :] = sums[i]
        wait_store(1 - slot)
        wait_store(slot)


def feed(at, x1, c, g2, b2, bup, bdown, source):
    length, width = x1.shape
    hidden = bup.shape[1]
    steps = 4
    chunk = hidden // steps
    pieces = len(source) == 12
    if pieces:
        rows = width // Z_SIZE
        stored = [shape_of((PIECES, rows, COLUMNS), BF16)] * 2
    else:
        stored = [shape_of((width, hidden), BF16), shape_of((hidden, width), BF16)]
    return call(
        functools.partial(feed_kernel, block=length // 4, pieces=pieces, steps=steps),
        (steps,),
        [
            full((length, width)),
            full((length, width)),
            full((1, width)),
            full((1, width)),
            pl.BlockSpec((1, chunk), lambda j, *ids: (0, j)),
            full((1, width)),
        ]
        + [ANY] * len(source),
        [
            full((length, width)),
            full((length, width)),
            full((length, width)),
            pl.BlockSpec((1, chunk), lambda j, *ids: (0, j)),
            full((8, width)),
            ANY,
            ANY,
        ],
        [
            shape_of((length, width), BF16),
            shape_of((length, width), F32),
            shape_of((length, width), BF16),
            shape_of((1, hidden), F32),
            shape_of((8, width), F32),
        ]
        + stored,
        [
            pltpu.VMEM((length, width), BF16),
            pltpu.VMEM((length, width), F32),
            pltpu.VMEM((length, width), F32),
            pltpu.VMEM((length, chunk), BF16),
            pltpu.VMEM((length, chunk), BF16),
            pltpu.VMEM((2, width, chunk), BF16),
            pltpu.VMEM((2, chunk, width), BF16),
            pltpu.VMEM((2, width, chunk), BF16),
            pltpu.VMEM((2, chunk, width), BF16),
            pltpu.SemaphoreType.DMA((2, 2)),
            pltpu.SemaphoreType.DMA((2, 2)),
        ],
        name="feed",
        cost=(29e9, 40e6),
    )(at, x1, c, g2, b2, bup, bdown, *source)


def attend_back_kernel(
    plan, qkv_ref, da_ref, lse_ref, cos_ref, sin_ref, xp_ref, dx1_ref, g1_ref, wout_ref, wqkv_ref,
    *refs, base,
):
    dqkv_ref, dxp_ref, sums_ref, bias_ref, dout_ref, mask_ref = refs[-6:]
    gene = pl.program_id(0) + base
    span, width = da_ref.shape
    score_scale = 1.0 / math.sqrt(HEAD_DIM)
    dout_ref[...] = nt(da_ref[...], wout_ref[...]).astype(BF16)
    mask_ref[...] = jnp.where(allowed_pairs(plan, gene, span), 1.0, 0.0)
    cos, sin = cos_ref[...], sin_ref[...]
    masks = head_masks(span)

    def back(t):
        return (t * cos - swap_halves(t) * sin).astype(BF16)

    for p in range(width // LANES):
        here = slice(p * LANES, (p + 1) * LANES)
        q = qkv_ref[:, p * LANES : (p + 1) * LANES]
        k = qkv_ref[:, width + p * LANES : width + (p + 1) * LANES] * BF16(score_scale)
        v = qkv_ref[:, 2 * width + p * LANES : 2 * width + (p + 1) * LANES]
        dout = dout_ref[:, here]
        dq = jnp.zeros((span, LANES), F32)
        dk = jnp.zeros((span, LANES), F32)
        dv = jnp.zeros((span, LANES), F32)
        for h in range(2):
            kh = keep(masks[h], k)
            s = nt(kh, q)
            s = jnp.where(mask_ref[...] > 0.5, s, NEG_FILL)
            weights = jnp.exp(s - lse_ref[pl.ds(2 * p + h, 1), :])
            dw = nt(keep(masks[h], v), dout)
            dot = jnp.sum(weights * dw, 0, keepdims=True)
            ds = (weights * (dw - dot)).astype(BF16)
            dv = dv + nn(weights.astype(BF16), keep(masks[h], dout))
            dk = dk + nn(ds, keep(masks[h], q))
            dq = dq + tn(ds, kh)
        dqkv_ref[:, p * LANES : (p + 1) * LANES] = back(dq)
        dqkv_ref[:, width + p * LANES : width + (p + 1) * LANES] = back(dk * score_scale)
        dqkv_ref[:, 2 * width + p * LANES : 2 * width + (p + 1) * LANES] = dv.astype(BF16)

    dh = nt(dqkv_ref[...], wqkv_ref[...])
    xhat, scale = normalize(xp_ref[...].astype(F32))
    e = dh * g1_ref[...]
    dx = dx1_ref[...] + scale * (
        e - jnp.mean(e, -1, keepdims=True) - xhat * jnp.mean(e * xhat, -1, keepdims=True)
    )
    dxp_ref[...] = dx.astype(BF16)
    gain = jnp.sum(dh * xhat, 0, keepdims=True)
    bias = jnp.sum(dh, 0, keepdims=True)

    bqkv = jnp.sum(dqkv_ref[...].astype(F32), 0, keepdims=True)

    @pl.when(gene == base)
    def _():
        sums_ref[0:1, :] = gain
        sums_ref[1:2, :] = bias
        bias_ref[0:1, :] = bqkv

    @pl.when(gene > base)
    def _():
        sums_ref[0:1, :] += gain
        sums_ref[1:2, :] += bias
        bias_ref[0:1, :] += bqkv


def attend_back(plan, qkv, da, lse, cos, sin, xp, dx1, g1, wout, wqkv, base, count, before=()):
    length, width = da.shape
    span = length // GENES
    rows = lambda shape: pl.BlockSpec(shape, lambda g, *ids: (g + base, 0))
    return call(
        functools.partial(attend_back_kernel, base=base),
        (count,),
        [
            rows((span, 3 * width)),
            rows((span, width)),
            pl.BlockSpec((16, span), lambda g, *ids: (0, g + base)),
            rows((span, LANES)),
            rows((span, LANES)),
            rows((span, width)),
            rows((span, width)),
            full((1, width)),
            full((width, width)),
            full((width, 3 * width)),
        ]
        + [ANY] * len(before),
        [rows((span, 3 * width)), rows((span, width)), full((8, width)), full((8, 3 * width))],
        [
            shape_of((length, 3 * width), BF16),
            shape_of((length, width), BF16),
            shape_of((8, width), F32),
            shape_of((8, 3 * width), F32),
        ],
        [pltpu.VMEM((span, width), BF16), pltpu.VMEM((span, span), F32)],
        name="attend_back",
        cost=(4e9 * count, 6e6 * count),
        aliases={11 + i: i for i in range(len(before))},
    )(plan, qkv, da, lse, cos, sin, xp, dx1, g1, wout, wqkv, *before)


def grads_kernel(at, *refs, pieces):
    (xp_ref, g1_ref, b1_ref, o_ref, da_ref, dqkv_ref), refs = refs[:6], refs[6:]
    if pieces:
        vectors, refs = refs[:8], refs[8:]
        first_ref, second_ref, a1_ref, grad_ref, sem, small_ref, small_sem = refs
    else:
        first_ref, second_ref, a1_ref, grad_ref, sem = refs
    step = pl.program_id(0)
    width = xp_ref.shape[1]
    slot = lax.rem(step, 2)
    rows = width // (4 * Z_SIZE)

    def wait(to):
        pltpu.make_async_copy(grad_ref.at[to], grad_ref.at[to], sem.at[to]).wait()

    def store(half, base, to):
        def one(dz, carry):
            for dx, dy, dc in EVERY:
                f, y, c = spot(at, Z_SIZE - dz, dx, dy, dc)
                src = grad_ref.at[to, at_rows(f * 2 * rows + c * rows, rows), at_columns(y * COLUMNS, COLUMNS)]
                dst = (first_ref, second_ref)[dc].at[piece_index(half, dz, dx, dy), pl.ds(base * rows, rows)]
                pltpu.make_async_copy(src, dst, sem.at[to]).start()
            return carry

        lax.fori_loop(0, Z_SIZE, one, 0)

    def pack():
        small_ref[...] = jnp.zeros_like(small_ref)
        shards = 2 * Z_SIZE
        columns = []
        for ref in vectors:
            size = ref.shape[1] // shards
            whole = jnp.broadcast_to(ref[...], (shards, ref.shape[1]))
            mask = iota(whole.shape, 1) // size == iota(whole.shape, 0)
            own = jnp.where(mask, whole, 0.0).astype(BF16)
            columns.append(nt(own, spread(size, ref.shape[1])).astype(BF16))
        rows = jnp.concatenate(columns, 1).astype(F32)
        for f in range(shards):
            for i in range(4):
                part = rows[f : f + 1, i * COLUMNS : (i + 1) * COLUMNS]
                small_ref[f, i // 2, i % 2, 0] = jnp.broadcast_to(part, (8, COLUMNS)).astype(BF16)

    def smalls(act):
        def one(dz, carry):
            for dx, dy, dc in EVERY:
                f, y, c = spot(at, Z_SIZE - dz, dx, dy, dc)
                for half in range(2):
                    src = small_ref.at[f, y, c, half]
                    dst = (first_ref, second_ref)[dc].at[piece_index(half, dz, dx, dy), pl.ds(2 * rows, 8)]
                    act(pltpu.make_async_copy(src, dst, small_sem))
            return carry

        lax.fori_loop(0, Z_SIZE, one, 0)

    @pl.when(step >= 2)
    def _():
        wait(slot)

    for j in range(4):

        @pl.when(step == j)
        def _(j=j):
            if j == 0:
                if pieces:
                    pack()
                    smalls(lambda copy: copy.start())
                xhat, _ = normalize(xp_ref[...].astype(F32))
                a1_ref[...] = (xhat * g1_ref[...] + b1_ref[...]).astype(BF16)
            if j < 3:
                grad_ref[j % 2] = tn(a1_ref[...], dqkv_ref[...]).astype(BF16)
            else:
                grad_ref[j % 2] = tn(o_ref[...], da_ref[...]).astype(BF16)
            if pieces:
                store(j // 2, j % 2, j % 2)
            elif j < 3:
                dst = first_ref.at[:, pl.ds(j * width, width)]
                pltpu.make_async_copy(grad_ref.at[j % 2], dst, sem.at[j % 2]).start()
            else:
                pltpu.make_async_copy(grad_ref.at[j % 2], second_ref, sem.at[j % 2]).start()
            if j == 3:
                wait(0)
                wait(1)
                if pieces:
                    smalls(lambda copy: copy.wait())


def grads(at, xp, g1, b1, o, da, dqkv, vectors):
    length, width = xp.shape
    pieces = bool(vectors)
    if pieces:
        rows = width // (2 * Z_SIZE) + 8
        stored = [shape_of((PIECES, rows, COLUMNS), BF16)] * 2
    else:
        stored = [shape_of((width, 3 * width), BF16), shape_of((width, width), BF16)]
    return call(
        functools.partial(grads_kernel, pieces=pieces),
        (4,),
        [
            full((length, width)),
            full((1, width)),
            full((1, width)),
            full((length, width)),
            full((length, width)),
            pl.BlockSpec((length, width), lambda j, *ids: (0, jnp.minimum(j, 2))),
        ]
        + [full(v.shape) for v in vectors],
        [ANY, ANY],
        stored,
        [
            pltpu.VMEM((length, width), BF16),
            pltpu.VMEM((2, width, width), BF16),
            pltpu.SemaphoreType.DMA((2,)),
        ]
        + (
            [pltpu.VMEM((2 * Z_SIZE, 2, 2, 2, 8, COLUMNS), BF16), pltpu.SemaphoreType.DMA]
            if pieces
            else []
        ),
        name="grads",
        cost=(5e9, 12e6),
    )(at, xp, g1, b1, o, da, dqkv, *vectors)


def restore_kernel(plan, outp_ref, dxp_ref, out_ref, dx_ref):
    span, width = out_ref.shape
    slots = iota((1, span), 1)
    source = jnp.concatenate([source_of_slots(plan, g, slots) for g in range(GENES)], 1)
    codon = iota((span, outp_ref.shape[0]), 0) + pl.program_id(0) * span
    pick = jnp.where(codon == source, 1.0, 0.0).astype(BF16)
    out_ref[...] = nn(pick, outp_ref[...]).astype(BF16)
    dx_ref[...] = nn(pick, dxp_ref[...]).astype(BF16)


def restore(plan, outp, dxp):
    length, width = outp.shape
    span = length // GENES
    return call(
        restore_kernel,
        (GENES,),
        [full((length, width)), full((length, width))],
        [rows_of((span, width))] * 2,
        [shape_of((length, width), BF16)] * 2,
        name="restore",
        cost=(3.3e9, 8e6),
    )(plan, outp, dxp)


def deliver_kernel(at, mine1, other1, mine2, other2, *out):
    wqkv, wout, wup, wdown = out[:4]
    vectors, row_ref = out[4:12], out[12]
    width = wout.shape[1]
    rows = wout.shape[0] // 2
    for dc, (one, two) in enumerate(((mine1, mine2), (other1, other2))):
        c = lax.bitwise_xor(at[3], dc)
        here = pl.ds(pl.multiple_of(c * rows, 8), rows)
        for y in range(2):
            for b in range(4):
                ref, base = (wqkv, b * width) if b < 3 else (wout, 0)
                start = base + y * COLUMNS
                piece = one[y, b // 2, (b % 2) * rows : (b % 2 + 1) * rows, :]
                ref[here, start : start + COLUMNS] = piece.astype(F32)
                start = b * width + y * COLUMNS
                wup[here, start : start + COLUMNS] = two[y, 0, b * rows : (b + 1) * rows, :].astype(F32)
            down = pl.ds(pl.multiple_of(c * 4 * rows, 8), 4 * rows)
            wdown[down, y * COLUMNS : (y + 1) * COLUMNS] = two[y, 1].astype(F32)
            start = at_columns((y * 2 + c) * COLUMNS, COLUMNS)
            row_ref[:, start] = one[y, 0, 2 * rows : 2 * rows + 8, :].astype(F32)
    for ref, start in zip(vectors, SLOTS):
        ref[...] = row_ref[0:1, start : start + ref.shape[0]].reshape(ref.shape[0])


def deliver(at, mine1, other1, mine2, other2, sizes):
    rows = mine2.shape[2] // 4
    width = 2 * COLUMNS
    shapes = [(2 * rows, 3 * width), (2 * rows, width), (2 * rows, 4 * width), (8 * rows, width)]
    shapes += [(n,) for n in sizes]
    return call(
        deliver_kernel,
        (1,),
        [full(v.shape) for v in (mine1, other1, mine2, other2)],
        [full(s) for s in shapes],
        [shape_of(s, F32) for s in shapes],
        [pltpu.VMEM((8, PACKED), F32)],
        name="deliver",
        cost=(0, 6e6),
    )(at, mine1, other1, mine2, other2)


def gather(shard):
    return lax.all_gather(shard, "fsdp", axis=0, tiled=True)


def reduce_rows(grad):
    part = lax.psum_scatter(grad, "fsdp", scatter_dimension=0, tiled=True)
    return lax.psum(part.astype(BF16), "replica").astype(F32)


def low(value):
    return value.astype(BF16)


def add(*values):
    total = values[0].astype(F32)
    for v in values[1:]:
        total = total + v.astype(F32)
    return total


def to_z(arrays):
    arrays = arrays if isinstance(arrays, list) else [arrays] * 3
    return [move(v, ALONG_Z[d]) for d, v in zip((1, 2, 3), arrays)]


def over_x(array):
    return move(array, ACROSS_X)


def over_y(array):
    return move(array, ACROSS_Y)


def over_core(array):
    return move(array, ACROSS_CORE)


def stack(arrays):
    return jnp.stack(list(arrays))


class Sum:
    def __init__(self, kept, got):
        self.kept, self.got, self.more = kept, got, {}

    def near(self, start, stop):
        return add(self.kept[start:stop], self.got[start:stop])

    def plane_one(self):
        return low(self.near(6, 12)), low(self.near(18, 24)), low(self.near(28, 32))

    def plane_two(self, by_x, by_y):
        self.first = add(self.near(0, 6), by_x)
        self.second = add(self.near(12, 18), by_y)
        return low(self.first[3:]), low(self.second[3:])

    def along_z(self, by_y, by_x):
        first, second = add(self.first[:3], by_y), add(self.second[:3], by_x)
        return [low(stack([first[d], second[d]])) for d in range(Z_SIZE - 1)]

    def across_y(self, by_z, side):
        own = add(self.near(24, 28), side)
        return low(stack([add(own[:2], *by_z), own[2:]]))


def settle(at, part, got):
    mine = low(add(part[0], got[1]))
    other = low(add(got[0], part[1]))
    return jnp.where(at[2] == 0, stack([mine, other]), stack([other, mine]))


def body(
    layer_input, cotangent, segment_ids, pad_mask, ln1_gain, ln1_bias, w_qkv, b_qkv, w_out, b_out,
    ln2_gain, ln2_bias, w_up, b_up, w_down, b_down, *, tuned,
):
    vectors = (ln1_gain, ln1_bias, b_qkv, b_out, ln2_gain, ln2_bias, b_up, b_down)
    sizes = [v.shape[0] for v in vectors]
    x, c = layer_input[0], cotangent[0]
    if tuned:
        at = place()
        near1, near2, side = quarters(at, w_qkv, w_out, w_up, w_down, vectors)
        near1, near2, side, x = tie((near1, near2, side, x))
        z1 = to_z(near1)
        far_side = over_x(side)
        z2_one = move(near2, ALONG_Z[1])
        prepared = prepare(segment_ids, x, c)
        z1, z2_one, prepared = tie((z1, z2_one, prepared))
        plan, xp, cp, cos, sin = prepared

        count = near1.shape[1] - 8
        first1, second1 = stack(q[0, :count] for q in z1), stack(q[1] for q in z1)
        rows = stack(q[0, count:] for q in [near1] + z1)
        first1, second1, near2 = tie((first1, second1, near2))
        first_y, second_x = over_y(first1), over_x(second1)
        z2_three = move(near2, ALONG_Z[3])
        first_y, second_x, z2_three, near2, far_side = tie((first_y, second_x, z2_three, near2, far_side))

        first1, second1 = stack([first1, first_y]), stack([second1, second_x])[:, :, :count]
        far_rows = jnp.concatenate([far_side[0, :1, 3 * count :], second_x[:, count:]])
        first1, second1, rows, far_rows, near2 = tie((first1, second1, rows, far_rows, near2))
        far_first1, far_second1 = over_x(first1), over_y(second1)
        z2 = [z2_one, move(near2, ALONG_Z[2]), z2_three]
        params = unpack(at, rows, far_rows, sizes)
        far_first1, far_second1, params, z2, far_side = tie((far_first1, far_second1, params, z2, far_side))

        first2, second2 = (stack(q[h] for q in z2) for h in range(2))
        near_core1 = stack([first1, second1])
        far_first1, far_second1, near_core1, first2, second2 = tie(
            (far_first1, far_second1, near_core1, first2, second2)
        )
        far_core1 = over_core(far_first1), over_core(far_second1)
        near_core1 = over_core(near_core1)
        first_y, second_x = over_y(first2), over_x(second2)
        core_side = over_core(far_side)
        first_y, second_x, far_core1, near_core1, core_side = tie(
            (first_y, second_x, far_core1, near_core1, core_side)
        )

        attention = (
            w_qkv, w_out, far_side, core_side, first1, far_first1, second1, far_second1,
            near_core1, far_core1[0], near_core1, far_core1[1],
        )
        first2, second2 = stack([first2, first_y]), stack([second2, second_x])
        first2, second2, attention, params, plan = tie((first2, second2, attention, params, plan))
        far_first2, far_second2 = over_x(first2), over_y(second2)
        core2 = [over_core(v) for v in (first2, second2)]
    else:
        at = jnp.zeros((4,), jnp.int32)
        plan, xp, cp, cos, sin = prepare(segment_ids, x, c)
        params = [gather(v[None]).reshape(1, -1).astype(F32) for v in vectors]
        attention = gather(w_qkv), gather(w_out)
        forward = gather(w_up), gather(w_down)
    g1, b1, bqkv, bout, g2, b2, bup, bdown = params
    (qkv, o, lse, x1), (wqkv, wout) = attend(plan, at, xp, cos, sin, g1, b1, bqkv, bout, attention)
    if tuned:
        far_first2, far_second2, core2, x1 = tie((far_first2, far_second2, core2, x1))
        far_core2 = over_core(far_first2), over_core(far_second2)
        forward = (
            w_up, w_down, far_side, core_side, first2, far_first2, second2, far_second2,
            core2[0], far_core2[0], core2[1], far_core2[1],
        )
    outp, dx1, da, gbup, sums2, *parts2 = feed(at, x1, cp, g2, b2, bup, bdown, forward)
    back = functools.partial(attend_back, plan, qkv, da, lse, cos, sin, xp, dx1, g1, wout, wqkv)
    half = GENES // 2
    if tuned:
        kept2, sent2 = parts2
        got2 = over_core(sent2)
        dqkv, dxp, *sums_low = back(0, half)
        got2, dqkv = tie((got2, dqkv))
        group2 = Sum(kept2, got2)
        to_x, to_y, side2, dqkv = tie(group2.plane_one() + (dqkv,))
        by_x, by_y = over_x(to_x), over_y(to_y)
        dqkv, dxp, *sums_high = back(half, half, (dqkv, dxp))
        by_x, by_y, dqkv = tie((by_x, by_y, dqkv))
        to_y, to_x = group2.plane_two(by_x, by_y)
        to_y, to_x, side2, dqkv = tie((to_y, to_x, side2, dqkv))
        by_y, by_x, by_side2 = over_y(to_y), over_x(to_x), over_x(side2)
    else:
        dqkv, dxp, *sums_low = back(0, half)
        dqkv, dxp, *sums_high = back(half, half, (dqkv, dxp))
    sums1, sumsb = (a + b for a, b in zip(sums_low, sums_high))
    row = lambda array, i: array[i : i + 1]
    small = [
        row(sums1, 0), row(sums1, 1), row(sumsb, 0), row(sums2, 3), row(sums2, 0), row(sums2, 1), gbup, row(sums2, 2),
    ]
    parts1 = grads(at, xp, g1, b1, o, da, dqkv, small if tuned else ())
    if tuned:
        by_y, by_x, by_side2, parts1 = tie((by_y, by_x, by_side2, parts1))
        kept1, sent1 = parts1
        to_z2 = group2.along_z(by_y, by_x)
        to_z2, sent1 = tie((to_z2, sent1))
        got1 = over_core(sent1)
        z2 = to_z(to_z2)
        got1 = tie(got1)
        group1 = Sum(kept1, got1)
        to_x, to_y, side1 = tie(group1.plane_one())
        by_x, by_y = over_x(to_x), over_y(to_y)
        by_x, by_y = tie((by_x, by_y))
        to_y, to_x = tie(group1.plane_two(by_x, by_y))
        by_y, by_x = over_y(to_y), over_x(to_x)
        by_y, by_x, z2 = tie((by_y, by_x, z2))
        to_z1 = group1.along_z(by_y, by_x)
        part2 = group2.across_y(z2, by_side2)
        to_z1, side1, part2, outp, dxp = tie((to_z1, side1, part2, outp, dxp))
        z1 = to_z(to_z1)
        by_side1, by_part2 = over_x(side1), over_y(part2)
        layer_out, input_grad = restore(plan, outp, dxp)
        z1, by_side1, by_part2, layer_out, input_grad = tie((z1, by_side1, by_part2, layer_out, input_grad))
        part1 = group1.across_y(z1, by_side1)
        final2 = settle(at, part2, by_part2)
        part1, final2 = tie((part1, final2))
        by_part1, other2 = over_y(part1), over_core(final2)
        final1 = settle(at, part1, by_part1)
        other1 = over_core(final1)
        wqkv, wout, wup, wdown, *small = deliver(at, final1, other1, final2, other2, sizes)
    else:
        layer_out, input_grad = restore(plan, outp, dxp)
        wqkv, wout = map(reduce_rows, parts1)
        wup, wdown = map(reduce_rows, parts2)
        small = [reduce_rows(v.reshape(-1)) for v in small]
    dg1, db1, dbqkv, dbout, dg2, db2, dbup, dbdown = small
    return (
        layer_out[None], input_grad[None], dg1, db1, wqkv, dbqkv, wout, dbout, dg2, db2,
        wup, dbup, wdown, dbdown,
    )


def solution(mesh):
    rows = ("fsdp", "replica")
    by_row = P(rows, None, None)
    vector, matrix = P("fsdp"), P("fsdp", None)
    params = (
        vector, vector, matrix, vector, matrix, vector, vector, vector, matrix, vector, matrix, vector,
    )
    in_specs = (by_row, by_row, P(rows, None), P(rows, None)) + params
    out_specs = (by_row, by_row) + params
    return jax.shard_map(
        functools.partial(body, tuned=tuned_mesh(mesh)),
        mesh=mesh, in_specs=in_specs, out_specs=out_specs, check_vma=False,
    )
```

time: 427 us -> 307 us (0.72)
  the two profiles are of different devices: /device:TPU:0 before, /device:TPU:9 now
where the time goes in v2:
time: 307 us; the launch traced here: 301 us
  Pallas kernels  144 us (47%)
  waiting for transfers between devices  81.6 us (27%)
  starting transfers between devices  41 us (13%)
  other arithmetic  21.9 us (7%)
  local copies, waits for them, and re-layouts  10.5 us (3%)
    ppermute x45, waiting for transfers between devices, move(): return lax.ppermute(array, AXES, table)  81.6 us
    pallas_call x1, Pallas kernels, feed(): call(functools.partial(feed_kernel, block=length // 4, pieces=pieces, ste...  48.3 us
    ppermute x45, starting transfers between devices, move(): return lax.ppermute(array, AXES, table)  41 us
    pallas_call x2, Pallas kernels, attend_back(): call(functools.partial(attend_back_kernel, base=base), (count,), [rows((s...  32 us
    pallas_call x1, Pallas kernels, attend(): call(functools.partial(attend_kernel, pieces=pieces), (GENES,), [rows_of(...  22.2 us
    pallas_call x1, Pallas kernels, grads(): call(functools.partial(grads_kernel, pieces=pieces), (4,), [full((length,...  14 us
    pallas_call x1, Pallas kernels, prepare(): call(prepare_kernel, (GENES,), [full((1, length)), full((length, width)),...  8.68 us
    pallas_call x1, Pallas kernels, restore(): call(restore_kernel, (GENES,), [full((length, width)), full((length, widt...  7.29 us
  transfers between devices with their start and end apart: 45, of which 20 were waited for; matrix products, arithmetic and copies ran while one was open for 3% of the time, Pallas kernels for 29%

profile of v2, /device:TPU:9, one launch (start us, length us, event | category | flops | bytes accessed | tf_op | source)
XLA Modules:
  0.0 300.9 jit_solution(9137424899509650397)
XLA Ops:
  1.3 3.4 %quarters.1 = (bf16[2,104,384]{2,1,0:T(8,128)(2,1)}, bf16[2,192,384]{2,1,0:T(8,128)(2,1)}, bf16[2,2,296,384]{3,2,1,0:T(8,128)(2,1)}) custom-call(s32[4]{0:T(128)} %pad_add_fusion.at, bf16[96,2304]{1,0:T(8,128)(2,1)} %refs_7_.3, bf16[96,768]{1,0:T(8,128)(2,1)} %refs_8_.2, bf16[96,3072]{1,0:T(8,128)(2,1)} %refs_6_.3, bf16[384,768]{1,0:T(8,128)(2,1)} %refs_7_.4, ...), custom_call_target="tpu_custom_call" | custom-call | bytes 6000000 | tf_op jit(solution)/shard_map/quarters/pallas_call | solution.py:200
  6.0 2.3 collective-permute-start.1
  8.4 2.2 collective-permute-start
  10.6 8.7 %prepare.1 = (s32[16]{0:T(128)}, bf16[1024,768]{1,0:T(8,128)(2,1)}, bf16[1024,768]{1,0:T(8,128)(2,1)}, f32[1024,128]{1,0:T(8,128)}, f32[1024,128]{1,0:T(8,128)}) custom-call(s32[1,1024]{1,0:T(1,128)} %seg_ref.1, bf16[1024,768]{1,0:T(8,128)(2,1)} %bitcast.38, bf16[1024,768]{1,0:T(8,128)(2,1)} %bitcast.39, f32[1,128]{1,0:T(1,128)} %constant.47.clone.freq_ref), custom_call_target="tpu_custom_call" | custom-call | flops 3300000000 | bytes 8000000 | tf_op jit(solution)/shard_map/prepare/pallas_call | solution.py:307
  19.3 2.7 collective-permute-done
  22.0 6.3 %collective-permute-done.3 = bf16[2,192,384]{2,1,0:T(8,128)(2,1)S(1)} collective-permute-done((bf16[2,192,384]{2,1,0:T(8,128)(2,1)}, bf16[2,192,384]{2,1,0:T(8,128)(2,1)S(1)}, u32[]{:S(2)}, u32[]{:S(2)}) %collective-permute-start.3) | collective-permute-done | bytes 294944 | tf_op jit(solution)/shard_map/ppermute | solution.py:133
  31.9 3.4 %collective-permute-done.4 = bf16[3,96,384]{2,1,0:T(8,128)(2,1)S(1)} collective-permute-done((bf16[3,96,384]{2,1,0:T(8,128)(2,1)S(1)}, bf16[3,96,384]{2,1,0:T(8,128)(2,1)S(1)}, u32[]{:S(2)}, u32[]{:S(2)}) %collective-permute-start.4) | collective-permute-done | bytes 221216 | tf_op jit(solution)/shard_map/ppermute | solution.py:133
  39.2 2.1 collective-permute-start.10
  41.2 4.3 %unpack.1 = (f32[1,768]{1,0:T(1,128)}, f32[1,768]{1,0:T(1,128)}, f32[1,2304]{1,0:T(1,128)}, f32[1,768]{1,0:T(1,128)}, f32[1,768]{1,0:T(1,128)}, /*index=5*/f32[1...) custom-call(s32[4]{0:T(128)} %pad_add_fusion.at, bf16[4,8,384]{2,1,0:T(8,128)(2,1)} %get-tuple-element.220.near_ref, ...), custom_call_target="tpu_custom_call" | custom-call | flops 100000000 | bytes 100000 | tf_op jit(solution)/shard_map/unpack/pallas_call | solution.py:246
  45.7 8.6 %collective-permute-done.10 = bf16[2,192,384]{2,1,0:T(8,128)(2,1)S(1)} collective-permute-done((bf16[2,192,384]{2,1,0:T(8,128)(2,1)S(1)}, bf16[2,192,384]{2,1,0:T(8,128)(2,1)S(1)}, u32[]{:S(2)}, u32[]{:S(2)}) %collective-permute-start.10) | collective-permute-done | bytes 294944 | tf_op jit(solution)/shard_map/ppermute | solution.py:133
  58.2 9.6 %collective-permute-done.11 = bf16[3,192,384]{2,1,0:T(8,128)(2,1)S(1)} collective-permute-done((bf16[3,192,384]{2,1,0:T(8,128)(2,1)S(1)}, bf16[3,192,384]{2,1,0:T(8,128)(2,1)S(1)}, u32[]{:S(2)}, u32[]{:S(2)}) %collective-permute-start.11) | collective-permute-done | bytes 442400 | tf_op jit(solution)/shard_map/ppermute | solution.py:133
  73.5 22.2 %attend.1 = (bf16[1024,2304]{1,0:T(8,128)(2,1)}, bf16[1024,768]{1,0:T(8,128)(2,1)}, f32[16,1024]{1,0:T(8,128)}, f32[1024,768]{1,0:T(8,128)}, bf16[768,2304]{1,0:T(8,128)(2,1)}, /*index=5*/bf16[768,768]{1,0:T(8,128)(2,1)}) custom-call(s32[16]{0:T(128)} %get-tuple-element.261.plan, s32[4]{0:T(128)} %pad_add_fusion.at, ...), custom_call_target="tpu_custom_call" | custom-call | flops 11000000512 | bytes 20000000 | tf_op jit(solution)/shard_map/attend/pallas_call | solution.py:434
  96.4 2.4 collective-permute-done.21.refs_15_
  100.8 48.3 %feed.1 = (bf16[1024,768]{1,0:T(8,128)(2,1)}, f32[1024,768]{1,0:T(8,128)}, bf16[1024,768]{1,0:T(8,128)(2,1)}, f32[1,3072]{1,0:T(1,128)}, f32[8,768]{1,0:T(8,128)...) custom-call(s32[4]{0:T(128)} %pad_add_fusion.at, f32[1024,768]{1,0:T(8,128)} %get-tuple-element.282.refs_0_, ...), custom_call_target="tpu_custom_call" | custom-call | flops 28999999488 | bytes 40000000 | tf_op jit(solution)/shard_map/feed/pallas_call | solution.py:663
  151.1 16.1 %attend_back.2 = (bf16[1024,2304]{1,0:T(8,128)(2,1)}, bf16[1024,768]{1,0:T(8,128)(2,1)}, f32[8,768]{1,0:T(8,128)}, f32[8,2304]{1,0:T(8,128)}) custom-call(s32[16]{0:T(128)} %get-tuple-element.261.plan, bf16[1024,2304]{1,0:T(8,128)(2,1)} %get-tuple-element.294.qkv_ref, bf16[1024,768]{1,0:T(8,128)(2,1)} %get-tuple-element.295.da_ref.refs_4_, ...), custom_call_target="tpu_custom_call" | custom-call | flops 8000000000 | bytes 12000000 | tf_op jit(solution)/shard_map/attend_back/pallas_call | solution.py:779
  168.6 2.4 add_convert_fusion
  172.5 15.9 %attend_back.3 = (bf16[1024,2304]{1,0:T(8,128)(2,1)}, bf16[1024,768]{1,0:T(8,128)(2,1)}, f32[8,768]{1,0:T(8,128)}, f32[8,2304]{1,0:T(8,128)}) custom-call(s32[16]{0:T(128)} %get-tuple-element.261.plan, bf16[1024,2304]{1,0:T(8,128)(2,1)} %get-tuple-element.294.qkv_ref, ...), custom_call_target="tpu_custom_call", output_to_operand_aliasing={{0}: (11, {}), {1}: (12, {})} | custom-call | flops 8000000000 | bytes 12000000 | tf_op jit(solution)/shard_map/attend_back/pallas_call | solution.py:779
  194.0 3.1 %convert_add_fusion.1 = (f32[6,192,384]{2,1,0:T(8,128)S(1)}, f32[6,192,384]{2,1,0:T(8,128)S(1)}) fusion(bf16[6,192,384]{2,1,0:T(8,128)(2,1)} %copy-done.6, bf16[32,192,384]{2,1,0:T(8,128)(2,1)} %collective-permute-done.23, bf16[32,192,384]{2,1,0:T(8,128)(2,1)} %get-tuple-element.292, bf16[6,192,384]{2,1,0:T(8,128)(2,1)} %copy-done.7), kind=kLoop, calls=%fused_computation.1 | loop fusion | flops 4423680 | bytes 8847360 | tf_op jit(solution)/shard_map/add | solution.py:1013
  202.0 14.0 %grads.1 = (bf16[32,104,384]{2,1,0:T(8,128)(2,1)}, bf16[32,104,384]{2,1,0:T(8,128)(2,1)}) custom-call(s32[4]{0:T(128)} %pad_add_fusion.at, bf16[1024,768]{1,0:T(8,128)(2,1)} %get-tuple-element.262.refs_0_.xp_ref, f32[1,768]{1,0:T(1,128)} %get-tuple-element.265.refs_3_.g1_ref.refs_1_, f32[1,768]{1,0:T(1,128)} %get-tuple-element.266.refs_4_.refs_2_, ...), custom_call_target="tpu_custom_call" | custom-call | flops 5000000000 | bytes 12000000 | tf_op jit(solution)/shard_map/grads/pallas_call | solution.py:903
  216.0 6.2 %collective-permute-done.27 = bf16[3,192,384]{2,1,0:T(8,128)(2,1)} collective-permute-done((bf16[3,192,384]{2,1,0:T(8,128)(2,1)}, bf16[3,192,384]{2,1,0:T(8,128)(2,1)}, u32[]{:S(2)}, u32[]{:S(2)}) %collective-permute-start.27) | collective-permute-done | bytes 442400 | tf_op jit(solution)/shard_map/ppermute | solution.py:133
  225.2 1.9 collective-permute-start.29
  227.1 4.4 %collective-permute-done.29 = bf16[32,104,384]{2,1,0:T(8,128)(2,1)S(1)} collective-permute-done((bf16[32,104,384]{2,1,0:T(8,128)(2,1)S(1)}, bf16[32,104,384]{2,1,0:T(8,128)(2,1)S(1)}, u32[]{:S(2)}, u32[]{:S(2)}) %collective-permute-start.29) | collective-permute-done | bytes 2555936 | tf_op jit(solution)/shard_map/ppermute | solution.py:133
  234.2 3.6 %collective-permute-start.35 = (bf16[2,192,384]{2,1,0:T(8,128)(2,1)S(1)}, bf16[2,192,384]{2,1,0:T(8,128)(2,1)S(1)}, u32[]{:S(2)}, u32[]{:S(2)}) collective-permute-start(bf16[2,192,384]{2,1,0:T(8,128)(2,1)S(1)} %pad_maximum_fusion.10), channel_id=1, source_target_pairs={{0,16},{1,17},{2,18},{3,19},{4,20},{5,21},{6,22},{7,23},{8,24},{9,... | collective-permute-start | bytes 884744 | tf_op jit(solution)/shard_map/ppermute | solution.py:133
  238.8 1.6 convert_add_fusion.2
  240.4 4.6 %collective-permute-done.30 = bf16[6,104,384]{2,1,0:T(8,128)(2,1)S(1)} collective-permute-done((bf16[6,104,384]{2,1,0:T(8,128)(2,1)S(1)}, bf16[6,104,384]{2,1,0:T(8,128)(2,1)S(1)}, u32[]{:S(2)}, u32[]{:S(2)}) %collective-permute-start.30) | collective-permute-done | bytes 479264 | tf_op jit(solution)/shard_map/ppermute | solution.py:133
  247.8 11.1 %collective-permute-done.35 = bf16[2,192,384]{2,1,0:T(8,128)(2,1)S(1)} collective-permute-done((bf16[2,192,384]{2,1,0:T(8,128)(2,1)S(1)}, bf16[2,192,384]{2,1,0:T(8,128)(2,1)S(1)}, u32[]{:S(2)}, u32[]{:S(2)}) %collective-permute-start.35) | collective-permute-done | bytes 294944 | tf_op jit(solution)/shard_map/ppermute | solution.py:133
  258.9 4.9 %collective-permute-done.36 = bf16[2,192,384]{2,1,0:T(8,128)(2,1)S(1)} collective-permute-done((bf16[2,192,384]{2,1,0:T(8,128)(2,1)S(1)}, bf16[2,192,384]{2,1,0:T(8,128)(2,1)S(1)}, u32[]{:S(2)}, u32[]{:S(2)}) %collective-permute-start.36) | collective-permute-done | bytes 294944 | tf_op jit(solution)/shard_map/ppermute | solution.py:133
  269.3 7.3 %restore.1 = (bf16[1024,768]{1,0:T(8,128)(2,1)}, bf16[1024,768]{1,0:T(8,128)(2,1)}) custom-call(s32[16]{0:T(128)} %get-tuple-element.261.plan, bf16[1024,768]{1,0:T(8,128)(2,1)} %get-tuple-element.353.outp_ref, bf16[1024,768]{1,0:T(8,128)(2,1)} %get-tuple-element.354.dxp_ref), custom_call_target="tpu_custom_call" | custom-call | flops 3300000000 | bytes 8000000 | tf_op jit(solution)/shard_map/restore/pallas_call | solution.py:945
  276.6 4.1 %collective-permute-done.38 = bf16[2,104,384]{2,1,0:T(8,128)(2,1)S(1)} collective-permute-done((bf16[2,104,384]{2,1,0:T(8,128)(2,1)}, bf16[2,104,384]{2,1,0:T(8,128)(2,1)S(1)}, u32[]{:S(2)}, u32[]{:S(2)}) %collective-permute-start.38) | collective-permute-done | bytes 159776 | tf_op jit(solution)/shard_map/ppermute | solution.py:133
  286.9 5.5 %collective-permute-done.42 = bf16[2,2,104,384]{3,2,1,0:T(8,128)(2,1)S(1)} collective-permute-done((bf16[2,2,104,384]{3,2,1,0:T(8,128)(2,1)S(1)}, bf16[2,2,104,384]{3,2,1,0:T(8,128)(2,1)S(1)}, u32[]{:S(2)}, u32[]{:S(2)}) %collective-permute-start.42) | collective-permute-done | bytes 319520 | tf_op jit(solution)/shard_map/ppermute | solution.py:133
  292.5 2.1 collective-permute-start.43
  296.5 4.0 %deliver.1 = (f32[96,2304]{1,0:T(8,128)}, f32[96,768]{1,0:T(8,128)}, f32[96,3072]{1,0:T(8,128)}, f32[384,768]{1,0:T(8,128)}, f32[96]{0:T(128)}, /*index=5*/f32[9...) custom-call(s32[4]{0:T(128)} %pad_add_fusion.at, ...), custom_call_target="tpu_custom_call" | custom-call | bytes 6000000 | tf_op jit(solution)/shard_map/deliver/pallas_call | solution.py:985
  (185 shorter events, 59.8 us)
Async XLA Ops:
  4.7 32.1 %collective-permute-start.7 = (bf16[2,2,296,384]{3,2,1,0:T(8,128)(2,1)}, bf16[2,2,296,384]{3,2,1,0:T(8,128)(2,1)S(1)}, u32[]{:S(2)}, u32[]{:S(2)}) collective-permute-start(bf16[2,2,296,384]{3,2,1,0:T(8,128)(2,1)} %get-tuple-element.213), channel_id=1, source_target_pairs={{0,4},{1,5},{2,6},{3,7},{4,0},{5,1},{6,2},{7,3},{8,12},{9,13},{10,... | collective-permute-start | bytes 2727944 | tf_op jit(solution)/shard_map/ppermute | solution.py:133
  5.9 13.4 %collective-permute-start.2 = (bf16[2,104,384]{2,1,0:T(8,128)(2,1)}, bf16[2,104,384]{2,1,0:T(8,128)(2,1)S(1)}, u32[]{:S(2)}, u32[]{:S(2)}) collective-permute-start(bf16[2,104,384]{2,1,0:T(8,128)(2,1)} %get-tuple-element.199), channel_id=1, source_target_pairs={{0,24},{1,25},{2,26},{3,27},{4,28},{5,29},{6,30},{7,31},{8,0},{9,1... | collective-permute-start | bytes 479240 | tf_op jit(solution)/shard_map/ppermute | solution.py:133
  6.0 13.2 %collective-permute-start.1 = (bf16[2,104,384]{2,1,0:T(8,128)(2,1)}, bf16[2,104,384]{2,1,0:T(8,128)(2,1)S(1)}, u32[]{:S(2)}, u32[]{:S(2)}) collective-permute-start(bf16[2,104,384]{2,1,0:T(8,128)(2,1)} %get-tuple-element.199), channel_id=1, source_target_pairs={{0,16},{1,17},{2,18},{3,19},{4,20},{5,21},{6,22},{7,23},{8,24},{9,... | collective-permute-start | bytes 479240 | tf_op jit(solution)/shard_map/ppermute | solution.py:133
  8.4 13.7 %collective-permute-start = (bf16[2,104,384]{2,1,0:T(8,128)(2,1)}, bf16[2,104,384]{2,1,0:T(8,128)(2,1)S(1)}, u32[]{:S(2)}, u32[]{:S(2)}) collective-permute-start(bf16[2,104,384]{2,1,0:T(8,128)(2,1)} %get-tuple-element.199), channel_id=1, source_target_pairs={{0,8},{1,9},{2,10},{3,11},{4,12},{5,13},{6,14},{7,15},{8,16},{9,17... | collective-permute-start | bytes 479240 | tf_op jit(solution)/shard_map/ppermute | solution.py:133
  10.5 17.8 %collective-permute-start.3 = (bf16[2,192,384]{2,1,0:T(8,128)(2,1)}, bf16[2,192,384]{2,1,0:T(8,128)(2,1)S(1)}, u32[]{:S(2)}, u32[]{:S(2)}) collective-permute-start(bf16[2,192,384]{2,1,0:T(8,128)(2,1)} %get-tuple-element.231), channel_id=1, source_target_pairs={{0,8},{1,9},{2,10},{3,11},{4,12},{5,13},{6,14},{7,15},{8,16},{9,17... | collective-permute-start | bytes 884744 | tf_op jit(solution)/shard_map/ppermute | solution.py:133
  37.7 16.6 %collective-permute-start.8 = (bf16[2,3,96,384]{3,2,1,0:T(8,128)(2,1)S(1)}, bf16[2,3,96,384]{3,2,1,0:T(8,128)(2,1)S(1)}, u32[]{:S(2)}, u32[]{:S(2)}) collective-permute-start(bf16[2,3,96,384]{3,2,1,0:T(8,128)(2,1)S(1)} %get-tuple-element.273.refs_11_), channel_id=1, source_target_pairs={{0,4},{1,5},{2,6},{3,7},{4,0},{5,1},{6,2},{7,3},{8,12},{9,13},{10,... | collective-permute-start | bytes 1327112 | tf_op jit(solution)/shard_map/ppermute | solution.py:133
  37.9 16.4 %collective-permute-start.9 = (bf16[2,3,96,384]{3,2,1,0:T(8,128)(2,1)S(1)}, bf16[2,3,96,384]{3,2,1,0:T(8,128)(2,1)S(1)}, u32[]{:S(2)}, u32[]{:S(2)}) collective-permute-start(bf16[2,3,96,384]{3,2,1,0:T(8,128)(2,1)S(1)} %get-tuple-element.275.refs_13_), channel_id=1, source_target_pairs={{0,2},{1,3},{2,0},{3,1},{4,6},{5,7},{6,4},{7,5},{8,10},{9,11},{10,... | collective-permute-start | bytes 1327112 | tf_op jit(solution)/shard_map/ppermute | solution.py:133
  39.2 15.1 %collective-permute-start.10 = (bf16[2,192,384]{2,1,0:T(8,128)(2,1)S(1)}, bf16[2,192,384]{2,1,0:T(8,128)(2,1)S(1)}, u32[]{:S(2)}, u32[]{:S(2)}) collective-permute-start(bf16[2,192,384]{2,1,0:T(8,128)(2,1)S(1)} %copy-done.25), channel_id=1, source_target_pairs={{0,16},{1,17},{2,18},{3,19},{4,20},{5,21},{6,22},{7,23},{8,24},{9,... | collective-permute-start | bytes 884744 | tf_op jit(solution)/shard_map/ppermute | solution.py:133
  55.2 14.8 %collective-permute-start.16 = (bf16[2,2,296,384]{3,2,1,0:T(8,128)(2,1)S(1)}, bf16[2,2,296,384]{3,2,1,0:T(8,128)(2,1)S(1)}, u32[]{:S(2)}, u32[]{:S(2)}) collective-permute-start(bf16[2,2,296,384]{3,2,1,0:T(8,128)(2,1)S(1)} %collective-permute-done.7.refs_9_.refs_8_), channel_id=1, source_target_pairs={{0,1},{1,0},{2,3},{3,2},{4,5},{5,4},{6,7},{7,6},{8,9},{9,8},{10,11... | collective-permute-start | bytes 2727944 | tf_op jit(solution)/shard_map/ppermute | solution.py:133
  56.1 13.8 %collective-permute-start.15 = (bf16[2,2,3,96,384]{4,3,2,1,0:T(8,128)(2,1)S(1)}, bf16[2,2,3,96,384]{4,3,2,1,0:T(8,128)(2,1)S(1)}, u32[]{:S(2)}, u32[]{:S(2)}) collective-permute-start(bf16[2,2,3,96,384]{4,3,2,1,0:T(8,128)(2,1)S(1)} %pad_maximum_fusion), channel_id=1, source_target_pairs={{0,1},{1,0},{2,3},{3,2},{4,5},{5,4},{6,7},{7,6},{8,9},{9,8},{10,11... | collective-permute-start | bytes 2654216 | tf_op jit(solution)/shard_map/ppermute | solution.py:133
  56.4 12.1 %collective-permute-start.12 = (bf16[3,192,384]{2,1,0:T(8,128)(2,1)S(1)}, bf16[3,192,384]{2,1,0:T(8,128)(2,1)S(1)}, u32[]{:S(2)}, u32[]{:S(2)}) collective-permute-start(bf16[3,192,384]{2,1,0:T(8,128)(2,1)S(1)} %pad_maximum_fusion.7), channel_id=1, source_target_pairs={{0,4},{1,5},{2,6},{3,7},{4,0},{5,1},{6,2},{7,3},{8,12},{9,13},{10,... | collective-permute-start | bytes 1327112 | tf_op jit(solution)/shard_map/ppermute | solution.py:133
  71.3 24.5 %collective-permute-start.19 = (bf16[2,3,192,384]{3,2,1,0:T(8,128)(2,1)S(1)}, bf16[2,3,192,384]{3,2,1,0:T(8,128)(2,1)S(1)}, u32[]{:S(2)}, u32[]{:S(2)}) collective-permute-start(bf16[2,3,192,384]{3,2,1,0:T(8,128)(2,1)S(1)} %pad_maximum_fusion.1.refs_10_), channel_id=1, source_target_pairs={{0,1},{1,0},{2,3},{3,2},{4,5},{5,4},{6,7},{7,6},{8,9},{9,8},{10,11... | collective-permute-start | bytes 2654216 | tf_op jit(solution)/shard_map/ppermute | solution.py:133
  71.7 24.1 %collective-permute-start.17 = (bf16[2,3,192,384]{3,2,1,0:T(8,128)(2,1)S(1)}, bf16[2,3,192,384]{3,2,1,0:T(8,128)(2,1)S(1)}, u32[]{:S(2)}, u32[]{:S(2)}) collective-permute-start(bf16[2,3,192,384]{3,2,1,0:T(8,128)(2,1)S(1)} %pad_maximum_fusion.1.refs_10_), channel_id=1, source_target_pairs={{0,4},{1,5},{2,6},{3,7},{4,0},{5,1},{6,2},{7,3},{8,12},{9,13},{10,... | collective-permute-start | bytes 2654216 | tf_op jit(solution)/shard_map/ppermute | solution.py:133
  72.9 22.9 %collective-permute-start.20 = (bf16[2,3,192,384]{3,2,1,0:T(8,128)(2,1)S(1)}, bf16[2,3,192,384]{3,2,1,0:T(8,128)(2,1)}, u32[]{:S(2)}, u32[]{:S(2)}) collective-permute-start(bf16[2,3,192,384]{3,2,1,0:T(8,128)(2,1)S(1)} %pad_maximum_fusion.2.refs_12_), channel_id=1, source_target_pairs={{0,1},{1,0},{2,3},{3,2},{4,5},{5,4},{6,7},{7,6},{8,9},{9,8},{10,11... | collective-permute-start | bytes 2654216 | tf_op jit(solution)/shard_map/ppermute | solution.py:133
  73.3 22.5 %collective-permute-start.18 = (bf16[2,3,192,384]{3,2,1,0:T(8,128)(2,1)S(1)}, bf16[2,3,192,384]{3,2,1,0:T(8,128)(2,1)}, u32[]{:S(2)}, u32[]{:S(2)}) collective-permute-start(bf16[2,3,192,384]{3,2,1,0:T(8,128)(2,1)S(1)} %pad_maximum_fusion.2.refs_12_), channel_id=1, source_target_pairs={{0,2},{1,3},{2,0},{3,1},{4,6},{5,7},{6,4},{7,5},{8,10},{9,11},{10,... | collective-permute-start | bytes 2654216 | tf_op jit(solution)/shard_map/ppermute | solution.py:133
  149.1 18.1 %collective-permute-start.23 = (bf16[32,192,384]{2,1,0:T(8,128)(2,1)}, bf16[32,192,384]{2,1,0:T(8,128)(2,1)}, u32[]{:S(2)}, u32[]{:S(2)}) collective-permute-start(bf16[32,192,384]{2,1,0:T(8,128)(2,1)} %get-tuple-element.293), channel_id=1, source_target_pairs={{0,1},{1,0},{2,3},{3,2},{4,5},{5,4},{6,7},{7,6},{8,9},{9,8},{10,11... | collective-permute-start | bytes 14155784 | tf_op jit(solution)/shard_map/ppermute | solution.py:133
  171.0 21.2 %collective-permute-start.24 = (bf16[6,192,384]{2,1,0:T(8,128)(2,1)S(1)}, bf16[6,192,384]{2,1,0:T(8,128)(2,1)S(1)}, u32[]{:S(2)}, u32[]{:S(2)}) collective-permute-start(bf16[6,192,384]{2,1,0:T(8,128)(2,1)S(1)} %get-tuple-element.303), channel_id=1, source_target_pairs={{0,4},{1,5},{2,6},{3,7},{4,0},{5,1},{6,2},{7,3},{8,12},{9,13},{10,... | collective-permute-start | bytes 2654216 | tf_op jit(solution)/shard_map/ppermute | solution.py:133
  171.3 20.9 %collective-permute-start.25 = (bf16[6,192,384]{2,1,0:T(8,128)(2,1)S(1)}, bf16[6,192,384]{2,1,0:T(8,128)(2,1)S(1)}, u32[]{:S(2)}, u32[]{:S(2)}) collective-permute-start(bf16[6,192,384]{2,1,0:T(8,128)(2,1)S(1)} %get-tuple-element.304), channel_id=1, source_target_pairs={{0,2},{1,3},{2,0},{3,1},{4,6},{5,7},{6,4},{7,5},{8,10},{9,11},{10,... | collective-permute-start | bytes 2654216 | tf_op jit(solution)/shard_map/ppermute | solution.py:133
  198.8 23.5 %collective-permute-start.28 = (bf16[4,192,384]{2,1,0:T(8,128)(2,1)S(1)}, bf16[4,192,384]{2,1,0:T(8,128)(2,1)}, u32[]{:S(2)}, u32[]{:S(2)}) collective-permute-start(bf16[4,192,384]{2,1,0:T(8,128)(2,1)S(1)} %add_convert_fusion.2), channel_id=1, source_target_pairs={{0,4},{1,5},{2,6},{3,7},{4,0},{5,1},{6,2},{7,3},{8,12},{9,13},{10,... | collective-permute-start | bytes 1769480 | tf_op jit(solution)/shard_map/ppermute | solution.py:133
  199.6 16.4 %collective-permute-start.26 = (bf16[3,192,384]{2,1,0:T(8,128)(2,1)}, bf16[3,192,384]{2,1,0:T(8,128)(2,1)}, u32[]{:S(2)}, u32[]{:S(2)}) collective-permute-start(bf16[3,192,384]{2,1,0:T(8,128)(2,1)} %slice.458), channel_id=1, source_target_pairs={{0,2},{1,3},{2,0},{3,1},{4,6},{5,7},{6,4},{7,5},{8,10},{9,11},{10,... | collective-permute-start | bytes 1327112 | tf_op jit(solution)/shard_map/ppermute | solution.py:133
  200.8 21.5 %collective-permute-start.27 = (bf16[3,192,384]{2,1,0:T(8,128)(2,1)}, bf16[3,192,384]{2,1,0:T(8,128)(2,1)}, u32[]{:S(2)}, u32[]{:S(2)}) collective-permute-start(bf16[3,192,384]{2,1,0:T(8,128)(2,1)} %slice.457), channel_id=1, source_target_pairs={{0,4},{1,5},{2,6},{3,7},{4,0},{5,1},{6,2},{7,3},{8,12},{9,13},{10,... | collective-permute-start | bytes 1327112 | tf_op jit(solution)/shard_map/ppermute | solution.py:133
  232.7 12.2 %collective-permute-start.30 = (bf16[6,104,384]{2,1,0:T(8,128)(2,1)S(1)}, bf16[6,104,384]{2,1,0:T(8,128)(2,1)S(1)}, u32[]{:S(2)}, u32[]{:S(2)}) collective-permute-start(bf16[6,104,384]{2,1,0:T(8,128)(2,1)S(1)} %get-tuple-element.330), channel_id=1, source_target_pairs={{0,4},{1,5},{2,6},{3,7},{4,0},{5,1},{6,2},{7,3},{8,12},{9,13},{10,... | collective-permute-start | bytes 1437704 | tf_op jit(solution)/shard_map/ppermute | solution.py:133
  233.0 11.9 %collective-permute-start.31 = (bf16[6,104,384]{2,1,0:T(8,128)(2,1)S(1)}, bf16[6,104,384]{2,1,0:T(8,128)(2,1)S(1)}, u32[]{:S(2)}, u32[]{:S(2)}) collective-permute-start(bf16[6,104,384]{2,1,0:T(8,128)(2,1)S(1)} %get-tuple-element.331), channel_id=1, source_target_pairs={{0,2},{1,3},{2,0},{3,1},{4,6},{5,7},{6,4},{7,5},{8,10},{9,11},{10,... | collective-permute-start | bytes 1437704 | tf_op jit(solution)/shard_map/ppermute | solution.py:133
  234.2 13.6 %collective-permute-start.34 = (bf16[2,192,384]{2,1,0:T(8,128)(2,1)S(1)}, bf16[2,192,384]{2,1,0:T(8,128)(2,1)S(1)}, u32[]{:S(2)}, u32[]{:S(2)}) collective-permute-start(bf16[2,192,384]{2,1,0:T(8,128)(2,1)S(1)} %pad_maximum_fusion.9), channel_id=1, source_target_pairs={{0,8},{1,9},{2,10},{3,11},{4,12},{5,13},{6,14},{7,15},{8,16},{9,17... | collective-permute-start | bytes 884744 | tf_op jit(solution)/shard_map/ppermute | solution.py:133
  234.2 24.7 %collective-permute-start.35 = (bf16[2,192,384]{2,1,0:T(8,128)(2,1)S(1)}, bf16[2,192,384]{2,1,0:T(8,128)(2,1)S(1)}, u32[]{:S(2)}, u32[]{:S(2)}) collective-permute-start(bf16[2,192,384]{2,1,0:T(8,128)(2,1)S(1)} %pad_maximum_fusion.10), channel_id=1, source_target_pairs={{0,16},{1,17},{2,18},{3,19},{4,20},{5,21},{6,22},{7,23},{8,24},{9,... | collective-permute-start | bytes 884744 | tf_op jit(solution)/shard_map/ppermute | solution.py:133
  237.8 26.0 %collective-permute-start.36 = (bf16[2,192,384]{2,1,0:T(8,128)(2,1)S(1)}, bf16[2,192,384]{2,1,0:T(8,128)(2,1)S(1)}, u32[]{:S(2)}, u32[]{:S(2)}) collective-permute-start(bf16[2,192,384]{2,1,0:T(8,128)(2,1)S(1)} %pad_maximum_fusion.11), channel_id=1, source_target_pairs={{0,24},{1,25},{2,26},{3,27},{4,28},{5,29},{6,30},{7,31},{8,0},{9,1... | collective-permute-start | bytes 884744 | tf_op jit(solution)/shard_map/ppermute | solution.py:133
  245.4 18.4 %collective-permute-start.32 = (bf16[3,104,384]{2,1,0:T(8,128)(2,1)S(1)}, bf16[3,104,384]{2,1,0:T(8,128)(2,1)S(1)}, u32[]{:S(2)}, u32[]{:S(2)}) collective-permute-start(bf16[3,104,384]{2,1,0:T(8,128)(2,1)S(1)} %slice.460), channel_id=1, source_target_pairs={{0,2},{1,3},{2,0},{3,1},{4,6},{5,7},{6,4},{7,5},{8,10},{9,11},{10,... | collective-permute-start | bytes 718856 | tf_op jit(solution)/shard_map/ppermute | solution.py:133
  246.6 17.2 %collective-permute-start.33 = (bf16[3,104,384]{2,1,0:T(8,128)(2,1)S(1)}, bf16[3,104,384]{2,1,0:T(8,128)(2,1)S(1)}, u32[]{:S(2)}, u32[]{:S(2)}) collective-permute-start(bf16[3,104,384]{2,1,0:T(8,128)(2,1)S(1)} %slice.459), channel_id=1, source_target_pairs={{0,4},{1,5},{2,6},{3,7},{4,0},{5,1},{6,2},{7,3},{8,12},{9,13},{10,... | collective-permute-start | bytes 718856 | tf_op jit(solution)/shard_map/ppermute | solution.py:133
  266.3 15.4 %collective-permute-start.41 = (bf16[2,2,192,384]{3,2,1,0:T(8,128)(2,1)S(1)}, bf16[2,2,192,384]{3,2,1,0:T(8,128)(2,1)}, u32[]{:S(2)}, u32[]{:S(2)}) collective-permute-start(bf16[2,2,192,384]{3,2,1,0:T(8,128)(2,1)S(1)} %pad_maximum_fusion.3), channel_id=1, source_target_pairs={{0,2},{1,3},{2,0},{3,1},{4,6},{5,7},{6,4},{7,5},{8,10},{9,11},{10,... | collective-permute-start | bytes 1769480 | tf_op jit(solution)/shard_map/ppermute | solution.py:133
  266.6 15.1 %collective-permute-start.40 = (bf16[4,104,384]{2,1,0:T(8,128)(2,1)}, bf16[4,104,384]{2,1,0:T(8,128)(2,1)S(1)}, u32[]{:S(2)}, u32[]{:S(2)}) collective-permute-start(bf16[4,104,384]{2,1,0:T(8,128)(2,1)} %add_convert_fusion.5), channel_id=1, source_target_pairs={{0,4},{1,5},{2,6},{3,7},{4,0},{5,1},{6,2},{7,3},{8,12},{9,13},{10,... | collective-permute-start | bytes 958472 | tf_op jit(solution)/shard_map/ppermute | solution.py:133
  267.9 12.9 %collective-permute-start.38 = (bf16[2,104,384]{2,1,0:T(8,128)(2,1)}, bf16[2,104,384]{2,1,0:T(8,128)(2,1)S(1)}, u32[]{:S(2)}, u32[]{:S(2)}) collective-permute-start(bf16[2,104,384]{2,1,0:T(8,128)(2,1)} %pad_maximum_fusion.15), channel_id=1, source_target_pairs={{0,16},{1,17},{2,18},{3,19},{4,20},{5,21},{6,22},{7,23},{8,24},{9,... | collective-permute-start | bytes 479240 | tf_op jit(solution)/shard_map/ppermute | solution.py:133
  267.9 13.8 %collective-permute-start.39 = (bf16[2,104,384]{2,1,0:T(8,128)(2,1)}, bf16[2,104,384]{2,1,0:T(8,128)(2,1)S(1)}, u32[]{:S(2)}, u32[]{:S(2)}) collective-permute-start(bf16[2,104,384]{2,1,0:T(8,128)(2,1)} %pad_maximum_fusion.16), channel_id=1, source_target_pairs={{0,24},{1,25},{2,26},{3,27},{4,28},{5,29},{6,30},{7,31},{8,0},{9,1... | collective-permute-start | bytes 479240 | tf_op jit(solution)/shard_map/ppermute | solution.py:133
  (39 other events, 273.5 us)

commit v3 on v2

--- a/solution.py
+++ b/solution.py
@@ -18,6 +18,8 @@
 F32 = jnp.float32
 BF16 = jnp.bfloat16
 MIB = 1 << 20
+UNROLL_F = 6
+UNROLL_B = 2
 
 
 def nn(left, right):
@@ -144,11 +146,7 @@
 
 
 def piece_index(half, dz, dx, dy):
-    own = 24 + dx * 4 + dy * 2 + half
-    if isinstance(dz, int) and dz == 0:
-        return own
-    far = (12 + dy * 6 + dx * 3 if half else dx * 6 + dy * 3) + dz - 1
-    return far if isinstance(dz, int) else jnp.where(dz == 0, own, far)
+    return (16 + dy * 8 + dx * 4 if half else dx * 8 + dy * 4) + dz
 
 
 def at_rows(start, size):
@@ -209,10 +207,11 @@
     )(at, *matrices, *vectors)
 
 
-def rel_mask(at, shards, columns, size, x_bit):
-    z = (at[0] + Z_SIZE - iota((shards, columns), 0)) % Z_SIZE
-    shard = z * 2 + lax.bitwise_xor(at[1], x_bit)
-    return (iota((shards, columns), 1) // size == shard) & (iota((shards, columns), 0) < Z_SIZE)
+def rel_mask(at, columns, size):
+    row = iota((2 * Z_SIZE, columns), 0)
+    z = (at[0] + Z_SIZE - row % Z_SIZE) % Z_SIZE
+    shard = z * 2 + jnp.where(row < Z_SIZE, at[1], 1 - at[1])
+    return iota((2 * Z_SIZE, columns), 1) // size == shard
 
 
 def spread(size, columns):
@@ -223,22 +222,17 @@
 
 def unpack_kernel(at, near_ref, far_ref, *refs):
     out, row_ref = refs[:8], refs[8]
-    row_ref[...] = jnp.zeros_like(row_ref)
     for x_bit, rows in enumerate((near_ref, far_ref)):
         for d in range(Z_SIZE):
+            here = x_bit * Z_SIZE + d
             for i in range(4):
-                row_ref[x_bit, d : d + 1, i * COLUMNS : (i + 1) * COLUMNS] = rows[d, i : i + 1, :].astype(F32)
+                row_ref[here : here + 1, i * COLUMNS : (i + 1) * COLUMNS] = rows[d, i : i + 1, :].astype(F32)
     for ref, start in zip(out, SLOTS):
         columns = ref.shape[1]
         size = columns // (2 * Z_SIZE)
         table = spread(size, columns)
-        lanes = slice(start, start + table.shape[0])
-        total = jnp.zeros((1, columns), F32)
-        for x_bit in range(2):
-            got = nn(row_ref[x_bit, :, lanes].astype(BF16), table)
-            mask = rel_mask(at, 8, columns, size, x_bit)
-            total = total + jnp.sum(jnp.where(mask, got, 0.0), 0, keepdims=True)
-        ref[...] = total
+        got = nn(row_ref[:, start : start + table.shape[0]].astype(BF16), table)
+        ref[...] = jnp.sum(jnp.where(rel_mask(at, columns, size), got, 0.0), 0, keepdims=True)
 
 
 def unpack(at, near, far, sizes):
@@ -249,7 +243,7 @@
         [full(near.shape)] * 2,
         [full(s) for s in shapes],
         [shape_of(s, F32) for s in shapes],
-        [pltpu.VMEM((2, 8, PACKED), F32)],
+        [pltpu.VMEM((2 * Z_SIZE, PACKED), F32)],
         name="unpack",
         cost=(1e8, 1e5),
     )(at, near, far)
@@ -402,11 +396,11 @@
             qkv_ref[:, base + p * LANES : base + (p + 1) * LANES] = piece.astype(BF16)
     mask_ref[...] = jnp.where(allowed_pairs(plan, gene, span), 1.0, 0.0)
     masks = head_masks(span)
-    for p in range(width // LANES):
-        here = slice(p * LANES, (p + 1) * LANES)
-        q = qkv_ref[:, p * LANES : (p + 1) * LANES]
-        k = qkv_ref[:, width + p * LANES : width + (p + 1) * LANES] * BF16(1.0 / math.sqrt(HEAD_DIM))
-        v = qkv_ref[:, 2 * width + p * LANES : 2 * width + (p + 1) * LANES]
+    def pair(p, carry):
+        part = lambda i: at_columns(i * width + p * LANES, LANES)
+        q = qkv_ref[:, part(0)]
+        k = qkv_ref[:, part(1)] * BF16(1.0 / math.sqrt(HEAD_DIM))
+        v = qkv_ref[:, part(2)]
         o = jnp.zeros((span, LANES), F32)
         for h in range(2):
             s = nt(keep(masks[h], k), q)
@@ -417,7 +411,10 @@
             weights = (e * (1.0 / total)).astype(BF16)
             o = o + tn(weights, keep(masks[h], v))
             lse_ref[pl.ds(2 * p + h, 1), :] = peak + jnp.log(total)
-        o_ref[:, here] = o.astype(BF16)
+        o_ref[:, part(0)] = o.astype(BF16)
+        return carry
+
+    lax.fori_loop(0, width // LANES, pair, 0, unroll=UNROLL_F)
     x1_ref[...] = x + nn(o_ref[...], wout_ref[...]) + bout_ref[...]
     if pieces:
 
@@ -472,10 +469,11 @@
 
 
 def feed_kernel(at, *refs, block, pieces, steps):
-    (x1_ref, c_ref, g2_ref, b2_ref, bup_ref, bdown_ref), refs = refs[:6], refs[6:]
+    (x1_hbm, c_hbm, g2_ref, b2_ref, bup_ref, bdown_ref), refs = refs[:6], refs[6:]
     source, refs = (refs[:12], refs[12:]) if pieces else (refs[:2], refs[2:])
-    (out_ref, dx1_ref, da_ref, gbup_ref, sums_ref, first_ref, second_ref), refs = refs[:7], refs[7:]
-    a2_ref, acc_ref, dh_ref, gr_ref, du_ref, wups, wdowns, gups, gdowns, load_sem, store_sem = refs
+    (out_hbm, dx1_hbm, da_hbm, gbup_ref, sums_ref, first_ref, second_ref), refs = refs[:7], refs[7:]
+    x1_ref, c_ref, out_ref, da_ref, a2_ref, acc_ref, dh_ref, gr_ref, du_ref = refs[:9]
+    wups, wdowns, gups, gdowns, load_sem, store_sem, in_sem, out_sem = refs[9:]
     step = pl.program_id(0)
     length, width = x1_ref.shape
     chunk = bup_ref.shape[1]
@@ -564,17 +562,41 @@
         pltpu.make_async_copy(gups.at[to], gups.at[to], store_sem.at[0, to]).wait()
         pltpu.make_async_copy(gdowns.at[to], gdowns.at[to], store_sem.at[1, to]).wait()
 
+    def bring(i):
+        here = at_rows(i * block, block)
+        return [
+            pltpu.make_async_copy(x1_hbm.at[here, :], x1_ref.at[here, :], in_sem.at[0, i]),
+            pltpu.make_async_copy(c_hbm.at[here, :], c_ref.at[here, :], in_sem.at[1, i]),
+        ]
+
+    def give(i):
+        here = at_rows(i * block, block)
+        return [
+            pltpu.make_async_copy(out_ref.at[here, :], out_hbm.at[here, :], out_sem.at[0, i]),
+            pltpu.make_async_copy(x1_ref.at[here, :], dx1_hbm.at[here, :], out_sem.at[1, i]),
+            pltpu.make_async_copy(da_ref.at[here, :], da_hbm.at[here, :], out_sem.at[2, i]),
+        ]
+
     @pl.when(step == 0)
     def _():
+        for i in range(blocks):
+            bring(i)[0].start()
         load(0, 0)
+        for i in range(blocks):
+            bring(i)[1].start()
 
         def one(i, carry):
             here = pl.ds(i * block, block)
+            bring(i)[0].wait()
             xhat, _ = normalize(x1_ref[here, :])
             a2_ref[here, :] = (xhat * g2_ref[...] + b2_ref[...]).astype(BF16)
+            acc_ref[here, :] = jnp.zeros((block, width), F32)
+            dh_ref[here, :] = jnp.zeros((block, width), F32)
             return carry
 
         lax.fori_loop(0, blocks, one, 0)
+        for i in range(blocks):
+            bring(i)[1].wait()
 
     wait_load(slot)
 
@@ -596,16 +618,8 @@
         out = nn(gr, wdown_ref[...])
         dh = nt(du, wup_ref[...])
 
-        @pl.when(step == 0)
-        def _():
-            acc_ref[here, :] = out
-            dh_ref[here, :] = dh
-
-        @pl.when(step > 0)
-        def _():
-            acc_ref[here, :] += out
-            dh_ref[here, :] += dh
-
+        acc_ref[here, :] += out
+        dh_ref[here, :] += dh
         return bias_sum + jnp.sum(du.astype(F32), 0, keepdims=True)
 
     gbup_ref[...] = lax.fori_loop(0, blocks, one, jnp.zeros((1, chunk), F32))
@@ -631,9 +645,11 @@
             dx1 = c + scale * (
                 e - jnp.mean(e, -1, keepdims=True) - xhat * jnp.mean(e * xhat, -1, keepdims=True)
             )
-            dx1_ref[here, :] = dx1
+            x1_ref[here, :] = dx1
             da = dx1.astype(BF16)
             da_ref[here, :] = da
+            for copy in give(i):
+                copy.start()
             new = (
                 jnp.sum(dh * xhat, 0, keepdims=True),
                 jnp.sum(dh, 0, keepdims=True),
@@ -645,6 +661,9 @@
         sums = lax.fori_loop(0, blocks, one, (jnp.zeros((1, width), F32),) * 4)
         for i in range(4):
             sums_ref[i : i + 1, :] = sums[i]
+        for i in range(blocks):
+            for copy in give(i):
+                copy.wait()
         wait_store(1 - slot)
         wait_store(slot)
 
@@ -661,11 +680,11 @@
     else:
         stored = [shape_of((width, hidden), BF16), shape_of((hidden, width), BF16)]
     return call(
-        functools.partial(feed_kernel, block=length // 4, pieces=pieces, steps=steps),
+        functools.partial(feed_kernel, block=length // 2, pieces=pieces, steps=steps),
         (steps,),
         [
-            full((length, width)),
-            full((length, width)),
+            ANY,
+            ANY,
             full((1, width)),
             full((1, width)),
             pl.BlockSpec((1, chunk), lambda j, *ids: (0, j)),
@@ -673,9 +692,9 @@
         ]
         + [ANY] * len(source),
         [
-            full((length, width)),
-            full((length, width)),
-            full((length, width)),
+            ANY,
+            ANY,
+            ANY,
             pl.BlockSpec((1, chunk), lambda j, *ids: (0, j)),
             full((8, width)),
             ANY,
@@ -690,6 +709,10 @@
         ]
         + stored,
         [
+            pltpu.VMEM((length, width), F32),
+            pltpu.VMEM((length, width), BF16),
+            pltpu.VMEM((length, width), BF16),
+            pltpu.VMEM((length, width), BF16),
             pltpu.VMEM((length, width), BF16),
             pltpu.VMEM((length, width), F32),
             pltpu.VMEM((length, width), F32),
@@ -701,6 +724,8 @@
             pltpu.VMEM((2, chunk, width), BF16),
             pltpu.SemaphoreType.DMA((2, 2)),
             pltpu.SemaphoreType.DMA((2, 2)),
+            pltpu.SemaphoreType.DMA((2, 4)),
+            pltpu.SemaphoreType.DMA((3, 4)),
         ],
         name="feed",
         cost=(29e9, 40e6),
@@ -708,10 +733,9 @@
 
 
 def attend_back_kernel(
-    plan, qkv_ref, da_ref, lse_ref, cos_ref, sin_ref, xp_ref, dx1_ref, g1_ref, wout_ref, wqkv_ref,
-    *refs, base,
+    plan, qkv_ref, da_ref, lse_ref, cos_ref, sin_ref, wout_ref, *refs, base,
 ):
-    dqkv_ref, dxp_ref, sums_ref, bias_ref, dout_ref, mask_ref = refs[-6:]
+    dqkv_ref, bias_ref, dout_ref, mask_ref = refs[-4:]
     gene = pl.program_id(0) + base
     span, width = da_ref.shape
     score_scale = 1.0 / math.sqrt(HEAD_DIM)
@@ -723,12 +747,12 @@
     def back(t):
         return (t * cos - swap_halves(t) * sin).astype(BF16)
 
-    for p in range(width // LANES):
-        here = slice(p * LANES, (p + 1) * LANES)
-        q = qkv_ref[:, p * LANES : (p + 1) * LANES]
-        k = qkv_ref[:, width + p * LANES : width + (p + 1) * LANES] * BF16(score_scale)
-        v = qkv_ref[:, 2 * width + p * LANES : 2 * width + (p + 1) * LANES]
-        dout = dout_ref[:, here]
+    def pair(p, carry):
+        part = lambda i: at_columns(i * width + p * LANES, LANES)
+        q = qkv_ref[:, part(0)]
+        k = qkv_ref[:, part(1)] * BF16(score_scale)
+        v = qkv_ref[:, part(2)]
+        dout = dout_ref[:, part(0)]
         dq = jnp.zeros((span, LANES), F32)
         dk = jnp.zeros((span, LANES), F32)
         dv = jnp.zeros((span, LANES), F32)
@@ -743,36 +767,25 @@
             dv = dv + nn(weights.astype(BF16), keep(masks[h], dout))
             dk = dk + nn(ds, keep(masks[h], q))
             dq = dq + tn(ds, kh)
-        dqkv_ref[:, p * LANES : (p + 1) * LANES] = back(dq)
-        dqkv_ref[:, width + p * LANES : width + (p + 1) * LANES] = back(dk * score_scale)
-        dqkv_ref[:, 2 * width + p * LANES : 2 * width + (p + 1) * LANES] = dv.astype(BF16)
-
-    dh = nt(dqkv_ref[...], wqkv_ref[...])
-    xhat, scale = normalize(xp_ref[...].astype(F32))
-    e = dh * g1_ref[...]
-    dx = dx1_ref[...] + scale * (
-        e - jnp.mean(e, -1, keepdims=True) - xhat * jnp.mean(e * xhat, -1, keepdims=True)
-    )
-    dxp_ref[...] = dx.astype(BF16)
-    gain = jnp.sum(dh * xhat, 0, keepdims=True)
-    bias = jnp.sum(dh, 0, keepdims=True)
+        dqkv_ref[:, part(0)] = back(dq)
+        dqkv_ref[:, part(1)] = back(dk * score_scale)
+        dqkv_ref[:, part(2)] = dv.astype(BF16)
+        return carry
+
+    lax.fori_loop(0, width // LANES, pair, 0, unroll=UNROLL_B)
 
     bqkv = jnp.sum(dqkv_ref[...].astype(F32), 0, keepdims=True)
 
     @pl.when(gene == base)
     def _():
-        sums_ref[0:1, :] = gain
-        sums_ref[1:2, :] = bias
         bias_ref[0:1, :] = bqkv
 
     @pl.when(gene > base)
     def _():
-        sums_ref[0:1, :] += gain
-        sums_ref[1:2, :] += bias
         bias_ref[0:1, :] += bqkv
 
 
-def attend_back(plan, qkv, da, lse, cos, sin, xp, dx1, g1, wout, wqkv, base, count, before=()):
+def attend_back(plan, qkv, da, lse, cos, sin, wout, base, count, before=()):
     length, width = da.shape
     span = length // GENES
     rows = lambda shape: pl.BlockSpec(shape, lambda g, *ids: (g + base, 0))
@@ -785,38 +798,75 @@
             pl.BlockSpec((16, span), lambda g, *ids: (0, g + base)),
             rows((span, LANES)),
             rows((span, LANES)),
-            rows((span, width)),
-            rows((span, width)),
-            full((1, width)),
             full((width, width)),
-            full((width, 3 * width)),
         ]
         + [ANY] * len(before),
-        [rows((span, 3 * width)), rows((span, width)), full((8, width)), full((8, 3 * width))],
-        [
-            shape_of((length, 3 * width), BF16),
-            shape_of((length, width), BF16),
-            shape_of((8, width), F32),
-            shape_of((8, 3 * width), F32),
-        ],
+        [rows((span, 3 * width)), full((8, 3 * width))],
+        [shape_of((length, 3 * width), BF16), shape_of((8, 3 * width), F32)],
         [pltpu.VMEM((span, width), BF16), pltpu.VMEM((span, span), F32)],
         name="attend_back",
         cost=(4e9 * count, 6e6 * count),
-        aliases={11 + i: i for i in range(len(before))},
-    )(plan, qkv, da, lse, cos, sin, xp, dx1, g1, wout, wqkv, *before)
+        aliases={7 + i: i for i in range(len(before))},
+    )(plan, qkv, da, lse, cos, sin, wout, *before)
+
+
+def project_back_kernel(xp_ref, g1_ref, dx1_ref, dqkv_ref, wqkv_ref, dxp_ref, sums_ref):
+    step = pl.program_id(0)
+    dh = nt(dqkv_ref[...], wqkv_ref[...])
+    xhat, scale = normalize(xp_ref[...].astype(F32))
+    e = dh * g1_ref[...]
+    dx = dx1_ref[...] + scale * (
+        e - jnp.mean(e, -1, keepdims=True) - xhat * jnp.mean(e * xhat, -1, keepdims=True)
+    )
+    dxp_ref[...] = dx.astype(BF16)
+
+    @pl.when(step == 0)
+    def _():
+        sums_ref[...] = jnp.zeros_like(sums_ref)
+
+    sums_ref[0:1, :] += jnp.sum(dh * xhat, 0, keepdims=True)
+    sums_ref[1:2, :] += jnp.sum(dh, 0, keepdims=True)
+
+
+def project_back(xp, g1, dx1, dqkv, wqkv):
+    length, width = xp.shape
+    span = length // GENES
+    return call(
+        project_back_kernel,
+        (GENES,),
+        [
+            rows_of((span, width)),
+            full((1, width)),
+            rows_of((span, width)),
+            rows_of((span, 3 * width)),
+            full((width, 3 * width)),
+        ],
+        [rows_of((span, width)), full((8, width))],
+        [shape_of((length, width), BF16), shape_of((8, width), F32)],
+        prefetch=0,
+        name="project_back",
+        cost=(0, 0),
+    )(xp, g1, dx1, dqkv, wqkv)
 
 
 def grads_kernel(at, *refs, pieces):
-    (xp_ref, g1_ref, b1_ref, o_ref, da_ref, dqkv_ref), refs = refs[:6], refs[6:]
-    if pieces:
-        vectors, refs = refs[:8], refs[8:]
-        first_ref, second_ref, a1_ref, grad_ref, sem, small_ref, small_sem = refs
-    else:
-        first_ref, second_ref, a1_ref, grad_ref, sem = refs
+    (xp_hbm, o_hbm, da_hbm, dqkv_hbm, g1_ref, b1_ref), refs = refs[:6], refs[6:]
+    sums, refs = (refs[:5], refs[5:]) if pieces else ((), refs)
+    first_ref, second_ref, xp_ref, o_ref, da_ref, dqkv_ref, a1_ref, grad_ref, in_sem, sem, *rest = refs
+    small_ref, small_sem = rest if pieces else (None, None)
     step = pl.program_id(0)
     width = xp_ref.shape[1]
+    rows = width // (4 * Z_SIZE)
     slot = lax.rem(step, 2)
-    rows = width // (4 * Z_SIZE)
+
+    def bring(j):
+        part = dqkv_hbm.at[:, at_columns(j * width, width)]
+        return pltpu.make_async_copy(part, dqkv_ref.at[lax.rem(j, 2)], in_sem.at[3 + lax.rem(j, 2)])
+
+    whole = [
+        pltpu.make_async_copy(src, dst, in_sem.at[i])
+        for i, (src, dst) in enumerate(((o_hbm, o_ref), (da_hbm, da_ref), (xp_hbm, xp_ref)))
+    ]
 
     def wait(to):
         pltpu.make_async_copy(grad_ref.at[to], grad_ref.at[to], sem.at[to]).wait()
@@ -826,75 +876,97 @@
             for dx, dy, dc in EVERY:
                 f, y, c = spot(at, Z_SIZE - dz, dx, dy, dc)
                 src = grad_ref.at[to, at_rows(f * 2 * rows + c * rows, rows), at_columns(y * COLUMNS, COLUMNS)]
-                dst = (first_ref, second_ref)[dc].at[piece_index(half, dz, dx, dy), pl.ds(base * rows, rows)]
+                dst = (first_ref, second_ref)[dc].at[
+                    jnp.where(half == 0, piece_index(0, dz, dx, dy), piece_index(1, dz, dx, dy)),
+                    at_rows(base * rows, rows),
+                ]
                 pltpu.make_async_copy(src, dst, sem.at[to]).start()
             return carry
 
         lax.fori_loop(0, Z_SIZE, one, 0)
 
     def pack():
-        small_ref[...] = jnp.zeros_like(small_ref)
+        sums1, low_ref, high_ref, sums2, gbup = sums
+        line = lambda ref, i: ref[i : i + 1, :]
+        vectors = [
+            line(sums1, 0), line(sums1, 1), line(low_ref, 0) + line(high_ref, 0), line(sums2, 3),
+            line(sums2, 0), line(sums2, 1), gbup[...], line(sums2, 2),
+        ]
         shards = 2 * Z_SIZE
         columns = []
-        for ref in vectors:
-            size = ref.shape[1] // shards
-            whole = jnp.broadcast_to(ref[...], (shards, ref.shape[1]))
-            mask = iota(whole.shape, 1) // size == iota(whole.shape, 0)
-            own = jnp.where(mask, whole, 0.0).astype(BF16)
-            columns.append(nt(own, spread(size, ref.shape[1])).astype(BF16))
-        rows = jnp.concatenate(columns, 1).astype(F32)
+        for value in vectors:
+            size = value.shape[1] // shards
+            spread_out = jnp.broadcast_to(value, (shards, value.shape[1]))
+            mask = iota(spread_out.shape, 1) // size == iota(spread_out.shape, 0)
+            own = jnp.where(mask, spread_out, 0.0).astype(BF16)
+            columns.append(nt(own, spread(size, value.shape[1])).astype(BF16))
+        packed = jnp.concatenate(columns, 1).astype(F32)
         for f in range(shards):
             for i in range(4):
-                part = rows[f : f + 1, i * COLUMNS : (i + 1) * COLUMNS]
-                small_ref[f, i // 2, i % 2, 0] = jnp.broadcast_to(part, (8, COLUMNS)).astype(BF16)
+                part = packed[f : f + 1, i * COLUMNS : (i + 1) * COLUMNS]
+                small_ref[f, i // 2, i % 2] = jnp.broadcast_to(part, (8, COLUMNS)).astype(BF16)
 
     def smalls(act):
         def one(dz, carry):
             for dx, dy, dc in EVERY:
                 f, y, c = spot(at, Z_SIZE - dz, dx, dy, dc)
                 for half in range(2):
-                    src = small_ref.at[f, y, c, half]
+                    src = small_ref.at[f, y, c]
                     dst = (first_ref, second_ref)[dc].at[piece_index(half, dz, dx, dy), pl.ds(2 * rows, 8)]
                     act(pltpu.make_async_copy(src, dst, small_sem))
             return carry
 
         lax.fori_loop(0, Z_SIZE, one, 0)
 
-    @pl.when(step >= 2)
+    @pl.when(step == 0)
     def _():
-        wait(slot)
-
-    for j in range(4):
-
-        @pl.when(step == j)
-        def _(j=j):
-            if j == 0:
-                if pieces:
-                    pack()
-                    smalls(lambda copy: copy.start())
-                xhat, _ = normalize(xp_ref[...].astype(F32))
-                a1_ref[...] = (xhat * g1_ref[...] + b1_ref[...]).astype(BF16)
-            if j < 3:
-                grad_ref[j % 2] = tn(a1_ref[...], dqkv_ref[...]).astype(BF16)
-            else:
-                grad_ref[j % 2] = tn(o_ref[...], da_ref[...]).astype(BF16)
-            if pieces:
-                store(j // 2, j % 2, j % 2)
-            elif j < 3:
-                dst = first_ref.at[:, pl.ds(j * width, width)]
-                pltpu.make_async_copy(grad_ref.at[j % 2], dst, sem.at[j % 2]).start()
-            else:
-                pltpu.make_async_copy(grad_ref.at[j % 2], second_ref, sem.at[j % 2]).start()
-            if j == 3:
-                wait(0)
-                wait(1)
-                if pieces:
-                    smalls(lambda copy: copy.wait())
-
-
-def grads(at, xp, g1, b1, o, da, dqkv, vectors):
+        for copy in whole:
+            copy.start()
+        bring(step).start()
+        if pieces:
+            pack()
+            smalls(lambda copy: copy.start())
+        whole[0].wait()
+        whole[1].wait()
+        grad_ref[0] = tn(o_ref[...], da_ref[...]).astype(BF16)
+        if pieces:
+            store(1, 1, 0)
+        else:
+            pltpu.make_async_copy(grad_ref.at[0], second_ref, sem.at[0]).start()
+        whole[2].wait()
+        xhat, _ = normalize(xp_ref[...].astype(F32))
+        a1_ref[...] = (xhat * g1_ref[...] + b1_ref[...]).astype(BF16)
+
+    @pl.when(step > 0)
+    def _():
+        bring(step - 1).wait()
+
+        @pl.when(step < 3)
+        def _():
+            bring(step).start()
+
+        @pl.when(step >= 2)
+        def _():
+            wait(slot)
+
+        grad_ref[slot] = tn(a1_ref[...], dqkv_ref[lax.rem(step - 1, 2)]).astype(BF16)
+        if pieces:
+            store(lax.div(step - 1, 2), lax.rem(step - 1, 2), slot)
+        else:
+            dst = first_ref.at[:, at_columns((step - 1) * width, width)]
+            pltpu.make_async_copy(grad_ref.at[slot], dst, sem.at[slot]).start()
+
+    @pl.when(step == 3)
+    def _():
+        wait(0)
+        wait(1)
+        if pieces:
+            smalls(lambda copy: copy.wait())
+
+
+def grads(at, xp, g1, b1, o, da, dqkv, sums):
+    pieces = bool(sums)
     length, width = xp.shape
-    pieces = bool(vectors)
     if pieces:
         rows = width // (2 * Z_SIZE) + 8
         stored = [shape_of((PIECES, rows, COLUMNS), BF16)] * 2
@@ -903,30 +975,21 @@
     return call(
         functools.partial(grads_kernel, pieces=pieces),
         (4,),
-        [
-            full((length, width)),
-            full((1, width)),
-            full((1, width)),
-            full((length, width)),
-            full((length, width)),
-            pl.BlockSpec((length, width), lambda j, *ids: (0, jnp.minimum(j, 2))),
-        ]
-        + [full(v.shape) for v in vectors],
+        [ANY] * 4 + [full((1, width))] * 2 + [full(v.shape) for v in sums],
         [ANY, ANY],
         stored,
-        [
+        [pltpu.VMEM((length, width), BF16)] * 3
+        + [
+            pltpu.VMEM((2, length, width), BF16),
             pltpu.VMEM((length, width), BF16),
             pltpu.VMEM((2, width, width), BF16),
+            pltpu.SemaphoreType.DMA((5,)),
             pltpu.SemaphoreType.DMA((2,)),
         ]
-        + (
-            [pltpu.VMEM((2 * Z_SIZE, 2, 2, 2, 8, COLUMNS), BF16), pltpu.SemaphoreType.DMA]
-            if pieces
-            else []
-        ),
+        + ([pltpu.VMEM((2 * Z_SIZE, 2, 2, 8, COLUMNS), BF16), pltpu.SemaphoreType.DMA] if pieces else []),
         name="grads",
         cost=(5e9, 12e6),
-    )(at, xp, g1, b1, o, da, dqkv, *vectors)
+    )(at, xp, o, da, dqkv, g1, b1, *sums)
 
 
 def restore_kernel(plan, outp_ref, dxp_ref, out_ref, dx_ref):
@@ -953,12 +1016,11 @@
     )(plan, outp, dxp)
 
 
-def deliver_kernel(at, mine1, other1, mine2, other2, *out):
-    wqkv, wout, wup, wdown = out[:4]
-    vectors, row_ref = out[4:12], out[12]
+def deliver_first_kernel(at, mine, other, wqkv, wout, *rest):
+    vectors, row_ref = rest[:8], rest[8]
     width = wout.shape[1]
     rows = wout.shape[0] // 2
-    for dc, (one, two) in enumerate(((mine1, mine2), (other1, other2))):
+    for dc, one in enumerate((mine, other)):
         c = lax.bitwise_xor(at[3], dc)
         here = pl.ds(pl.multiple_of(c * rows, 8), rows)
         for y in range(2):
@@ -967,31 +1029,55 @@
                 start = base + y * COLUMNS
                 piece = one[y, b // 2, (b % 2) * rows : (b % 2 + 1) * rows, :]
                 ref[here, start : start + COLUMNS] = piece.astype(F32)
-                start = b * width + y * COLUMNS
-                wup[here, start : start + COLUMNS] = two[y, 0, b * rows : (b + 1) * rows, :].astype(F32)
-            down = pl.ds(pl.multiple_of(c * 4 * rows, 8), 4 * rows)
-            wdown[down, y * COLUMNS : (y + 1) * COLUMNS] = two[y, 1].astype(F32)
             start = at_columns((y * 2 + c) * COLUMNS, COLUMNS)
             row_ref[:, start] = one[y, 0, 2 * rows : 2 * rows + 8, :].astype(F32)
     for ref, start in zip(vectors, SLOTS):
         ref[...] = row_ref[0:1, start : start + ref.shape[0]].reshape(ref.shape[0])
 
 
-def deliver(at, mine1, other1, mine2, other2, sizes):
-    rows = mine2.shape[2] // 4
+def deliver_first(at, mine, other, sizes):
+    rows = (mine.shape[2] - 8) // 2
     width = 2 * COLUMNS
-    shapes = [(2 * rows, 3 * width), (2 * rows, width), (2 * rows, 4 * width), (8 * rows, width)]
-    shapes += [(n,) for n in sizes]
+    shapes = [(2 * rows, 3 * width), (2 * rows, width)] + [(n,) for n in sizes]
     return call(
-        deliver_kernel,
+        deliver_first_kernel,
         (1,),
-        [full(v.shape) for v in (mine1, other1, mine2, other2)],
+        [full(mine.shape)] * 2,
         [full(s) for s in shapes],
         [shape_of(s, F32) for s in shapes],
         [pltpu.VMEM((8, PACKED), F32)],
-        name="deliver",
-        cost=(0, 6e6),
-    )(at, mine1, other1, mine2, other2)
+        name="deliver_first",
+        cost=(0, 2e6),
+    )(at, mine, other)
+
+
+def deliver_second_kernel(at, mine, other, wup, wdown):
+    width = wdown.shape[1]
+    rows = wup.shape[0] // 2
+    for dc, two in enumerate((mine, other)):
+        c = lax.bitwise_xor(at[3], dc)
+        here = pl.ds(pl.multiple_of(c * rows, 8), rows)
+        down = pl.ds(pl.multiple_of(c * 4 * rows, 8), 4 * rows)
+        for y in range(2):
+            for b in range(4):
+                start = b * width + y * COLUMNS
+                wup[here, start : start + COLUMNS] = two[y, 0, b * rows : (b + 1) * rows, :].astype(F32)
+            wdown[down, y * COLUMNS : (y + 1) * COLUMNS] = two[y, 1].astype(F32)
+
+
+def deliver_second(at, mine, other):
+    rows = mine.shape[2] // 4
+    width = 2 * COLUMNS
+    shapes = [(2 * rows, 4 * width), (8 * rows, width)]
+    return call(
+        deliver_second_kernel,
+        (1,),
+        [full(mine.shape)] * 2,
+        [full(s) for s in shapes],
+        [shape_of(s, F32) for s in shapes],
+        name="deliver_second",
+        cost=(0, 4e6),
+    )(at, mine, other)
 
 
 def gather(shard):
@@ -1037,32 +1123,30 @@
 
 class Sum:
     def __init__(self, kept, got):
-        self.kept, self.got, self.more = kept, got, {}
+        self.kept, self.got = kept, got
 
     def near(self, start, stop):
         return add(self.kept[start:stop], self.got[start:stop])
 
     def plane_one(self):
-        return low(self.near(6, 12)), low(self.near(18, 24)), low(self.near(28, 32))
+        return low(self.near(8, 16)), low(self.near(24, 32))
 
     def plane_two(self, by_x, by_y):
-        self.first = add(self.near(0, 6), by_x)
-        self.second = add(self.near(12, 18), by_y)
-        return low(self.first[3:]), low(self.second[3:])
+        self.first = add(self.near(0, 8), by_x)
+        self.second = add(self.near(16, 24), by_y)
+        return low(self.first[Z_SIZE:]), low(self.second[Z_SIZE:])
 
     def along_z(self, by_y, by_x):
-        first, second = add(self.first[:3], by_y), add(self.second[:3], by_x)
-        return [low(stack([first[d], second[d]])) for d in range(Z_SIZE - 1)]
-
-    def across_y(self, by_z, side):
-        own = add(self.near(24, 28), side)
-        return low(stack([add(own[:2], *by_z), own[2:]]))
-
-
-def settle(at, part, got):
-    mine = low(add(part[0], got[1]))
-    other = low(add(got[0], part[1]))
-    return jnp.where(at[2] == 0, stack([mine, other]), stack([other, mine]))
+        first, second = add(self.first[:Z_SIZE], by_y), add(self.second[:Z_SIZE], by_x)
+        self.own = stack([first[0], second[0]])
+        return [low(stack([first[d], second[d]])) for d in range(1, Z_SIZE)]
+
+    def total(self, by_z):
+        return low(add(self.own, *by_z))
+
+
+def settle(bit, mine, other):
+    return jnp.where(bit == 0, stack([mine, other]), stack([other, mine]))
 
 
 def body(
@@ -1093,30 +1177,33 @@
 
         first1, second1 = stack([first1, first_y]), stack([second1, second_x])[:, :, :count]
         far_rows = jnp.concatenate([far_side[0, :1, 3 * count :], second_x[:, count:]])
-        first1, second1, rows, far_rows, near2 = tie((first1, second1, rows, far_rows, near2))
+        early = [stack(q[h] for q in (z2_one, z2_three)) for h in range(2)]
+        first1, second1, rows, far_rows, near2, early = tie((first1, second1, rows, far_rows, near2, early))
         far_first1, far_second1 = over_x(first1), over_y(second1)
-        z2 = [z2_one, move(near2, ALONG_Z[2]), z2_three]
+        z2_two = move(near2, ALONG_Z[2])
+        early_far = [over_y(early[0]), over_x(early[1])]
         params = unpack(at, rows, far_rows, sizes)
-        far_first1, far_second1, params, z2, far_side = tie((far_first1, far_second1, params, z2, far_side))
-
-        first2, second2 = (stack(q[h] for q in z2) for h in range(2))
+        far_first1, far_second1, params, z2_two, early_far, far_side = tie(
+            (far_first1, far_second1, params, z2_two, early_far, far_side)
+        )
+
+        late = [z2_two[h : h + 1] for h in range(2)]
         near_core1 = stack([first1, second1])
-        far_first1, far_second1, near_core1, first2, second2 = tie(
-            (far_first1, far_second1, near_core1, first2, second2)
-        )
-        far_core1 = over_core(far_first1), over_core(far_second1)
+        far_first1, far_second1, near_core1, late = tie((far_first1, far_second1, near_core1, late))
+        far_core1 = over_core(stack([far_first1, far_second1]))
         near_core1 = over_core(near_core1)
-        first_y, second_x = over_y(first2), over_x(second2)
+        late_far = [over_y(late[0]), over_x(late[1])]
         core_side = over_core(far_side)
-        first_y, second_x, far_core1, near_core1, core_side = tie(
-            (first_y, second_x, far_core1, near_core1, core_side)
-        )
+        late_far, far_core1, near_core1, core_side = tie((late_far, far_core1, near_core1, core_side))
 
         attention = (
             w_qkv, w_out, far_side, core_side, first1, far_first1, second1, far_second1,
-            near_core1, far_core1[0], near_core1, far_core1[1],
+            near_core1, far_core1, near_core1, far_core1,
         )
-        first2, second2 = stack([first2, first_y]), stack([second2, second_x])
+        order = lambda e, l: jnp.concatenate([e[:1], l, e[1:]])
+        first2, second2 = (
+            stack([order(early[h], late[h]), order(early_far[h], late_far[h])]) for h in range(2)
+        )
         first2, second2, attention, params, plan = tie((first2, second2, attention, params, plan))
         far_first2, far_second2 = over_x(first2), over_y(second2)
         core2 = [over_core(v) for v in (first2, second2)]
@@ -1136,64 +1223,63 @@
             core2[0], far_core2[0], core2[1], far_core2[1],
         )
     outp, dx1, da, gbup, sums2, *parts2 = feed(at, x1, cp, g2, b2, bup, bdown, forward)
-    back = functools.partial(attend_back, plan, qkv, da, lse, cos, sin, xp, dx1, g1, wout, wqkv)
-    half = GENES // 2
+    back = functools.partial(attend_back, plan, qkv, da, lse, cos, sin, wout)
+    split = 1
     if tuned:
         kept2, sent2 = parts2
         got2 = over_core(sent2)
-        dqkv, dxp, *sums_low = back(0, half)
+        dqkv, bias_low = back(0, split)
         got2, dqkv = tie((got2, dqkv))
         group2 = Sum(kept2, got2)
-        to_x, to_y, side2, dqkv = tie(group2.plane_one() + (dqkv,))
+        to_x, to_y, dqkv = tie(group2.plane_one() + (dqkv,))
         by_x, by_y = over_x(to_x), over_y(to_y)
-        dqkv, dxp, *sums_high = back(half, half, (dqkv, dxp))
-        by_x, by_y, dqkv = tie((by_x, by_y, dqkv))
+    else:
+        dqkv, bias_low = back(0, split)
+    dqkv, bias_high = back(split, GENES - split, (dqkv,))
+    dxp, sums1 = project_back(xp, g1, dx1, dqkv, wqkv)
+    sums = [sums1, bias_low, bias_high, sums2, gbup]
+    if tuned:
+        by_x, by_y, sums, dxp, dqkv = tie((by_x, by_y, sums, dxp, dqkv))
         to_y, to_x = group2.plane_two(by_x, by_y)
-        to_y, to_x, side2, dqkv = tie((to_y, to_x, side2, dqkv))
-        by_y, by_x, by_side2 = over_y(to_y), over_x(to_x), over_x(side2)
+        to_y, to_x, dqkv = tie((to_y, to_x, dqkv))
+        by_y, by_x = over_y(to_y), over_x(to_x)
+        kept1, sent1 = grads(at, xp, g1, b1, o, da, dqkv, sums)
+        by_y, by_x, kept1, sent1 = tie((by_y, by_x, kept1, sent1))
+        got1 = over_core(sent1)
+        got1, *to_z2 = tie([got1] + group2.along_z(by_y, by_x))
+        group1 = Sum(kept1, got1)
+        to_x, to_y, *to_z2 = tie([*group1.plane_one(), *to_z2])
+        two = move(to_z2[1], ALONG_Z[2])
+        by_x, by_y, two, *to_z2 = tie((over_x(to_x), over_y(to_y), two, to_z2[0], to_z2[2]))
+        to_y, to_x, *to_z2 = tie([*group1.plane_two(by_x, by_y), *to_z2])
+        one, three = move(to_z2[0], ALONG_Z[1]), move(to_z2[1], ALONG_Z[3])
+        by_y, by_x, one, three = tie((over_y(to_y), over_x(to_x), one, three))
+        z2 = one, two, three
+        to_z1 = group1.along_z(by_y, by_x)
+        total2 = group2.total(z2)
+        to_z1, total2, outp, dxp = tie((to_z1, total2, outp, dxp))
+        z1 = to_z(to_z1)
+        by_y = over_y(total2)
+        layer_out, input_grad = restore(plan, outp, dxp)
+        z1, by_y, layer_out, input_grad = tie((z1, by_y, layer_out, input_grad))
+        total1 = group1.total(z1)
+        final2 = settle(at[2], total2, by_y)
+        total1, final2 = tie((total1, final2))
+        by_y, other2 = over_y(total1), over_core(final2)
+        by_y, other2 = tie((by_y, other2))
+        final1 = settle(at[2], total1, by_y)
+        other1 = over_core(final1)
+        wup, wdown = deliver_second(at, final2, other2)
+        other1, wup, wdown = tie((other1, wup, wdown))
+        wqkv, wout, *small = deliver_first(at, final1, other1, sizes)
     else:
-        dqkv, dxp, *sums_low = back(0, half)
-        dqkv, dxp, *sums_high = back(half, half, (dqkv, dxp))
-    sums1, sumsb = (a + b for a, b in zip(sums_low, sums_high))
-    row = lambda array, i: array[i : i + 1]
-    small = [
-        row(sums1, 0), row(sums1, 1), row(sumsb, 0), row(sums2, 3), row(sums2, 0), row(sums2, 1), gbup, row(sums2, 2),
-    ]
-    parts1 = grads(at, xp, g1, b1, o, da, dqkv, small if tuned else ())
-    if tuned:
-        by_y, by_x, by_side2, parts1 = tie((by_y, by_x, by_side2, parts1))
-        kept1, sent1 = parts1
-        to_z2 = group2.along_z(by_y, by_x)
-        to_z2, sent1 = tie((to_z2, sent1))
-        got1 = over_core(sent1)
-        z2 = to_z(to_z2)
-        got1 = tie(got1)
-        group1 = Sum(kept1, got1)
-        to_x, to_y, side1 = tie(group1.plane_one())
-        by_x, by_y = over_x(to_x), over_y(to_y)
-        by_x, by_y = tie((by_x, by_y))
-        to_y, to_x = tie(group1.plane_two(by_x, by_y))
-        by_y, by_x = over_y(to_y), over_x(to_x)
-        by_y, by_x, z2 = tie((by_y, by_x, z2))
-        to_z1 = group1.along_z(by_y, by_x)
-        part2 = group2.across_y(z2, by_side2)
-        to_z1, side1, part2, outp, dxp = tie((to_z1, side1, part2, outp, dxp))
-        z1 = to_z(to_z1)
-        by_side1, by_part2 = over_x(side1), over_y(part2)
-        layer_out, input_grad = restore(plan, outp, dxp)
-        z1, by_side1, by_part2, layer_out, input_grad = tie((z1, by_side1, by_part2, layer_out, input_grad))
-        part1 = group1.across_y(z1, by_side1)
-        final2 = settle(at, part2, by_part2)
-        part1, final2 = tie((part1, final2))
-        by_part1, other2 = over_y(part1), over_core(final2)
-        final1 = settle(at, part1, by_part1)
-        other1 = over_core(final1)
-        wqkv, wout, wup, wdown, *small = deliver(at, final1, other1, final2, other2, sizes)
-    else:
+        parts1 = grads(at, xp, g1, b1, o, da, dqkv, ())
         layer_out, input_grad = restore(plan, outp, dxp)
         wqkv, wout = map(reduce_rows, parts1)
         wup, wdown = map(reduce_rows, parts2)
-        small = [reduce_rows(v.reshape(-1)) for v in small]
+        bias = bias_low + bias_high
+        small = [sums1[0], sums1[1], bias[0], sums2[3], sums2[0], sums2[1], gbup[0], sums2[2]]
+        small = [reduce_rows(v) for v in small]
     dg1, db1, dbqkv, dbout, dg2, db2, dbup, dbdown = small
     return (
         layer_out[None], input_grad[None], dg1, db1, wqkv, dbqkv, wout, dbout, dg2, db2,

time: 307 us -> 281 us (0.915)
  the two profiles are of different devices: /device:TPU:9 before, /device:TPU:0 now
where the time goes in v3:
time: 281 us; the launch traced here: 280 us
  Pallas kernels  142 us (51%)
  waiting for transfers between devices  59.6 us (21%)
  starting transfers between devices  46.5 us (17%)
  other arithmetic  18.4 us (7%)
  local copies, waits for them, and re-layouts  12.7 us (5%)
    ppermute x44, waiting for transfers between devices, move(): return lax.ppermute(array, AXES, table)  59.6 us
    ppermute x44, starting transfers between devices, move(): return lax.ppermute(array, AXES, table)  46.5 us
    pallas_call x1, Pallas kernels, feed(): call(functools.partial(feed_kernel, block=length // 2, pieces=pieces, ste...  42.9 us
    pallas_call x2, Pallas kernels, attend_back(): call(functools.partial(attend_back_kernel, base=base), (count,), [rows((s...  25.5 us
    pallas_call x1, Pallas kernels, attend(): call(functools.partial(attend_kernel, pieces=pieces), (GENES,), [rows_of(...  22.2 us
    pallas_call x1, Pallas kernels, grads(): call(functools.partial(grads_kernel, pieces=pieces), (4,), [ANY] * 4 + [f...  12.2 us
    pallas_call x1, Pallas kernels, project_back(): call(project_back_kernel, (GENES,), [rows_of((span, width)), full((1, wid...  9.9 us
    pallas_call x1, Pallas kernels, prepare(): call(prepare_kernel, (GENES,), [full((1, length)), full((length, width)),...  8.67 us
  transfers between devices with their start and end apart: 44, of which 15 were waited for; matrix products, arithmetic and copies ran while one was open for 3% of the time, Pallas kernels for 33%

profile of v3, /device:TPU:0, one launch (start us, length us, event | category | flops | bytes accessed | tf_op | source)
XLA Modules:
  0.0 280.3 jit_solution(4558437557524644857)
XLA Ops:
  1.3 3.4 %quarters.1 = (bf16[2,104,384]{2,1,0:T(8,128)(2,1)}, bf16[2,192,384]{2,1,0:T(8,128)(2,1)}, bf16[2,2,296,384]{3,2,1,0:T(8,128)(2,1)}) custom-call(s32[4]{0:T(128)} %pad_add_fusion.at, bf16[96,2304]{1,0:T(8,128)(2,1)} %refs_7_.3, bf16[96,768]{1,0:T(8,128)(2,1)} %refs_8_.2, bf16[96,3072]{1,0:T(8,128)(2,1)} %refs_6_.3, bf16[384,768]{1,0:T(8,128)(2,1)} %refs_7_.4, ...), custom_call_target="tpu_custom_call" | custom-call | bytes 6000000 | tf_op jit(solution)/shard_map/quarters/pallas_call | solution.py:198
  4.7 2.9 %collective-permute-start.7 = (bf16[2,2,296,384]{3,2,1,0:T(8,128)(2,1)}, bf16[2,2,296,384]{3,2,1,0:T(8,128)(2,1)S(1)}, u32[]{:S(2)}, u32[]{:S(2)}) collective-permute-start(bf16[2,2,296,384]{3,2,1,0:T(8,128)(2,1)} %get-tuple-element.224), channel_id=1, source_target_pairs={{0,4},{1,5},{2,6},{3,7},{4,0},{5,1},{6,2},{7,3},{8,12},{9,13},{10,... | collective-permute-start | bytes 2727944 | tf_op jit(solution)/shard_map/ppermute | solution.py:135
  7.6 3.6 %collective-permute-start.2 = (bf16[2,104,384]{2,1,0:T(8,128)(2,1)}, bf16[2,104,384]{2,1,0:T(8,128)(2,1)S(1)}, u32[]{:S(2)}, u32[]{:S(2)}) collective-permute-start(bf16[2,104,384]{2,1,0:T(8,128)(2,1)} %get-tuple-element.210), channel_id=1, source_target_pairs={{0,24},{1,25},{2,26},{3,27},{4,28},{5,29},{6,30},{7,31},{8,0},{9,1... | collective-permute-start | bytes 479240 | tf_op jit(solution)/shard_map/ppermute | solution.py:135
  12.2 2.5 collective-permute-start.3
  14.7 8.7 %prepare.1 = (s32[16]{0:T(128)}, bf16[1024,768]{1,0:T(8,128)(2,1)}, bf16[1024,768]{1,0:T(8,128)(2,1)}, f32[1024,128]{1,0:T(8,128)}, f32[1024,128]{1,0:T(8,128)}) custom-call(s32[1,1024]{1,0:T(1,128)} %seg_ref.1, bf16[1024,768]{1,0:T(8,128)(2,1)} %bitcast.42, bf16[1024,768]{1,0:T(8,128)(2,1)} %bitcast.43, f32[1,128]{1,0:T(1,128)} %constant.47.clone.freq_ref), custom_call_target="tpu_custom_call" | custom-call | flops 3300000000 | bytes 8000000 | tf_op jit(solution)/shard_map/prepare/pallas_call | solution.py:301
  23.4 7.6 %collective-permute-done.1 = bf16[2,104,384]{2,1,0:T(8,128)(2,1)S(1)} collective-permute-done((bf16[2,104,384]{2,1,0:T(8,128)(2,1)}, bf16[2,104,384]{2,1,0:T(8,128)(2,1)S(1)}, u32[]{:S(2)}, u32[]{:S(2)}) %collective-permute-start.1) | collective-permute-done | bytes 159776 | tf_op jit(solution)/shard_map/ppermute | solution.py:135
  34.3 5.2 %collective-permute-done.4 = bf16[3,96,384]{2,1,0:T(8,128)(2,1)S(1)} collective-permute-done((bf16[3,96,384]{2,1,0:T(8,128)(2,1)S(1)}, bf16[3,96,384]{2,1,0:T(8,128)(2,1)S(1)}, u32[]{:S(2)}, u32[]{:S(2)}) %collective-permute-start.4) | collective-permute-done | bytes 221216 | tf_op jit(solution)/shard_map/ppermute | solution.py:135
  44.4 2.1 collective-permute-start.10
  48.5 3.2 %unpack.1 = (f32[1,768]{1,0:T(1,128)}, f32[1,768]{1,0:T(1,128)}, f32[1,2304]{1,0:T(1,128)}, f32[1,768]{1,0:T(1,128)}, f32[1,768]{1,0:T(1,128)}, /*index=5*/f32[1...) custom-call(s32[4]{0:T(128)} %pad_add_fusion.at, bf16[4,8,384]{2,1,0:T(8,128)(2,1)} %get-tuple-element.234.near_ref, ...), custom_call_target="tpu_custom_call" | custom-call | flops 100000000 | bytes 100000 | tf_op jit(solution)/shard_map/unpack/pallas_call | solution.py:240
  51.8 7.0 %collective-permute-done.10 = bf16[2,192,384]{2,1,0:T(8,128)(2,1)S(1)} collective-permute-done((bf16[2,192,384]{2,1,0:T(8,128)(2,1)}, bf16[2,192,384]{2,1,0:T(8,128)(2,1)S(1)}, u32[]{:S(2)}, u32[]{:S(2)}) %collective-permute-start.10) | collective-permute-done | bytes 294944 | tf_op jit(solution)/shard_map/ppermute | solution.py:135
  63.3 3.4 %collective-permute-done.13 = bf16[1,192,384]{2,1,0:T(8,128)(2,1)S(1)} collective-permute-done((bf16[1,192,384]{2,1,0:T(8,128)(2,1)S(1)}, bf16[1,192,384]{2,1,0:T(8,128)(2,1)S(1)}, u32[]{:S(2)}, u32[]{:S(2)}) %collective-permute-start.13) | collective-permute-done | bytes 147488 | tf_op jit(solution)/shard_map/ppermute | solution.py:135
  71.3 22.2 %attend.1 = (bf16[1024,2304]{1,0:T(8,128)(2,1)}, bf16[1024,768]{1,0:T(8,128)(2,1)}, f32[16,1024]{1,0:T(8,128)}, f32[1024,768]{1,0:T(8,128)}, bf16[768,2304]{1,0:T(8,128)(2,1)}, /*index=5*/bf16[768,768]{1,0:T(8,128)(2,1)}) custom-call(s32[16]{0:T(128)} %get-tuple-element.273.plan, s32[4]{0:T(128)} %pad_add_fusion.at, ...), custom_call_target="tpu_custom_call" | custom-call | flops 11000000512 | bytes 20000000 | tf_op jit(solution)/shard_map/attend/pallas_call | solution.py:431
  94.2 2.4 collective-permute-done.22.refs_15_
  98.6 42.9 %feed.1 = (bf16[1024,768]{1,0:T(8,128)(2,1)}, f32[1024,768]{1,0:T(8,128)}, bf16[1024,768]{1,0:T(8,128)(2,1)}, f32[1,3072]{1,0:T(1,128)}, f32[8,768]{1,0:T(8,128)...) custom-call(s32[4]{0:T(128)} %pad_add_fusion.at, f32[1024,768]{1,0:T(8,128)} %get-tuple-element.294.refs_0_, ...), custom_call_target="tpu_custom_call" | custom-call | flops 28999999488 | bytes 40000000 | tf_op jit(solution)/shard_map/feed/pallas_call | solution.py:682
  141.7 8.0 %attend_back.2 = (bf16[1024,2304]{1,0:T(8,128)(2,1)}, f32[8,2304]{1,0:T(8,128)}) custom-call(s32[16]{0:T(128)} %get-tuple-element.273.plan, bf16[1024,2304]{1,0:T(8,128)(2,1)} %get-tuple-element.306.qkv_ref, bf16[1024,768]{1,0:T(8,128)(2,1)} %get-tuple-element.307.da_ref.refs_2_, f32[16,1024]{1,0:T(8,128)} %get-tuple-element.308.lse_ref, ...), custom_call_target="tpu_custom_call" | custom-call | flops 4000000000 | bytes 6000000 | tf_op jit(solution)/shard_map/attend_back/pallas_call | solution.py:792
  149.8 4.0 %add_convert_fusion = (bf16[8,192,384]{2,1,0:T(8,128)(2,1)S(1)}, bf16[8,192,384]{2,1,0:T(8,128)(2,1)}) fusion(bf16[32,192,384]{2,1,0:T(8,128)(2,1)} %collective-permute-done.24, bf16[32,192,384]{2,1,0:T(8,128)(2,1)} %get-tuple-element.304), kind=kLoop, calls=%fused_computation.2 | loop fusion | flops 4718592 | bytes 7077888 | tf_op jit(solution)/shard_map/convert_element_type | solution.py:1093
  156.4 17.6 %attend_back.3 = (bf16[1024,2304]{1,0:T(8,128)(2,1)}, f32[8,2304]{1,0:T(8,128)}) custom-call(s32[16]{0:T(128)} %get-tuple-element.273.plan, bf16[1024,2304]{1,0:T(8,128)(2,1)} %get-tuple-element.306.qkv_ref, bf16[1024,768]{1,0:T(8,128)(2,1)} %get-tuple-element.307.da_ref.refs_2_, ...), custom_call_target="tpu_custom_call", output_to_operand_aliasing={{0}: (7, {})} | custom-call | flops 12000000000 | bytes 18000000 | tf_op jit(solution)/shard_map/attend_back/pallas_call | solution.py:792
  173.9 9.9 %project_back.1 = (bf16[1024,768]{1,0:T(8,128)(2,1)}, f32[8,768]{1,0:T(8,128)}) custom-call(bf16[1024,768]{1,0:T(8,128)(2,1)} %get-tuple-element.274.refs_0_.xp_ref, f32[1,768]{1,0:T(1,128)} %get-tuple-element.277.refs_3_.g1_ref.refs_4_, f32[1024,768]{1,0:T(8,128)} %get-tuple-element.315.dx1_ref, bf16[1024,2304]{1,0:T(8,128)(2,1)} %get-tuple-element.331.dqkv_ref.refs_3_, ...), custom_call_target="tpu_custom_call" | custom-call | tf_op jit(solution)/shard_map/project_back/pallas_call | solution.py:834
  184.9 3.6 %convert_add_fusion = (f32[8,192,384]{2,1,0:T(8,128)S(1)}, f32[8,192,384]{2,1,0:T(8,128)S(1)}) fusion(bf16[8,192,384]{2,1,0:T(8,128)(2,1)} %copy-done.6, bf16[32,192,384]{2,1,0:T(8,128)(2,1)} %collective-permute-done.24, bf16[32,192,384]{2,1,0:T(8,128)(2,1)} %get-tuple-element.304, bf16[8,192,384]{2,1,0:T(8,128)(2,1)S(1)} %collective-permute-done.25), kind=kLoop, calls=%fused_computation | loop fusion | flops 5898240 | bytes 11796480 | tf_op jit(solution)/shard_map/add | solution.py:1099
  192.4 12.2 %grads.1 = (bf16[32,104,384]{2,1,0:T(8,128)(2,1)}, bf16[32,104,384]{2,1,0:T(8,128)(2,1)}) custom-call(s32[4]{0:T(128)} %pad_add_fusion.at, bf16[1024,768]{1,0:T(8,128)(2,1)} %get-tuple-element.274.refs_0_.xp_ref, bf16[1024,768]{1,0:T(8,128)(2,1)} %get-tuple-element.330.refs_1_, bf16[1024,768]{1,0:T(8,128)(2,1)} %get-tuple-element.307.da_ref.refs_2_, ...), custom_call_target="tpu_custom_call" | custom-call | flops 5000000000 | bytes 12000000 | tf_op jit(solution)/shard_map/grads/pallas_call | solution.py:975
  206.0 2.4 fusion.9
  214.4 2.1 collective-permute-start.32
  216.5 14.0 %collective-permute-done.32 = bf16[2,192,384]{2,1,0:T(8,128)(2,1)S(1)} collective-permute-done((bf16[2,192,384]{2,1,0:T(8,128)(2,1)S(1)}, bf16[2,192,384]{2,1,0:T(8,128)(2,1)S(1)}, u32[]{:S(2)}, u32[]{:S(2)}) %collective-permute-start.32) | collective-permute-done | bytes 294944 | tf_op jit(solution)/shard_map/ppermute | solution.py:135
  233.3 3.8 %collective-permute-start.36 = (bf16[2,192,384]{2,1,0:T(8,128)(2,1)}, bf16[2,192,384]{2,1,0:T(8,128)(2,1)}, u32[]{:S(2)}, u32[]{:S(2)}) collective-permute-start(bf16[2,192,384]{2,1,0:T(8,128)(2,1)} %pad_maximum_fusion.10), channel_id=1, source_target_pairs={{0,24},{1,25},{2,26},{3,27},{4,28},{5,29},{6,30},{7,31},{8,0},{9,1... | collective-permute-start | bytes 884744 | tf_op jit(solution)/shard_map/ppermute | solution.py:135
  239.1 6.3 %collective-permute-done.35 = bf16[2,192,384]{2,1,0:T(8,128)(2,1)} collective-permute-done((bf16[2,192,384]{2,1,0:T(8,128)(2,1)}, bf16[2,192,384]{2,1,0:T(8,128)(2,1)}, u32[]{:S(2)}, u32[]{:S(2)}) %collective-permute-start.35) | collective-permute-done | bytes 294944 | tf_op jit(solution)/shard_map/ppermute | solution.py:135
  245.4 2.7 collective-permute-done.36
  251.3 1.9 collective-permute-start.37
  254.7 2.0 collective-permute-start.39
  258.2 7.3 %restore.1 = (bf16[1024,768]{1,0:T(8,128)(2,1)}, bf16[1024,768]{1,0:T(8,128)(2,1)}) custom-call(s32[16]{0:T(128)} %get-tuple-element.273.plan, bf16[1024,768]{1,0:T(8,128)(2,1)} %get-tuple-element.371.outp_ref, bf16[1024,768]{1,0:T(8,128)(2,1)} %get-tuple-element.372.dxp_ref), custom_call_target="tpu_custom_call" | custom-call | flops 3300000000 | bytes 8000000 | tf_op jit(solution)/shard_map/restore/pallas_call | solution.py:1008
  266.4 5.9 %collective-permute-done.41 = bf16[2,104,384]{2,1,0:T(8,128)(2,1)S(1)} collective-permute-done((bf16[2,104,384]{2,1,0:T(8,128)(2,1)S(1)}, bf16[2,104,384]{2,1,0:T(8,128)(2,1)S(1)}, u32[]{:S(2)}, u32[]{:S(2)}) %collective-permute-start.41) | collective-permute-done | bytes 159776 | tf_op jit(solution)/shard_map/ppermute | solution.py:135
  273.2 3.4 %deliver_second.1 = (f32[96,3072]{1,0:T(8,128)}, f32[384,768]{1,0:T(8,128)}) custom-call(s32[4]{0:T(128)} %pad_add_fusion.at, bf16[2,2,192,384]{3,2,1,0:T(8,128)(2,1)} %copy-done.2, bf16[2,2,192,384]{3,2,1,0:T(8,128)(2,1)} %copy-done.9), custom_call_target="tpu_custom_call" | custom-call | bytes 4000000 | tf_op jit(solution)/shard_map/deliver_second/pallas_call | solution.py:1072
  277.3 2.8 deliver_first.1
  (179 shorter events, 51.7 us)
Async XLA Ops:
  4.7 35.2 %collective-permute-start.7 = (bf16[2,2,296,384]{3,2,1,0:T(8,128)(2,1)}, bf16[2,2,296,384]{3,2,1,0:T(8,128)(2,1)S(1)}, u32[]{:S(2)}, u32[]{:S(2)}) collective-permute-start(bf16[2,2,296,384]{3,2,1,0:T(8,128)(2,1)} %get-tuple-element.224), channel_id=1, source_target_pairs={{0,4},{1,5},{2,6},{3,7},{4,0},{5,1},{6,2},{7,3},{8,12},{9,13},{10,... | collective-permute-start | bytes 2727944 | tf_op jit(solution)/shard_map/ppermute | solution.py:135
  7.6 15.8 %collective-permute-start.2 = (bf16[2,104,384]{2,1,0:T(8,128)(2,1)}, bf16[2,104,384]{2,1,0:T(8,128)(2,1)S(1)}, u32[]{:S(2)}, u32[]{:S(2)}) collective-permute-start(bf16[2,104,384]{2,1,0:T(8,128)(2,1)} %get-tuple-element.210), channel_id=1, source_target_pairs={{0,24},{1,25},{2,26},{3,27},{4,28},{5,29},{6,30},{7,31},{8,0},{9,1... | collective-permute-start | bytes 479240 | tf_op jit(solution)/shard_map/ppermute | solution.py:135
  11.2 19.8 %collective-permute-start.1 = (bf16[2,104,384]{2,1,0:T(8,128)(2,1)}, bf16[2,104,384]{2,1,0:T(8,128)(2,1)S(1)}, u32[]{:S(2)}, u32[]{:S(2)}) collective-permute-start(bf16[2,104,384]{2,1,0:T(8,128)(2,1)} %get-tuple-element.210), channel_id=1, source_target_pairs={{0,16},{1,17},{2,18},{3,19},{4,20},{5,21},{6,22},{7,23},{8,24},{9,... | collective-permute-start | bytes 479240 | tf_op jit(solution)/shard_map/ppermute | solution.py:135
  11.2 19.8 %collective-permute-start = (bf16[2,104,384]{2,1,0:T(8,128)(2,1)}, bf16[2,104,384]{2,1,0:T(8,128)(2,1)S(1)}, u32[]{:S(2)}, u32[]{:S(2)}) collective-permute-start(bf16[2,104,384]{2,1,0:T(8,128)(2,1)} %get-tuple-element.210), channel_id=1, source_target_pairs={{0,8},{1,9},{2,10},{3,11},{4,12},{5,13},{6,14},{7,15},{8,16},{9,17... | collective-permute-start | bytes 479240 | tf_op jit(solution)/shard_map/ppermute | solution.py:135
  12.2 18.8 %collective-permute-start.3 = (bf16[2,192,384]{2,1,0:T(8,128)(2,1)}, bf16[2,192,384]{2,1,0:T(8,128)(2,1)S(1)}, u32[]{:S(2)}, u32[]{:S(2)}) collective-permute-start(bf16[2,192,384]{2,1,0:T(8,128)(2,1)} %get-tuple-element.244), channel_id=1, source_target_pairs={{0,8},{1,9},{2,10},{3,11},{4,12},{5,13},{6,14},{7,15},{8,16},{9,17... | collective-permute-start | bytes 884744 | tf_op jit(solution)/shard_map/ppermute | solution.py:135
  31.2 8.7 %collective-permute-start.6 = (bf16[2,192,384]{2,1,0:T(8,128)(2,1)}, bf16[2,192,384]{2,1,0:T(8,128)(2,1)S(1)}, u32[]{:S(2)}, u32[]{:S(2)}) collective-permute-start(bf16[2,192,384]{2,1,0:T(8,128)(2,1)} %get-tuple-element.244), channel_id=1, source_target_pairs={{0,24},{1,25},{2,26},{3,27},{4,28},{5,29},{6,30},{7,31},{8,0},{9,1... | collective-permute-start | bytes 884744 | tf_op jit(solution)/shard_map/ppermute | solution.py:135
  41.8 17.8 %collective-permute-start.8 = (bf16[2,3,96,384]{3,2,1,0:T(8,128)(2,1)S(1)}, bf16[2,3,96,384]{3,2,1,0:T(8,128)(2,1)S(1)}, u32[]{:S(2)}, u32[]{:S(2)}) collective-permute-start(bf16[2,3,96,384]{3,2,1,0:T(8,128)(2,1)S(1)} %get-tuple-element.285.refs_11_), channel_id=1, source_target_pairs={{0,4},{1,5},{2,6},{3,7},{4,0},{5,1},{6,2},{7,3},{8,12},{9,13},{10,... | collective-permute-start | bytes 1327112 | tf_op jit(solution)/shard_map/ppermute | solution.py:135
  42.9 16.7 %collective-permute-start.9 = (bf16[2,3,96,384]{3,2,1,0:T(8,128)(2,1)S(1)}, bf16[2,3,96,384]{3,2,1,0:T(8,128)(2,1)S(1)}, u32[]{:S(2)}, u32[]{:S(2)}) collective-permute-start(bf16[2,3,96,384]{3,2,1,0:T(8,128)(2,1)S(1)} %get-tuple-element.287.refs_13_), channel_id=1, source_target_pairs={{0,2},{1,3},{2,0},{3,1},{4,6},{5,7},{6,4},{7,5},{8,10},{9,11},{10,... | collective-permute-start | bytes 1327112 | tf_op jit(solution)/shard_map/ppermute | solution.py:135
  44.4 14.3 %collective-permute-start.10 = (bf16[2,192,384]{2,1,0:T(8,128)(2,1)}, bf16[2,192,384]{2,1,0:T(8,128)(2,1)S(1)}, u32[]{:S(2)}, u32[]{:S(2)}) collective-permute-start(bf16[2,192,384]{2,1,0:T(8,128)(2,1)} %get-tuple-element.244), channel_id=1, source_target_pairs={{0,16},{1,17},{2,18},{3,19},{4,20},{5,21},{6,22},{7,23},{8,24},{9,... | collective-permute-start | bytes 884744 | tf_op jit(solution)/shard_map/ppermute | solution.py:135
  46.6 13.0 %collective-permute-start.11 = (bf16[2,192,384]{2,1,0:T(8,128)(2,1)S(1)}, bf16[2,192,384]{2,1,0:T(8,128)(2,1)S(1)}, u32[]{:S(2)}, u32[]{:S(2)}) collective-permute-start(bf16[2,192,384]{2,1,0:T(8,128)(2,1)S(1)} %get-tuple-element.231), channel_id=1, source_target_pairs={{0,2},{1,3},{2,0},{3,1},{4,6},{5,7},{6,4},{7,5},{8,10},{9,11},{10,... | collective-permute-start | bytes 884744 | tf_op jit(solution)/shard_map/ppermute | solution.py:135
  47.1 12.5 %collective-permute-start.12 = (bf16[2,192,384]{2,1,0:T(8,128)(2,1)S(1)}, bf16[2,192,384]{2,1,0:T(8,128)(2,1)S(1)}, u32[]{:S(2)}, u32[]{:S(2)}) collective-permute-start(bf16[2,192,384]{2,1,0:T(8,128)(2,1)S(1)} %get-tuple-element.245), channel_id=1, source_target_pairs={{0,4},{1,5},{2,6},{3,7},{4,0},{5,1},{6,2},{7,3},{8,12},{9,13},{10,... | collective-permute-start | bytes 884744 | tf_op jit(solution)/shard_map/ppermute | solution.py:135
  59.8 8.2 %collective-permute-start.15 = (bf16[2,2,3,96,384]{4,3,2,1,0:T(8,128)(2,1)S(1)}, bf16[2,2,3,96,384]{4,3,2,1,0:T(8,128)(2,1)S(1)}, u32[]{:S(2)}, u32[]{:S(2)}) collective-permute-start(bf16[2,2,3,96,384]{4,3,2,1,0:T(8,128)(2,1)S(1)} %pad_maximum_fusion.1), channel_id=1, source_target_pairs={{0,1},{1,0},{2,3},{3,2},{4,5},{5,4},{6,7},{7,6},{8,9},{9,8},{10,11... | collective-permute-start | bytes 2654216 | tf_op jit(solution)/shard_map/ppermute | solution.py:135
  69.5 24.0 %collective-permute-start.20 = (bf16[2,3,192,384]{3,2,1,0:T(8,128)(2,1)S(1)}, bf16[2,3,192,384]{3,2,1,0:T(8,128)(2,1)S(1)}, u32[]{:S(2)}, u32[]{:S(2)}) collective-permute-start(bf16[2,3,192,384]{3,2,1,0:T(8,128)(2,1)S(1)} %pad_maximum_fusion.2.refs_10_), channel_id=1, source_target_pairs={{0,1},{1,0},{2,3},{3,2},{4,5},{5,4},{6,7},{7,6},{8,9},{9,8},{10,11... | collective-permute-start | bytes 2654216 | tf_op jit(solution)/shard_map/ppermute | solution.py:135
  69.6 24.0 %collective-permute-start.18 = (bf16[2,3,192,384]{3,2,1,0:T(8,128)(2,1)S(1)}, bf16[2,3,192,384]{3,2,1,0:T(8,128)(2,1)S(1)}, u32[]{:S(2)}, u32[]{:S(2)}) collective-permute-start(bf16[2,3,192,384]{3,2,1,0:T(8,128)(2,1)S(1)} %pad_maximum_fusion.2.refs_10_), channel_id=1, source_target_pairs={{0,4},{1,5},{2,6},{3,7},{4,0},{5,1},{6,2},{7,3},{8,12},{9,13},{10,... | collective-permute-start | bytes 2654216 | tf_op jit(solution)/shard_map/ppermute | solution.py:135
  70.7 22.9 %collective-permute-start.21 = (bf16[2,3,192,384]{3,2,1,0:T(8,128)(2,1)S(1)}, bf16[2,3,192,384]{3,2,1,0:T(8,128)(2,1)}, u32[]{:S(2)}, u32[]{:S(2)}) collective-permute-start(bf16[2,3,192,384]{3,2,1,0:T(8,128)(2,1)S(1)} %pad_maximum_fusion.3.refs_12_), channel_id=1, source_target_pairs={{0,1},{1,0},{2,3},{3,2},{4,5},{5,4},{6,7},{7,6},{8,9},{9,8},{10,11... | collective-permute-start | bytes 2654216 | tf_op jit(solution)/shard_map/ppermute | solution.py:135
  70.8 22.8 %collective-permute-start.19 = (bf16[2,3,192,384]{3,2,1,0:T(8,128)(2,1)S(1)}, bf16[2,3,192,384]{3,2,1,0:T(8,128)(2,1)}, u32[]{:S(2)}, u32[]{:S(2)}) collective-permute-start(bf16[2,3,192,384]{3,2,1,0:T(8,128)(2,1)S(1)} %pad_maximum_fusion.3.refs_12_), channel_id=1, source_target_pairs={{0,2},{1,3},{2,0},{3,1},{4,6},{5,7},{6,4},{7,5},{8,10},{9,11},{10,... | collective-permute-start | bytes 2654216 | tf_op jit(solution)/shard_map/ppermute | solution.py:135
  141.5 8.3 %collective-permute-start.24 = (bf16[32,192,384]{2,1,0:T(8,128)(2,1)}, bf16[32,192,384]{2,1,0:T(8,128)(2,1)}, u32[]{:S(2)}, u32[]{:S(2)}) collective-permute-start(bf16[32,192,384]{2,1,0:T(8,128)(2,1)} %get-tuple-element.305), channel_id=1, source_target_pairs={{0,1},{1,0},{2,3},{3,2},{4,5},{5,4},{6,7},{7,6},{8,9},{9,8},{10,11... | collective-permute-start | bytes 14155784 | tf_op jit(solution)/shard_map/ppermute | solution.py:135
  153.8 30.0 %collective-permute-start.25 = (bf16[8,192,384]{2,1,0:T(8,128)(2,1)}, bf16[8,192,384]{2,1,0:T(8,128)(2,1)S(1)}, u32[]{:S(2)}, u32[]{:S(2)}) collective-permute-start(bf16[8,192,384]{2,1,0:T(8,128)(2,1)} %get-tuple-element.313), channel_id=1, source_target_pairs={{0,4},{1,5},{2,6},{3,7},{4,0},{5,1},{6,2},{7,3},{8,12},{9,13},{10,... | collective-permute-start | bytes 3538952 | tf_op jit(solution)/shard_map/ppermute | solution.py:135
  154.9 29.0 %collective-permute-start.26 = (bf16[8,192,384]{2,1,0:T(8,128)(2,1)S(1)}, bf16[8,192,384]{2,1,0:T(8,128)(2,1)S(1)}, u32[]{:S(2)}, u32[]{:S(2)}) collective-permute-start(bf16[8,192,384]{2,1,0:T(8,128)(2,1)S(1)} %get-tuple-element.314), channel_id=1, source_target_pairs={{0,2},{1,3},{2,0},{3,1},{4,6},{5,7},{6,4},{7,5},{8,10},{9,11},{10,... | collective-permute-start | bytes 3538952 | tf_op jit(solution)/shard_map/ppermute | solution.py:135
  190.9 15.1 %collective-permute-start.27 = (bf16[4,192,384]{2,1,0:T(8,128)(2,1)}, bf16[4,192,384]{2,1,0:T(8,128)(2,1)S(1)}, u32[]{:S(2)}, u32[]{:S(2)}) collective-permute-start(bf16[4,192,384]{2,1,0:T(8,128)(2,1)} %slice.334), channel_id=1, source_target_pairs={{0,2},{1,3},{2,0},{3,1},{4,6},{5,7},{6,4},{7,5},{8,10},{9,11},{10,... | collective-permute-start | bytes 1769480 | tf_op jit(solution)/shard_map/ppermute | solution.py:135
  191.4 14.6 %collective-permute-start.28 = (bf16[4,192,384]{2,1,0:T(8,128)(2,1)S(1)}, bf16[4,192,384]{2,1,0:T(8,128)(2,1)S(1)}, u32[]{:S(2)}, u32[]{:S(2)}) collective-permute-start(bf16[4,192,384]{2,1,0:T(8,128)(2,1)S(1)} %slice.333), channel_id=1, source_target_pairs={{0,4},{1,5},{2,6},{3,7},{4,0},{5,1},{6,2},{7,3},{8,12},{9,13},{10,... | collective-permute-start | bytes 1769480 | tf_op jit(solution)/shard_map/ppermute | solution.py:135
  211.8 18.7 %collective-permute-start.30 = (bf16[8,104,384]{2,1,0:T(8,128)(2,1)S(1)}, bf16[8,104,384]{2,1,0:T(8,128)(2,1)S(1)}, u32[]{:S(2)}, u32[]{:S(2)}) collective-permute-start(bf16[8,104,384]{2,1,0:T(8,128)(2,1)S(1)} %get-tuple-element.347), channel_id=1, source_target_pairs={{0,4},{1,5},{2,6},{3,7},{4,0},{5,1},{6,2},{7,3},{8,12},{9,13},{10,... | collective-permute-start | bytes 1916936 | tf_op jit(solution)/shard_map/ppermute | solution.py:135
  212.9 18.3 %collective-permute-start.31 = (bf16[8,104,384]{2,1,0:T(8,128)(2,1)S(1)}, bf16[8,104,384]{2,1,0:T(8,128)(2,1)S(1)}, u32[]{:S(2)}, u32[]{:S(2)}) collective-permute-start(bf16[8,104,384]{2,1,0:T(8,128)(2,1)S(1)} %get-tuple-element.348), channel_id=1, source_target_pairs={{0,2},{1,3},{2,0},{3,1},{4,6},{5,7},{6,4},{7,5},{8,10},{9,11},{10,... | collective-permute-start | bytes 1916936 | tf_op jit(solution)/shard_map/ppermute | solution.py:135
  214.4 16.1 %collective-permute-start.32 = (bf16[2,192,384]{2,1,0:T(8,128)(2,1)S(1)}, bf16[2,192,384]{2,1,0:T(8,128)(2,1)S(1)}, u32[]{:S(2)}, u32[]{:S(2)}) collective-permute-start(bf16[2,192,384]{2,1,0:T(8,128)(2,1)S(1)} %pad_maximum_fusion.9), channel_id=1, source_target_pairs={{0,16},{1,17},{2,18},{3,19},{4,20},{5,21},{6,22},{7,23},{8,24},{9,... | collective-permute-start | bytes 884744 | tf_op jit(solution)/shard_map/ppermute | solution.py:135
  231.7 16.4 %collective-permute-start.33 = (bf16[4,104,384]{2,1,0:T(8,128)(2,1)S(1)}, bf16[4,104,384]{2,1,0:T(8,128)(2,1)}, u32[]{:S(2)}, u32[]{:S(2)}) collective-permute-start(bf16[4,104,384]{2,1,0:T(8,128)(2,1)S(1)} %slice.336), channel_id=1, source_target_pairs={{0,2},{1,3},{2,0},{3,1},{4,6},{5,7},{6,4},{7,5},{8,10},{9,11},{10,... | collective-permute-start | bytes 958472 | tf_op jit(solution)/shard_map/ppermute | solution.py:135
  232.3 15.8 %collective-permute-start.34 = (bf16[4,104,384]{2,1,0:T(8,128)(2,1)S(1)}, bf16[4,104,384]{2,1,0:T(8,128)(2,1)S(1)}, u32[]{:S(2)}, u32[]{:S(2)}) collective-permute-start(bf16[4,104,384]{2,1,0:T(8,128)(2,1)S(1)} %slice.335), channel_id=1, source_target_pairs={{0,4},{1,5},{2,6},{3,7},{4,0},{5,1},{6,2},{7,3},{8,12},{9,13},{10,... | collective-permute-start | bytes 958472 | tf_op jit(solution)/shard_map/ppermute | solution.py:135
  233.3 12.1 %collective-permute-start.35 = (bf16[2,192,384]{2,1,0:T(8,128)(2,1)}, bf16[2,192,384]{2,1,0:T(8,128)(2,1)}, u32[]{:S(2)}, u32[]{:S(2)}) collective-permute-start(bf16[2,192,384]{2,1,0:T(8,128)(2,1)} %pad_maximum_fusion.8), channel_id=1, source_target_pairs={{0,8},{1,9},{2,10},{3,11},{4,12},{5,13},{6,14},{7,15},{8,16},{9,17... | collective-permute-start | bytes 884744 | tf_op jit(solution)/shard_map/ppermute | solution.py:135
  233.3 14.8 %collective-permute-start.36 = (bf16[2,192,384]{2,1,0:T(8,128)(2,1)}, bf16[2,192,384]{2,1,0:T(8,128)(2,1)}, u32[]{:S(2)}, u32[]{:S(2)}) collective-permute-start(bf16[2,192,384]{2,1,0:T(8,128)(2,1)} %pad_maximum_fusion.10), channel_id=1, source_target_pairs={{0,24},{1,25},{2,26},{3,27},{4,28},{5,29},{6,30},{7,31},{8,0},{9,1... | collective-permute-start | bytes 884744 | tf_op jit(solution)/shard_map/ppermute | solution.py:135
  251.3 14.2 %collective-permute-start.37 = (bf16[2,104,384]{2,1,0:T(8,128)(2,1)S(1)}, bf16[2,104,384]{2,1,0:T(8,128)(2,1)S(1)}, u32[]{:S(2)}, u32[]{:S(2)}) collective-permute-start(bf16[2,104,384]{2,1,0:T(8,128)(2,1)S(1)} %pad_maximum_fusion.13), channel_id=1, source_target_pairs={{0,8},{1,9},{2,10},{3,11},{4,12},{5,13},{6,14},{7,15},{8,16},{9,17... | collective-permute-start | bytes 479240 | tf_op jit(solution)/shard_map/ppermute | solution.py:135
  253.3 12.2 %collective-permute-start.38 = (bf16[2,104,384]{2,1,0:T(8,128)(2,1)S(1)}, bf16[2,104,384]{2,1,0:T(8,128)(2,1)S(1)}, u32[]{:S(2)}, u32[]{:S(2)}) collective-permute-start(bf16[2,104,384]{2,1,0:T(8,128)(2,1)S(1)} %pad_maximum_fusion.14), channel_id=1, source_target_pairs={{0,16},{1,17},{2,18},{3,19},{4,20},{5,21},{6,22},{7,23},{8,24},{9,... | collective-permute-start | bytes 479240 | tf_op jit(solution)/shard_map/ppermute | solution.py:135
  254.7 10.8 %collective-permute-start.39 = (bf16[2,104,384]{2,1,0:T(8,128)(2,1)S(1)}, bf16[2,104,384]{2,1,0:T(8,128)(2,1)S(1)}, u32[]{:S(2)}, u32[]{:S(2)}) collective-permute-start(bf16[2,104,384]{2,1,0:T(8,128)(2,1)S(1)} %pad_maximum_fusion.15), channel_id=1, source_target_pairs={{0,24},{1,25},{2,26},{3,27},{4,28},{5,29},{6,30},{7,31},{8,0},{9,1... | collective-permute-start | bytes 479240 | tf_op jit(solution)/shard_map/ppermute | solution.py:135
  256.7 8.8 %collective-permute-start.40 = (bf16[2,192,384]{2,1,0:T(8,128)(2,1)S(1)}, bf16[2,192,384]{2,1,0:T(8,128)(2,1)S(1)}, u32[]{:S(2)}, u32[]{:S(2)}) collective-permute-start(bf16[2,192,384]{2,1,0:T(8,128)(2,1)S(1)} %fusion.2), channel_id=1, source_target_pairs={{0,2},{1,3},{2,0},{3,1},{4,6},{5,7},{6,4},{7,5},{8,10},{9,11},{10,... | collective-permute-start | bytes 884744 | tf_op jit(solution)/shard_map/ppermute | solution.py:135
  (36 other events, 192.1 us)

commit v4 on v3

--- a/solution.py
+++ b/solution.py
@@ -18,8 +18,6 @@
 F32 = jnp.float32
 BF16 = jnp.bfloat16
 MIB = 1 << 20
-UNROLL_F = 6
-UNROLL_B = 2
 
 
 def nn(left, right):
@@ -87,6 +85,14 @@
 def head_masks(rows):
     lane = iota((rows, LANES), 1)
     return [(lane < HEAD_DIM), (lane >= HEAD_DIM)]
+
+
+def both(masks, value):
+    return jnp.concatenate([keep(mask, value) for mask in masks], 0)
+
+
+def beside(value):
+    return jnp.concatenate([value[0], value[1]], 1)
 
 
 def allowed_pairs(plan, gene, span):
@@ -362,29 +368,58 @@
     (qkv_ref, o_ref, lse_ref, x1_ref), refs = refs[:4], refs[4:]
     if pieces:
         whole, refs = refs[:2], refs[2:]
-    wqkv_ref, wout_ref, mask_ref, sem = refs
-    gene = pl.program_id(0)
-    span, width = xp_ref.shape
+    wqkv_ref, wout_ref, mask_ref, a1_ref, sem = refs
+    step = pl.program_id(0)
+    gene = jnp.maximum(step - 1, 0)
+    span = cos_ref.shape[0]
+    width = xp_ref.shape[1]
 
     def wait_both():
         pltpu.make_async_copy(wqkv_ref, wqkv_ref, sem.at[0]).wait()
         pltpu.make_async_copy(wout_ref, wout_ref, sem.at[1]).wait()
 
-    @pl.when(gene == 0)
+    @pl.when(step == 0)
     def _():
         if pieces:
             load_matrices(at, source, wqkv_ref, wout_ref, sem)
         else:
             pltpu.make_async_copy(source[0], wqkv_ref, sem.at[0]).start()
             pltpu.make_async_copy(source[1], wout_ref, sem.at[1]).start()
+
+        def norm(i, carry):
+            here = pl.ds(i * span, span)
+            xhat, _ = normalize(xp_ref[here, :].astype(F32))
+            a1_ref[here, :] = (xhat * g1_ref[...] + b1_ref[...]).astype(BF16)
+            return carry
+
+        lax.fori_loop(0, GENES, norm, 0)
         wait_both()
         if pieces:
             pltpu.make_async_copy(wqkv_ref, whole[0], sem.at[0]).start()
             pltpu.make_async_copy(wout_ref, whole[1], sem.at[1]).start()
 
-    x = xp_ref[...].astype(F32)
-    xhat, _ = normalize(x)
-    a1 = (xhat * g1_ref[...] + b1_ref[...]).astype(BF16)
+    @pl.when(step > 0)
+    def _():
+        attend_gene(
+            plan, gene, xp_ref, a1_ref, cos_ref, sin_ref, bqkv_ref, bout_ref, wqkv_ref, wout_ref, mask_ref,
+            qkv_ref, o_ref, lse_ref, x1_ref,
+        )
+
+    if pieces:
+
+        @pl.when(step == pl.num_programs(0) - 1)
+        def _():
+            wait_both()
+
+
+def attend_gene(
+    plan, gene, xp_ref, a1_ref, cos_ref, sin_ref, bqkv_ref, bout_ref, wqkv_ref, wout_ref, mask_ref,
+    qkv_ref, o_ref, lse_ref, x1_ref,
+):
+    span, width = o_ref.shape
+    here = pl.ds(gene * span, span)
+    x = xp_ref[here, :].astype(F32)
+    a1 = a1_ref[here, :]
     cos, sin = cos_ref[...], sin_ref[...]
     for part in range(3):
         base = part * width
@@ -401,40 +436,35 @@
         q = qkv_ref[:, part(0)]
         k = qkv_ref[:, part(1)] * BF16(1.0 / math.sqrt(HEAD_DIM))
         v = qkv_ref[:, part(2)]
-        o = jnp.zeros((span, LANES), F32)
+        s = nt(both(masks, k), q).reshape(2, span, span)
+        s = jnp.where((mask_ref[...] > 0.5)[None], s, NEG_FILL)
+        peak = jnp.max(s, 1, keepdims=True)
+        e = jnp.exp(s - peak)
+        total = jnp.sum(e, 1, keepdims=True)
+        weights = (e * (1.0 / total)).astype(BF16).reshape(2 * span, span)
+        lse = peak + jnp.log(total)
         for h in range(2):
-            s = nt(keep(masks[h], k), q)
-            s = jnp.where(mask_ref[...] > 0.5, s, NEG_FILL)
-            peak = jnp.max(s, 0, keepdims=True)
-            e = jnp.exp(s - peak)
-            total = jnp.sum(e, 0, keepdims=True)
-            weights = (e * (1.0 / total)).astype(BF16)
-            o = o + tn(weights, keep(masks[h], v))
-            lse_ref[pl.ds(2 * p + h, 1), :] = peak + jnp.log(total)
-        o_ref[:, part(0)] = o.astype(BF16)
+            lse_ref[pl.ds(2 * p + h, 1), :] = lse[h]
+        o_ref[:, part(0)] = tn(weights, both(masks, v)).astype(BF16)
         return carry
 
-    lax.fori_loop(0, width // LANES, pair, 0, unroll=UNROLL_F)
+    lax.fori_loop(0, width // LANES, pair, 0, unroll=True)
     x1_ref[...] = x + nn(o_ref[...], wout_ref[...]) + bout_ref[...]
-    if pieces:
-
-        @pl.when(gene == pl.num_programs(0) - 1)
-        def _():
-            wait_both()
 
 
 def attend(plan, at, xp, cos, sin, g1, b1, bqkv, bout, source):
     length, width = xp.shape
     span = length // GENES
     pieces = len(source) == 12
+    behind = lambda shape: pl.BlockSpec(shape, lambda g, *ids: (jnp.maximum(g - 1, 0), 0))
     weights = [shape_of((width, 3 * width), BF16), shape_of((width, width), BF16)]
     got = call(
         functools.partial(attend_kernel, pieces=pieces),
-        (GENES,),
+        (GENES + 1,),
         [
-            rows_of((span, width)),
-            rows_of((span, LANES)),
-            rows_of((span, LANES)),
+            full((length, width)),
+            behind((span, LANES)),
+            behind((span, LANES)),
             full((1, width)),
             full((1, width)),
             full((1, 3 * width)),
@@ -442,10 +472,10 @@
         ]
         + [ANY] * len(source),
         [
-            rows_of((span, 3 * width)),
-            rows_of((span, width)),
-            pl.BlockSpec((16, span), lambda g, *ids: (0, g)),
-            rows_of((span, width)),
+            behind((span, 3 * width)),
+            behind((span, width)),
+            pl.BlockSpec((16, span), lambda g, *ids: (0, jnp.maximum(g - 1, 0))),
+            behind((span, width)),
         ]
         + [ANY] * (2 if pieces else 0),
         [
@@ -459,6 +489,7 @@
             pltpu.VMEM((width, 3 * width), BF16),
             pltpu.VMEM((width, width), BF16),
             pltpu.VMEM((span, span), F32),
+            pltpu.VMEM((length, width), BF16),
             pltpu.SemaphoreType.DMA((2,)),
         ],
         prefetch=2,
@@ -733,7 +764,7 @@
 
 
 def attend_back_kernel(
-    plan, qkv_ref, da_ref, lse_ref, cos_ref, sin_ref, wout_ref, *refs, base,
+    plan, qkv_ref, da_ref, lse_ref, cos_ref, sin_ref, wout_ref, *refs, base, count,
 ):
     dqkv_ref, bias_ref, dout_ref, mask_ref = refs[-4:]
     gene = pl.program_id(0) + base
@@ -753,26 +784,23 @@
         k = qkv_ref[:, part(1)] * BF16(score_scale)
         v = qkv_ref[:, part(2)]
         dout = dout_ref[:, part(0)]
-        dq = jnp.zeros((span, LANES), F32)
-        dk = jnp.zeros((span, LANES), F32)
-        dv = jnp.zeros((span, LANES), F32)
-        for h in range(2):
-            kh = keep(masks[h], k)
-            s = nt(kh, q)
-            s = jnp.where(mask_ref[...] > 0.5, s, NEG_FILL)
-            weights = jnp.exp(s - lse_ref[pl.ds(2 * p + h, 1), :])
-            dw = nt(keep(masks[h], v), dout)
-            dot = jnp.sum(weights * dw, 0, keepdims=True)
-            ds = (weights * (dw - dot)).astype(BF16)
-            dv = dv + nn(weights.astype(BF16), keep(masks[h], dout))
-            dk = dk + nn(ds, keep(masks[h], q))
-            dq = dq + tn(ds, kh)
+        kh = both(masks, k)
+        s = nt(kh, q).reshape(2, span, span)
+        s = jnp.where((mask_ref[...] > 0.5)[None], s, NEG_FILL)
+        weights = jnp.exp(s - stack(lse_ref[pl.ds(2 * p + h, 1), :] for h in range(2)))
+        dw = nt(both(masks, v), dout).reshape(2, span, span)
+        dot = jnp.sum(weights * dw, 1, keepdims=True)
+        ds = (weights * (dw - dot)).astype(BF16)
+        weights = weights.astype(BF16)
+        dv = nn(beside(weights), both(masks, dout))
+        dk = nn(beside(ds), both(masks, q))
+        dq = tn(ds.reshape(2 * span, span), kh)
         dqkv_ref[:, part(0)] = back(dq)
         dqkv_ref[:, part(1)] = back(dk * score_scale)
         dqkv_ref[:, part(2)] = dv.astype(BF16)
         return carry
 
-    lax.fori_loop(0, width // LANES, pair, 0, unroll=UNROLL_B)
+    lax.fori_loop(0, width // LANES, pair, 0, unroll=2 if count == 1 else True)
 
     bqkv = jnp.sum(dqkv_ref[...].astype(F32), 0, keepdims=True)
 
@@ -790,7 +818,7 @@
     span = length // GENES
     rows = lambda shape: pl.BlockSpec(shape, lambda g, *ids: (g + base, 0))
     return call(
-        functools.partial(attend_back_kernel, base=base),
+        functools.partial(attend_back_kernel, base=base, count=count),
         (count,),
         [
             rows((span, 3 * width)),
@@ -1042,7 +1070,7 @@
     return call(
         deliver_first_kernel,
         (1,),
-        [full(mine.shape)] * 2,
+        [pl.BlockSpec(memory_space=pltpu.VMEM)] * 2,
         [full(s) for s in shapes],
         [shape_of(s, F32) for s in shapes],
         [pltpu.VMEM((8, PACKED), F32)],
@@ -1072,7 +1100,7 @@
     return call(
         deliver_second_kernel,
         (1,),
-        [full(mine.shape)] * 2,
+        [pl.BlockSpec(memory_space=pltpu.VMEM)] * 2,
         [full(s) for s in shapes],
         [shape_of(s, F32) for s in shapes],
         name="deliver_second",
@@ -1125,21 +1153,24 @@
     def __init__(self, kept, got):
         self.kept, self.got = kept, got
 
-    def near(self, start, stop):
-        return add(self.kept[start:stop], self.got[start:stop])
-
     def plane_one(self):
-        return low(self.near(8, 16)), low(self.near(24, 32))
+        return self.part(8, 16), self.part(24, 32)
+
+    def part(self, start, stop, *more):
+        return low(add(self.kept[start:stop], self.got[start:stop], *more))
 
     def plane_two(self, by_x, by_y):
-        self.first = add(self.near(0, 8), by_x)
-        self.second = add(self.near(16, 24), by_y)
-        return low(self.first[Z_SIZE:]), low(self.second[Z_SIZE:])
+        self.by_x, self.by_y = by_x, by_y
+        return self.part(4, 8, by_x[Z_SIZE:]), self.part(20, 24, by_y[Z_SIZE:])
 
     def along_z(self, by_y, by_x):
-        first, second = add(self.first[:Z_SIZE], by_y), add(self.second[:Z_SIZE], by_x)
-        self.own = stack([first[0], second[0]])
-        return [low(stack([first[d], second[d]])) for d in range(1, Z_SIZE)]
+        def at_z(d, rounded):
+            first = add(self.kept[d], self.got[d], self.by_x[d], by_y[d])
+            second = add(self.kept[16 + d], self.got[16 + d], self.by_y[d], by_x[d])
+            return low(stack([first, second])) if rounded else stack([first, second])
+
+        self.own = at_z(0, False)
+        return [at_z(d, True) for d in range(1, Z_SIZE)]
 
     def total(self, by_z):
         return low(add(self.own, *by_z))
@@ -1175,31 +1206,32 @@
         z2_three = move(near2, ALONG_Z[3])
         first_y, second_x, z2_three, near2, far_side = tie((first_y, second_x, z2_three, near2, far_side))
 
-        first1, second1 = stack([first1, first_y]), stack([second1, second_x])[:, :, :count]
+        near1 = stack([stack([first1, first_y]), stack([second1, second_x])[:, :, :count]])
         far_rows = jnp.concatenate([far_side[0, :1, 3 * count :], second_x[:, count:]])
         early = [stack(q[h] for q in (z2_one, z2_three)) for h in range(2)]
-        first1, second1, rows, far_rows, near2, early = tie((first1, second1, rows, far_rows, near2, early))
-        far_first1, far_second1 = over_x(first1), over_y(second1)
+        unit = lambda v: v.reshape(-1, count // 2, COLUMNS)
+        to_x, to_y = (jnp.concatenate([unit(near1[h]), unit(early[1 - h])]) for h in range(2))
+        near1, to_x, to_y, rows, far_rows, near2, far_side, early = tie(
+            (near1, to_x, to_y, rows, far_rows, near2, far_side, early)
+        )
+        by_x, by_y = over_x(to_x), over_y(to_y)
+        near_core1, core_side = over_core(near1), over_core(far_side)
         z2_two = move(near2, ALONG_Z[2])
-        early_far = [over_y(early[0]), over_x(early[1])]
         params = unpack(at, rows, far_rows, sizes)
-        far_first1, far_second1, params, z2_two, early_far, far_side = tie(
-            (far_first1, far_second1, params, z2_two, early_far, far_side)
+        by_x, by_y, near_core1, core_side, params, z2_two = tie(
+            (by_x, by_y, near_core1, core_side, params, z2_two)
         )
 
         late = [z2_two[h : h + 1] for h in range(2)]
-        near_core1 = stack([first1, second1])
-        far_first1, far_second1, near_core1, late = tie((far_first1, far_second1, near_core1, late))
-        far_core1 = over_core(stack([far_first1, far_second1]))
-        near_core1 = over_core(near_core1)
+        units = unit(near1[0]).shape[0]
+        far1 = stack([v[:units].reshape(near1.shape[1:]) for v in (by_x, by_y)])
+        far1, late = tie((far1, late))
+        far_core1 = over_core(far1)
         late_far = [over_y(late[0]), over_x(late[1])]
-        core_side = over_core(far_side)
-        late_far, far_core1, near_core1, core_side = tie((late_far, far_core1, near_core1, core_side))
-
-        attention = (
-            w_qkv, w_out, far_side, core_side, first1, far_first1, second1, far_second1,
-            near_core1, far_core1, near_core1, far_core1,
-        )
+        late_far, far_core1 = tie((late_far, far_core1))
+
+        attention = (w_qkv, w_out, far_side, core_side) + (near1, far1) * 2 + (near_core1, far_core1) * 2
+        early_far = [v[units:].reshape(early[0].shape) for v in (by_y, by_x)]
         order = lambda e, l: jnp.concatenate([e[:1], l, e[1:]])
         first2, second2 = (
             stack([order(early[h], late[h]), order(early_far[h], late_far[h])]) for h in range(2)
@@ -1266,11 +1298,10 @@
         final2 = settle(at[2], total2, by_y)
         total1, final2 = tie((total1, final2))
         by_y, other2 = over_y(total1), over_core(final2)
-        by_y, other2 = tie((by_y, other2))
+        wup, wdown = deliver_second(at, final2, other2)
+        by_y, wup, wdown = tie((by_y, wup, wdown))
         final1 = settle(at[2], total1, by_y)
         other1 = over_core(final1)
-        wup, wdown = deliver_second(at, final2, other2)
-        other1, wup, wdown = tie((other1, wup, wdown))
         wqkv, wout, *small = deliver_first(at, final1, other1, sizes)
     else:
         parts1 = grads(at, xp, g1, b1, o, da, dqkv, ())

time: 281 us -> 276 us (0.982)
  local copies, waits for them, and re-layouts: 12.7 us -> 6.4 us
  waiting for transfers between devices: 59.6 us -> 65.6 us
  Pallas kernels: 142 us -> 137 us
  starting transfers between devices: 46.5 us -> 43.2 us
    ppermute x44 -> x42, waiting for transfers between devices: 59.6 us -> 65.6 us  [move(): return lax.ppermute(array, AXES, table)]
    another operation x4 -> x0, other arithmetic: 4.72 us -> none
    pallas_call x5, Pallas kernels: 54 us -> 49.5 us  [the longest x2 23.7 us: attend_back(): call(functools.partial(attend_back_kernel, base=base, count=count), (coun...]
    unnamed x48 -> x46, local copies, waits for them, and re-layouts: 8.52 us -> 4.64 us
    convert_element_type x4 -> x6, other arithmetic: 5.64 us -> 9.02 us  [low(): return value.astype(BF16)]
    ppermute x44 -> x42, starting transfers between devices: 46.5 us -> 43.2 us  [move(): return lax.ppermute(array, AXES, table)]
    slice x12 -> x2, local copies, waits for them, and re-layouts: 3.16 us -> 0.09 us  [body(): far1 = stack([v[:units].reshape(near1.shape[1:]) for v in (by_x, by_y)])]
    add x2 -> x4, other arithmetic: 3.96 us -> 6.35 us  [add(): total = total + v.astype(F32)]
  transfers between devices with their start and end apart: 44 -> 42, of which waited for: 15 -> 24; matrix products, arithmetic and copies ran while one was open for 3% -> 2% of each run, Pallas kernels for 33% -> 32%
where the time goes in v4:
time: 276 us; the launch traced here: 274 us
  Pallas kernels  137 us (50%)
  waiting for transfers between devices  65.6 us (24%)
  starting transfers between devices  43.2 us (16%)
  other arithmetic  20.5 us (7%)
  local copies, waits for them, and re-layouts  6.4 us (2%)
    ppermute x42, waiting for transfers between devices, move(): return lax.ppermute(array, AXES, table)  65.6 us
    ppermute x42, starting transfers between devices, move(): return lax.ppermute(array, AXES, table)  43.2 us
    pallas_call x1, Pallas kernels, feed(): call(functools.partial(feed_kernel, block=length // 2, pieces=pieces, ste...  42.9 us
    pallas_call x2, Pallas kernels, attend_back(): call(functools.partial(attend_back_kernel, base=base, count=count), (coun...  23.7 us
    pallas_call x1, Pallas kernels, attend(): call(functools.partial(attend_kernel, pieces=pieces), (GENES + 1,), [full...  19.6 us
    pallas_call x1, Pallas kernels, grads(): call(functools.partial(grads_kernel, pieces=pieces), (4,), [ANY] * 4 + [f...  12.4 us
    pallas_call x1, Pallas kernels, project_back(): call(project_back_kernel, (GENES,), [rows_of((span, width)), full((1, wid...  9.91 us
    convert_element_type x6, other arithmetic, low(): return value.astype(BF16)  9.02 us
  transfers between devices with their start and end apart: 42, of which 24 were waited for; matrix products, arithmetic and copies ran while one was open for 2% of the time, Pallas kernels for 32%

profile of v4, /device:TPU:0, one launch (start us, length us, event | category | flops | bytes accessed | tf_op | source)
XLA Modules:
  0.0 274.3 jit_solution(2216791223555609902)
XLA Ops:
  1.3 3.4 %quarters.1 = (bf16[2,104,384]{2,1,0:T(8,128)(2,1)}, bf16[2,192,384]{2,1,0:T(8,128)(2,1)}, bf16[2,2,296,384]{3,2,1,0:T(8,128)(2,1)}) custom-call(s32[4]{0:T(128)} %pad_add_fusion.at, bf16[96,2304]{1,0:T(8,128)(2,1)} %refs_7_.3, bf16[96,768]{1,0:T(8,128)(2,1)} %refs_8_.2, bf16[96,3072]{1,0:T(8,128)(2,1)} %refs_6_.3, bf16[384,768]{1,0:T(8,128)(2,1)} %refs_7_.4, ...), custom_call_target="tpu_custom_call" | custom-call | bytes 6000000 | tf_op jit(solution)/shard_map/quarters/pallas_call | solution.py:204
  4.7 2.9 %collective-permute-start.7 = (bf16[2,2,296,384]{3,2,1,0:T(8,128)(2,1)}, bf16[2,2,296,384]{3,2,1,0:T(8,128)(2,1)}, u32[]{:S(2)}, u32[]{:S(2)}) collective-permute-start(bf16[2,2,296,384]{3,2,1,0:T(8,128)(2,1)} %get-tuple-element.219), channel_id=1, source_target_pairs={{0,4},{1,5},{2,6},{3,7},{4,0},{5,1},{6,2},{7,3},{8,12},{9,13},{10,... | collective-permute-start | bytes 2727944 | tf_op jit(solution)/shard_map/ppermute | solution.py:141
  7.6 3.6 %collective-permute-start.2 = (bf16[2,104,384]{2,1,0:T(8,128)(2,1)}, bf16[2,104,384]{2,1,0:T(8,128)(2,1)S(1)}, u32[]{:S(2)}, u32[]{:S(2)}) collective-permute-start(bf16[2,104,384]{2,1,0:T(8,128)(2,1)} %get-tuple-element.205), channel_id=1, source_target_pairs={{0,24},{1,25},{2,26},{3,27},{4,28},{5,29},{6,30},{7,31},{8,0},{9,1... | collective-permute-start | bytes 479240 | tf_op jit(solution)/shard_map/ppermute | solution.py:141
  12.3 2.5 collective-permute-start.3
  14.7 8.7 %prepare.1 = (s32[16]{0:T(128)}, bf16[1024,768]{1,0:T(8,128)(2,1)}, bf16[1024,768]{1,0:T(8,128)(2,1)}, f32[1024,128]{1,0:T(8,128)}, f32[1024,128]{1,0:T(8,128)}) custom-call(s32[1,1024]{1,0:T(1,128)} %seg_ref.1, bf16[1024,768]{1,0:T(8,128)(2,1)} %bitcast.60, bf16[1024,768]{1,0:T(8,128)(2,1)} %bitcast.61, f32[1,128]{1,0:T(1,128)} %constant.47.clone.freq_ref), custom_call_target="tpu_custom_call" | custom-call | flops 3300000000 | bytes 8000000 | tf_op jit(solution)/shard_map/prepare/pallas_call | solution.py:307
  23.4 7.6 %collective-permute-done.1 = bf16[2,104,384]{2,1,0:T(8,128)(2,1)S(1)} collective-permute-done((bf16[2,104,384]{2,1,0:T(8,128)(2,1)}, bf16[2,104,384]{2,1,0:T(8,128)(2,1)S(1)}, u32[]{:S(2)}, u32[]{:S(2)}) %collective-permute-start.1) | collective-permute-done | bytes 159776 | tf_op jit(solution)/shard_map/ppermute | solution.py:141
  34.3 5.3 %collective-permute-done.4 = bf16[3,96,384]{2,1,0:T(8,128)(2,1)S(1)} collective-permute-done((bf16[3,96,384]{2,1,0:T(8,128)(2,1)S(1)}, bf16[3,96,384]{2,1,0:T(8,128)(2,1)S(1)}, u32[]{:S(2)}, u32[]{:S(2)}) %collective-permute-start.4) | collective-permute-done | bytes 221216 | tf_op jit(solution)/shard_map/ppermute | solution.py:141
  46.0 2.0 collective-permute-start.12
  48.0 3.2 %unpack.1 = (f32[1,768]{1,0:T(1,128)}, f32[1,768]{1,0:T(1,128)}, f32[1,2304]{1,0:T(1,128)}, f32[1,768]{1,0:T(1,128)}, f32[1,768]{1,0:T(1,128)}, /*index=5*/f32[1...) custom-call(s32[4]{0:T(128)} %pad_add_fusion.at, bf16[4,8,384]{2,1,0:T(8,128)(2,1)} %get-tuple-element.231.near_ref, ...), custom_call_target="tpu_custom_call" | custom-call | flops 100000000 | bytes 100000 | tf_op jit(solution)/shard_map/unpack/pallas_call | solution.py:246
  51.3 10.5 %collective-permute-done.12 = bf16[2,192,384]{2,1,0:T(8,128)(2,1)S(1)} collective-permute-done((bf16[2,192,384]{2,1,0:T(8,128)(2,1)}, bf16[2,192,384]{2,1,0:T(8,128)(2,1)S(1)}, u32[]{:S(2)}, u32[]{:S(2)}) %collective-permute-start.12) | collective-permute-done | bytes 294944 | tf_op jit(solution)/shard_map/ppermute | solution.py:141
  65.7 3.7 %collective-permute-done.13 = bf16[1,192,384]{2,1,0:T(8,128)(2,1)S(1)} collective-permute-done((bf16[1,192,384]{2,1,0:T(8,128)(2,1)S(1)}, bf16[1,192,384]{2,1,0:T(8,128)(2,1)S(1)}, u32[]{:S(2)}, u32[]{:S(2)}) %collective-permute-start.13) | collective-permute-done | bytes 147488 | tf_op jit(solution)/shard_map/ppermute | solution.py:141
  73.2 19.6 %attend.1 = (bf16[1024,2304]{1,0:T(8,128)(2,1)}, bf16[1024,768]{1,0:T(8,128)(2,1)}, f32[16,1024]{1,0:T(8,128)}, f32[1024,768]{1,0:T(8,128)}, bf16[768,2304]{1,0:T(8,128)(2,1)}, /*index=5*/bf16[768,768]{1,0:T(8,128)(2,1)}) custom-call(s32[16]{0:T(128)} %get-tuple-element.265.plan, s32[4]{0:T(128)} %pad_add_fusion.at, ...), custom_call_target="tpu_custom_call" | custom-call | flops 11000000512 | bytes 20000000 | tf_op jit(solution)/shard_map/attend/pallas_call | solution.py:461
  95.3 3.1 %collective-permute-done.20.refs_15_ = bf16[2,3,192,384]{3,2,1,0:T(8,128)(2,1)S(1)} collective-permute-done((bf16[2,3,192,384]{3,2,1,0:T(8,128)(2,1)S(1)}, bf16[2,3,192,384]{3,2,1,0:T(8,128)(2,1)S(1)}, u32[]{:S(2)}, u32[]{:S(2)}) %collective-permute-start.20) | collective-permute-done | bytes 884768 | tf_op jit(solution)/shard_map/ppermute | solution.py:141
  100.3 42.9 %feed.1 = (bf16[1024,768]{1,0:T(8,128)(2,1)}, f32[1024,768]{1,0:T(8,128)}, bf16[1024,768]{1,0:T(8,128)(2,1)}, f32[1,3072]{1,0:T(1,128)}, f32[8,768]{1,0:T(8,128)...) custom-call(s32[4]{0:T(128)} %pad_add_fusion.at, f32[1024,768]{1,0:T(8,128)} %get-tuple-element.286.refs_0_, ...), custom_call_target="tpu_custom_call" | custom-call | flops 28999999488 | bytes 40000000 | tf_op jit(solution)/shard_map/feed/pallas_call | solution.py:713
  143.3 8.0 %attend_back.2 = (bf16[1024,2304]{1,0:T(8,128)(2,1)}, f32[8,2304]{1,0:T(8,128)}) custom-call(s32[16]{0:T(128)} %get-tuple-element.265.plan, bf16[1024,2304]{1,0:T(8,128)(2,1)} %get-tuple-element.298.qkv_ref, bf16[1024,768]{1,0:T(8,128)(2,1)} %get-tuple-element.299.da_ref.refs_2_, f32[16,1024]{1,0:T(8,128)} %get-tuple-element.300.lse_ref, ...), custom_call_target="tpu_custom_call" | custom-call | flops 4000000000 | bytes 6000000 | tf_op jit(solution)/shard_map/attend_back/pallas_call | solution.py:820
  151.5 4.0 %add_convert_fusion = (bf16[8,192,384]{2,1,0:T(8,128)(2,1)S(1)}, bf16[8,192,384]{2,1,0:T(8,128)(2,1)}) fusion(bf16[32,192,384]{2,1,0:T(8,128)(2,1)} %collective-permute-done.22, bf16[32,192,384]{2,1,0:T(8,128)(2,1)} %get-tuple-element.296), kind=kLoop, calls=%fused_computation | loop fusion | flops 4718592 | bytes 7077888 | tf_op jit(solution)/shard_map/convert_element_type | solution.py:1121
  157.2 15.6 %attend_back.3 = (bf16[1024,2304]{1,0:T(8,128)(2,1)}, f32[8,2304]{1,0:T(8,128)}) custom-call(s32[16]{0:T(128)} %get-tuple-element.265.plan, bf16[1024,2304]{1,0:T(8,128)(2,1)} %get-tuple-element.298.qkv_ref, bf16[1024,768]{1,0:T(8,128)(2,1)} %get-tuple-element.299.da_ref.refs_2_, ...), custom_call_target="tpu_custom_call", output_to_operand_aliasing={{0}: (7, {})} | custom-call | flops 12000000000 | bytes 18000000 | tf_op jit(solution)/shard_map/attend_back/pallas_call | solution.py:820
  172.8 9.9 %project_back.1 = (bf16[1024,768]{1,0:T(8,128)(2,1)}, f32[8,768]{1,0:T(8,128)}) custom-call(bf16[1024,768]{1,0:T(8,128)(2,1)} %get-tuple-element.266.refs_0_.xp_ref, f32[1,768]{1,0:T(1,128)} %get-tuple-element.269.refs_3_.g1_ref.refs_4_, f32[1024,768]{1,0:T(8,128)} %get-tuple-element.307.dx1_ref, bf16[1024,2304]{1,0:T(8,128)(2,1)} %get-tuple-element.323.dqkv_ref.refs_3_, ...), custom_call_target="tpu_custom_call" | custom-call | tf_op jit(solution)/shard_map/project_back/pallas_call | solution.py:862
  184.6 2.1 add_convert_fusion.4
  188.1 12.4 %grads.1 = (bf16[32,104,384]{2,1,0:T(8,128)(2,1)}, bf16[32,104,384]{2,1,0:T(8,128)(2,1)}) custom-call(s32[4]{0:T(128)} %pad_add_fusion.at, bf16[1024,768]{1,0:T(8,128)(2,1)} %get-tuple-element.266.refs_0_.xp_ref, bf16[1024,768]{1,0:T(8,128)(2,1)} %get-tuple-element.322.refs_1_, bf16[1024,768]{1,0:T(8,128)(2,1)} %get-tuple-element.299.da_ref.refs_2_, ...), custom_call_target="tpu_custom_call" | custom-call | flops 5000000000 | bytes 12000000 | tf_op jit(solution)/shard_map/grads/pallas_call | solution.py:1003
  201.5 1.6 convert_add_fusion
  203.2 1.9 convert_add_fusion.1
  209.7 2.0 collective-permute-start.30
  211.7 14.1 %collective-permute-done.30 = bf16[2,192,384]{2,1,0:T(8,128)(2,1)S(1)} collective-permute-done((bf16[2,192,384]{2,1,0:T(8,128)(2,1)S(1)}, bf16[2,192,384]{2,1,0:T(8,128)(2,1)S(1)}, u32[]{:S(2)}, u32[]{:S(2)}) %collective-permute-start.30) | collective-permute-done | bytes 294944 | tf_op jit(solution)/shard_map/ppermute | solution.py:141
  229.4 3.0 %collective-permute-start.34 = (bf16[2,192,384]{2,1,0:T(8,128)(2,1)}, bf16[2,192,384]{2,1,0:T(8,128)(2,1)}, u32[]{:S(2)}, u32[]{:S(2)}) collective-permute-start(bf16[2,192,384]{2,1,0:T(8,128)(2,1)} %pad_maximum_fusion.12), channel_id=1, source_target_pairs={{0,24},{1,25},{2,26},{3,27},{4,28},{5,29},{6,30},{7,31},{8,0},{9,1... | collective-permute-start | bytes 884744 | tf_op jit(solution)/shard_map/ppermute | solution.py:141
  232.5 8.3 %collective-permute-done.33 = bf16[2,192,384]{2,1,0:T(8,128)(2,1)} collective-permute-done((bf16[2,192,384]{2,1,0:T(8,128)(2,1)}, bf16[2,192,384]{2,1,0:T(8,128)(2,1)}, u32[]{:S(2)}, u32[]{:S(2)}) %collective-permute-start.33) | collective-permute-done | bytes 294944 | tf_op jit(solution)/shard_map/ppermute | solution.py:141
  240.7 2.8 %collective-permute-done.34 = bf16[2,192,384]{2,1,0:T(8,128)(2,1)} collective-permute-done((bf16[2,192,384]{2,1,0:T(8,128)(2,1)}, bf16[2,192,384]{2,1,0:T(8,128)(2,1)}, u32[]{:S(2)}, u32[]{:S(2)}) %collective-permute-start.34) | collective-permute-done | bytes 294944 | tf_op jit(solution)/shard_map/ppermute | solution.py:141
  248.4 1.9 collective-permute-start.35
  250.3 1.7 collective-permute-start.36
  254.5 7.3 %restore.1 = (bf16[1024,768]{1,0:T(8,128)(2,1)}, bf16[1024,768]{1,0:T(8,128)(2,1)}) custom-call(s32[16]{0:T(128)} %get-tuple-element.265.plan, bf16[1024,768]{1,0:T(8,128)(2,1)} %get-tuple-element.363.outp_ref, bf16[1024,768]{1,0:T(8,128)(2,1)} %get-tuple-element.364.dxp_ref), custom_call_target="tpu_custom_call" | custom-call | flops 3300000000 | bytes 8000000 | tf_op jit(solution)/shard_map/restore/pallas_call | solution.py:1036
  265.1 3.4 %deliver_second.1 = (f32[96,3072]{1,0:T(8,128)}, f32[384,768]{1,0:T(8,128)}) custom-call(s32[4]{0:T(128)} %pad_add_fusion.at, bf16[2,2,192,384]{3,2,1,0:T(8,128)(2,1)} %copy-done.2, bf16[2,2,192,384]{3,2,1,0:T(8,128)(2,1)} %copy-done.13), custom_call_target="tpu_custom_call" | custom-call | bytes 4000000 | tf_op jit(solution)/shard_map/deliver_second/pallas_call | solution.py:1100
  271.3 2.8 %deliver_first.1 = (f32[96,2304]{1,0:T(8,128)}, f32[96,768]{1,0:T(8,128)}, f32[96]{0:T(128)}, f32[96]{0:T(128)}, f32[288]{0:T(512)}, /*index=5*/f32[96]{0:T(128)...) custom-call(s32[4]{0:T(128)} %pad_add_fusion.at, bf16[2,2,104,384]{3,2,1,0:T(8,128)(2,1)} %copy-done.3, ...), custom_call_target="tpu_custom_call" | custom-call | bytes 2000000 | tf_op jit(solution)/shard_map/deliver_first/pallas_call | solution.py:1070
  (167 shorter events, 50.8 us)
Async XLA Ops:
  4.7 35.2 %collective-permute-start.7 = (bf16[2,2,296,384]{3,2,1,0:T(8,128)(2,1)}, bf16[2,2,296,384]{3,2,1,0:T(8,128)(2,1)}, u32[]{:S(2)}, u32[]{:S(2)}) collective-permute-start(bf16[2,2,296,384]{3,2,1,0:T(8,128)(2,1)} %get-tuple-element.219), channel_id=1, source_target_pairs={{0,4},{1,5},{2,6},{3,7},{4,0},{5,1},{6,2},{7,3},{8,12},{9,13},{10,... | collective-permute-start | bytes 2727944 | tf_op jit(solution)/shard_map/ppermute | solution.py:141
  7.6 15.8 %collective-permute-start.2 = (bf16[2,104,384]{2,1,0:T(8,128)(2,1)}, bf16[2,104,384]{2,1,0:T(8,128)(2,1)S(1)}, u32[]{:S(2)}, u32[]{:S(2)}) collective-permute-start(bf16[2,104,384]{2,1,0:T(8,128)(2,1)} %get-tuple-element.205), channel_id=1, source_target_pairs={{0,24},{1,25},{2,26},{3,27},{4,28},{5,29},{6,30},{7,31},{8,0},{9,1... | collective-permute-start | bytes 479240 | tf_op jit(solution)/shard_map/ppermute | solution.py:141
  11.2 19.8 %collective-permute-start.1 = (bf16[2,104,384]{2,1,0:T(8,128)(2,1)}, bf16[2,104,384]{2,1,0:T(8,128)(2,1)S(1)}, u32[]{:S(2)}, u32[]{:S(2)}) collective-permute-start(bf16[2,104,384]{2,1,0:T(8,128)(2,1)} %get-tuple-element.205), channel_id=1, source_target_pairs={{0,16},{1,17},{2,18},{3,19},{4,20},{5,21},{6,22},{7,23},{8,24},{9,... | collective-permute-start | bytes 479240 | tf_op jit(solution)/shard_map/ppermute | solution.py:141
  11.2 19.8 %collective-permute-start = (bf16[2,104,384]{2,1,0:T(8,128)(2,1)}, bf16[2,104,384]{2,1,0:T(8,128)(2,1)S(1)}, u32[]{:S(2)}, u32[]{:S(2)}) collective-permute-start(bf16[2,104,384]{2,1,0:T(8,128)(2,1)} %get-tuple-element.205), channel_id=1, source_target_pairs={{0,8},{1,9},{2,10},{3,11},{4,12},{5,13},{6,14},{7,15},{8,16},{9,17... | collective-permute-start | bytes 479240 | tf_op jit(solution)/shard_map/ppermute | solution.py:141
  12.3 18.8 %collective-permute-start.3 = (bf16[2,192,384]{2,1,0:T(8,128)(2,1)}, bf16[2,192,384]{2,1,0:T(8,128)(2,1)S(1)}, u32[]{:S(2)}, u32[]{:S(2)}) collective-permute-start(bf16[2,192,384]{2,1,0:T(8,128)(2,1)} %get-tuple-element.241), channel_id=1, source_target_pairs={{0,8},{1,9},{2,10},{3,11},{4,12},{5,13},{6,14},{7,15},{8,16},{9,17... | collective-permute-start | bytes 884744 | tf_op jit(solution)/shard_map/ppermute | solution.py:141
  31.2 8.7 %collective-permute-start.6 = (bf16[2,192,384]{2,1,0:T(8,128)(2,1)}, bf16[2,192,384]{2,1,0:T(8,128)(2,1)S(1)}, u32[]{:S(2)}, u32[]{:S(2)}) collective-permute-start(bf16[2,192,384]{2,1,0:T(8,128)(2,1)} %get-tuple-element.241), channel_id=1, source_target_pairs={{0,24},{1,25},{2,26},{3,27},{4,28},{5,29},{6,30},{7,31},{8,0},{9,1... | collective-permute-start | bytes 884744 | tf_op jit(solution)/shard_map/ppermute | solution.py:141
  31.5 8.1 %collective-permute-start.5 = (bf16[3,104,384]{2,1,0:T(8,128)(2,1)S(1)}, bf16[3,104,384]{2,1,0:T(8,128)(2,1)S(1)}, u32[]{:S(2)}, u32[]{:S(2)}) collective-permute-start(bf16[3,104,384]{2,1,0:T(8,128)(2,1)S(1)} %pad_maximum_fusion.13), channel_id=1, source_target_pairs={{0,4},{1,5},{2,6},{3,7},{4,0},{5,1},{6,2},{7,3},{8,12},{9,13},{10,... | collective-permute-start | bytes 718856 | tf_op jit(solution)/shard_map/ppermute | solution.py:141
  42.8 19.8 %collective-permute-start.11 = (bf16[2,2,296,384]{3,2,1,0:T(8,128)(2,1)}, bf16[2,2,296,384]{3,2,1,0:T(8,128)(2,1)}, u32[]{:S(2)}, u32[]{:S(2)}) collective-permute-start(bf16[2,2,296,384]{3,2,1,0:T(8,128)(2,1)} %collective-permute-done.7.refs_9_.refs_8_), channel_id=1, source_target_pairs={{0,1},{1,0},{2,3},{3,2},{4,5},{5,4},{6,7},{7,6},{8,9},{9,8},{10,11... | collective-permute-start | bytes 2727944 | tf_op jit(solution)/shard_map/ppermute | solution.py:141
  42.8 19.8 %collective-permute-start.10 = (bf16[2,2,3,96,384]{4,3,2,1,0:T(8,128)(2,1)S(1)}, bf16[2,2,3,96,384]{4,3,2,1,0:T(8,128)(2,1)}, u32[]{:S(2)}, u32[]{:S(2)}) collective-permute-start(bf16[2,2,3,96,384]{4,3,2,1,0:T(8,128)(2,1)S(1)} %pad_maximum_fusion.refs_11_.refs_13_), channel_id=1, source_target_pairs={{0,1},{1,0},{2,3},{3,2},{4,5},{5,4},{6,7},{7,6},{8,9},{9,8},{10,11... | collective-permute-start | bytes 2654216 | tf_op jit(solution)/shard_map/ppermute | solution.py:141
  43.3 18.6 %collective-permute-start.8 = (bf16[20,48,384]{2,1,0:T(8,128)(2,1)}, bf16[20,48,384]{2,1,0:T(8,128)(2,1)S(1)}, u32[]{:S(2)}, u32[]{:S(2)}) collective-permute-start(bf16[20,48,384]{2,1,0:T(8,128)(2,1)} %pad_maximum_fusion.4), channel_id=1, source_target_pairs={{0,4},{1,5},{2,6},{3,7},{4,0},{5,1},{6,2},{7,3},{8,12},{9,13},{10,... | collective-permute-start | bytes 2211848 | tf_op jit(solution)/shard_map/ppermute | solution.py:141
  44.5 18.1 %collective-permute-start.9 = (bf16[20,48,384]{2,1,0:T(8,128)(2,1)S(1)}, bf16[20,48,384]{2,1,0:T(8,128)(2,1)S(1)}, u32[]{:S(2)}, u32[]{:S(2)}) collective-permute-start(bf16[20,48,384]{2,1,0:T(8,128)(2,1)S(1)} %pad_maximum_fusion.5), channel_id=1, source_target_pairs={{0,2},{1,3},{2,0},{3,1},{4,6},{5,7},{6,4},{7,5},{8,10},{9,11},{10,... | collective-permute-start | bytes 2211848 | tf_op jit(solution)/shard_map/ppermute | solution.py:141
  46.0 15.8 %collective-permute-start.12 = (bf16[2,192,384]{2,1,0:T(8,128)(2,1)}, bf16[2,192,384]{2,1,0:T(8,128)(2,1)S(1)}, u32[]{:S(2)}, u32[]{:S(2)}) collective-permute-start(bf16[2,192,384]{2,1,0:T(8,128)(2,1)} %get-tuple-element.241), channel_id=1, source_target_pairs={{0,16},{1,17},{2,18},{3,19},{4,20},{5,21},{6,22},{7,23},{8,24},{9,... | collective-permute-start | bytes 884744 | tf_op jit(solution)/shard_map/ppermute | solution.py:141
  71.6 21.2 %collective-permute-start.18 = (bf16[2,3,192,384]{3,2,1,0:T(8,128)(2,1)S(1)}, bf16[2,3,192,384]{3,2,1,0:T(8,128)(2,1)S(1)}, u32[]{:S(2)}, u32[]{:S(2)}) collective-permute-start(bf16[2,3,192,384]{3,2,1,0:T(8,128)(2,1)S(1)} %pad_maximum_fusion.2.refs_10_), channel_id=1, source_target_pairs={{0,1},{1,0},{2,3},{3,2},{4,5},{5,4},{6,7},{7,6},{8,9},{9,8},{10,11... | collective-permute-start | bytes 2654216 | tf_op jit(solution)/shard_map/ppermute | solution.py:141
  71.7 22.1 %collective-permute-start.16 = (bf16[2,3,192,384]{3,2,1,0:T(8,128)(2,1)S(1)}, bf16[2,3,192,384]{3,2,1,0:T(8,128)(2,1)S(1)}, u32[]{:S(2)}, u32[]{:S(2)}) collective-permute-start(bf16[2,3,192,384]{3,2,1,0:T(8,128)(2,1)S(1)} %pad_maximum_fusion.2.refs_10_), channel_id=1, source_target_pairs={{0,4},{1,5},{2,6},{3,7},{4,0},{5,1},{6,2},{7,3},{8,12},{9,13},{10,... | collective-permute-start | bytes 2654216 | tf_op jit(solution)/shard_map/ppermute | solution.py:141
  72.6 21.2 %collective-permute-start.19 = (bf16[2,3,192,384]{3,2,1,0:T(8,128)(2,1)S(1)}, bf16[2,3,192,384]{3,2,1,0:T(8,128)(2,1)}, u32[]{:S(2)}, u32[]{:S(2)}) collective-permute-start(bf16[2,3,192,384]{3,2,1,0:T(8,128)(2,1)S(1)} %pad_maximum_fusion.3.refs_12_), channel_id=1, source_target_pairs={{0,1},{1,0},{2,3},{3,2},{4,5},{5,4},{6,7},{7,6},{8,9},{9,8},{10,11... | collective-permute-start | bytes 2654216 | tf_op jit(solution)/shard_map/ppermute | solution.py:141
  72.7 22.0 %collective-permute-start.17 = (bf16[2,3,192,384]{3,2,1,0:T(8,128)(2,1)S(1)}, bf16[2,3,192,384]{3,2,1,0:T(8,128)(2,1)}, u32[]{:S(2)}, u32[]{:S(2)}) collective-permute-start(bf16[2,3,192,384]{3,2,1,0:T(8,128)(2,1)S(1)} %pad_maximum_fusion.3.refs_12_), channel_id=1, source_target_pairs={{0,2},{1,3},{2,0},{3,1},{4,6},{5,7},{6,4},{7,5},{8,10},{9,11},{10,... | collective-permute-start | bytes 2654216 | tf_op jit(solution)/shard_map/ppermute | solution.py:141
  143.1 8.3 %collective-permute-start.22 = (bf16[32,192,384]{2,1,0:T(8,128)(2,1)}, bf16[32,192,384]{2,1,0:T(8,128)(2,1)}, u32[]{:S(2)}, u32[]{:S(2)}) collective-permute-start(bf16[32,192,384]{2,1,0:T(8,128)(2,1)} %get-tuple-element.297), channel_id=1, source_target_pairs={{0,1},{1,0},{2,3},{3,2},{4,5},{5,4},{6,7},{7,6},{8,9},{9,8},{10,11... | collective-permute-start | bytes 14155784 | tf_op jit(solution)/shard_map/ppermute | solution.py:141
  155.5 28.4 %collective-permute-start.23 = (bf16[8,192,384]{2,1,0:T(8,128)(2,1)}, bf16[8,192,384]{2,1,0:T(8,128)(2,1)S(1)}, u32[]{:S(2)}, u32[]{:S(2)}) collective-permute-start(bf16[8,192,384]{2,1,0:T(8,128)(2,1)} %get-tuple-element.305), channel_id=1, source_target_pairs={{0,4},{1,5},{2,6},{3,7},{4,0},{5,1},{6,2},{7,3},{8,12},{9,13},{10,... | collective-permute-start | bytes 3538952 | tf_op jit(solution)/shard_map/ppermute | solution.py:141
  156.7 27.9 %collective-permute-start.24 = (bf16[8,192,384]{2,1,0:T(8,128)(2,1)S(1)}, bf16[8,192,384]{2,1,0:T(8,128)(2,1)S(1)}, u32[]{:S(2)}, u32[]{:S(2)}) collective-permute-start(bf16[8,192,384]{2,1,0:T(8,128)(2,1)S(1)} %get-tuple-element.306), channel_id=1, source_target_pairs={{0,2},{1,3},{2,0},{3,1},{4,6},{5,7},{6,4},{7,5},{8,10},{9,11},{10,... | collective-permute-start | bytes 3538952 | tf_op jit(solution)/shard_map/ppermute | solution.py:141
  186.7 14.6 %collective-permute-start.25 = (bf16[4,192,384]{2,1,0:T(8,128)(2,1)S(1)}, bf16[4,192,384]{2,1,0:T(8,128)(2,1)}, u32[]{:S(2)}, u32[]{:S(2)}) collective-permute-start(bf16[4,192,384]{2,1,0:T(8,128)(2,1)S(1)} %get-tuple-element.320), channel_id=1, source_target_pairs={{0,2},{1,3},{2,0},{3,1},{4,6},{5,7},{6,4},{7,5},{8,10},{9,11},{10,... | collective-permute-start | bytes 1769480 | tf_op jit(solution)/shard_map/ppermute | solution.py:141
  187.2 14.3 %collective-permute-start.26 = (bf16[4,192,384]{2,1,0:T(8,128)(2,1)S(1)}, bf16[4,192,384]{2,1,0:T(8,128)(2,1)S(1)}, u32[]{:S(2)}, u32[]{:S(2)}) collective-permute-start(bf16[4,192,384]{2,1,0:T(8,128)(2,1)S(1)} %get-tuple-element.321), channel_id=1, source_target_pairs={{0,4},{1,5},{2,6},{3,7},{4,0},{5,1},{6,2},{7,3},{8,12},{9,13},{10,... | collective-permute-start | bytes 1769480 | tf_op jit(solution)/shard_map/ppermute | solution.py:141
  207.0 18.7 %collective-permute-start.28 = (bf16[8,104,384]{2,1,0:T(8,128)(2,1)S(1)}, bf16[8,104,384]{2,1,0:T(8,128)(2,1)S(1)}, u32[]{:S(2)}, u32[]{:S(2)}) collective-permute-start(bf16[8,104,384]{2,1,0:T(8,128)(2,1)S(1)} %get-tuple-element.339), channel_id=1, source_target_pairs={{0,4},{1,5},{2,6},{3,7},{4,0},{5,1},{6,2},{7,3},{8,12},{9,13},{10,... | collective-permute-start | bytes 1916936 | tf_op jit(solution)/shard_map/ppermute | solution.py:141
  208.1 17.6 %collective-permute-start.29 = (bf16[8,104,384]{2,1,0:T(8,128)(2,1)S(1)}, bf16[8,104,384]{2,1,0:T(8,128)(2,1)S(1)}, u32[]{:S(2)}, u32[]{:S(2)}) collective-permute-start(bf16[8,104,384]{2,1,0:T(8,128)(2,1)S(1)} %get-tuple-element.340), channel_id=1, source_target_pairs={{0,2},{1,3},{2,0},{3,1},{4,6},{5,7},{6,4},{7,5},{8,10},{9,11},{10,... | collective-permute-start | bytes 1916936 | tf_op jit(solution)/shard_map/ppermute | solution.py:141
  209.7 16.1 %collective-permute-start.30 = (bf16[2,192,384]{2,1,0:T(8,128)(2,1)S(1)}, bf16[2,192,384]{2,1,0:T(8,128)(2,1)S(1)}, u32[]{:S(2)}, u32[]{:S(2)}) collective-permute-start(bf16[2,192,384]{2,1,0:T(8,128)(2,1)S(1)} %pad_maximum_fusion.11), channel_id=1, source_target_pairs={{0,16},{1,17},{2,18},{3,19},{4,20},{5,21},{6,22},{7,23},{8,24},{9,... | collective-permute-start | bytes 884744 | tf_op jit(solution)/shard_map/ppermute | solution.py:141
  227.1 16.4 %collective-permute-start.31 = (bf16[4,104,384]{2,1,0:T(8,128)(2,1)}, bf16[4,104,384]{2,1,0:T(8,128)(2,1)S(1)}, u32[]{:S(2)}, u32[]{:S(2)}) collective-permute-start(bf16[4,104,384]{2,1,0:T(8,128)(2,1)} %get-tuple-element.348), channel_id=1, source_target_pairs={{0,2},{1,3},{2,0},{3,1},{4,6},{5,7},{6,4},{7,5},{8,10},{9,11},{10,... | collective-permute-start | bytes 958472 | tf_op jit(solution)/shard_map/ppermute | solution.py:141
  227.7 16.6 %collective-permute-start.32 = (bf16[4,104,384]{2,1,0:T(8,128)(2,1)}, bf16[4,104,384]{2,1,0:T(8,128)(2,1)}, u32[]{:S(2)}, u32[]{:S(2)}) collective-permute-start(bf16[4,104,384]{2,1,0:T(8,128)(2,1)} %get-tuple-element.349), channel_id=1, source_target_pairs={{0,4},{1,5},{2,6},{3,7},{4,0},{5,1},{6,2},{7,3},{8,12},{9,13},{10,... | collective-permute-start | bytes 958472 | tf_op jit(solution)/shard_map/ppermute | solution.py:141
  228.6 12.1 %collective-permute-start.33 = (bf16[2,192,384]{2,1,0:T(8,128)(2,1)}, bf16[2,192,384]{2,1,0:T(8,128)(2,1)}, u32[]{:S(2)}, u32[]{:S(2)}) collective-permute-start(bf16[2,192,384]{2,1,0:T(8,128)(2,1)} %pad_maximum_fusion.10), channel_id=1, source_target_pairs={{0,8},{1,9},{2,10},{3,11},{4,12},{5,13},{6,14},{7,15},{8,16},{9,17... | collective-permute-start | bytes 884744 | tf_op jit(solution)/shard_map/ppermute | solution.py:141
  229.4 14.1 %collective-permute-start.34 = (bf16[2,192,384]{2,1,0:T(8,128)(2,1)}, bf16[2,192,384]{2,1,0:T(8,128)(2,1)}, u32[]{:S(2)}, u32[]{:S(2)}) collective-permute-start(bf16[2,192,384]{2,1,0:T(8,128)(2,1)} %pad_maximum_fusion.12), channel_id=1, source_target_pairs={{0,24},{1,25},{2,26},{3,27},{4,28},{5,29},{6,30},{7,31},{8,0},{9,1... | collective-permute-start | bytes 884744 | tf_op jit(solution)/shard_map/ppermute | solution.py:141
  248.4 13.4 %collective-permute-start.35 = (bf16[2,104,384]{2,1,0:T(8,128)(2,1)S(1)}, bf16[2,104,384]{2,1,0:T(8,128)(2,1)S(1)}, u32[]{:S(2)}, u32[]{:S(2)}) collective-permute-start(bf16[2,104,384]{2,1,0:T(8,128)(2,1)S(1)} %pad_maximum_fusion.15), channel_id=1, source_target_pairs={{0,8},{1,9},{2,10},{3,11},{4,12},{5,13},{6,14},{7,15},{8,16},{9,17... | collective-permute-start | bytes 479240 | tf_op jit(solution)/shard_map/ppermute | solution.py:141
  250.3 11.7 %collective-permute-start.36 = (bf16[2,104,384]{2,1,0:T(8,128)(2,1)S(1)}, bf16[2,104,384]{2,1,0:T(8,128)(2,1)S(1)}, u32[]{:S(2)}, u32[]{:S(2)}) collective-permute-start(bf16[2,104,384]{2,1,0:T(8,128)(2,1)S(1)} %pad_maximum_fusion.16), channel_id=1, source_target_pairs={{0,16},{1,17},{2,18},{3,19},{4,20},{5,21},{6,22},{7,23},{8,24},{9,... | collective-permute-start | bytes 479240 | tf_op jit(solution)/shard_map/ppermute | solution.py:141
  252.0 9.9 %collective-permute-start.37 = (bf16[2,104,384]{2,1,0:T(8,128)(2,1)S(1)}, bf16[2,104,384]{2,1,0:T(8,128)(2,1)S(1)}, u32[]{:S(2)}, u32[]{:S(2)}) collective-permute-start(bf16[2,104,384]{2,1,0:T(8,128)(2,1)S(1)} %pad_maximum_fusion.17), channel_id=1, source_target_pairs={{0,24},{1,25},{2,26},{3,27},{4,28},{5,29},{6,30},{7,31},{8,0},{9,1... | collective-permute-start | bytes 479240 | tf_op jit(solution)/shard_map/ppermute | solution.py:141
  253.3 8.7 %collective-permute-start.38 = (bf16[2,192,384]{2,1,0:T(8,128)(2,1)S(1)}, bf16[2,192,384]{2,1,0:T(8,128)(2,1)S(1)}, u32[]{:S(2)}, u32[]{:S(2)}) collective-permute-start(bf16[2,192,384]{2,1,0:T(8,128)(2,1)S(1)} %fusion.2), channel_id=1, source_target_pairs={{0,2},{1,3},{2,0},{3,1},{4,6},{5,7},{6,4},{7,5},{8,10},{9,11},{10,... | collective-permute-start | bytes 884744 | tf_op jit(solution)/shard_map/ppermute | solution.py:141
  (33 other events, 182.9 us)

commit v5 on v4

--- a/solution.py
+++ b/solution.py
@@ -165,7 +165,7 @@
 
 def quarters_kernel(at, *refs):
     wqkv, wout, wup, wdown = refs[:4]
-    vectors, (near1, near2, side, packed) = refs[4:12], refs[12:]
+    vectors, (near1, near2, near, side, packed) = refs[4:12], refs[12:]
     width = wout.shape[1]
     rows = wout.shape[0] // 2
     packed[...] = jnp.zeros_like(packed)
@@ -191,6 +191,8 @@
     near2[...] = side[at[2], :, 2 * rows : 6 * rows, :]
     for h in range(2):
         near1[h, 2 * rows : 2 * rows + 8, :] = tail
+    near[:, 0 : 2 * rows + 8, :] = near1[...]
+    near[:, 2 * rows + 8 : 6 * rows + 8, :] = near2[...]
 
 
 def quarters(at, wqkv, wout, wup, wdown, vectors):
@@ -198,6 +200,7 @@
     shapes = [
         (2, 2 * rows + 8, COLUMNS),
         (2, 4 * rows, COLUMNS),
+        (2, 6 * rows + 8, COLUMNS),
         (2, 2, 6 * rows + 8, COLUMNS),
     ]
     matrices = (wqkv, wout, wup, wdown)
@@ -1189,13 +1192,14 @@
     x, c = layer_input[0], cotangent[0]
     if tuned:
         at = place()
-        near1, near2, side = quarters(at, w_qkv, w_out, w_up, w_down, vectors)
-        near1, near2, side, x = tie((near1, near2, side, x))
-        z1 = to_z(near1)
+        near1, near2, near, side = quarters(at, w_qkv, w_out, w_up, w_down, vectors)
+        near1, near2, near, side, x = tie((near1, near2, near, side, x))
+        z_one, z1_two, z1_three = move(near, ALONG_Z[1]), move(near1, ALONG_Z[2]), move(near1, ALONG_Z[3])
         far_side = over_x(side)
-        z2_one = move(near2, ALONG_Z[1])
         prepared = prepare(segment_ids, x, c)
-        z1, z2_one, prepared = tie((z1, z2_one, prepared))
+        z_one, z1_two, z1_three, prepared = tie((z_one, z1_two, z1_three, prepared))
+        split = near1.shape[1]
+        z1, z2_one = [z_one[:, :split], z1_two, z1_three], z_one[:, split:]
         plan, xp, cp, cos, sin = prepared
 
         count = near1.shape[1] - 8
@@ -1282,12 +1286,17 @@
         group1 = Sum(kept1, got1)
         to_x, to_y, *to_z2 = tie([*group1.plane_one(), *to_z2])
         two = move(to_z2[1], ALONG_Z[2])
-        by_x, by_y, two, *to_z2 = tie((over_x(to_x), over_y(to_y), two, to_z2[0], to_z2[2]))
-        to_y, to_x, *to_z2 = tie([*group1.plane_two(by_x, by_y), *to_z2])
+        parts = [add(kept1[i : i + Z_SIZE], got1[i : i + Z_SIZE]) for i in (0, 4, 16, 20)]
+        by_x, by_y, two, parts, *to_z2 = tie((over_x(to_x), over_y(to_y), two, parts, to_z2[0], to_z2[2]))
+        to_y, to_x = low(parts[1] + by_x[Z_SIZE:]), low(parts[3] + by_y[Z_SIZE:])
+        to_y, to_x, *to_z2 = tie([to_y, to_x, *to_z2])
         one, three = move(to_z2[0], ALONG_Z[1]), move(to_z2[1], ALONG_Z[3])
-        by_y, by_x, one, three = tie((over_y(to_y), over_x(to_x), one, three))
+        parts = parts[0] + by_x[:Z_SIZE], parts[2] + by_y[:Z_SIZE]
+        by_y, by_x, one, three, parts = tie((over_y(to_y), over_x(to_x), one, three, parts))
         z2 = one, two, three
-        to_z1 = group1.along_z(by_y, by_x)
+        at_z = lambda d: stack([parts[0][d] + by_y[d], parts[1][d] + by_x[d]])
+        to_z1 = [low(at_z(d)) for d in range(1, Z_SIZE)]
+        group1.own = at_z(0)
         total2 = group2.total(z2)
         to_z1, total2, outp, dxp = tie((to_z1, total2, outp, dxp))
         z1 = to_z(to_z1)

time: 276 us -> 273 us (0.989)
  waiting for transfers between devices: 65.6 us -> 69.9 us
  starting transfers between devices: 43.2 us -> 39.3 us
  other arithmetic: 20.5 us -> 17.5 us
    ppermute x42 -> x41, waiting for transfers between devices: 65.6 us -> 69.9 us  [move(): return lax.ppermute(array, AXES, table)]
    ppermute x42 -> x41, starting transfers between devices: 43.2 us -> 39.3 us  [move(): return lax.ppermute(array, AXES, table)]
    add x4 -> x3, other arithmetic: 6.35 us -> 4 us  [add(): total = total + v.astype(F32)]
    convert_element_type x6 -> x5, other arithmetic: 9.02 us -> 8.08 us  [low(): return value.astype(BF16)]
  transfers between devices with their start and end apart: 42 -> 41, of which waited for: 24 -> 23; matrix products, arithmetic and copies ran while one was open for 2% -> 2% of each run, Pallas kernels for 32% -> 32%
where the time goes in v5:
time: 273 us; the launch traced here: 272 us
  Pallas kernels  137 us (50%)
  waiting for transfers between devices  69.9 us (26%)
  starting transfers between devices  39.3 us (14%)
  other arithmetic  17.5 us (6%)
  local copies, waits for them, and re-layouts  6.82 us (2%)
    ppermute x41, waiting for transfers between devices, move(): return lax.ppermute(array, AXES, table)  69.9 us
    pallas_call x1, Pallas kernels, feed(): call(functools.partial(feed_kernel, block=length // 2, pieces=pieces, ste...  42.8 us
    ppermute x41, starting transfers between devices, move(): return lax.ppermute(array, AXES, table)  39.3 us
    pallas_call x2, Pallas kernels, attend_back(): call(functools.partial(attend_back_kernel, base=base, count=count), (coun...  23.6 us
    pallas_call x1, Pallas kernels, attend(): call(functools.partial(attend_kernel, pieces=pieces), (GENES + 1,), [full...  19.7 us
    pallas_call x1, Pallas kernels, grads(): call(functools.partial(grads_kernel, pieces=pieces), (4,), [ANY] * 4 + [f...  12.4 us
    pallas_call x1, Pallas kernels, project_back(): call(project_back_kernel, (GENES,), [rows_of((span, width)), full((1, wid...  9.92 us
    pallas_call x1, Pallas kernels, prepare(): call(prepare_kernel, (GENES,), [full((1, length)), full((length, width)),...  8.68 us
  transfers between devices with their start and end apart: 41, of which 23 were waited for; matrix products, arithmetic and copies ran while one was open for 2% of the time, Pallas kernels for 32%

profile of v5, /device:TPU:0, one launch (start us, length us, event | category | flops | bytes accessed | tf_op | source)
XLA Modules:
  0.0 272.3 jit_solution(7167508052973585784)
XLA Ops:
  1.3 3.5 %quarters.1 = (bf16[2,104,384]{2,1,0:T(8,128)(2,1)}, bf16[2,192,384]{2,1,0:T(8,128)(2,1)}, bf16[2,296,384]{2,1,0:T(8,128)(2,1)}, bf16[2,2,296,384]{3,2,1,0:T(8,128)(2,1)}) custom-call(s32[4]{0:T(128)} %pad_add_fusion.at, bf16[96,2304]{1,0:T(8,128)(2,1)} %refs_7_.3, bf16[96,768]{1,0:T(8,128)(2,1)} %refs_8_.2, bf16[96,3072]{1,0:T(8,128)(2,1)} %refs_6_.3, ...), custom_call_target="tpu_custom_call" | custom-call | bytes 6000000 | tf_op jit(solution)/shard_map/quarters/pallas_call | solution.py:207
  4.8 3.0 %collective-permute-start = (bf16[2,296,384]{2,1,0:T(8,128)(2,1)}, bf16[2,296,384]{2,1,0:T(8,128)(2,1)S(1)}, u32[]{:S(2)}, u32[]{:S(2)}) collective-permute-start(bf16[2,296,384]{2,1,0:T(8,128)(2,1)} %get-tuple-element.213), channel_id=1, source_target_pairs={{0,8},{1,9},{2,10},{3,11},{4,12},{5,13},{6,14},{7,15},{8,16},{9,17... | collective-permute-start | bytes 1363976 | tf_op jit(solution)/shard_map/ppermute | solution.py:141
  9.3 2.2 collective-permute-start.2
  12.3 8.7 %prepare.1 = (s32[16]{0:T(128)}, bf16[1024,768]{1,0:T(8,128)(2,1)}, bf16[1024,768]{1,0:T(8,128)(2,1)}, f32[1024,128]{1,0:T(8,128)}, f32[1024,128]{1,0:T(8,128)}) custom-call(s32[1,1024]{1,0:T(1,128)} %seg_ref.1, bf16[1024,768]{1,0:T(8,128)(2,1)} %bitcast.60, bf16[1024,768]{1,0:T(8,128)(2,1)} %bitcast.61, f32[1,128]{1,0:T(1,128)} %constant.47.clone.freq_ref), custom_call_target="tpu_custom_call" | custom-call | flops 3300000000 | bytes 8000000 | tf_op jit(solution)/shard_map/prepare/pallas_call | solution.py:310
  21.0 2.9 %collective-permute-done.2 = bf16[2,104,384]{2,1,0:T(8,128)(2,1)S(1)} collective-permute-done((bf16[2,104,384]{2,1,0:T(8,128)(2,1)}, bf16[2,104,384]{2,1,0:T(8,128)(2,1)S(1)}, u32[]{:S(2)}, u32[]{:S(2)}) %collective-permute-start.2) | collective-permute-done | bytes 159776 | tf_op jit(solution)/shard_map/ppermute | solution.py:141
  23.9 6.8 %collective-permute-done.1 = bf16[2,104,384]{2,1,0:T(8,128)(2,1)S(1)} collective-permute-done((bf16[2,104,384]{2,1,0:T(8,128)(2,1)}, bf16[2,104,384]{2,1,0:T(8,128)(2,1)S(1)}, u32[]{:S(2)}, u32[]{:S(2)}) %collective-permute-start.1) | collective-permute-done | bytes 159776 | tf_op jit(solution)/shard_map/ppermute | solution.py:141
  30.9 1.7 collective-permute-start.5
  36.4 4.4 %collective-permute-done.3 = bf16[3,96,384]{2,1,0:T(8,128)(2,1)S(1)} collective-permute-done((bf16[3,96,384]{2,1,0:T(8,128)(2,1)S(1)}, bf16[3,96,384]{2,1,0:T(8,128)(2,1)S(1)}, u32[]{:S(2)}, u32[]{:S(2)}) %collective-permute-start.3) | collective-permute-done | bytes 221216 | tf_op jit(solution)/shard_map/ppermute | solution.py:141
  46.5 3.2 %unpack.1 = (f32[1,768]{1,0:T(1,128)}, f32[1,768]{1,0:T(1,128)}, f32[1,2304]{1,0:T(1,128)}, f32[1,768]{1,0:T(1,128)}, f32[1,768]{1,0:T(1,128)}, /*index=5*/f32[1...) custom-call(s32[4]{0:T(128)} %pad_add_fusion.at, bf16[4,8,384]{2,1,0:T(8,128)(2,1)} %get-tuple-element.239.near_ref, ...), custom_call_target="tpu_custom_call" | custom-call | flops 100000000 | bytes 100000 | tf_op jit(solution)/shard_map/unpack/pallas_call | solution.py:249
  49.8 12.5 %collective-permute-done.11 = bf16[2,192,384]{2,1,0:T(8,128)(2,1)S(1)} collective-permute-done((bf16[2,192,384]{2,1,0:T(8,128)(2,1)}, bf16[2,192,384]{2,1,0:T(8,128)(2,1)S(1)}, u32[]{:S(2)}, u32[]{:S(2)}) %collective-permute-start.11) | collective-permute-done | bytes 294944 | tf_op jit(solution)/shard_map/ppermute | solution.py:141
  66.5 3.3 %collective-permute-done.12 = bf16[1,192,384]{2,1,0:T(8,128)(2,1)S(1)} collective-permute-done((bf16[1,192,384]{2,1,0:T(8,128)(2,1)S(1)}, bf16[1,192,384]{2,1,0:T(8,128)(2,1)S(1)}, u32[]{:S(2)}, u32[]{:S(2)}) %collective-permute-start.12) | collective-permute-done | bytes 147488 | tf_op jit(solution)/shard_map/ppermute | solution.py:141
  74.1 19.7 %attend.1 = (bf16[1024,2304]{1,0:T(8,128)(2,1)}, bf16[1024,768]{1,0:T(8,128)(2,1)}, f32[16,1024]{1,0:T(8,128)}, f32[1024,768]{1,0:T(8,128)}, bf16[768,2304]{1,0:T(8,128)(2,1)}, /*index=5*/bf16[768,768]{1,0:T(8,128)(2,1)}) custom-call(s32[16]{0:T(128)} %get-tuple-element.273.plan, s32[4]{0:T(128)} %pad_add_fusion.at, ...), custom_call_target="tpu_custom_call" | custom-call | flops 11000000512 | bytes 20000000 | tf_op jit(solution)/shard_map/attend/pallas_call | solution.py:464
  96.1 3.1 %collective-permute-done.19.refs_15_ = bf16[2,3,192,384]{3,2,1,0:T(8,128)(2,1)S(1)} collective-permute-done((bf16[2,3,192,384]{3,2,1,0:T(8,128)(2,1)S(1)}, bf16[2,3,192,384]{3,2,1,0:T(8,128)(2,1)S(1)}, u32[]{:S(2)}, u32[]{:S(2)}) %collective-permute-start.19) | collective-permute-done | bytes 884768 | tf_op jit(solution)/shard_map/ppermute | solution.py:141
  101.1 42.8 %feed.1 = (bf16[1024,768]{1,0:T(8,128)(2,1)}, f32[1024,768]{1,0:T(8,128)}, bf16[1024,768]{1,0:T(8,128)(2,1)}, f32[1,3072]{1,0:T(1,128)}, f32[8,768]{1,0:T(8,128)...) custom-call(s32[4]{0:T(128)} %pad_add_fusion.at, f32[1024,768]{1,0:T(8,128)} %get-tuple-element.294.refs_0_, ...), custom_call_target="tpu_custom_call" | custom-call | flops 28999999488 | bytes 40000000 | tf_op jit(solution)/shard_map/feed/pallas_call | solution.py:716
  144.1 8.0 %attend_back.2 = (bf16[1024,2304]{1,0:T(8,128)(2,1)}, f32[8,2304]{1,0:T(8,128)}) custom-call(s32[16]{0:T(128)} %get-tuple-element.273.plan, bf16[1024,2304]{1,0:T(8,128)(2,1)} %get-tuple-element.306.qkv_ref, bf16[1024,768]{1,0:T(8,128)(2,1)} %get-tuple-element.307.da_ref.refs_2_, f32[16,1024]{1,0:T(8,128)} %get-tuple-element.308.lse_ref, ...), custom_call_target="tpu_custom_call" | custom-call | flops 4000000000 | bytes 6000000 | tf_op jit(solution)/shard_map/attend_back/pallas_call | solution.py:823
  152.2 4.4 %add_convert_fusion = (bf16[8,192,384]{2,1,0:T(8,128)(2,1)}, bf16[8,192,384]{2,1,0:T(8,128)(2,1)}) fusion(bf16[32,192,384]{2,1,0:T(8,128)(2,1)} %collective-permute-done.21, bf16[32,192,384]{2,1,0:T(8,128)(2,1)} %get-tuple-element.304), kind=kLoop, calls=%fused_computation | loop fusion | flops 4718592 | bytes 7077888 | tf_op jit(solution)/shard_map/convert_element_type | solution.py:1124
  158.0 15.6 %attend_back.3 = (bf16[1024,2304]{1,0:T(8,128)(2,1)}, f32[8,2304]{1,0:T(8,128)}) custom-call(s32[16]{0:T(128)} %get-tuple-element.273.plan, bf16[1024,2304]{1,0:T(8,128)(2,1)} %get-tuple-element.306.qkv_ref, bf16[1024,768]{1,0:T(8,128)(2,1)} %get-tuple-element.307.da_ref.refs_2_, ...), custom_call_target="tpu_custom_call", output_to_operand_aliasing={{0}: (7, {})} | custom-call | flops 12000000000 | bytes 18000000 | tf_op jit(solution)/shard_map/attend_back/pallas_call | solution.py:823
  173.6 9.9 %project_back.1 = (bf16[1024,768]{1,0:T(8,128)(2,1)}, f32[8,768]{1,0:T(8,128)}) custom-call(bf16[1024,768]{1,0:T(8,128)(2,1)} %get-tuple-element.274.refs_0_.xp_ref, f32[1,768]{1,0:T(1,128)} %get-tuple-element.277.refs_3_.g1_ref.refs_4_, f32[1024,768]{1,0:T(8,128)} %get-tuple-element.315.dx1_ref, bf16[1024,2304]{1,0:T(8,128)(2,1)} %get-tuple-element.331.dqkv_ref.refs_3_, ...), custom_call_target="tpu_custom_call" | custom-call | tf_op jit(solution)/shard_map/project_back/pallas_call | solution.py:865
  185.6 2.1 add_convert_fusion.4
  189.4 12.4 %grads.1 = (bf16[32,104,384]{2,1,0:T(8,128)(2,1)}, bf16[32,104,384]{2,1,0:T(8,128)(2,1)}) custom-call(s32[4]{0:T(128)} %pad_add_fusion.at, bf16[1024,768]{1,0:T(8,128)(2,1)} %get-tuple-element.274.refs_0_.xp_ref, bf16[1024,768]{1,0:T(8,128)(2,1)} %get-tuple-element.330.refs_1_, bf16[1024,768]{1,0:T(8,128)(2,1)} %get-tuple-element.307.da_ref.refs_2_, ...), custom_call_target="tpu_custom_call" | custom-call | flops 5000000000 | bytes 12000000 | tf_op jit(solution)/shard_map/grads/pallas_call | solution.py:1006
  202.4 1.8 convert_add_fusion.6
  204.3 1.9 convert_add_fusion.7
  211.1 15.8 %collective-permute-done.29 = bf16[2,192,384]{2,1,0:T(8,128)(2,1)S(1)} collective-permute-done((bf16[2,192,384]{2,1,0:T(8,128)(2,1)S(1)}, bf16[2,192,384]{2,1,0:T(8,128)(2,1)S(1)}, u32[]{:S(2)}, u32[]{:S(2)}) %collective-permute-start.29) | collective-permute-done | bytes 294944 | tf_op jit(solution)/shard_map/ppermute | solution.py:141
  229.5 3.3 %collective-permute-start.33 = (bf16[2,192,384]{2,1,0:T(8,128)(2,1)}, bf16[2,192,384]{2,1,0:T(8,128)(2,1)}, u32[]{:S(2)}, u32[]{:S(2)}) collective-permute-start(bf16[2,192,384]{2,1,0:T(8,128)(2,1)} %pad_maximum_fusion.12), channel_id=1, source_target_pairs={{0,24},{1,25},{2,26},{3,27},{4,28},{5,29},{6,30},{7,31},{8,0},{9,1... | collective-permute-start | bytes 884744 | tf_op jit(solution)/shard_map/ppermute | solution.py:141
  232.8 8.2 %collective-permute-done.32 = bf16[2,192,384]{2,1,0:T(8,128)(2,1)} collective-permute-done((bf16[2,192,384]{2,1,0:T(8,128)(2,1)}, bf16[2,192,384]{2,1,0:T(8,128)(2,1)}, u32[]{:S(2)}, u32[]{:S(2)}) %collective-permute-start.32) | collective-permute-done | bytes 294944 | tf_op jit(solution)/shard_map/ppermute | solution.py:141
  241.1 2.6 collective-permute-done.33
  246.6 1.9 collective-permute-start.35
  248.5 2.7 collective-permute-start.36
  252.7 7.3 %restore.1 = (bf16[1024,768]{1,0:T(8,128)(2,1)}, bf16[1024,768]{1,0:T(8,128)(2,1)}) custom-call(s32[16]{0:T(128)} %get-tuple-element.273.plan, bf16[1024,768]{1,0:T(8,128)(2,1)} %get-tuple-element.377.outp_ref, bf16[1024,768]{1,0:T(8,128)(2,1)} %get-tuple-element.378.dxp_ref), custom_call_target="tpu_custom_call" | custom-call | flops 3300000000 | bytes 8000000 | tf_op jit(solution)/shard_map/restore/pallas_call | solution.py:1039
  263.1 3.4 %deliver_second.1 = (f32[96,3072]{1,0:T(8,128)}, f32[384,768]{1,0:T(8,128)}) custom-call(s32[4]{0:T(128)} %pad_add_fusion.at, bf16[2,2,192,384]{3,2,1,0:T(8,128)(2,1)} %copy-done.1, bf16[2,2,192,384]{3,2,1,0:T(8,128)(2,1)} %copy-done.7), custom_call_target="tpu_custom_call" | custom-call | bytes 4000000 | tf_op jit(solution)/shard_map/deliver_second/pallas_call | solution.py:1103
  267.0 1.6 collective-permute-done.40.other
  269.3 2.8 %deliver_first.1 = (f32[96,2304]{1,0:T(8,128)}, f32[96,768]{1,0:T(8,128)}, f32[96]{0:T(128)}, f32[96]{0:T(128)}, f32[288]{0:T(512)}, /*index=5*/f32[96]{0:T(128)...) custom-call(s32[4]{0:T(128)} %pad_add_fusion.at, bf16[2,2,104,384]{3,2,1,0:T(8,128)(2,1)} %copy-done.2, ...), custom_call_target="tpu_custom_call" | custom-call | bytes 2000000 | tf_op jit(solution)/shard_map/deliver_first/pallas_call | solution.py:1073
  (153 shorter events, 47.1 us)
Async XLA Ops:
  4.8 26.0 %collective-permute-start = (bf16[2,296,384]{2,1,0:T(8,128)(2,1)}, bf16[2,296,384]{2,1,0:T(8,128)(2,1)S(1)}, u32[]{:S(2)}, u32[]{:S(2)}) collective-permute-start(bf16[2,296,384]{2,1,0:T(8,128)(2,1)} %get-tuple-element.213), channel_id=1, source_target_pairs={{0,8},{1,9},{2,10},{3,11},{4,12},{5,13},{6,14},{7,15},{8,16},{9,17... | collective-permute-start | bytes 1363976 | tf_op jit(solution)/shard_map/ppermute | solution.py:141
  7.8 33.0 %collective-permute-start.6 = (bf16[2,2,296,384]{3,2,1,0:T(8,128)(2,1)}, bf16[2,2,296,384]{3,2,1,0:T(8,128)(2,1)}, u32[]{:S(2)}, u32[]{:S(2)}) collective-permute-start(bf16[2,2,296,384]{3,2,1,0:T(8,128)(2,1)} %get-tuple-element.228), channel_id=1, source_target_pairs={{0,4},{1,5},{2,6},{3,7},{4,0},{5,1},{6,2},{7,3},{8,12},{9,13},{10,... | collective-permute-start | bytes 2727944 | tf_op jit(solution)/shard_map/ppermute | solution.py:141
  9.3 14.6 %collective-permute-start.2 = (bf16[2,104,384]{2,1,0:T(8,128)(2,1)}, bf16[2,104,384]{2,1,0:T(8,128)(2,1)S(1)}, u32[]{:S(2)}, u32[]{:S(2)}) collective-permute-start(bf16[2,104,384]{2,1,0:T(8,128)(2,1)} %get-tuple-element.214), channel_id=1, source_target_pairs={{0,24},{1,25},{2,26},{3,27},{4,28},{5,29},{6,30},{7,31},{8,0},{9,1... | collective-permute-start | bytes 479240 | tf_op jit(solution)/shard_map/ppermute | solution.py:141
  11.6 19.2 %collective-permute-start.1 = (bf16[2,104,384]{2,1,0:T(8,128)(2,1)}, bf16[2,104,384]{2,1,0:T(8,128)(2,1)S(1)}, u32[]{:S(2)}, u32[]{:S(2)}) collective-permute-start(bf16[2,104,384]{2,1,0:T(8,128)(2,1)} %get-tuple-element.214), channel_id=1, source_target_pairs={{0,16},{1,17},{2,18},{3,19},{4,20},{5,21},{6,22},{7,23},{8,24},{9,... | collective-permute-start | bytes 479240 | tf_op jit(solution)/shard_map/ppermute | solution.py:141
  30.9 9.8 %collective-permute-start.5 = (bf16[2,192,384]{2,1,0:T(8,128)(2,1)}, bf16[2,192,384]{2,1,0:T(8,128)(2,1)S(1)}, u32[]{:S(2)}, u32[]{:S(2)}) collective-permute-start(bf16[2,192,384]{2,1,0:T(8,128)(2,1)} %get-tuple-element.249), channel_id=1, source_target_pairs={{0,24},{1,25},{2,26},{3,27},{4,28},{5,29},{6,30},{7,31},{8,0},{9,1... | collective-permute-start | bytes 884744 | tf_op jit(solution)/shard_map/ppermute | solution.py:141
  32.6 8.1 %collective-permute-start.4 = (bf16[3,104,384]{2,1,0:T(8,128)(2,1)S(1)}, bf16[3,104,384]{2,1,0:T(8,128)(2,1)S(1)}, u32[]{:S(2)}, u32[]{:S(2)}) collective-permute-start(bf16[3,104,384]{2,1,0:T(8,128)(2,1)S(1)} %pad_maximum_fusion.13), channel_id=1, source_target_pairs={{0,4},{1,5},{2,6},{3,7},{4,0},{5,1},{6,2},{7,3},{8,12},{9,13},{10,... | collective-permute-start | bytes 718856 | tf_op jit(solution)/shard_map/ppermute | solution.py:141
  43.6 19.5 %collective-permute-start.10 = (bf16[2,2,296,384]{3,2,1,0:T(8,128)(2,1)}, bf16[2,2,296,384]{3,2,1,0:T(8,128)(2,1)}, u32[]{:S(2)}, u32[]{:S(2)}) collective-permute-start(bf16[2,2,296,384]{3,2,1,0:T(8,128)(2,1)} %collective-permute-done.6.refs_9_.refs_8_), channel_id=1, source_target_pairs={{0,1},{1,0},{2,3},{3,2},{4,5},{5,4},{6,7},{7,6},{8,9},{9,8},{10,11... | collective-permute-start | bytes 2727944 | tf_op jit(solution)/shard_map/ppermute | solution.py:141
  43.6 19.5 %collective-permute-start.9 = (bf16[2,2,3,96,384]{4,3,2,1,0:T(8,128)(2,1)S(1)}, bf16[2,2,3,96,384]{4,3,2,1,0:T(8,128)(2,1)}, u32[]{:S(2)}, u32[]{:S(2)}) collective-permute-start(bf16[2,2,3,96,384]{4,3,2,1,0:T(8,128)(2,1)S(1)} %pad_maximum_fusion.refs_11_.refs_13_), channel_id=1, source_target_pairs={{0,1},{1,0},{2,3},{3,2},{4,5},{5,4},{6,7},{7,6},{8,9},{9,8},{10,11... | collective-permute-start | bytes 2654216 | tf_op jit(solution)/shard_map/ppermute | solution.py:141
  44.1 18.6 %collective-permute-start.7 = (bf16[20,48,384]{2,1,0:T(8,128)(2,1)}, bf16[20,48,384]{2,1,0:T(8,128)(2,1)S(1)}, u32[]{:S(2)}, u32[]{:S(2)}) collective-permute-start(bf16[20,48,384]{2,1,0:T(8,128)(2,1)} %pad_maximum_fusion.4), channel_id=1, source_target_pairs={{0,4},{1,5},{2,6},{3,7},{4,0},{5,1},{6,2},{7,3},{8,12},{9,13},{10,... | collective-permute-start | bytes 2211848 | tf_op jit(solution)/shard_map/ppermute | solution.py:141
  45.0 18.1 %collective-permute-start.8 = (bf16[20,48,384]{2,1,0:T(8,128)(2,1)S(1)}, bf16[20,48,384]{2,1,0:T(8,128)(2,1)S(1)}, u32[]{:S(2)}, u32[]{:S(2)}) collective-permute-start(bf16[20,48,384]{2,1,0:T(8,128)(2,1)S(1)} %pad_maximum_fusion.5), channel_id=1, source_target_pairs={{0,2},{1,3},{2,0},{3,1},{4,6},{5,7},{6,4},{7,5},{8,10},{9,11},{10,... | collective-permute-start | bytes 2211848 | tf_op jit(solution)/shard_map/ppermute | solution.py:141
  46.5 15.8 %collective-permute-start.11 = (bf16[2,192,384]{2,1,0:T(8,128)(2,1)}, bf16[2,192,384]{2,1,0:T(8,128)(2,1)S(1)}, u32[]{:S(2)}, u32[]{:S(2)}) collective-permute-start(bf16[2,192,384]{2,1,0:T(8,128)(2,1)} %get-tuple-element.249), channel_id=1, source_target_pairs={{0,16},{1,17},{2,18},{3,19},{4,20},{5,21},{6,22},{7,23},{8,24},{9,... | collective-permute-start | bytes 884744 | tf_op jit(solution)/shard_map/ppermute | solution.py:141
  63.4 7.7 %collective-permute-start.14 = (bf16[2,2,3,96,384]{4,3,2,1,0:T(8,128)(2,1)S(1)}, bf16[2,2,3,96,384]{4,3,2,1,0:T(8,128)(2,1)S(1)}, u32[]{:S(2)}, u32[]{:S(2)}) collective-permute-start(bf16[2,2,3,96,384]{4,3,2,1,0:T(8,128)(2,1)S(1)} %pad_maximum_fusion.1.refs_12_.refs_14_), channel_id=1, source_target_pairs={{0,1},{1,0},{2,3},{3,2},{4,5},{5,4},{6,7},{7,6},{8,9},{9,8},{10,11... | collective-permute-start | bytes 2654216 | tf_op jit(solution)/shard_map/ppermute | solution.py:141
  72.1 21.7 %collective-permute-start.17 = (bf16[2,3,192,384]{3,2,1,0:T(8,128)(2,1)S(1)}, bf16[2,3,192,384]{3,2,1,0:T(8,128)(2,1)S(1)}, u32[]{:S(2)}, u32[]{:S(2)}) collective-permute-start(bf16[2,3,192,384]{3,2,1,0:T(8,128)(2,1)S(1)} %pad_maximum_fusion.2.refs_10_), channel_id=1, source_target_pairs={{0,1},{1,0},{2,3},{3,2},{4,5},{5,4},{6,7},{7,6},{8,9},{9,8},{10,11... | collective-permute-start | bytes 2654216 | tf_op jit(solution)/shard_map/ppermute | solution.py:141
  72.2 22.1 %collective-permute-start.15 = (bf16[2,3,192,384]{3,2,1,0:T(8,128)(2,1)S(1)}, bf16[2,3,192,384]{3,2,1,0:T(8,128)(2,1)S(1)}, u32[]{:S(2)}, u32[]{:S(2)}) collective-permute-start(bf16[2,3,192,384]{3,2,1,0:T(8,128)(2,1)S(1)} %pad_maximum_fusion.2.refs_10_), channel_id=1, source_target_pairs={{0,4},{1,5},{2,6},{3,7},{4,0},{5,1},{6,2},{7,3},{8,12},{9,13},{10,... | collective-permute-start | bytes 2654216 | tf_op jit(solution)/shard_map/ppermute | solution.py:141
  73.4 20.8 %collective-permute-start.18 = (bf16[2,3,192,384]{3,2,1,0:T(8,128)(2,1)S(1)}, bf16[2,3,192,384]{3,2,1,0:T(8,128)(2,1)}, u32[]{:S(2)}, u32[]{:S(2)}) collective-permute-start(bf16[2,3,192,384]{3,2,1,0:T(8,128)(2,1)S(1)} %pad_maximum_fusion.3.refs_12_), channel_id=1, source_target_pairs={{0,1},{1,0},{2,3},{3,2},{4,5},{5,4},{6,7},{7,6},{8,9},{9,8},{10,11... | collective-permute-start | bytes 2654216 | tf_op jit(solution)/shard_map/ppermute | solution.py:141
  73.6 22.0 %collective-permute-start.16 = (bf16[2,3,192,384]{3,2,1,0:T(8,128)(2,1)S(1)}, bf16[2,3,192,384]{3,2,1,0:T(8,128)(2,1)}, u32[]{:S(2)}, u32[]{:S(2)}) collective-permute-start(bf16[2,3,192,384]{3,2,1,0:T(8,128)(2,1)S(1)} %pad_maximum_fusion.3.refs_12_), channel_id=1, source_target_pairs={{0,2},{1,3},{2,0},{3,1},{4,6},{5,7},{6,4},{7,5},{8,10},{9,11},{10,... | collective-permute-start | bytes 2654216 | tf_op jit(solution)/shard_map/ppermute | solution.py:141
  143.9 8.3 %collective-permute-start.21 = (bf16[32,192,384]{2,1,0:T(8,128)(2,1)}, bf16[32,192,384]{2,1,0:T(8,128)(2,1)}, u32[]{:S(2)}, u32[]{:S(2)}) collective-permute-start(bf16[32,192,384]{2,1,0:T(8,128)(2,1)} %get-tuple-element.305), channel_id=1, source_target_pairs={{0,1},{1,0},{2,3},{3,2},{4,5},{5,4},{6,7},{7,6},{8,9},{9,8},{10,11... | collective-permute-start | bytes 14155784 | tf_op jit(solution)/shard_map/ppermute | solution.py:141
  156.6 28.4 %collective-permute-start.22 = (bf16[8,192,384]{2,1,0:T(8,128)(2,1)}, bf16[8,192,384]{2,1,0:T(8,128)(2,1)S(1)}, u32[]{:S(2)}, u32[]{:S(2)}) collective-permute-start(bf16[8,192,384]{2,1,0:T(8,128)(2,1)} %get-tuple-element.313), channel_id=1, source_target_pairs={{0,4},{1,5},{2,6},{3,7},{4,0},{5,1},{6,2},{7,3},{8,12},{9,13},{10,... | collective-permute-start | bytes 3538952 | tf_op jit(solution)/shard_map/ppermute | solution.py:141
  157.5 28.1 %collective-permute-start.23 = (bf16[8,192,384]{2,1,0:T(8,128)(2,1)}, bf16[8,192,384]{2,1,0:T(8,128)(2,1)S(1)}, u32[]{:S(2)}, u32[]{:S(2)}) collective-permute-start(bf16[8,192,384]{2,1,0:T(8,128)(2,1)} %get-tuple-element.314), channel_id=1, source_target_pairs={{0,2},{1,3},{2,0},{3,1},{4,6},{5,7},{6,4},{7,5},{8,10},{9,11},{10,... | collective-permute-start | bytes 3538952 | tf_op jit(solution)/shard_map/ppermute | solution.py:141
  187.7 14.6 %collective-permute-start.24 = (bf16[4,192,384]{2,1,0:T(8,128)(2,1)S(1)}, bf16[4,192,384]{2,1,0:T(8,128)(2,1)}, u32[]{:S(2)}, u32[]{:S(2)}) collective-permute-start(bf16[4,192,384]{2,1,0:T(8,128)(2,1)S(1)} %get-tuple-element.328), channel_id=1, source_target_pairs={{0,2},{1,3},{2,0},{3,1},{4,6},{5,7},{6,4},{7,5},{8,10},{9,11},{10,... | collective-permute-start | bytes 1769480 | tf_op jit(solution)/shard_map/ppermute | solution.py:141
  188.2 14.2 %collective-permute-start.25 = (bf16[4,192,384]{2,1,0:T(8,128)(2,1)S(1)}, bf16[4,192,384]{2,1,0:T(8,128)(2,1)}, u32[]{:S(2)}, u32[]{:S(2)}) collective-permute-start(bf16[4,192,384]{2,1,0:T(8,128)(2,1)S(1)} %get-tuple-element.329), channel_id=1, source_target_pairs={{0,4},{1,5},{2,6},{3,7},{4,0},{5,1},{6,2},{7,3},{8,12},{9,13},{10,... | collective-permute-start | bytes 1769480 | tf_op jit(solution)/shard_map/ppermute | solution.py:141
  208.1 18.8 %collective-permute-start.27 = (bf16[8,104,384]{2,1,0:T(8,128)(2,1)S(1)}, bf16[8,104,384]{2,1,0:T(8,128)(2,1)S(1)}, u32[]{:S(2)}, u32[]{:S(2)}) collective-permute-start(bf16[8,104,384]{2,1,0:T(8,128)(2,1)S(1)} %get-tuple-element.347), channel_id=1, source_target_pairs={{0,4},{1,5},{2,6},{3,7},{4,0},{5,1},{6,2},{7,3},{8,12},{9,13},{10,... | collective-permute-start | bytes 1916936 | tf_op jit(solution)/shard_map/ppermute | solution.py:141
  209.3 17.6 %collective-permute-start.28 = (bf16[8,104,384]{2,1,0:T(8,128)(2,1)S(1)}, bf16[8,104,384]{2,1,0:T(8,128)(2,1)S(1)}, u32[]{:S(2)}, u32[]{:S(2)}) collective-permute-start(bf16[8,104,384]{2,1,0:T(8,128)(2,1)S(1)} %get-tuple-element.348), channel_id=1, source_target_pairs={{0,2},{1,3},{2,0},{3,1},{4,6},{5,7},{6,4},{7,5},{8,10},{9,11},{10,... | collective-permute-start | bytes 1916936 | tf_op jit(solution)/shard_map/ppermute | solution.py:141
  210.9 16.1 %collective-permute-start.29 = (bf16[2,192,384]{2,1,0:T(8,128)(2,1)S(1)}, bf16[2,192,384]{2,1,0:T(8,128)(2,1)S(1)}, u32[]{:S(2)}, u32[]{:S(2)}) collective-permute-start(bf16[2,192,384]{2,1,0:T(8,128)(2,1)S(1)} %pad_maximum_fusion.11), channel_id=1, source_target_pairs={{0,16},{1,17},{2,18},{3,19},{4,20},{5,21},{6,22},{7,23},{8,24},{9,... | collective-permute-start | bytes 884744 | tf_op jit(solution)/shard_map/ppermute | solution.py:141
  227.7 16.0 %collective-permute-start.30 = (bf16[4,104,384]{2,1,0:T(8,128)(2,1)S(1)}, bf16[4,104,384]{2,1,0:T(8,128)(2,1)S(1)}, u32[]{:S(2)}, u32[]{:S(2)}) collective-permute-start(bf16[4,104,384]{2,1,0:T(8,128)(2,1)S(1)} %get-tuple-element.358), channel_id=1, source_target_pairs={{0,2},{1,3},{2,0},{3,1},{4,6},{5,7},{6,4},{7,5},{8,10},{9,11},{10,... | collective-permute-start | bytes 958472 | tf_op jit(solution)/shard_map/ppermute | solution.py:141
  228.2 15.5 %collective-permute-start.31 = (bf16[4,104,384]{2,1,0:T(8,128)(2,1)S(1)}, bf16[4,104,384]{2,1,0:T(8,128)(2,1)S(1)}, u32[]{:S(2)}, u32[]{:S(2)}) collective-permute-start(bf16[4,104,384]{2,1,0:T(8,128)(2,1)S(1)} %get-tuple-element.359), channel_id=1, source_target_pairs={{0,4},{1,5},{2,6},{3,7},{4,0},{5,1},{6,2},{7,3},{8,12},{9,13},{10,... | collective-permute-start | bytes 958472 | tf_op jit(solution)/shard_map/ppermute | solution.py:141
  229.0 12.1 %collective-permute-start.32 = (bf16[2,192,384]{2,1,0:T(8,128)(2,1)}, bf16[2,192,384]{2,1,0:T(8,128)(2,1)}, u32[]{:S(2)}, u32[]{:S(2)}) collective-permute-start(bf16[2,192,384]{2,1,0:T(8,128)(2,1)} %pad_maximum_fusion.10), channel_id=1, source_target_pairs={{0,8},{1,9},{2,10},{3,11},{4,12},{5,13},{6,14},{7,15},{8,16},{9,17... | collective-permute-start | bytes 884744 | tf_op jit(solution)/shard_map/ppermute | solution.py:141
  229.5 14.1 %collective-permute-start.33 = (bf16[2,192,384]{2,1,0:T(8,128)(2,1)}, bf16[2,192,384]{2,1,0:T(8,128)(2,1)}, u32[]{:S(2)}, u32[]{:S(2)}) collective-permute-start(bf16[2,192,384]{2,1,0:T(8,128)(2,1)} %pad_maximum_fusion.12), channel_id=1, source_target_pairs={{0,24},{1,25},{2,26},{3,27},{4,28},{5,29},{6,30},{7,31},{8,0},{9,1... | collective-permute-start | bytes 884744 | tf_op jit(solution)/shard_map/ppermute | solution.py:141
  245.8 14.2 %collective-permute-start.34 = (bf16[2,104,384]{2,1,0:T(8,128)(2,1)S(1)}, bf16[2,104,384]{2,1,0:T(8,128)(2,1)S(1)}, u32[]{:S(2)}, u32[]{:S(2)}) collective-permute-start(bf16[2,104,384]{2,1,0:T(8,128)(2,1)S(1)} %pad_maximum_fusion.15), channel_id=1, source_target_pairs={{0,8},{1,9},{2,10},{3,11},{4,12},{5,13},{6,14},{7,15},{8,16},{9,17... | collective-permute-start | bytes 479240 | tf_op jit(solution)/shard_map/ppermute | solution.py:141
  246.6 13.4 %collective-permute-start.35 = (bf16[2,104,384]{2,1,0:T(8,128)(2,1)S(1)}, bf16[2,104,384]{2,1,0:T(8,128)(2,1)S(1)}, u32[]{:S(2)}, u32[]{:S(2)}) collective-permute-start(bf16[2,104,384]{2,1,0:T(8,128)(2,1)S(1)} %pad_maximum_fusion.16), channel_id=1, source_target_pairs={{0,16},{1,17},{2,18},{3,19},{4,20},{5,21},{6,22},{7,23},{8,24},{9,... | collective-permute-start | bytes 479240 | tf_op jit(solution)/shard_map/ppermute | solution.py:141
  248.5 11.5 %collective-permute-start.36 = (bf16[2,104,384]{2,1,0:T(8,128)(2,1)S(1)}, bf16[2,104,384]{2,1,0:T(8,128)(2,1)S(1)}, u32[]{:S(2)}, u32[]{:S(2)}) collective-permute-start(bf16[2,104,384]{2,1,0:T(8,128)(2,1)S(1)} %pad_maximum_fusion.17), channel_id=1, source_target_pairs={{0,24},{1,25},{2,26},{3,27},{4,28},{5,29},{6,30},{7,31},{8,0},{9,1... | collective-permute-start | bytes 479240 | tf_op jit(solution)/shard_map/ppermute | solution.py:141
  251.1 8.8 %collective-permute-start.37 = (bf16[2,192,384]{2,1,0:T(8,128)(2,1)S(1)}, bf16[2,192,384]{2,1,0:T(8,128)(2,1)S(1)}, u32[]{:S(2)}, u32[]{:S(2)}) collective-permute-start(bf16[2,192,384]{2,1,0:T(8,128)(2,1)S(1)} %fusion.2), channel_id=1, source_target_pairs={{0,2},{1,3},{2,0},{3,1},{4,6},{5,7},{6,4},{7,5},{8,10},{9,11},{10,... | collective-permute-start | bytes 884744 | tf_op jit(solution)/shard_map/ppermute | solution.py:141
  (25 other events, 133.3 us)

commit v6 on v5

--- a/solution.py
+++ b/solution.py
@@ -167,7 +167,7 @@
     wqkv, wout, wup, wdown = refs[:4]
     vectors, (near1, near2, near, side, packed) = refs[4:12], refs[12:]
     width = wout.shape[1]
-    rows = wout.shape[0] // 2
+    rows = wout.shape[0]
     packed[...] = jnp.zeros_like(packed)
     for ref, start in zip(vectors, SLOTS):
         packed[:, start : start + ref.shape[0]] = ref[...].reshape(1, -1)
@@ -175,16 +175,15 @@
     for i in range(4):
         part = jnp.broadcast_to(packed[:, i * COLUMNS : (i + 1) * COLUMNS], (8, COLUMNS))
         tail = jnp.where(iota((8, COLUMNS), 0) == i, part, tail)
-    mine = at_rows(at[3] * rows, rows)
     for y in range(2):
         for b in range(4):
             ref, base = (wqkv, b * width) if b < 3 else (wout, 0)
             start = base + y * COLUMNS
-            side[y, b // 2, (b % 2) * rows : (b % 2 + 1) * rows, :] = ref[mine, start : start + COLUMNS]
+            side[y, b // 2, (b % 2) * rows : (b % 2 + 1) * rows, :] = ref[:, start : start + COLUMNS]
             start = b * width + y * COLUMNS
-            side[y, 0, (2 + b) * rows : (3 + b) * rows, :] = wup[mine, start : start + COLUMNS]
+            side[y, 0, (2 + b) * rows : (3 + b) * rows, :] = wup[:, start : start + COLUMNS]
         here = slice(y * COLUMNS, (y + 1) * COLUMNS)
-        side[y, 1, 2 * rows : 6 * rows, :] = wdown[at_rows(at[3] * 4 * rows, 4 * rows), here]
+        side[y, 1, 2 * rows : 6 * rows, :] = wdown[:, here]
         for h in range(2):
             side[y, h, 6 * rows : 6 * rows + 8, :] = tail
     near1[:, 0 : 2 * rows, :] = side[at[2], :, 0 : 2 * rows, :]
@@ -204,10 +203,11 @@
         (2, 2, 6 * rows + 8, COLUMNS),
     ]
     matrices = (wqkv, wout, wup, wdown)
+    mine = lambda v: pl.BlockSpec((v.shape[0] // 2, v.shape[1]), lambda i, at: (at[3], 0))
     return call(
         quarters_kernel,
         (1,),
-        [full(v.shape) for v in matrices + tuple(vectors)],
+        [mine(v) for v in matrices] + [full(v.shape) for v in vectors],
         [full(s) for s in shapes],
         [shape_of(s, BF16) for s in shapes],
         [pltpu.VMEM((1, PACKED), BF16)],
@@ -1215,9 +1215,7 @@
         early = [stack(q[h] for q in (z2_one, z2_three)) for h in range(2)]
         unit = lambda v: v.reshape(-1, count // 2, COLUMNS)
         to_x, to_y = (jnp.concatenate([unit(near1[h]), unit(early[1 - h])]) for h in range(2))
-        near1, to_x, to_y, rows, far_rows, near2, far_side, early = tie(
-            (near1, to_x, to_y, rows, far_rows, near2, far_side, early)
-        )
+        to_x, to_y, near2, far_side = tie((to_x, to_y, near2, far_side))
         by_x, by_y = over_x(to_x), over_y(to_y)
         near_core1, core_side = over_core(near1), over_core(far_side)
         z2_two = move(near2, ALONG_Z[2])
@@ -1297,8 +1295,8 @@
         at_z = lambda d: stack([parts[0][d] + by_y[d], parts[1][d] + by_x[d]])
         to_z1 = [low(at_z(d)) for d in range(1, Z_SIZE)]
         group1.own = at_z(0)
+        to_z1, z2, outp, dxp = tie((to_z1, z2, outp, dxp))
         total2 = group2.total(z2)
-        to_z1, total2, outp, dxp = tie((to_z1, total2, outp, dxp))
         z1 = to_z(to_z1)
         by_y = over_y(total2)
         layer_out, input_grad = restore(plan, outp, dxp)

time: 273 us -> 271 us (level)
  waiting for transfers between devices: 69.9 us -> 66.2 us
    ppermute x41, waiting for transfers between devices: 69.9 us -> 66.2 us  [move(): return lax.ppermute(array, AXES, table)]
  transfers between devices with their start and end apart: 41 -> 41, of which waited for: 23 -> 20; matrix products, arithmetic and copies ran while one was open for 2% -> 4% of each run, Pallas kernels for 32% -> 33%
where the time goes in v6:
time: 271 us
  Pallas kernels  137 us (51%)
  waiting for transfers between devices  66.2 us (24%)
  starting transfers between devices  40.3 us (15%)
  other arithmetic  18.1 us (7%)
  local copies, waits for them, and re-layouts  7.41 us (3%)
    ppermute x41, waiting for transfers between devices, move(): return lax.ppermute(array, AXES, table)  66.2 us
    pallas_call x1, Pallas kernels, feed(): call(functools.partial(feed_kernel, block=length // 2, pieces=pieces, ste...  42.8 us
    ppermute x41, starting transfers between devices, move(): return lax.ppermute(array, AXES, table)  40.3 us
    pallas_call x2, Pallas kernels, attend_back(): call(functools.partial(attend_back_kernel, base=base, count=count), (coun...  23.6 us
    pallas_call x1, Pallas kernels, attend(): call(functools.partial(attend_kernel, pieces=pieces), (GENES + 1,), [full...  19.6 us
    pallas_call x1, Pallas kernels, grads(): call(functools.partial(grads_kernel, pieces=pieces), (4,), [ANY] * 4 + [f...  12.4 us
    pallas_call x1, Pallas kernels, project_back(): call(project_back_kernel, (GENES,), [rows_of((span, width)), full((1, wid...  9.91 us
    pallas_call x1, Pallas kernels, prepare(): call(prepare_kernel, (GENES,), [full((1, length)), full((length, width)),...  8.7 us
  transfers between devices with their start and end apart: 41, of which 20 were waited for; matrix products, arithmetic and copies ran while one was open for 4% of the time, Pallas kernels for 33%

profile of v6, /device:TPU:0, one launch (start us, length us, event | category | flops | bytes accessed | tf_op | source)
XLA Modules:
  0.0 270.5 jit_solution(10628570639814710399)
XLA Ops:
  1.3 3.2 %quarters.1 = (bf16[2,104,384]{2,1,0:T(8,128)(2,1)}, bf16[2,192,384]{2,1,0:T(8,128)(2,1)}, bf16[2,296,384]{2,1,0:T(8,128)(2,1)}, bf16[2,2,296,384]{3,2,1,0:T(8,128)(2,1)}) custom-call(s32[4]{0:T(128)} %pad_add_fusion.at, bf16[96,2304]{1,0:T(8,128)(2,1)} %refs_7_.3, bf16[96,768]{1,0:T(8,128)(2,1)} %refs_8_.2, bf16[96,3072]{1,0:T(8,128)(2,1)} %refs_6_.3, ...), custom_call_target="tpu_custom_call" | custom-call | bytes 6000000 | tf_op jit(solution)/shard_map/quarters/pallas_call | solution.py:207
  4.6 3.0 %collective-permute-start = (bf16[2,296,384]{2,1,0:T(8,128)(2,1)}, bf16[2,296,384]{2,1,0:T(8,128)(2,1)S(1)}, u32[]{:S(2)}, u32[]{:S(2)}) collective-permute-start(bf16[2,296,384]{2,1,0:T(8,128)(2,1)} %get-tuple-element.210), channel_id=1, source_target_pairs={{0,8},{1,9},{2,10},{3,11},{4,12},{5,13},{6,14},{7,15},{8,16},{9,17... | collective-permute-start | bytes 1363976 | tf_op jit(solution)/shard_map/ppermute | solution.py:141
  9.1 2.2 collective-permute-start.2
  12.1 8.7 %prepare.1 = (s32[16]{0:T(128)}, bf16[1024,768]{1,0:T(8,128)(2,1)}, bf16[1024,768]{1,0:T(8,128)(2,1)}, f32[1024,128]{1,0:T(8,128)}, f32[1024,128]{1,0:T(8,128)}) custom-call(s32[1,1024]{1,0:T(1,128)} %seg_ref.1, bf16[1024,768]{1,0:T(8,128)(2,1)} %bitcast.60, bf16[1024,768]{1,0:T(8,128)(2,1)} %bitcast.61, f32[1,128]{1,0:T(1,128)} %constant.47.clone.freq_ref), custom_call_target="tpu_custom_call" | custom-call | flops 3300000000 | bytes 8000000 | tf_op jit(solution)/shard_map/prepare/pallas_call | solution.py:310
  20.8 2.9 %collective-permute-done.2 = bf16[2,104,384]{2,1,0:T(8,128)(2,1)S(1)} collective-permute-done((bf16[2,104,384]{2,1,0:T(8,128)(2,1)}, bf16[2,104,384]{2,1,0:T(8,128)(2,1)S(1)}, u32[]{:S(2)}, u32[]{:S(2)}) %collective-permute-start.2) | collective-permute-done | bytes 159776 | tf_op jit(solution)/shard_map/ppermute | solution.py:141
  23.7 6.8 %collective-permute-done.1 = bf16[2,104,384]{2,1,0:T(8,128)(2,1)S(1)} collective-permute-done((bf16[2,104,384]{2,1,0:T(8,128)(2,1)}, bf16[2,104,384]{2,1,0:T(8,128)(2,1)S(1)}, u32[]{:S(2)}, u32[]{:S(2)}) %collective-permute-start.1) | collective-permute-done | bytes 159776 | tf_op jit(solution)/shard_map/ppermute | solution.py:141
  30.7 1.7 collective-permute-start.5
  35.5 4.4 %collective-permute-done.3 = bf16[3,96,384]{2,1,0:T(8,128)(2,1)S(1)} collective-permute-done((bf16[3,96,384]{2,1,0:T(8,128)(2,1)S(1)}, bf16[3,96,384]{2,1,0:T(8,128)(2,1)S(1)}, u32[]{:S(2)}, u32[]{:S(2)}) %collective-permute-start.3) | collective-permute-done | bytes 221216 | tf_op jit(solution)/shard_map/ppermute | solution.py:141
  49.0 3.2 %unpack.1 = (f32[1,768]{1,0:T(1,128)}, f32[1,768]{1,0:T(1,128)}, f32[1,2304]{1,0:T(1,128)}, f32[1,768]{1,0:T(1,128)}, f32[1,768]{1,0:T(1,128)}, /*index=5*/f32[1...) custom-call(s32[4]{0:T(128)} %pad_add_fusion.at, bf16[4,8,384]{2,1,0:T(8,128)(2,1)} %pad_maximum_fusion.18.near_ref, ...), custom_call_target="tpu_custom_call" | custom-call | flops 100000000 | bytes 100000 | tf_op jit(solution)/shard_map/unpack/pallas_call | solution.py:249
  52.3 11.1 %collective-permute-done.11 = bf16[2,192,384]{2,1,0:T(8,128)(2,1)S(1)} collective-permute-done((bf16[2,192,384]{2,1,0:T(8,128)(2,1)}, bf16[2,192,384]{2,1,0:T(8,128)(2,1)S(1)}, u32[]{:S(2)}, u32[]{:S(2)}) %collective-permute-start.11) | collective-permute-done | bytes 294944 | tf_op jit(solution)/shard_map/ppermute | solution.py:141
  65.3 4.8 %collective-permute-done.12 = bf16[1,192,384]{2,1,0:T(8,128)(2,1)S(1)} collective-permute-done((bf16[1,192,384]{2,1,0:T(8,128)(2,1)S(1)}, bf16[1,192,384]{2,1,0:T(8,128)(2,1)S(1)}, u32[]{:S(2)}, u32[]{:S(2)}) %collective-permute-start.12) | collective-permute-done | bytes 147488 | tf_op jit(solution)/shard_map/ppermute | solution.py:141
  74.1 19.6 %attend.1 = (bf16[1024,2304]{1,0:T(8,128)(2,1)}, bf16[1024,768]{1,0:T(8,128)(2,1)}, f32[16,1024]{1,0:T(8,128)}, f32[1024,768]{1,0:T(8,128)}, bf16[768,2304]{1,0:T(8,128)(2,1)}, /*index=5*/bf16[768,768]{1,0:T(8,128)(2,1)}) custom-call(s32[16]{0:T(128)} %get-tuple-element.265.plan, s32[4]{0:T(128)} %pad_add_fusion.at, ...), custom_call_target="tpu_custom_call" | custom-call | flops 11000000512 | bytes 20000000 | tf_op jit(solution)/shard_map/attend/pallas_call | solution.py:464
  95.1 3.1 %collective-permute-done.19.refs_15_ = bf16[2,3,192,384]{3,2,1,0:T(8,128)(2,1)S(1)} collective-permute-done((bf16[2,3,192,384]{3,2,1,0:T(8,128)(2,1)S(1)}, bf16[2,3,192,384]{3,2,1,0:T(8,128)(2,1)S(1)}, u32[]{:S(2)}, u32[]{:S(2)}) %collective-permute-start.19) | collective-permute-done | bytes 884768 | tf_op jit(solution)/shard_map/ppermute | solution.py:141
  100.0 42.8 %feed.1 = (bf16[1024,768]{1,0:T(8,128)(2,1)}, f32[1024,768]{1,0:T(8,128)}, bf16[1024,768]{1,0:T(8,128)(2,1)}, f32[1,3072]{1,0:T(1,128)}, f32[8,768]{1,0:T(8,128)...) custom-call(s32[4]{0:T(128)} %pad_add_fusion.at, f32[1024,768]{1,0:T(8,128)} %get-tuple-element.286.refs_0_, ...), custom_call_target="tpu_custom_call" | custom-call | flops 28999999488 | bytes 40000000 | tf_op jit(solution)/shard_map/feed/pallas_call | solution.py:716
  143.1 8.0 %attend_back.2 = (bf16[1024,2304]{1,0:T(8,128)(2,1)}, f32[8,2304]{1,0:T(8,128)}) custom-call(s32[16]{0:T(128)} %get-tuple-element.265.plan, bf16[1024,2304]{1,0:T(8,128)(2,1)} %get-tuple-element.298.qkv_ref, bf16[1024,768]{1,0:T(8,128)(2,1)} %get-tuple-element.299.da_ref.refs_2_, f32[16,1024]{1,0:T(8,128)} %get-tuple-element.300.lse_ref, ...), custom_call_target="tpu_custom_call" | custom-call | flops 4000000000 | bytes 6000000 | tf_op jit(solution)/shard_map/attend_back/pallas_call | solution.py:823
  151.2 4.4 %add_convert_fusion = (bf16[8,192,384]{2,1,0:T(8,128)(2,1)}, bf16[8,192,384]{2,1,0:T(8,128)(2,1)}) fusion(bf16[32,192,384]{2,1,0:T(8,128)(2,1)} %collective-permute-done.21, bf16[32,192,384]{2,1,0:T(8,128)(2,1)} %get-tuple-element.296), kind=kLoop, calls=%fused_computation | loop fusion | flops 4718592 | bytes 7077888 | tf_op jit(solution)/shard_map/convert_element_type | solution.py:1124
  158.4 15.6 %attend_back.3 = (bf16[1024,2304]{1,0:T(8,128)(2,1)}, f32[8,2304]{1,0:T(8,128)}) custom-call(s32[16]{0:T(128)} %get-tuple-element.265.plan, bf16[1024,2304]{1,0:T(8,128)(2,1)} %get-tuple-element.298.qkv_ref, bf16[1024,768]{1,0:T(8,128)(2,1)} %get-tuple-element.299.da_ref.refs_2_, ...), custom_call_target="tpu_custom_call", output_to_operand_aliasing={{0}: (7, {})} | custom-call | flops 12000000000 | bytes 18000000 | tf_op jit(solution)/shard_map/attend_back/pallas_call | solution.py:823
  174.0 9.9 %project_back.1 = (bf16[1024,768]{1,0:T(8,128)(2,1)}, f32[8,768]{1,0:T(8,128)}) custom-call(bf16[1024,768]{1,0:T(8,128)(2,1)} %get-tuple-element.266.refs_0_.xp_ref, f32[1,768]{1,0:T(1,128)} %get-tuple-element.269.refs_3_.g1_ref.refs_4_, f32[1024,768]{1,0:T(8,128)} %get-tuple-element.307.dx1_ref, bf16[1024,2304]{1,0:T(8,128)(2,1)} %get-tuple-element.323.dqkv_ref.refs_3_, ...), custom_call_target="tpu_custom_call" | custom-call | tf_op jit(solution)/shard_map/project_back/pallas_call | solution.py:865
  185.0 2.1 add_convert_fusion.4
  189.4 12.4 %grads.1 = (bf16[32,104,384]{2,1,0:T(8,128)(2,1)}, bf16[32,104,384]{2,1,0:T(8,128)(2,1)}) custom-call(s32[4]{0:T(128)} %pad_add_fusion.at, bf16[1024,768]{1,0:T(8,128)(2,1)} %get-tuple-element.266.refs_0_.xp_ref, bf16[1024,768]{1,0:T(8,128)(2,1)} %get-tuple-element.322.refs_1_, bf16[1024,768]{1,0:T(8,128)(2,1)} %get-tuple-element.299.da_ref.refs_2_, ...), custom_call_target="tpu_custom_call" | custom-call | flops 5000000000 | bytes 12000000 | tf_op jit(solution)/shard_map/grads/pallas_call | solution.py:1006
  202.9 1.8 convert_add_fusion.6
  204.7 1.9 convert_add_fusion.7
  210.1 15.5 %collective-permute-done.29 = bf16[2,192,384]{2,1,0:T(8,128)(2,1)S(1)} collective-permute-done((bf16[2,192,384]{2,1,0:T(8,128)(2,1)S(1)}, bf16[2,192,384]{2,1,0:T(8,128)(2,1)S(1)}, u32[]{:S(2)}, u32[]{:S(2)}) %collective-permute-start.29) | collective-permute-done | bytes 294944 | tf_op jit(solution)/shard_map/ppermute | solution.py:141
  228.2 3.8 %collective-permute-start.33 = (bf16[2,192,384]{2,1,0:T(8,128)(2,1)}, bf16[2,192,384]{2,1,0:T(8,128)(2,1)}, u32[]{:S(2)}, u32[]{:S(2)}) collective-permute-start(bf16[2,192,384]{2,1,0:T(8,128)(2,1)} %pad_maximum_fusion.12), channel_id=1, source_target_pairs={{0,24},{1,25},{2,26},{3,27},{4,28},{5,29},{6,30},{7,31},{8,0},{9,1... | collective-permute-start | bytes 884744 | tf_op jit(solution)/shard_map/ppermute | solution.py:141
  232.0 8.2 %collective-permute-done.32 = bf16[2,192,384]{2,1,0:T(8,128)(2,1)} collective-permute-done((bf16[2,192,384]{2,1,0:T(8,128)(2,1)}, bf16[2,192,384]{2,1,0:T(8,128)(2,1)}, u32[]{:S(2)}, u32[]{:S(2)}) %collective-permute-start.32) | collective-permute-done | bytes 294944 | tf_op jit(solution)/shard_map/ppermute | solution.py:141
  240.2 2.9 %collective-permute-done.33 = bf16[2,192,384]{2,1,0:T(8,128)(2,1)} collective-permute-done((bf16[2,192,384]{2,1,0:T(8,128)(2,1)}, bf16[2,192,384]{2,1,0:T(8,128)(2,1)}, u32[]{:S(2)}, u32[]{:S(2)}) %collective-permute-start.33) | collective-permute-done | bytes 294944 | tf_op jit(solution)/shard_map/ppermute | solution.py:141
  243.4 1.6 collective-permute-start.34
  246.5 2.3 collective-permute-start.36
  250.9 7.3 %restore.1 = (bf16[1024,768]{1,0:T(8,128)(2,1)}, bf16[1024,768]{1,0:T(8,128)(2,1)}) custom-call(s32[16]{0:T(128)} %get-tuple-element.265.plan, bf16[1024,768]{1,0:T(8,128)(2,1)} %get-tuple-element.371.outp_ref, bf16[1024,768]{1,0:T(8,128)(2,1)} %get-tuple-element.372.dxp_ref), custom_call_target="tpu_custom_call" | custom-call | flops 3300000000 | bytes 8000000 | tf_op jit(solution)/shard_map/restore/pallas_call | solution.py:1039
  261.4 3.4 %deliver_second.1 = (f32[96,3072]{1,0:T(8,128)}, f32[384,768]{1,0:T(8,128)}) custom-call(s32[4]{0:T(128)} %pad_add_fusion.at, bf16[2,2,192,384]{3,2,1,0:T(8,128)(2,1)} %copy-done.1, bf16[2,2,192,384]{3,2,1,0:T(8,128)(2,1)} %copy-done.7), custom_call_target="tpu_custom_call" | custom-call | bytes 4000000 | tf_op jit(solution)/shard_map/deliver_second/pallas_call | solution.py:1103
  265.2 1.6 collective-permute-done.40.other
  267.6 2.8 %deliver_first.1 = (f32[96,2304]{1,0:T(8,128)}, f32[96,768]{1,0:T(8,128)}, f32[96]{0:T(128)}, f32[96]{0:T(128)}, f32[288]{0:T(512)}, /*index=5*/f32[96]{0:T(128)...) custom-call(s32[4]{0:T(128)} %pad_add_fusion.at, bf16[2,2,104,384]{3,2,1,0:T(8,128)(2,1)} %copy-done.2, ...), custom_call_target="tpu_custom_call" | custom-call | bytes 2000000 | tf_op jit(solution)/shard_map/deliver_first/pallas_call | solution.py:1073
  (155 shorter events, 45.7 us)
Async XLA Ops:
  4.6 26.0 %collective-permute-start = (bf16[2,296,384]{2,1,0:T(8,128)(2,1)}, bf16[2,296,384]{2,1,0:T(8,128)(2,1)S(1)}, u32[]{:S(2)}, u32[]{:S(2)}) collective-permute-start(bf16[2,296,384]{2,1,0:T(8,128)(2,1)} %get-tuple-element.210), channel_id=1, source_target_pairs={{0,8},{1,9},{2,10},{3,11},{4,12},{5,13},{6,14},{7,15},{8,16},{9,17... | collective-permute-start | bytes 1363976 | tf_op jit(solution)/shard_map/ppermute | solution.py:141
  7.6 32.3 %collective-permute-start.6 = (bf16[2,2,296,384]{3,2,1,0:T(8,128)(2,1)}, bf16[2,2,296,384]{3,2,1,0:T(8,128)(2,1)}, u32[]{:S(2)}, u32[]{:S(2)}) collective-permute-start(bf16[2,2,296,384]{3,2,1,0:T(8,128)(2,1)} %get-tuple-element.225), channel_id=1, source_target_pairs={{0,4},{1,5},{2,6},{3,7},{4,0},{5,1},{6,2},{7,3},{8,12},{9,13},{10,... | collective-permute-start | bytes 2727944 | tf_op jit(solution)/shard_map/ppermute | solution.py:141
  9.1 14.6 %collective-permute-start.2 = (bf16[2,104,384]{2,1,0:T(8,128)(2,1)}, bf16[2,104,384]{2,1,0:T(8,128)(2,1)S(1)}, u32[]{:S(2)}, u32[]{:S(2)}) collective-permute-start(bf16[2,104,384]{2,1,0:T(8,128)(2,1)} %get-tuple-element.211), channel_id=1, source_target_pairs={{0,24},{1,25},{2,26},{3,27},{4,28},{5,29},{6,30},{7,31},{8,0},{9,1... | collective-permute-start | bytes 479240 | tf_op jit(solution)/shard_map/ppermute | solution.py:141
  11.3 19.2 %collective-permute-start.1 = (bf16[2,104,384]{2,1,0:T(8,128)(2,1)}, bf16[2,104,384]{2,1,0:T(8,128)(2,1)S(1)}, u32[]{:S(2)}, u32[]{:S(2)}) collective-permute-start(bf16[2,104,384]{2,1,0:T(8,128)(2,1)} %get-tuple-element.211), channel_id=1, source_target_pairs={{0,16},{1,17},{2,18},{3,19},{4,20},{5,21},{6,22},{7,23},{8,24},{9,... | collective-permute-start | bytes 479240 | tf_op jit(solution)/shard_map/ppermute | solution.py:141
  30.7 9.2 %collective-permute-start.5 = (bf16[2,192,384]{2,1,0:T(8,128)(2,1)}, bf16[2,192,384]{2,1,0:T(8,128)(2,1)S(1)}, u32[]{:S(2)}, u32[]{:S(2)}) collective-permute-start(bf16[2,192,384]{2,1,0:T(8,128)(2,1)} %get-tuple-element.242), channel_id=1, source_target_pairs={{0,24},{1,25},{2,26},{3,27},{4,28},{5,29},{6,30},{7,31},{8,0},{9,1... | collective-permute-start | bytes 884744 | tf_op jit(solution)/shard_map/ppermute | solution.py:141
  32.4 7.4 %collective-permute-start.4 = (bf16[3,104,384]{2,1,0:T(8,128)(2,1)S(1)}, bf16[3,104,384]{2,1,0:T(8,128)(2,1)S(1)}, u32[]{:S(2)}, u32[]{:S(2)}) collective-permute-start(bf16[3,104,384]{2,1,0:T(8,128)(2,1)S(1)} %pad_maximum_fusion.13), channel_id=1, source_target_pairs={{0,4},{1,5},{2,6},{3,7},{4,0},{5,1},{6,2},{7,3},{8,12},{9,13},{10,... | collective-permute-start | bytes 718856 | tf_op jit(solution)/shard_map/ppermute | solution.py:141
  41.3 22.1 %collective-permute-start.10 = (bf16[2,2,296,384]{3,2,1,0:T(8,128)(2,1)}, bf16[2,2,296,384]{3,2,1,0:T(8,128)(2,1)}, u32[]{:S(2)}, u32[]{:S(2)}) collective-permute-start(bf16[2,2,296,384]{3,2,1,0:T(8,128)(2,1)} %collective-permute-done.6.refs_9_.refs_8_), channel_id=1, source_target_pairs={{0,1},{1,0},{2,3},{3,2},{4,5},{5,4},{6,7},{7,6},{8,9},{9,8},{10,11... | collective-permute-start | bytes 2727944 | tf_op jit(solution)/shard_map/ppermute | solution.py:141
  41.4 21.9 %collective-permute-start.9 = (bf16[2,2,3,96,384]{4,3,2,1,0:T(8,128)(2,1)S(1)}, bf16[2,2,3,96,384]{4,3,2,1,0:T(8,128)(2,1)}, u32[]{:S(2)}, u32[]{:S(2)}) collective-permute-start(bf16[2,2,3,96,384]{4,3,2,1,0:T(8,128)(2,1)S(1)} %pad_maximum_fusion.refs_11_.refs_13_), channel_id=1, source_target_pairs={{0,1},{1,0},{2,3},{3,2},{4,5},{5,4},{6,7},{7,6},{8,9},{9,8},{10,11... | collective-permute-start | bytes 2654216 | tf_op jit(solution)/shard_map/ppermute | solution.py:141
  42.0 21.4 %collective-permute-start.7 = (bf16[20,48,384]{2,1,0:T(8,128)(2,1)}, bf16[20,48,384]{2,1,0:T(8,128)(2,1)S(1)}, u32[]{:S(2)}, u32[]{:S(2)}) collective-permute-start(bf16[20,48,384]{2,1,0:T(8,128)(2,1)} %pad_maximum_fusion.4), channel_id=1, source_target_pairs={{0,4},{1,5},{2,6},{3,7},{4,0},{5,1},{6,2},{7,3},{8,12},{9,13},{10,... | collective-permute-start | bytes 2211848 | tf_op jit(solution)/shard_map/ppermute | solution.py:141
  43.5 19.9 %collective-permute-start.8 = (bf16[20,48,384]{2,1,0:T(8,128)(2,1)S(1)}, bf16[20,48,384]{2,1,0:T(8,128)(2,1)S(1)}, u32[]{:S(2)}, u32[]{:S(2)}) collective-permute-start(bf16[20,48,384]{2,1,0:T(8,128)(2,1)S(1)} %pad_maximum_fusion.5), channel_id=1, source_target_pairs={{0,2},{1,3},{2,0},{3,1},{4,6},{5,7},{6,4},{7,5},{8,10},{9,11},{10,... | collective-permute-start | bytes 2211848 | tf_op jit(solution)/shard_map/ppermute | solution.py:141
  47.7 15.7 %collective-permute-start.11 = (bf16[2,192,384]{2,1,0:T(8,128)(2,1)}, bf16[2,192,384]{2,1,0:T(8,128)(2,1)S(1)}, u32[]{:S(2)}, u32[]{:S(2)}) collective-permute-start(bf16[2,192,384]{2,1,0:T(8,128)(2,1)} %get-tuple-element.242), channel_id=1, source_target_pairs={{0,16},{1,17},{2,18},{3,19},{4,20},{5,21},{6,22},{7,23},{8,24},{9,... | collective-permute-start | bytes 884744 | tf_op jit(solution)/shard_map/ppermute | solution.py:141
  63.7 6.6 %collective-permute-start.14 = (bf16[2,2,3,96,384]{4,3,2,1,0:T(8,128)(2,1)S(1)}, bf16[2,2,3,96,384]{4,3,2,1,0:T(8,128)(2,1)S(1)}, u32[]{:S(2)}, u32[]{:S(2)}) collective-permute-start(bf16[2,2,3,96,384]{4,3,2,1,0:T(8,128)(2,1)S(1)} %pad_maximum_fusion.1.refs_12_.refs_14_), channel_id=1, source_target_pairs={{0,1},{1,0},{2,3},{3,2},{4,5},{5,4},{6,7},{7,6},{8,9},{9,8},{10,11... | collective-permute-start | bytes 2654216 | tf_op jit(solution)/shard_map/ppermute | solution.py:141
  71.5 22.2 %collective-permute-start.17 = (bf16[2,3,192,384]{3,2,1,0:T(8,128)(2,1)S(1)}, bf16[2,3,192,384]{3,2,1,0:T(8,128)(2,1)S(1)}, u32[]{:S(2)}, u32[]{:S(2)}) collective-permute-start(bf16[2,3,192,384]{3,2,1,0:T(8,128)(2,1)S(1)} %pad_maximum_fusion.2.refs_10_), channel_id=1, source_target_pairs={{0,1},{1,0},{2,3},{3,2},{4,5},{5,4},{6,7},{7,6},{8,9},{9,8},{10,11... | collective-permute-start | bytes 2654216 | tf_op jit(solution)/shard_map/ppermute | solution.py:141
  71.6 22.1 %collective-permute-start.15 = (bf16[2,3,192,384]{3,2,1,0:T(8,128)(2,1)S(1)}, bf16[2,3,192,384]{3,2,1,0:T(8,128)(2,1)S(1)}, u32[]{:S(2)}, u32[]{:S(2)}) collective-permute-start(bf16[2,3,192,384]{3,2,1,0:T(8,128)(2,1)S(1)} %pad_maximum_fusion.2.refs_10_), channel_id=1, source_target_pairs={{0,4},{1,5},{2,6},{3,7},{4,0},{5,1},{6,2},{7,3},{8,12},{9,13},{10,... | collective-permute-start | bytes 2654216 | tf_op jit(solution)/shard_map/ppermute | solution.py:141
  72.4 21.4 %collective-permute-start.18 = (bf16[2,3,192,384]{3,2,1,0:T(8,128)(2,1)S(1)}, bf16[2,3,192,384]{3,2,1,0:T(8,128)(2,1)}, u32[]{:S(2)}, u32[]{:S(2)}) collective-permute-start(bf16[2,3,192,384]{3,2,1,0:T(8,128)(2,1)S(1)} %pad_maximum_fusion.3.refs_12_), channel_id=1, source_target_pairs={{0,1},{1,0},{2,3},{3,2},{4,5},{5,4},{6,7},{7,6},{8,9},{9,8},{10,11... | collective-permute-start | bytes 2654216 | tf_op jit(solution)/shard_map/ppermute | solution.py:141
  72.5 22.0 %collective-permute-start.16 = (bf16[2,3,192,384]{3,2,1,0:T(8,128)(2,1)S(1)}, bf16[2,3,192,384]{3,2,1,0:T(8,128)(2,1)}, u32[]{:S(2)}, u32[]{:S(2)}) collective-permute-start(bf16[2,3,192,384]{3,2,1,0:T(8,128)(2,1)S(1)} %pad_maximum_fusion.3.refs_12_), channel_id=1, source_target_pairs={{0,2},{1,3},{2,0},{3,1},{4,6},{5,7},{6,4},{7,5},{8,10},{9,11},{10,... | collective-permute-start | bytes 2654216 | tf_op jit(solution)/shard_map/ppermute | solution.py:141
  142.9 8.3 %collective-permute-start.21 = (bf16[32,192,384]{2,1,0:T(8,128)(2,1)}, bf16[32,192,384]{2,1,0:T(8,128)(2,1)}, u32[]{:S(2)}, u32[]{:S(2)}) collective-permute-start(bf16[32,192,384]{2,1,0:T(8,128)(2,1)} %get-tuple-element.297), channel_id=1, source_target_pairs={{0,1},{1,0},{2,3},{3,2},{4,5},{5,4},{6,7},{7,6},{8,9},{9,8},{10,11... | collective-permute-start | bytes 14155784 | tf_op jit(solution)/shard_map/ppermute | solution.py:141
  155.6 28.4 %collective-permute-start.22 = (bf16[8,192,384]{2,1,0:T(8,128)(2,1)}, bf16[8,192,384]{2,1,0:T(8,128)(2,1)S(1)}, u32[]{:S(2)}, u32[]{:S(2)}) collective-permute-start(bf16[8,192,384]{2,1,0:T(8,128)(2,1)} %get-tuple-element.305), channel_id=1, source_target_pairs={{0,4},{1,5},{2,6},{3,7},{4,0},{5,1},{6,2},{7,3},{8,12},{9,13},{10,... | collective-permute-start | bytes 3538952 | tf_op jit(solution)/shard_map/ppermute | solution.py:141
  156.9 28.1 %collective-permute-start.23 = (bf16[8,192,384]{2,1,0:T(8,128)(2,1)}, bf16[8,192,384]{2,1,0:T(8,128)(2,1)S(1)}, u32[]{:S(2)}, u32[]{:S(2)}) collective-permute-start(bf16[8,192,384]{2,1,0:T(8,128)(2,1)} %get-tuple-element.306), channel_id=1, source_target_pairs={{0,2},{1,3},{2,0},{3,1},{4,6},{5,7},{6,4},{7,5},{8,10},{9,11},{10,... | collective-permute-start | bytes 3538952 | tf_op jit(solution)/shard_map/ppermute | solution.py:141
  187.1 14.8 %collective-permute-start.24 = (bf16[4,192,384]{2,1,0:T(8,128)(2,1)S(1)}, bf16[4,192,384]{2,1,0:T(8,128)(2,1)}, u32[]{:S(2)}, u32[]{:S(2)}) collective-permute-start(bf16[4,192,384]{2,1,0:T(8,128)(2,1)S(1)} %get-tuple-element.320), channel_id=1, source_target_pairs={{0,2},{1,3},{2,0},{3,1},{4,6},{5,7},{6,4},{7,5},{8,10},{9,11},{10,... | collective-permute-start | bytes 1769480 | tf_op jit(solution)/shard_map/ppermute | solution.py:141
  188.6 14.2 %collective-permute-start.25 = (bf16[4,192,384]{2,1,0:T(8,128)(2,1)S(1)}, bf16[4,192,384]{2,1,0:T(8,128)(2,1)}, u32[]{:S(2)}, u32[]{:S(2)}) collective-permute-start(bf16[4,192,384]{2,1,0:T(8,128)(2,1)S(1)} %get-tuple-element.321), channel_id=1, source_target_pairs={{0,4},{1,5},{2,6},{3,7},{4,0},{5,1},{6,2},{7,3},{8,12},{9,13},{10,... | collective-permute-start | bytes 1769480 | tf_op jit(solution)/shard_map/ppermute | solution.py:141
  208.5 17.1 %collective-permute-start.27 = (bf16[8,104,384]{2,1,0:T(8,128)(2,1)S(1)}, bf16[8,104,384]{2,1,0:T(8,128)(2,1)S(1)}, u32[]{:S(2)}, u32[]{:S(2)}) collective-permute-start(bf16[8,104,384]{2,1,0:T(8,128)(2,1)S(1)} %get-tuple-element.339), channel_id=1, source_target_pairs={{0,4},{1,5},{2,6},{3,7},{4,0},{5,1},{6,2},{7,3},{8,12},{9,13},{10,... | collective-permute-start | bytes 1916936 | tf_op jit(solution)/shard_map/ppermute | solution.py:141
  209.3 16.5 %collective-permute-start.28 = (bf16[8,104,384]{2,1,0:T(8,128)(2,1)S(1)}, bf16[8,104,384]{2,1,0:T(8,128)(2,1)S(1)}, u32[]{:S(2)}, u32[]{:S(2)}) collective-permute-start(bf16[8,104,384]{2,1,0:T(8,128)(2,1)S(1)} %get-tuple-element.340), channel_id=1, source_target_pairs={{0,2},{1,3},{2,0},{3,1},{4,6},{5,7},{6,4},{7,5},{8,10},{9,11},{10,... | collective-permute-start | bytes 1916936 | tf_op jit(solution)/shard_map/ppermute | solution.py:141
  209.8 15.8 %collective-permute-start.29 = (bf16[2,192,384]{2,1,0:T(8,128)(2,1)S(1)}, bf16[2,192,384]{2,1,0:T(8,128)(2,1)S(1)}, u32[]{:S(2)}, u32[]{:S(2)}) collective-permute-start(bf16[2,192,384]{2,1,0:T(8,128)(2,1)S(1)} %pad_maximum_fusion.11), channel_id=1, source_target_pairs={{0,16},{1,17},{2,18},{3,19},{4,20},{5,21},{6,22},{7,23},{8,24},{9,... | collective-permute-start | bytes 884744 | tf_op jit(solution)/shard_map/ppermute | solution.py:141
  226.3 16.9 %collective-permute-start.30 = (bf16[4,104,384]{2,1,0:T(8,128)(2,1)S(1)}, bf16[4,104,384]{2,1,0:T(8,128)(2,1)S(1)}, u32[]{:S(2)}, u32[]{:S(2)}) collective-permute-start(bf16[4,104,384]{2,1,0:T(8,128)(2,1)S(1)} %get-tuple-element.350), channel_id=1, source_target_pairs={{0,2},{1,3},{2,0},{3,1},{4,6},{5,7},{6,4},{7,5},{8,10},{9,11},{10,... | collective-permute-start | bytes 958472 | tf_op jit(solution)/shard_map/ppermute | solution.py:141
  226.8 16.4 %collective-permute-start.31 = (bf16[4,104,384]{2,1,0:T(8,128)(2,1)S(1)}, bf16[4,104,384]{2,1,0:T(8,128)(2,1)S(1)}, u32[]{:S(2)}, u32[]{:S(2)}) collective-permute-start(bf16[4,104,384]{2,1,0:T(8,128)(2,1)S(1)} %get-tuple-element.351), channel_id=1, source_target_pairs={{0,4},{1,5},{2,6},{3,7},{4,0},{5,1},{6,2},{7,3},{8,12},{9,13},{10,... | collective-permute-start | bytes 958472 | tf_op jit(solution)/shard_map/ppermute | solution.py:141
  228.2 12.1 %collective-permute-start.32 = (bf16[2,192,384]{2,1,0:T(8,128)(2,1)}, bf16[2,192,384]{2,1,0:T(8,128)(2,1)}, u32[]{:S(2)}, u32[]{:S(2)}) collective-permute-start(bf16[2,192,384]{2,1,0:T(8,128)(2,1)} %pad_maximum_fusion.10), channel_id=1, source_target_pairs={{0,8},{1,9},{2,10},{3,11},{4,12},{5,13},{6,14},{7,15},{8,16},{9,17... | collective-permute-start | bytes 884744 | tf_op jit(solution)/shard_map/ppermute | solution.py:141
  228.2 15.0 %collective-permute-start.33 = (bf16[2,192,384]{2,1,0:T(8,128)(2,1)}, bf16[2,192,384]{2,1,0:T(8,128)(2,1)}, u32[]{:S(2)}, u32[]{:S(2)}) collective-permute-start(bf16[2,192,384]{2,1,0:T(8,128)(2,1)} %pad_maximum_fusion.12), channel_id=1, source_target_pairs={{0,24},{1,25},{2,26},{3,27},{4,28},{5,29},{6,30},{7,31},{8,0},{9,1... | collective-permute-start | bytes 884744 | tf_op jit(solution)/shard_map/ppermute | solution.py:141
  243.4 14.8 %collective-permute-start.34 = (bf16[2,104,384]{2,1,0:T(8,128)(2,1)S(1)}, bf16[2,104,384]{2,1,0:T(8,128)(2,1)S(1)}, u32[]{:S(2)}, u32[]{:S(2)}) collective-permute-start(bf16[2,104,384]{2,1,0:T(8,128)(2,1)S(1)} %pad_maximum_fusion.15), channel_id=1, source_target_pairs={{0,8},{1,9},{2,10},{3,11},{4,12},{5,13},{6,14},{7,15},{8,16},{9,17... | collective-permute-start | bytes 479240 | tf_op jit(solution)/shard_map/ppermute | solution.py:141
  245.0 13.2 %collective-permute-start.35 = (bf16[2,104,384]{2,1,0:T(8,128)(2,1)S(1)}, bf16[2,104,384]{2,1,0:T(8,128)(2,1)S(1)}, u32[]{:S(2)}, u32[]{:S(2)}) collective-permute-start(bf16[2,104,384]{2,1,0:T(8,128)(2,1)S(1)} %pad_maximum_fusion.16), channel_id=1, source_target_pairs={{0,16},{1,17},{2,18},{3,19},{4,20},{5,21},{6,22},{7,23},{8,24},{9,... | collective-permute-start | bytes 479240 | tf_op jit(solution)/shard_map/ppermute | solution.py:141
  246.5 11.7 %collective-permute-start.36 = (bf16[2,104,384]{2,1,0:T(8,128)(2,1)S(1)}, bf16[2,104,384]{2,1,0:T(8,128)(2,1)S(1)}, u32[]{:S(2)}, u32[]{:S(2)}) collective-permute-start(bf16[2,104,384]{2,1,0:T(8,128)(2,1)S(1)} %pad_maximum_fusion.17), channel_id=1, source_target_pairs={{0,24},{1,25},{2,26},{3,27},{4,28},{5,29},{6,30},{7,31},{8,0},{9,1... | collective-permute-start | bytes 479240 | tf_op jit(solution)/shard_map/ppermute | solution.py:141
  250.0 8.2 %collective-permute-start.37 = (bf16[2,192,384]{2,1,0:T(8,128)(2,1)S(1)}, bf16[2,192,384]{2,1,0:T(8,128)(2,1)S(1)}, u32[]{:S(2)}, u32[]{:S(2)}) collective-permute-start(bf16[2,192,384]{2,1,0:T(8,128)(2,1)S(1)} %fusion.2), channel_id=1, source_target_pairs={{0,2},{1,3},{2,0},{3,1},{4,6},{5,7},{6,4},{7,5},{8,10},{9,11},{10,... | collective-permute-start | bytes 884744 | tf_op jit(solution)/shard_map/ppermute | solution.py:141
  (27 other events, 155.1 us)
